TPU v7x, 256 devices: a whole 4x4x8 slice. The times are simulated.
256 devices in a mesh: section: 4 (over y), dp: 16 (over x, z_lo, core), expert: 4 (over z_hi).
Axes of the slice: x: 4, y: 4, z: 8 (z_hi: 4, z_lo: 2; z = z_hi * 2 + z_lo), core: 2. Of those that a mesh axis runs over, the one named last changes fastest.
Arguments:
- init_state: bfloat16 [4, 2048, 5280], P(None, ('dp', 'expert')), may hold values from -5 to 5
- inject: bfloat16 [4, 2048, 5280], P(None, ('dp', 'expert')), may hold values from -24 to 24
- routes: int32 [2, 4, 4, 2048, 1], P(None, 'section', None, ('dp', 'expert')), may hold values from 0 to 3; in each aligned block of 32 rows (0 to 31, 32 to 63, ..., all dimensions but the last counted through in order) at most 12 rows name the same one
- norm_gain: float32 [4, 5280], P('section'), may hold values from 0.25 to 1.75
- router: bfloat16 [4, 4, 5280], P('section'), may hold values from -0.078125 to 0.078125
- w_up: bfloat16 [4, 4, 5280, 768], P('section', 'expert', 'dp'), may hold values from -0.078125 to 0.078125
- w_down: bfloat16 [4, 4, 768, 5280], P('section', 'expert', None, 'dp'), may hold values from -0.21875 to 0.21875
Outputs:
- final_state: bfloat16 [4, 2048, 5280], P('section', ('dp', 'expert'))
Inputs may be any that keep to these rules, and one draw needn't show every extreme that they name: In each aligned block of 32 tokens of routes, no expert is named by more than 12 tokens.
All inputs are finite; a program needn't handle non-finite values.
Results may differ from a plain program's by a relative error of at most 0.014.
Values may be sent and summed in bfloat16 or wider, within the bound.
A program may use at most 128 MiB of HBM per device.

v0:
```python
import jax
import jax.numpy as jnp
from jax import lax
from jax.sharding import PartitionSpec as P

RECUR = 2
CAP = 12


def shifted(block, axis, distance):
    devices = range(lax.axis_size(axis))
    route = [((i - distance) % len(devices), i) for i in devices]
    return lax.ppermute(block, axis, route)


def normalize(current, gain_row):
    as_float = current.astype(jnp.float32)
    inv_rms = lax.rsqrt(jnp.mean(as_float * as_float, axis=-1, keepdims=True) + 1e-05)
    return (as_float * inv_rms * gain_row).astype(jnp.bfloat16)


def expert_rows(item_rows, w_first, w_second):
    extent = item_rows.shape
    flat_rows = item_rows.reshape(-1, extent[-1])
    hidden = jax.nn.gelu(jnp.dot(flat_rows, w_first, preferred_element_type=jnp.float32)).astype(
        jnp.bfloat16
    )
    result = jnp.dot(hidden, w_second, preferred_element_type=jnp.float32).astype(jnp.bfloat16)
    return result.reshape(extent)


def whole_round(buffer, w_first, w_second):
    processed = expert_rows(
        lax.all_to_all(buffer, "expert", split_axis=0, concat_axis=0, tiled=True), w_first, w_second
    )
    return lax.all_to_all(processed, "expert", split_axis=0, concat_axis=0, tiled=True)


def core_block(current, gain_row, router_rows, w_first, w_second, assign):
    tokens = current.shape[0]
    experts = router_rows.shape[0]
    normed = normalize(current, gain_row)
    logits = jnp.dot(normed, router_rows.T, preferred_element_type=jnp.float32)
    labels = lax.broadcasted_iota(jnp.int32, (tokens, experts), 1)
    onehot = (assign[:, None] == labels).astype(jnp.float32)
    gate_value = jax.nn.sigmoid(jnp.sum(onehot * logits, axis=-1))
    earlier = (
        lax.broadcasted_iota(jnp.int32, (tokens, tokens), 0)
        > lax.broadcasted_iota(jnp.int32, (tokens, tokens), 1)
    ).astype(jnp.float32)
    counts = jnp.dot(earlier, onehot, preferred_element_type=jnp.float32)
    slot_index = jnp.sum(onehot * counts, axis=-1).astype(jnp.int32)
    target = assign * CAP + slot_index
    places = (
        lax.broadcasted_iota(jnp.int32, (experts * CAP, tokens), 0) == target[None, :]
    ).astype(jnp.bfloat16)
    buffer = (
        jnp.dot(places, normed, preferred_element_type=jnp.float32)
        .astype(jnp.bfloat16)
        .reshape(experts, CAP, -1)
    )
    returned = whole_round(buffer, w_first, w_second)
    flat_back = returned.reshape(experts * CAP, -1)
    expert_out = jnp.einsum("st,sd->td", places, flat_back, preferred_element_type=jnp.float32)
    updated = current.astype(jnp.float32) + gate_value[:, None] * expert_out
    return updated.astype(jnp.bfloat16)


def body(init_state, inject, routes, norm_gain, router, w_up, w_down):
    sections = lax.axis_size("section")
    section_index = lax.axis_index("section")
    up_all, down_all = (
        lax.all_gather(w_up, "dp", axis=2, tiled=True),
        lax.all_gather(w_down, "dp", axis=3, tiled=True),
    )
    w_first = up_all[0, 0]
    w_second = down_all[0, 0]
    gain_row = norm_gain[0]
    router_rows = router[0]
    tokens = init_state.shape[1]
    active_span = sections * RECUR
    total_steps = active_span + sections - 1

    def advance(moment, hidden_state):
        offset = moment - section_index
        is_live = (offset >= 0) & (offset < active_span)
        clipped = jnp.clip(offset, 0, active_span - 1)
        loop_round = clipped // sections
        entry_slot = clipped % sections
        micro_idx = jnp.mod(sections - 2 - entry_slot, sections)
        initial = lax.dynamic_index_in_dim(init_state, micro_idx, 0, keepdims=False)
        injected_row = lax.dynamic_index_in_dim(inject, micro_idx, 0, keepdims=False)
        incoming = jnp.where(loop_round == 0, initial, hidden_state)
        injected = (incoming.astype(jnp.float32) + injected_row.astype(jnp.float32)).astype(
            jnp.bfloat16
        )
        entering = is_live & (section_index == 0)
        current = jnp.where(entering, injected, hidden_state)
        assign = lax.dynamic_slice(
            routes, (loop_round, 0, micro_idx, 0, 0), (1, 1, 1, tokens, 1)
        ).reshape(tokens)
        result = core_block(current, gain_row, router_rows, w_first, w_second, assign)
        return jnp.where(is_live, result, hidden_state)

    def advance_one(moment, hidden_state):
        arrived = shifted(hidden_state, "section", 1)
        return advance(moment, arrived)

    hidden_state = jnp.zeros(init_state.shape[1:], jnp.bfloat16)
    hidden_state = advance(0, hidden_state)
    hidden_state = lax.fori_loop(1, total_steps, advance_one, hidden_state)
    return hidden_state[None]


def solution(mesh):
    return jax.shard_map(
        body,
        mesh=mesh,
        in_specs=(
            P(None, ("dp", "expert"), None),
            P(None, ("dp", "expert"), None),
            P(None, "section", None, ("dp", "expert"), None),
            P("section", None),
            P("section", None, None),
            P("section", "expert", "dp", None),
            P("section", "expert", None, "dp"),
        ),
        out_specs=P("section", ("dp", "expert"), None),
        check_vma=False,
    )
```

profile of v0, /device:TPU:2, one launch (start us, length us, event | category | flops | bytes accessed | tf_op | source)
XLA Modules:
  0.0 900.0 jit_solution(12760272385883102140)
XLA Ops:
  16.4 28.7 %all_to_all.36 = bf16[4,12,5280]{2,1,0:T(8,128)(2,1)S(1)} all-to-all(bf16[4,12,5280]{2,1,0:T(8,128)(2,1)S(1)} %reshape.144), channel_id=1, replica_groups=mesh['section'=4,'dp'=16,'expert'=4] {'expert'}, dimensions={0} | all-to-all | bytes 1013760 | tf_op jit(solution)/shard_map/all_to_all | solution.py:34
  45.4 67.2 %all-gather.3.cloned.1.call-done = bf16[1,1,5280,768]{3,1,0,2:T(2,128)(2,1)} async-done(((bf16[1,1,330,768]{3,1,0,2:T(2,128)(2,1)}), bf16[1,1,5280,768]{3,1,0,2:T(2,128)(2,1)}) %all-gather.3.cloned.1.call-update) | async-done | bytes 8110096 | tf_op jit(solution)/shard_map/all_gather | solution.py:73
  112.5 11.5 %copy.26 = bf16[1,1,5280,768]{3,2,0,1:T(8,128)(2,1)} copy(bf16[1,1,5280,768]{3,1,0,2:T(2,128)(2,1)} %all-gather.3.cloned.1.call-done) | data formatting | bytes 16220160
  124.1 88.0 %all-gather.5.cloned.1.call-done = bf16[1,1,768,5280]{2,1,0,3:T(2,128)(2,1)} async-done(((bf16[1,1,768,330]{2,1,0,3:T(2,128)(2,1)}), bf16[1,1,768,5280]{2,1,0,3:T(2,128)(2,1)}) %all-gather.5.cloned.1.call-update) | async-done | bytes 8110096 | tf_op jit(solution)/shard_map/all_gather | solution.py:74
  212.1 12.2 %fusion.36 = bf16[48,5280]{1,0:T(8,128)(2,1)S(1)} fusion(bf16[1,1,768,5280]{2,1,0,3:T(2,128)(2,1)} %all-gather.5.cloned.1.call-done, bf16[48,5280]{1,0:T(8,128)(2,1)S(1)} %reshape.145, bf16[5280,768]{1,0:T(8,128)(2,1)} %bitcast.70), kind=kOutput, calls=%fused_computation.51 | convolution fusion | flops 779152896 | bytes 17233920 | tf_op jit(solution)/shard_map/dot_general | solution.py:28
  225.2 7.0 all-to-all-start.3
  232.6 34.5 %copy.18 = bf16[1,1,768,5280]{3,2,0,1:T(8,128)(2,1)} copy(bf16[1,1,768,5280]{2,1,0,3:T(2,128)(2,1)} %all-gather.5.cloned.1.call-done) | data formatting | bytes 16220160
  267.7 624.8 %while.15 = (s32[]{:T(128)}, bf16[32,5280]{1,0:T(8,128)(2,1)S(1)}, s32[]{:T(128)}, pred[]{:T(512)}, bf16[4,32,5280]{2,1,0:T(8,128)(2,1)}, /*index=5*/bf16[4,32,5...) while((s32[]{:T(128)}, bf16[32,5280]{1,0:T(8,128)(2,1)S(1)}, ...), condition=%wide.region_7.8_spmd, body=%wide.region_3.7_spmd.sunk | while | flops 816928896 | bytes 29722380 | solution.py:111
  270.8 8.1 collective-permute-done
  280.8 26.1 %all_to_all.37 = bf16[4,12,5280]{2,1,0:T(8,128)(2,1)S(1)} all-to-all(bf16[4,12,5280]{2,1,0:T(8,128)(2,1)S(1)} %reshape.159), channel_id=1, replica_groups=mesh['section'=4,'dp'=16,'expert'=4] {'expert'}, dimensions={0} | all-to-all | bytes 1013760 | tf_op jit(solution)/shard_map/while/body/eval_jaxpr/all_to_all | solution.py:34
  307.2 9.1 %convolution_convert_fusion.6 = bf16[48,5280]{1,0:T(8,128)(2,1)S(1)} fusion(bf16[768,5280]{1,0:T(8,128)(2,1)} %get-tuple-element.426, bf16[48,5280]{1,0:T(8,128)(2,1)S(1)} %reshape.160, bf16[5280,768]{1,0:T(8,128)(2,1)} %get-tuple-element.425), kind=kOutput, calls=%fused_computation.clone.1 | convolution fusion | flops 779152896 | bytes 17233920 | tf_op jit(solution)/shard_map/while/body/eval_jaxpr/dot_general | solution.py:28
  321.1 17.1 %all-to-all-done.1 = bf16[4,12,5280]{2,1,0:T(8,128)(2,1)S(1)} async-done(((bf16[4,12,5280]{2,1,0:T(8,128)(2,1)}), bf16[4,12,5280]{2,1,0:T(8,128)(2,1)S(1)}, u32[]{:S(2)}, u32[]{:S(2)}) %all-to-all-start.1) | async-done | bytes 506912 | tf_op jit(solution)/shard_map/while/body/eval_jaxpr/all_to_all | solution.py:36
  340.6 6.7 collective-permute-done
  349.2 20.9 %all_to_all.37 = bf16[4,12,5280]{2,1,0:T(8,128)(2,1)S(1)} all-to-all(bf16[4,12,5280]{2,1,0:T(8,128)(2,1)S(1)} %reshape.159), channel_id=1, replica_groups=mesh['section'=4,'dp'=16,'expert'=4] {'expert'}, dimensions={0} | all-to-all | bytes 1013760 | tf_op jit(solution)/shard_map/while/body/eval_jaxpr/all_to_all | solution.py:34
  370.3 9.1 %convolution_convert_fusion.6 = bf16[48,5280]{1,0:T(8,128)(2,1)S(1)} fusion(bf16[768,5280]{1,0:T(8,128)(2,1)} %get-tuple-element.426, bf16[48,5280]{1,0:T(8,128)(2,1)S(1)} %reshape.160, bf16[5280,768]{1,0:T(8,128)(2,1)} %get-tuple-element.425), kind=kOutput, calls=%fused_computation.clone.1 | convolution fusion | flops 779152896 | bytes 17233920 | tf_op jit(solution)/shard_map/while/body/eval_jaxpr/dot_general | solution.py:28
  384.2 13.0 %all-to-all-done.1 = bf16[4,12,5280]{2,1,0:T(8,128)(2,1)S(1)} async-done(((bf16[4,12,5280]{2,1,0:T(8,128)(2,1)}), bf16[4,12,5280]{2,1,0:T(8,128)(2,1)S(1)}, u32[]{:S(2)}, u32[]{:S(2)}) %all-to-all-start.1) | async-done | bytes 506912 | tf_op jit(solution)/shard_map/while/body/eval_jaxpr/all_to_all | solution.py:36
  399.5 6.9 collective-permute-done
  408.2 20.2 %all_to_all.37 = bf16[4,12,5280]{2,1,0:T(8,128)(2,1)S(1)} all-to-all(bf16[4,12,5280]{2,1,0:T(8,128)(2,1)S(1)} %reshape.159), channel_id=1, replica_groups=mesh['section'=4,'dp'=16,'expert'=4] {'expert'}, dimensions={0} | all-to-all | bytes 1013760 | tf_op jit(solution)/shard_map/while/body/eval_jaxpr/all_to_all | solution.py:34
  428.6 9.1 %convolution_convert_fusion.6 = bf16[48,5280]{1,0:T(8,128)(2,1)S(1)} fusion(bf16[768,5280]{1,0:T(8,128)(2,1)} %get-tuple-element.426, bf16[48,5280]{1,0:T(8,128)(2,1)S(1)} %reshape.160, bf16[5280,768]{1,0:T(8,128)(2,1)} %get-tuple-element.425), kind=kOutput, calls=%fused_computation.clone.1 | convolution fusion | flops 779152896 | bytes 17233920 | tf_op jit(solution)/shard_map/while/body/eval_jaxpr/dot_general | solution.py:28
  438.8 5.6 all-to-all-start.1
  444.7 17.0 %all-to-all-done.1 = bf16[4,12,5280]{2,1,0:T(8,128)(2,1)S(1)} async-done(((bf16[4,12,5280]{2,1,0:T(8,128)(2,1)}), bf16[4,12,5280]{2,1,0:T(8,128)(2,1)S(1)}, u32[]{:S(2)}, u32[]{:S(2)}) %all-to-all-start.1) | async-done | bytes 506912 | tf_op jit(solution)/shard_map/while/body/eval_jaxpr/all_to_all | solution.py:36
  463.9 6.9 collective-permute-done
  472.7 23.2 %all_to_all.37 = bf16[4,12,5280]{2,1,0:T(8,128)(2,1)S(1)} all-to-all(bf16[4,12,5280]{2,1,0:T(8,128)(2,1)S(1)} %reshape.159), channel_id=1, replica_groups=mesh['section'=4,'dp'=16,'expert'=4] {'expert'}, dimensions={0} | all-to-all | bytes 1013760 | tf_op jit(solution)/shard_map/while/body/eval_jaxpr/all_to_all | solution.py:34
  496.2 9.1 %convolution_convert_fusion.6 = bf16[48,5280]{1,0:T(8,128)(2,1)S(1)} fusion(bf16[768,5280]{1,0:T(8,128)(2,1)} %get-tuple-element.426, bf16[48,5280]{1,0:T(8,128)(2,1)S(1)} %reshape.160, bf16[5280,768]{1,0:T(8,128)(2,1)} %get-tuple-element.425), kind=kOutput, calls=%fused_computation.clone.1 | convolution fusion | flops 779152896 | bytes 17233920 | tf_op jit(solution)/shard_map/while/body/eval_jaxpr/dot_general | solution.py:28
  511.5 19.8 %all-to-all-done.1 = bf16[4,12,5280]{2,1,0:T(8,128)(2,1)S(1)} async-done(((bf16[4,12,5280]{2,1,0:T(8,128)(2,1)}), bf16[4,12,5280]{2,1,0:T(8,128)(2,1)S(1)}, u32[]{:S(2)}, u32[]{:S(2)}) %all-to-all-start.1) | async-done | bytes 506912 | tf_op jit(solution)/shard_map/while/body/eval_jaxpr/all_to_all | solution.py:36
  533.6 6.9 collective-permute-done
  542.4 22.6 %all_to_all.37 = bf16[4,12,5280]{2,1,0:T(8,128)(2,1)S(1)} all-to-all(bf16[4,12,5280]{2,1,0:T(8,128)(2,1)S(1)} %reshape.159), channel_id=1, replica_groups=mesh['section'=4,'dp'=16,'expert'=4] {'expert'}, dimensions={0} | all-to-all | bytes 1013760 | tf_op jit(solution)/shard_map/while/body/eval_jaxpr/all_to_all | solution.py:34
  565.2 9.1 %convolution_convert_fusion.6 = bf16[48,5280]{1,0:T(8,128)(2,1)S(1)} fusion(bf16[768,5280]{1,0:T(8,128)(2,1)} %get-tuple-element.426, bf16[48,5280]{1,0:T(8,128)(2,1)S(1)} %reshape.160, bf16[5280,768]{1,0:T(8,128)(2,1)} %get-tuple-element.425), kind=kOutput, calls=%fused_computation.clone.1 | convolution fusion | flops 779152896 | bytes 17233920 | tf_op jit(solution)/shard_map/while/body/eval_jaxpr/dot_general | solution.py:28
  579.1 14.2 %all-to-all-done.1 = bf16[4,12,5280]{2,1,0:T(8,128)(2,1)S(1)} async-done(((bf16[4,12,5280]{2,1,0:T(8,128)(2,1)}), bf16[4,12,5280]{2,1,0:T(8,128)(2,1)S(1)}, u32[]{:S(2)}, u32[]{:S(2)}) %all-to-all-start.1) | async-done | bytes 506912 | tf_op jit(solution)/shard_map/while/body/eval_jaxpr/all_to_all | solution.py:36
  595.6 6.9 collective-permute-done
  604.4 19.0 %all_to_all.37 = bf16[4,12,5280]{2,1,0:T(8,128)(2,1)S(1)} all-to-all(bf16[4,12,5280]{2,1,0:T(8,128)(2,1)S(1)} %reshape.159), channel_id=1, replica_groups=mesh['section'=4,'dp'=16,'expert'=4] {'expert'}, dimensions={0} | all-to-all | bytes 1013760 | tf_op jit(solution)/shard_map/while/body/eval_jaxpr/all_to_all | solution.py:34
  623.7 9.1 %convolution_convert_fusion.6 = bf16[48,5280]{1,0:T(8,128)(2,1)S(1)} fusion(bf16[768,5280]{1,0:T(8,128)(2,1)} %get-tuple-element.426, bf16[48,5280]{1,0:T(8,128)(2,1)S(1)} %reshape.160, bf16[5280,768]{1,0:T(8,128)(2,1)} %get-tuple-element.425), kind=kOutput, calls=%fused_computation.clone.1 | convolution fusion | flops 779152896 | bytes 17233920 | tf_op jit(solution)/shard_map/while/body/eval_jaxpr/dot_general | solution.py:28
  637.6 13.0 %all-to-all-done.1 = bf16[4,12,5280]{2,1,0:T(8,128)(2,1)S(1)} async-done(((bf16[4,12,5280]{2,1,0:T(8,128)(2,1)}), bf16[4,12,5280]{2,1,0:T(8,128)(2,1)S(1)}, u32[]{:S(2)}, u32[]{:S(2)}) %all-to-all-start.1) | async-done | bytes 506912 | tf_op jit(solution)/shard_map/while/body/eval_jaxpr/all_to_all | solution.py:36
  652.8 6.9 collective-permute-done
  661.6 18.5 %all_to_all.37 = bf16[4,12,5280]{2,1,0:T(8,128)(2,1)S(1)} all-to-all(bf16[4,12,5280]{2,1,0:T(8,128)(2,1)S(1)} %reshape.159), channel_id=1, replica_groups=mesh['section'=4,'dp'=16,'expert'=4] {'expert'}, dimensions={0} | all-to-all | bytes 1013760 | tf_op jit(solution)/shard_map/while/body/eval_jaxpr/all_to_all | solution.py:34
  680.3 9.1 %convolution_convert_fusion.6 = bf16[48,5280]{1,0:T(8,128)(2,1)S(1)} fusion(bf16[768,5280]{1,0:T(8,128)(2,1)} %get-tuple-element.426, bf16[48,5280]{1,0:T(8,128)(2,1)S(1)} %reshape.160, bf16[5280,768]{1,0:T(8,128)(2,1)} %get-tuple-element.425), kind=kOutput, calls=%fused_computation.clone.1 | convolution fusion | flops 779152896 | bytes 17233920 | tf_op jit(solution)/shard_map/while/body/eval_jaxpr/dot_general | solution.py:28
  694.9 13.2 %all-to-all-done.1 = bf16[4,12,5280]{2,1,0:T(8,128)(2,1)S(1)} async-done(((bf16[4,12,5280]{2,1,0:T(8,128)(2,1)}), bf16[4,12,5280]{2,1,0:T(8,128)(2,1)S(1)}, u32[]{:S(2)}, u32[]{:S(2)}) %all-to-all-start.1) | async-done | bytes 506912 | tf_op jit(solution)/shard_map/while/body/eval_jaxpr/all_to_all | solution.py:36
  710.3 6.9 collective-permute-done
  719.1 30.5 %all_to_all.37 = bf16[4,12,5280]{2,1,0:T(8,128)(2,1)S(1)} all-to-all(bf16[4,12,5280]{2,1,0:T(8,128)(2,1)S(1)} %reshape.159), channel_id=1, replica_groups=mesh['section'=4,'dp'=16,'expert'=4] {'expert'}, dimensions={0} | all-to-all | bytes 1013760 | tf_op jit(solution)/shard_map/while/body/eval_jaxpr/all_to_all | solution.py:34
  749.9 9.1 %convolution_convert_fusion.6 = bf16[48,5280]{1,0:T(8,128)(2,1)S(1)} fusion(bf16[768,5280]{1,0:T(8,128)(2,1)} %get-tuple-element.426, bf16[48,5280]{1,0:T(8,128)(2,1)S(1)} %reshape.160, bf16[5280,768]{1,0:T(8,128)(2,1)} %get-tuple-element.425), kind=kOutput, calls=%fused_computation.clone.1 | convolution fusion | flops 779152896 | bytes 17233920 | tf_op jit(solution)/shard_map/while/body/eval_jaxpr/dot_general | solution.py:28
  763.8 15.4 %all-to-all-done.1 = bf16[4,12,5280]{2,1,0:T(8,128)(2,1)S(1)} async-done(((bf16[4,12,5280]{2,1,0:T(8,128)(2,1)}), bf16[4,12,5280]{2,1,0:T(8,128)(2,1)S(1)}, u32[]{:S(2)}, u32[]{:S(2)}) %all-to-all-start.1) | async-done | bytes 506912 | tf_op jit(solution)/shard_map/while/body/eval_jaxpr/all_to_all | solution.py:36
  781.5 6.9 collective-permute-done
  790.2 20.3 %all_to_all.37 = bf16[4,12,5280]{2,1,0:T(8,128)(2,1)S(1)} all-to-all(bf16[4,12,5280]{2,1,0:T(8,128)(2,1)S(1)} %reshape.159), channel_id=1, replica_groups=mesh['section'=4,'dp'=16,'expert'=4] {'expert'}, dimensions={0} | all-to-all | bytes 1013760 | tf_op jit(solution)/shard_map/while/body/eval_jaxpr/all_to_all | solution.py:34
  810.8 9.1 %convolution_convert_fusion.6 = bf16[48,5280]{1,0:T(8,128)(2,1)S(1)} fusion(bf16[768,5280]{1,0:T(8,128)(2,1)} %get-tuple-element.426, bf16[48,5280]{1,0:T(8,128)(2,1)S(1)} %reshape.160, bf16[5280,768]{1,0:T(8,128)(2,1)} %get-tuple-element.425), kind=kOutput, calls=%fused_computation.clone.1 | convolution fusion | flops 779152896 | bytes 17233920 | tf_op jit(solution)/shard_map/while/body/eval_jaxpr/dot_general | solution.py:28
  824.7 12.0 %all-to-all-done.1 = bf16[4,12,5280]{2,1,0:T(8,128)(2,1)S(1)} async-done(((bf16[4,12,5280]{2,1,0:T(8,128)(2,1)}), bf16[4,12,5280]{2,1,0:T(8,128)(2,1)S(1)}, u32[]{:S(2)}, u32[]{:S(2)}) %all-to-all-start.1) | async-done | bytes 506912 | tf_op jit(solution)/shard_map/while/body/eval_jaxpr/all_to_all | solution.py:36
  848.0 18.7 %all_to_all.37 = bf16[4,12,5280]{2,1,0:T(8,128)(2,1)S(1)} all-to-all(bf16[4,12,5280]{2,1,0:T(8,128)(2,1)S(1)} %reshape.159), channel_id=1, replica_groups=mesh['section'=4,'dp'=16,'expert'=4] {'expert'}, dimensions={0} | all-to-all | bytes 1013760 | tf_op jit(solution)/shard_map/while/body/eval_jaxpr/all_to_all | solution.py:34
  866.9 9.1 %convolution_convert_fusion.6 = bf16[48,5280]{1,0:T(8,128)(2,1)S(1)} fusion(bf16[768,5280]{1,0:T(8,128)(2,1)} %get-tuple-element.426, bf16[48,5280]{1,0:T(8,128)(2,1)S(1)} %reshape.160, bf16[5280,768]{1,0:T(8,128)(2,1)} %get-tuple-element.425), kind=kOutput, calls=%fused_computation.clone.1 | convolution fusion | flops 779152896 | bytes 17233920 | tf_op jit(solution)/shard_map/while/body/eval_jaxpr/dot_general | solution.py:28
  880.8 11.1 %all-to-all-done.1 = bf16[4,12,5280]{2,1,0:T(8,128)(2,1)S(1)} async-done(((bf16[4,12,5280]{2,1,0:T(8,128)(2,1)}), bf16[4,12,5280]{2,1,0:T(8,128)(2,1)S(1)}, u32[]{:S(2)}, u32[]{:S(2)}) %all-to-all-start.1) | async-done | bytes 506912 | tf_op jit(solution)/shard_map/while/body/eval_jaxpr/all_to_all | solution.py:36
  (187 shorter events, 110.5 us)
Async XLA Ops:
  6.5 106.0 %all-gather.3.cloned.1.call-start = ((), (), s32[]{:S(2)}) async-start(), calls=%async_computation.4 | async-start | bytes 17233920 | tf_op jit(solution)/shard_map/all_gather | solution.py:73
  9.3 202.7 %all-gather.5.cloned.1.call-start = ((), (), s32[]{:S(2)}) async-start(), calls=%async_computation.5 | async-start | bytes 17233920 | tf_op jit(solution)/shard_map/all_gather | solution.py:74
  212.1 20.2 %copy-start.2 = (bf16[1,4,5280]{2,1,0:T(4,128)(2,1)S(1)}, bf16[1,4,5280]{2,1,0:T(4,128)(2,1)}, u32[]{:S(2)}) copy-start(bf16[1,4,5280]{2,1,0:T(4,128)(2,1)} %param.13) | copy-start | bytes 126724
  225.2 41.8 %all-to-all-start.3 = ((bf16[4,12,5280]{2,1,0:T(8,128)(2,1)}), bf16[4,12,5280]{2,1,0:T(8,128)(2,1)S(1)}, u32[]{:S(2)}, u32[]{:S(2)}) async-start(bf16[4,12,5280]{2,1,0:T(8,128)(2,1)} %reshape.146), calls=%async_computation.3 | async-start | bytes 1376256 | tf_op jit(solution)/shard_map/all_to_all | solution.py:36
  232.6 35.1 %copy-start = (f32[1,5280]{1,0:T(1,128)S(1)}, f32[1,5280]{1,0:T(1,128)}, u32[]{:S(2)}) copy-start(f32[1,5280]{1,0:T(1,128)} %param.12) | copy-start | bytes 63364
  267.7 11.2 %collective-permute-start = (bf16[32,5280]{1,0:T(8,128)(2,1)S(1)}, bf16[32,5280]{1,0:T(8,128)(2,1)S(1)}, u32[]{:S(2)}, u32[]{:S(2)}) collective-permute-start(bf16[32,5280]{1,0:T(8,128)(2,1)S(1)} %get-tuple-element.397), channel_id=1, source_target_pairs={{192,0},{0,64},{64,128},{128,192},{193,1},{1,65},{65,129},{129,193... | collective-permute-start | bytes 1013768 | tf_op jit(solution)/shard_map/while/body/eval_jaxpr/ppermute | solution.py:13
  317.3 20.9 %all-to-all-start.1 = ((bf16[4,12,5280]{2,1,0:T(8,128)(2,1)}), bf16[4,12,5280]{2,1,0:T(8,128)(2,1)S(1)}, u32[]{:S(2)}, u32[]{:S(2)}) async-start(bf16[4,12,5280]{2,1,0:T(8,128)(2,1)} %reshape.161), calls=%async_computation.1 | async-start | bytes 1376256 | tf_op jit(solution)/shard_map/while/body/eval_jaxpr/all_to_all | solution.py:36
  338.8 8.5 collective-permute-start
  380.4 16.8 %all-to-all-start.1 = ((bf16[4,12,5280]{2,1,0:T(8,128)(2,1)}), bf16[4,12,5280]{2,1,0:T(8,128)(2,1)S(1)}, u32[]{:S(2)}, u32[]{:S(2)}) async-start(bf16[4,12,5280]{2,1,0:T(8,128)(2,1)} %reshape.161), calls=%async_computation.1 | async-start | bytes 1376256 | tf_op jit(solution)/shard_map/while/body/eval_jaxpr/all_to_all | solution.py:36
  397.8 8.5 collective-permute-start
  438.8 22.9 %all-to-all-start.1 = ((bf16[4,12,5280]{2,1,0:T(8,128)(2,1)}), bf16[4,12,5280]{2,1,0:T(8,128)(2,1)S(1)}, u32[]{:S(2)}, u32[]{:S(2)}) async-start(bf16[4,12,5280]{2,1,0:T(8,128)(2,1)} %reshape.161), calls=%async_computation.1 | async-start | bytes 1376256 | tf_op jit(solution)/shard_map/while/body/eval_jaxpr/all_to_all | solution.py:36
  462.3 8.5 collective-permute-start
  506.3 25.1 %all-to-all-start.1 = ((bf16[4,12,5280]{2,1,0:T(8,128)(2,1)}), bf16[4,12,5280]{2,1,0:T(8,128)(2,1)S(1)}, u32[]{:S(2)}, u32[]{:S(2)}) async-start(bf16[4,12,5280]{2,1,0:T(8,128)(2,1)} %reshape.161), calls=%async_computation.1 | async-start | bytes 1376256 | tf_op jit(solution)/shard_map/while/body/eval_jaxpr/all_to_all | solution.py:36
  532.0 8.5 collective-permute-start
  575.4 18.0 %all-to-all-start.1 = ((bf16[4,12,5280]{2,1,0:T(8,128)(2,1)}), bf16[4,12,5280]{2,1,0:T(8,128)(2,1)S(1)}, u32[]{:S(2)}, u32[]{:S(2)}) async-start(bf16[4,12,5280]{2,1,0:T(8,128)(2,1)} %reshape.161), calls=%async_computation.1 | async-start | bytes 1376256 | tf_op jit(solution)/shard_map/while/body/eval_jaxpr/all_to_all | solution.py:36
  594.0 8.5 collective-permute-start
  633.8 16.7 %all-to-all-start.1 = ((bf16[4,12,5280]{2,1,0:T(8,128)(2,1)}), bf16[4,12,5280]{2,1,0:T(8,128)(2,1)S(1)}, u32[]{:S(2)}, u32[]{:S(2)}) async-start(bf16[4,12,5280]{2,1,0:T(8,128)(2,1)} %reshape.161), calls=%async_computation.1 | async-start | bytes 1376256 | tf_op jit(solution)/shard_map/while/body/eval_jaxpr/all_to_all | solution.py:36
  651.2 8.5 collective-permute-start
  690.4 17.6 %all-to-all-start.1 = ((bf16[4,12,5280]{2,1,0:T(8,128)(2,1)}), bf16[4,12,5280]{2,1,0:T(8,128)(2,1)S(1)}, u32[]{:S(2)}, u32[]{:S(2)}) async-start(bf16[4,12,5280]{2,1,0:T(8,128)(2,1)} %reshape.161), calls=%async_computation.1 | async-start | bytes 1376256 | tf_op jit(solution)/shard_map/while/body/eval_jaxpr/all_to_all | solution.py:36
  708.7 8.5 collective-permute-start
  760.0 19.2 %all-to-all-start.1 = ((bf16[4,12,5280]{2,1,0:T(8,128)(2,1)}), bf16[4,12,5280]{2,1,0:T(8,128)(2,1)S(1)}, u32[]{:S(2)}, u32[]{:S(2)}) async-start(bf16[4,12,5280]{2,1,0:T(8,128)(2,1)} %reshape.161), calls=%async_computation.1 | async-start | bytes 1376256 | tf_op jit(solution)/shard_map/while/body/eval_jaxpr/all_to_all | solution.py:36
  779.8 8.5 collective-permute-start
  820.9 15.8 %all-to-all-start.1 = ((bf16[4,12,5280]{2,1,0:T(8,128)(2,1)}), bf16[4,12,5280]{2,1,0:T(8,128)(2,1)S(1)}, u32[]{:S(2)}, u32[]{:S(2)}) async-start(bf16[4,12,5280]{2,1,0:T(8,128)(2,1)} %reshape.161), calls=%async_computation.1 | async-start | bytes 1376256 | tf_op jit(solution)/shard_map/while/body/eval_jaxpr/all_to_all | solution.py:36
  837.3 8.7 collective-permute-start
  877.0 14.9 %all-to-all-start.1 = ((bf16[4,12,5280]{2,1,0:T(8,128)(2,1)}), bf16[4,12,5280]{2,1,0:T(8,128)(2,1)S(1)}, u32[]{:S(2)}, u32[]{:S(2)}) async-start(bf16[4,12,5280]{2,1,0:T(8,128)(2,1)} %reshape.161), calls=%async_computation.1 | async-start | bytes 1376256 | tf_op jit(solution)/shard_map/while/body/eval_jaxpr/all_to_all | solution.py:36
  892.5 0.7 copy-start.1
Sparse Core Ops, SparseCore 0:
  9.5 103.0 all-gather.2
  114.4 97.6 all-gather.4
where the time goes:
time: 910 us; the launch traced here: 900 us
  waiting for transfers between devices  367 us (40%)
  blocking collectives  249 us (27%)
  matrix products  116 us (13%)
  local copies, waits for them, and re-layouts  77.1 us (8%)
  starting transfers between devices  52.6 us (6%)
  other arithmetic  24 us (3%)
  between operations  13.5 us (1%)
    all_to_all x11, blocking collectives, whole_round(): lax.all_to_all(buffer, 'expert', split_axis=0, concat_axis=0, tiled=True)  249 us
    all_to_all x11, waiting for transfers between devices, whole_round(): lax.all_to_all(processed, 'expert', split_axis=0, concat_axis=0, tiled=True)  146 us
    dot_general x11, matrix products, expert_rows(): jnp.dot(hidden, w_second, preferred_element_type=jnp.float32)  104 us
    all_gather x1, waiting for transfers between devices, body(): lax.all_gather(w_down, 'dp', axis=3, tiled=True)  88 us
    all_gather x1, waiting for transfers between devices, body(): lax.all_gather(w_up, 'dp', axis=2, tiled=True)  67.2 us
    ppermute x10, waiting for transfers between devices, shifted(): return lax.ppermute(block, axis, route)  66.2 us
    unnamed x10, local copies, waits for them, and re-layouts  52.4 us
    all_to_all x11, starting transfers between devices, whole_round(): lax.all_to_all(processed, 'expert', split_axis=0, concat_axis=0, tiled=True)  46.1 us
  transfers between devices with their start and end apart: 23, of which 22 were waited for; matrix products, arithmetic and copies ran while one was open for 8% of the time, Pallas kernels for 0%

commit v1 on v0

--- a/solution.py
+++ b/solution.py
@@ -30,10 +30,12 @@
 
 
 def whole_round(buffer, w_first, w_second):
-    processed = expert_rows(
-        lax.all_to_all(buffer, "expert", split_axis=0, concat_axis=0, tiled=True), w_first, w_second
+    groups = buffer.shape[0]
+    arrived = jnp.stack([buffer[0]] + [shifted(buffer[j], "expert", j) for j in range(1, groups)])
+    processed = expert_rows(arrived, w_first, w_second)
+    return jnp.stack(
+        [processed[0]] + [shifted(processed[j], "expert", groups - j) for j in range(1, groups)]
     )
-    return lax.all_to_all(processed, "expert", split_axis=0, concat_axis=0, tiled=True)
 
 
 def core_block(current, gain_row, router_rows, w_first, w_second, assign):
@@ -50,7 +52,8 @@
     ).astype(jnp.float32)
     counts = jnp.dot(earlier, onehot, preferred_element_type=jnp.float32)
     slot_index = jnp.sum(onehot * counts, axis=-1).astype(jnp.int32)
-    target = assign * CAP + slot_index
+    relative = jnp.mod(assign - lax.axis_index("expert"), experts)
+    target = relative * CAP + slot_index
     places = (
         lax.broadcasted_iota(jnp.int32, (experts * CAP, tokens), 0) == target[None, :]
     ).astype(jnp.bfloat16)

time: 910 us -> 877 us (0.964)
  blocking collectives: 249 us -> 0 us
  starting transfers between devices: 52.6 us -> 164 us
  waiting for transfers between devices: 367 us -> 477 us
  local copies, waits for them, and re-layouts: 77.1 us -> 67 us
    ppermute x10 -> x76, waiting for transfers between devices: 66.2 us -> 319 us  [shifted(): return lax.ppermute(block, axis, route)]
    all_to_all x11 -> x0, blocking collectives: 249 us -> none  [whole_round(): lax.all_to_all(buffer, 'expert', split_axis=0, concat_axis=0, tiled=True)]
    ppermute x10 -> x76, starting transfers between devices: 6.44 us -> 164 us  [shifted(): return lax.ppermute(block, axis, route)]
    all_to_all x11 -> x0, waiting for transfers between devices: 146 us -> none  [whole_round(): lax.all_to_all(processed, 'expert', split_axis=0, concat_axis=0, tiled=True)]
    all_to_all x11 -> x0, starting transfers between devices: 46.1 us -> none  [whole_round(): lax.all_to_all(processed, 'expert', split_axis=0, concat_axis=0, tiled=True)]
    reshape x22 -> x0, local copies, waits for them, and re-layouts: 12.2 us -> none  [the longest x11 10.8 us: expert_rows(): return result.reshape(extent)]
  transfers between devices with their start and end apart: 23 -> 78, of which waited for: 22 -> 64; matrix products, arithmetic and copies ran while one was open for 8% -> 8% of each run, Pallas kernels for 0% -> 0%
where the time goes in v1:
time: 877 us; the launch traced here: 865 us
  waiting for transfers between devices  477 us (54%)
  starting transfers between devices  164 us (19%)
  matrix products  115 us (13%)
  local copies, waits for them, and re-layouts  67 us (8%)
  other arithmetic  26.9 us (3%)
  between operations  13.5 us (2%)
    ppermute x76, waiting for transfers between devices, shifted(): return lax.ppermute(block, axis, route)  319 us
    ppermute x76, starting transfers between devices, shifted(): return lax.ppermute(block, axis, route)  164 us
    dot_general x11, matrix products, expert_rows(): jnp.dot(hidden, w_second, preferred_element_type=jnp.float32)  103 us
    all_gather x1, waiting for transfers between devices, body(): lax.all_gather(w_down, 'dp', axis=3, tiled=True)  86.1 us
    all_gather x1, waiting for transfers between devices, body(): lax.all_gather(w_up, 'dp', axis=2, tiled=True)  71.3 us
    unnamed x10, local copies, waits for them, and re-layouts  52.4 us
  transfers between devices with their start and end apart: 78, of which 64 were waited for; matrix products, arithmetic and copies ran while one was open for 8% of the time, Pallas kernels for 0%

profile of v1, /device:TPU:2, one launch (start us, length us, event | category | flops | bytes accessed | tf_op | source)
XLA Modules:
  0.0 864.9 jit_solution(17639278797616163375)
XLA Ops:
  28.9 7.7 collective-permute-done.8
  41.2 71.3 %all-gather.3.cloned.1.call-done = bf16[1,1,5280,768]{3,1,0,2:T(2,128)(2,1)} async-done(((bf16[1,1,330,768]{3,1,0,2:T(2,128)(2,1)}), bf16[1,1,5280,768]{3,1,0,2:T(2,128)(2,1)}) %all-gather.3.cloned.1.call-update) | async-done | bytes 8110096 | tf_op jit(solution)/shard_map/all_gather | solution.py:76
  112.5 11.6 %copy.26 = bf16[1,1,5280,768]{3,2,0,1:T(8,128)(2,1)} copy(bf16[1,1,5280,768]{3,1,0,2:T(2,128)(2,1)} %all-gather.3.cloned.1.call-done) | data formatting | bytes 16220160
  124.1 86.1 %all-gather.5.cloned.1.call-done = bf16[1,1,768,5280]{2,1,0,3:T(2,128)(2,1)} async-done(((bf16[1,1,768,330]{2,1,0,3:T(2,128)(2,1)}), bf16[1,1,768,5280]{2,1,0,3:T(2,128)(2,1)}) %all-gather.5.cloned.1.call-update) | async-done | bytes 8110096 | tf_op jit(solution)/shard_map/all_gather | solution.py:77
  210.2 12.2 %fusion.39 = bf16[48,5280]{1,0:T(8,128)(2,1)S(1)} fusion(bf16[1,1,768,5280]{2,1,0,3:T(2,128)(2,1)} %all-gather.5.cloned.1.call-done, bf16[48,5280]{1,0:T(8,128)(2,1)S(1)} %reshape.183, bf16[5280,768]{1,0:T(8,128)(2,1)} %bitcast.106), kind=kOutput, calls=%fused_computation.60 | convolution fusion | flops 779152896 | bytes 17233920 | tf_op jit(solution)/shard_map/dot_general | solution.py:28
  231.2 34.5 %copy.18 = bf16[1,1,768,5280]{3,2,0,1:T(8,128)(2,1)} copy(bf16[1,1,768,5280]{2,1,0,3:T(2,128)(2,1)} %all-gather.5.cloned.1.call-done) | data formatting | bytes 16220160
  266.4 590.9 %while.15 = (s32[]{:T(128)}, bf16[32,5280]{1,0:T(8,128)(2,1)S(1)}, s32[]{:T(128)}, pred[]{:T(512)}, bf16[4,32,5280]{2,1,0:T(8,128)(2,1)}, /*index=5*/bf16[4,32,5...) while((s32[]{:T(128)}, bf16[32,5280]{1,0:T(8,128)(2,1)S(1)}, ...), condition=%wide.region_7.8_spmd, body=%wide.region_3.7_spmd.sunk | while | flops 818449920 | bytes 31894524 | solution.py:114
  269.5 7.6 collective-permute-done
  284.9 6.2 collective-permute-done.1
  296.4 9.1 %convolution_convert_fusion.6 = bf16[48,5280]{1,0:T(8,128)(2,1)S(1)} fusion(bf16[768,5280]{1,0:T(8,128)(2,1)} %get-tuple-element.460, bf16[48,5280]{1,0:T(8,128)(2,1)S(1)} %reshape.194, bf16[5280,768]{1,0:T(8,128)(2,1)} %get-tuple-element.459), kind=kOutput, calls=%fused_computation.clone.1 | convolution fusion | flops 779152896 | bytes 17233920 | tf_op jit(solution)/shard_map/while/body/eval_jaxpr/dot_general | solution.py:28
  313.0 6.6 collective-permute-done.4
  319.6 7.3 collective-permute-done.6
  329.5 6.7 collective-permute-done
  346.4 10.3 %collective-permute-done.1 = bf16[12,5280]{1,0:T(8,128)(2,1)S(1)} collective-permute-done((bf16[12,5280]{1,0:T(8,128)(2,1)S(1)}, bf16[12,5280]{1,0:T(8,128)(2,1)S(1)}, u32[]{:S(2)}, u32[]{:S(2)}) %collective-permute-start.1) | collective-permute-done | bytes 126752 | tf_op jit(solution)/shard_map/while/body/eval_jaxpr/ppermute | solution.py:13
  357.1 9.1 %convolution_convert_fusion.6 = bf16[48,5280]{1,0:T(8,128)(2,1)S(1)} fusion(bf16[768,5280]{1,0:T(8,128)(2,1)} %get-tuple-element.460, bf16[48,5280]{1,0:T(8,128)(2,1)S(1)} %reshape.194, bf16[5280,768]{1,0:T(8,128)(2,1)} %get-tuple-element.459), kind=kOutput, calls=%fused_computation.clone.1 | convolution fusion | flops 779152896 | bytes 17233920 | tf_op jit(solution)/shard_map/while/body/eval_jaxpr/dot_general | solution.py:28
  375.1 6.4 collective-permute-done.5
  381.5 7.2 collective-permute-done.6
  391.1 6.9 collective-permute-done
  408.6 6.5 collective-permute-done.2
  415.8 9.1 %convolution_convert_fusion.6 = bf16[48,5280]{1,0:T(8,128)(2,1)S(1)} fusion(bf16[768,5280]{1,0:T(8,128)(2,1)} %get-tuple-element.460, bf16[48,5280]{1,0:T(8,128)(2,1)S(1)} %reshape.194, bf16[5280,768]{1,0:T(8,128)(2,1)} %get-tuple-element.459), kind=kOutput, calls=%fused_computation.clone.1 | convolution fusion | flops 779152896 | bytes 17233920 | tf_op jit(solution)/shard_map/while/body/eval_jaxpr/dot_general | solution.py:28
  439.6 7.5 collective-permute-done.6
  449.6 6.9 collective-permute-done
  465.7 9.5 %collective-permute-done.1 = bf16[12,5280]{1,0:T(8,128)(2,1)S(1)} collective-permute-done((bf16[12,5280]{1,0:T(8,128)(2,1)S(1)}, bf16[12,5280]{1,0:T(8,128)(2,1)S(1)}, u32[]{:S(2)}, u32[]{:S(2)}) %collective-permute-start.1) | collective-permute-done | bytes 126752 | tf_op jit(solution)/shard_map/while/body/eval_jaxpr/ppermute | solution.py:13
  475.6 9.1 %convolution_convert_fusion.6 = bf16[48,5280]{1,0:T(8,128)(2,1)S(1)} fusion(bf16[768,5280]{1,0:T(8,128)(2,1)} %get-tuple-element.460, bf16[48,5280]{1,0:T(8,128)(2,1)S(1)} %reshape.194, bf16[5280,768]{1,0:T(8,128)(2,1)} %get-tuple-element.459), kind=kOutput, calls=%fused_computation.clone.1 | convolution fusion | flops 779152896 | bytes 17233920 | tf_op jit(solution)/shard_map/while/body/eval_jaxpr/dot_general | solution.py:28
  484.9 6.9 collective-permute-start.5
  494.0 8.5 collective-permute-done.5
  507.1 8.8 %collective-permute-done = bf16[32,5280]{1,0:T(8,128)(2,1)S(1)} collective-permute-done((bf16[32,5280]{1,0:T(8,128)(2,1)S(1)}, bf16[32,5280]{1,0:T(8,128)(2,1)S(1)}, u32[]{:S(2)}, u32[]{:S(2)}) %collective-permute-start) | collective-permute-done | bytes 337952 | tf_op jit(solution)/shard_map/while/body/eval_jaxpr/ppermute | solution.py:13
  523.8 9.3 %collective-permute-done.1 = bf16[12,5280]{1,0:T(8,128)(2,1)S(1)} collective-permute-done((bf16[12,5280]{1,0:T(8,128)(2,1)S(1)}, bf16[12,5280]{1,0:T(8,128)(2,1)S(1)}, u32[]{:S(2)}, u32[]{:S(2)}) %collective-permute-start.1) | collective-permute-done | bytes 126752 | tf_op jit(solution)/shard_map/while/body/eval_jaxpr/ppermute | solution.py:13
  537.3 9.1 %convolution_convert_fusion.6 = bf16[48,5280]{1,0:T(8,128)(2,1)S(1)} fusion(bf16[768,5280]{1,0:T(8,128)(2,1)} %get-tuple-element.460, bf16[48,5280]{1,0:T(8,128)(2,1)S(1)} %reshape.194, bf16[5280,768]{1,0:T(8,128)(2,1)} %get-tuple-element.459), kind=kOutput, calls=%fused_computation.clone.1 | convolution fusion | flops 779152896 | bytes 17233920 | tf_op jit(solution)/shard_map/while/body/eval_jaxpr/dot_general | solution.py:28
  564.7 6.9 collective-permute-done
  573.4 8.6 collective-permute-start.1
  585.7 10.2 %collective-permute-done.1 = bf16[12,5280]{1,0:T(8,128)(2,1)S(1)} collective-permute-done((bf16[12,5280]{1,0:T(8,128)(2,1)S(1)}, bf16[12,5280]{1,0:T(8,128)(2,1)S(1)}, u32[]{:S(2)}, u32[]{:S(2)}) %collective-permute-start.1) | collective-permute-done | bytes 126752 | tf_op jit(solution)/shard_map/while/body/eval_jaxpr/ppermute | solution.py:13
  597.5 9.1 %convolution_convert_fusion.6 = bf16[48,5280]{1,0:T(8,128)(2,1)S(1)} fusion(bf16[768,5280]{1,0:T(8,128)(2,1)} %get-tuple-element.460, bf16[48,5280]{1,0:T(8,128)(2,1)S(1)} %reshape.194, bf16[5280,768]{1,0:T(8,128)(2,1)} %get-tuple-element.459), kind=kOutput, calls=%fused_computation.clone.1 | convolution fusion | flops 779152896 | bytes 17233920 | tf_op jit(solution)/shard_map/while/body/eval_jaxpr/dot_general | solution.py:28
  614.2 6.8 collective-permute-done.4
  621.3 6.3 collective-permute-done.6
  630.0 6.9 collective-permute-done
  646.9 10.4 %collective-permute-done.1 = bf16[12,5280]{1,0:T(8,128)(2,1)S(1)} collective-permute-done((bf16[12,5280]{1,0:T(8,128)(2,1)S(1)}, bf16[12,5280]{1,0:T(8,128)(2,1)S(1)}, u32[]{:S(2)}, u32[]{:S(2)}) %collective-permute-start.1) | collective-permute-done | bytes 126752 | tf_op jit(solution)/shard_map/while/body/eval_jaxpr/ppermute | solution.py:13
  657.7 9.1 %convolution_convert_fusion.6 = bf16[48,5280]{1,0:T(8,128)(2,1)S(1)} fusion(bf16[768,5280]{1,0:T(8,128)(2,1)} %get-tuple-element.460, bf16[48,5280]{1,0:T(8,128)(2,1)S(1)} %reshape.194, bf16[5280,768]{1,0:T(8,128)(2,1)} %get-tuple-element.459), kind=kOutput, calls=%fused_computation.clone.1 | convolution fusion | flops 779152896 | bytes 17233920 | tf_op jit(solution)/shard_map/while/body/eval_jaxpr/dot_general | solution.py:28
  692.3 6.9 collective-permute-done
  707.6 7.2 collective-permute-done.1
  720.6 9.1 %convolution_convert_fusion.6 = bf16[48,5280]{1,0:T(8,128)(2,1)S(1)} fusion(bf16[768,5280]{1,0:T(8,128)(2,1)} %get-tuple-element.460, bf16[48,5280]{1,0:T(8,128)(2,1)S(1)} %reshape.194, bf16[5280,768]{1,0:T(8,128)(2,1)} %get-tuple-element.459), kind=kOutput, calls=%fused_computation.clone.1 | convolution fusion | flops 779152896 | bytes 17233920 | tf_op jit(solution)/shard_map/while/body/eval_jaxpr/dot_general | solution.py:28
  742.2 6.5 collective-permute-done.6
  751.0 6.9 collective-permute-done
  765.2 7.7 collective-permute-done.1
  773.8 6.4 collective-permute-done.3
  780.5 9.1 %convolution_convert_fusion.6 = bf16[48,5280]{1,0:T(8,128)(2,1)S(1)} fusion(bf16[768,5280]{1,0:T(8,128)(2,1)} %get-tuple-element.460, bf16[48,5280]{1,0:T(8,128)(2,1)S(1)} %reshape.194, bf16[5280,768]{1,0:T(8,128)(2,1)} %get-tuple-element.459), kind=kOutput, calls=%fused_computation.clone.1 | convolution fusion | flops 779152896 | bytes 17233920 | tf_op jit(solution)/shard_map/while/body/eval_jaxpr/dot_general | solution.py:28
  807.2 6.9 collective-permute-done
  831.9 9.1 %convolution_convert_fusion.6 = bf16[48,5280]{1,0:T(8,128)(2,1)S(1)} fusion(bf16[768,5280]{1,0:T(8,128)(2,1)} %get-tuple-element.460, bf16[48,5280]{1,0:T(8,128)(2,1)S(1)} %reshape.194, bf16[5280,768]{1,0:T(8,128)(2,1)} %get-tuple-element.459), kind=kOutput, calls=%fused_computation.clone.1 | convolution fusion | flops 779152896 | bytes 17233920 | tf_op jit(solution)/shard_map/while/body/eval_jaxpr/dot_general | solution.py:28
  (308 shorter events, 302.2 us)
Async XLA Ops:
  6.5 106.0 %all-gather.3.cloned.1.call-start = ((), (), s32[]{:S(2)}) async-start(), calls=%async_computation | async-start | bytes 17233920 | tf_op jit(solution)/shard_map/all_gather | solution.py:76
  9.4 200.8 %all-gather.5.cloned.1.call-start = ((), (), s32[]{:S(2)}) async-start(), calls=%async_computation.1 | async-start | bytes 17233920 | tf_op jit(solution)/shard_map/all_gather | solution.py:77
  16.4 12.5 %collective-permute-start.7 = (bf16[12,5280]{1,0:T(8,128)(2,1)S(1)}, bf16[12,5280]{1,0:T(8,128)(2,1)S(1)}, u32[]{:S(2)}, u32[]{:S(2)}) collective-permute-start(bf16[12,5280]{1,0:T(8,128)(2,1)S(1)} %get-tuple-element.320), channel_id=1, source_target_pairs={{3,0},{0,1},{1,2},{2,3},{7,4},{4,5},{5,6},{6,7},{11,8},{8,9},{9,10... | collective-permute-start | bytes 380168 | tf_op jit(solution)/shard_map/ppermute | solution.py:13
  19.7 16.9 %collective-permute-start.8 = (bf16[12,5280]{1,0:T(8,128)(2,1)S(1)}, bf16[12,5280]{1,0:T(8,128)(2,1)S(1)}, u32[]{:S(2)}, u32[]{:S(2)}) collective-permute-start(bf16[12,5280]{1,0:T(8,128)(2,1)S(1)} %get-tuple-element.319), channel_id=1, source_target_pairs={{2,0},{3,1},{0,2},{1,3},{6,4},{7,5},{4,6},{5,7},{10,8},{11,9},{8,1... | collective-permute-start | bytes 380168 | tf_op jit(solution)/shard_map/ppermute | solution.py:13
  25.1 15.7 %collective-permute-start.9 = (bf16[12,5280]{1,0:T(8,128)(2,1)S(1)}, bf16[12,5280]{1,0:T(8,128)(2,1)S(1)}, u32[]{:S(2)}, u32[]{:S(2)}) collective-permute-start(bf16[12,5280]{1,0:T(8,128)(2,1)S(1)} %get-tuple-element.318), channel_id=1, source_target_pairs={{1,0},{2,1},{3,2},{0,3},{5,4},{6,5},{7,6},{4,7},{9,8},{10,9},{11,1... | collective-permute-start | bytes 380168 | tf_op jit(solution)/shard_map/ppermute | solution.py:13
  222.4 43.3 %collective-permute-start.10 = (bf16[12,5280]{1,0:T(8,128)(2,1)S(1)}, bf16[12,5280]{1,0:T(8,128)(2,1)S(1)}, u32[]{:S(2)}, u32[]{:S(2)}) collective-permute-start(bf16[12,5280]{1,0:T(8,128)(2,1)S(1)} %get-tuple-element.316), channel_id=1, source_target_pairs={{1,0},{2,1},{3,2},{0,3},{5,4},{6,5},{7,6},{4,7},{9,8},{10,9},{11,1... | collective-permute-start | bytes 380168 | tf_op jit(solution)/shard_map/ppermute | solution.py:13
  226.6 39.1 %collective-permute-start.11 = (bf16[12,5280]{1,0:T(8,128)(2,1)S(1)}, bf16[12,5280]{1,0:T(8,128)(2,1)S(1)}, u32[]{:S(2)}, u32[]{:S(2)}) collective-permute-start(bf16[12,5280]{1,0:T(8,128)(2,1)S(1)} %get-tuple-element.315), channel_id=1, source_target_pairs={{2,0},{3,1},{0,2},{1,3},{6,4},{7,5},{4,6},{5,7},{10,8},{11,9},{8,1... | collective-permute-start | bytes 380168 | tf_op jit(solution)/shard_map/ppermute | solution.py:13
  228.6 37.1 %collective-permute-start.12 = (bf16[12,5280]{1,0:T(8,128)(2,1)S(1)}, bf16[12,5280]{1,0:T(8,128)(2,1)S(1)}, u32[]{:S(2)}, u32[]{:S(2)}) collective-permute-start(bf16[12,5280]{1,0:T(8,128)(2,1)S(1)} %get-tuple-element.314), channel_id=1, source_target_pairs={{3,0},{0,1},{1,2},{2,3},{7,4},{4,5},{5,6},{6,7},{11,8},{8,9},{9,10... | collective-permute-start | bytes 380168 | tf_op jit(solution)/shard_map/ppermute | solution.py:13
  279.0 12.1 %collective-permute-start.1 = (bf16[12,5280]{1,0:T(8,128)(2,1)S(1)}, bf16[12,5280]{1,0:T(8,128)(2,1)S(1)}, u32[]{:S(2)}, u32[]{:S(2)}) collective-permute-start(bf16[12,5280]{1,0:T(8,128)(2,1)S(1)} %get-tuple-element.400), channel_id=1, source_target_pairs={{1,0},{2,1},{3,2},{0,3},{5,4},{6,5},{7,6},{4,7},{9,8},{10,9},{11,1... | collective-permute-start | bytes 380168 | tf_op jit(solution)/shard_map/while/body/eval_jaxpr/ppermute | solution.py:13
  280.6 12.7 %collective-permute-start.2 = (bf16[12,5280]{1,0:T(8,128)(2,1)S(1)}, bf16[12,5280]{1,0:T(8,128)(2,1)S(1)}, u32[]{:S(2)}, u32[]{:S(2)}) collective-permute-start(bf16[12,5280]{1,0:T(8,128)(2,1)S(1)} %get-tuple-element.401), channel_id=1, source_target_pairs={{2,0},{3,1},{0,2},{1,3},{6,4},{7,5},{4,6},{5,7},{10,8},{11,9},{8,1... | collective-permute-start | bytes 380168 | tf_op jit(solution)/shard_map/while/body/eval_jaxpr/ppermute | solution.py:13
  305.6 14.0 %collective-permute-start.4 = (bf16[12,5280]{1,0:T(8,128)(2,1)S(1)}, bf16[12,5280]{1,0:T(8,128)(2,1)S(1)}, u32[]{:S(2)}, u32[]{:S(2)}) collective-permute-start(bf16[12,5280]{1,0:T(8,128)(2,1)S(1)} %get-tuple-element.404), channel_id=1, source_target_pairs={{3,0},{0,1},{1,2},{2,3},{7,4},{4,5},{5,6},{6,7},{11,8},{8,9},{9,10... | collective-permute-start | bytes 380168 | tf_op jit(solution)/shard_map/while/body/eval_jaxpr/ppermute | solution.py:13
  309.6 17.4 %collective-permute-start.6 = (bf16[12,5280]{1,0:T(8,128)(2,1)S(1)}, bf16[12,5280]{1,0:T(8,128)(2,1)S(1)}, u32[]{:S(2)}, u32[]{:S(2)}) collective-permute-start(bf16[12,5280]{1,0:T(8,128)(2,1)S(1)} %get-tuple-element.406), channel_id=1, source_target_pairs={{1,0},{2,1},{3,2},{0,3},{5,4},{6,5},{7,6},{4,7},{9,8},{10,9},{11,1... | collective-permute-start | bytes 380168 | tf_op jit(solution)/shard_map/while/body/eval_jaxpr/ppermute | solution.py:13
  338.1 18.6 %collective-permute-start.1 = (bf16[12,5280]{1,0:T(8,128)(2,1)S(1)}, bf16[12,5280]{1,0:T(8,128)(2,1)S(1)}, u32[]{:S(2)}, u32[]{:S(2)}) collective-permute-start(bf16[12,5280]{1,0:T(8,128)(2,1)S(1)} %get-tuple-element.400), channel_id=1, source_target_pairs={{1,0},{2,1},{3,2},{0,3},{5,4},{6,5},{7,6},{4,7},{9,8},{10,9},{11,1... | collective-permute-start | bytes 380168 | tf_op jit(solution)/shard_map/while/body/eval_jaxpr/ppermute | solution.py:13
  342.7 14.0 %collective-permute-start.2 = (bf16[12,5280]{1,0:T(8,128)(2,1)S(1)}, bf16[12,5280]{1,0:T(8,128)(2,1)S(1)}, u32[]{:S(2)}, u32[]{:S(2)}) collective-permute-start(bf16[12,5280]{1,0:T(8,128)(2,1)S(1)} %get-tuple-element.401), channel_id=1, source_target_pairs={{2,0},{3,1},{0,2},{1,3},{6,4},{7,5},{4,6},{5,7},{10,8},{11,9},{8,1... | collective-permute-start | bytes 380168 | tf_op jit(solution)/shard_map/while/body/eval_jaxpr/ppermute | solution.py:13
  368.4 13.2 %collective-permute-start.5 = (bf16[12,5280]{1,0:T(8,128)(2,1)S(1)}, bf16[12,5280]{1,0:T(8,128)(2,1)S(1)}, u32[]{:S(2)}, u32[]{:S(2)}) collective-permute-start(bf16[12,5280]{1,0:T(8,128)(2,1)S(1)} %get-tuple-element.405), channel_id=1, source_target_pairs={{2,0},{3,1},{0,2},{1,3},{6,4},{7,5},{4,6},{5,7},{10,8},{11,9},{8,1... | collective-permute-start | bytes 380168 | tf_op jit(solution)/shard_map/while/body/eval_jaxpr/ppermute | solution.py:13
  373.5 15.2 %collective-permute-start.6 = (bf16[12,5280]{1,0:T(8,128)(2,1)S(1)}, bf16[12,5280]{1,0:T(8,128)(2,1)S(1)}, u32[]{:S(2)}, u32[]{:S(2)}) collective-permute-start(bf16[12,5280]{1,0:T(8,128)(2,1)S(1)} %get-tuple-element.406), channel_id=1, source_target_pairs={{1,0},{2,1},{3,2},{0,3},{5,4},{6,5},{7,6},{4,7},{9,8},{10,9},{11,1... | collective-permute-start | bytes 380168 | tf_op jit(solution)/shard_map/while/body/eval_jaxpr/ppermute | solution.py:13
  427.4 12.2 %collective-permute-start.5 = (bf16[12,5280]{1,0:T(8,128)(2,1)S(1)}, bf16[12,5280]{1,0:T(8,128)(2,1)S(1)}, u32[]{:S(2)}, u32[]{:S(2)}) collective-permute-start(bf16[12,5280]{1,0:T(8,128)(2,1)S(1)} %get-tuple-element.405), channel_id=1, source_target_pairs={{2,0},{3,1},{0,2},{1,3},{6,4},{7,5},{4,6},{5,7},{10,8},{11,9},{8,1... | collective-permute-start | bytes 380168 | tf_op jit(solution)/shard_map/while/body/eval_jaxpr/ppermute | solution.py:13
  429.7 17.5 %collective-permute-start.6 = (bf16[12,5280]{1,0:T(8,128)(2,1)S(1)}, bf16[12,5280]{1,0:T(8,128)(2,1)S(1)}, u32[]{:S(2)}, u32[]{:S(2)}) collective-permute-start(bf16[12,5280]{1,0:T(8,128)(2,1)S(1)} %get-tuple-element.406), channel_id=1, source_target_pairs={{1,0},{2,1},{3,2},{0,3},{5,4},{6,5},{7,6},{4,7},{9,8},{10,9},{11,1... | collective-permute-start | bytes 380168 | tf_op jit(solution)/shard_map/while/body/eval_jaxpr/ppermute | solution.py:13
  458.3 16.9 %collective-permute-start.1 = (bf16[12,5280]{1,0:T(8,128)(2,1)S(1)}, bf16[12,5280]{1,0:T(8,128)(2,1)S(1)}, u32[]{:S(2)}, u32[]{:S(2)}) collective-permute-start(bf16[12,5280]{1,0:T(8,128)(2,1)S(1)} %get-tuple-element.400), channel_id=1, source_target_pairs={{1,0},{2,1},{3,2},{0,3},{5,4},{6,5},{7,6},{4,7},{9,8},{10,9},{11,1... | collective-permute-start | bytes 380168 | tf_op jit(solution)/shard_map/while/body/eval_jaxpr/ppermute | solution.py:13
  462.9 12.3 %collective-permute-start.2 = (bf16[12,5280]{1,0:T(8,128)(2,1)S(1)}, bf16[12,5280]{1,0:T(8,128)(2,1)S(1)}, u32[]{:S(2)}, u32[]{:S(2)}) collective-permute-start(bf16[12,5280]{1,0:T(8,128)(2,1)S(1)} %get-tuple-element.401), channel_id=1, source_target_pairs={{2,0},{3,1},{0,2},{1,3},{6,4},{7,5},{4,6},{5,7},{10,8},{11,9},{8,1... | collective-permute-start | bytes 380168 | tf_op jit(solution)/shard_map/while/body/eval_jaxpr/ppermute | solution.py:13
  462.9 12.3 %collective-permute-start.3 = (bf16[12,5280]{1,0:T(8,128)(2,1)S(1)}, bf16[12,5280]{1,0:T(8,128)(2,1)S(1)}, u32[]{:S(2)}, u32[]{:S(2)}) collective-permute-start(bf16[12,5280]{1,0:T(8,128)(2,1)S(1)} %get-tuple-element.402), channel_id=1, source_target_pairs={{3,0},{0,1},{1,2},{2,3},{7,4},{4,5},{5,6},{6,7},{11,8},{8,9},{9,10... | collective-permute-start | bytes 380168 | tf_op jit(solution)/shard_map/while/body/eval_jaxpr/ppermute | solution.py:13
  484.9 17.7 %collective-permute-start.5 = (bf16[12,5280]{1,0:T(8,128)(2,1)S(1)}, bf16[12,5280]{1,0:T(8,128)(2,1)S(1)}, u32[]{:S(2)}, u32[]{:S(2)}) collective-permute-start(bf16[12,5280]{1,0:T(8,128)(2,1)S(1)} %get-tuple-element.405), channel_id=1, source_target_pairs={{2,0},{3,1},{0,2},{1,3},{6,4},{7,5},{4,6},{5,7},{10,8},{11,9},{8,1... | collective-permute-start | bytes 380168 | tf_op jit(solution)/shard_map/while/body/eval_jaxpr/ppermute | solution.py:13
  491.8 12.9 %collective-permute-start.6 = (bf16[12,5280]{1,0:T(8,128)(2,1)S(1)}, bf16[12,5280]{1,0:T(8,128)(2,1)S(1)}, u32[]{:S(2)}, u32[]{:S(2)}) collective-permute-start(bf16[12,5280]{1,0:T(8,128)(2,1)S(1)} %get-tuple-element.406), channel_id=1, source_target_pairs={{1,0},{2,1},{3,2},{0,3},{5,4},{6,5},{7,6},{4,7},{9,8},{10,9},{11,1... | collective-permute-start | bytes 380168 | tf_op jit(solution)/shard_map/while/body/eval_jaxpr/ppermute | solution.py:13
  517.7 15.4 %collective-permute-start.1 = (bf16[12,5280]{1,0:T(8,128)(2,1)S(1)}, bf16[12,5280]{1,0:T(8,128)(2,1)S(1)}, u32[]{:S(2)}, u32[]{:S(2)}) collective-permute-start(bf16[12,5280]{1,0:T(8,128)(2,1)S(1)} %get-tuple-element.400), channel_id=1, source_target_pairs={{1,0},{2,1},{3,2},{0,3},{5,4},{6,5},{7,6},{4,7},{9,8},{10,9},{11,1... | collective-permute-start | bytes 380168 | tf_op jit(solution)/shard_map/while/body/eval_jaxpr/ppermute | solution.py:13
  517.8 15.3 %collective-permute-start.2 = (bf16[12,5280]{1,0:T(8,128)(2,1)S(1)}, bf16[12,5280]{1,0:T(8,128)(2,1)S(1)}, u32[]{:S(2)}, u32[]{:S(2)}) collective-permute-start(bf16[12,5280]{1,0:T(8,128)(2,1)S(1)} %get-tuple-element.401), channel_id=1, source_target_pairs={{2,0},{3,1},{0,2},{1,3},{6,4},{7,5},{4,6},{5,7},{10,8},{11,9},{8,1... | collective-permute-start | bytes 380168 | tf_op jit(solution)/shard_map/while/body/eval_jaxpr/ppermute | solution.py:13
  522.0 14.9 %collective-permute-start.3 = (bf16[12,5280]{1,0:T(8,128)(2,1)S(1)}, bf16[12,5280]{1,0:T(8,128)(2,1)S(1)}, u32[]{:S(2)}, u32[]{:S(2)}) collective-permute-start(bf16[12,5280]{1,0:T(8,128)(2,1)S(1)} %get-tuple-element.402), channel_id=1, source_target_pairs={{3,0},{0,1},{1,2},{2,3},{7,4},{4,5},{5,6},{6,7},{11,8},{8,9},{9,10... | collective-permute-start | bytes 380168 | tf_op jit(solution)/shard_map/while/body/eval_jaxpr/ppermute | solution.py:13
  546.5 13.5 %collective-permute-start.4 = (bf16[12,5280]{1,0:T(8,128)(2,1)S(1)}, bf16[12,5280]{1,0:T(8,128)(2,1)S(1)}, u32[]{:S(2)}, u32[]{:S(2)}) collective-permute-start(bf16[12,5280]{1,0:T(8,128)(2,1)S(1)} %get-tuple-element.404), channel_id=1, source_target_pairs={{3,0},{0,1},{1,2},{2,3},{7,4},{4,5},{5,6},{6,7},{11,8},{8,9},{9,10... | collective-permute-start | bytes 380168 | tf_op jit(solution)/shard_map/while/body/eval_jaxpr/ppermute | solution.py:13
  546.6 13.4 %collective-permute-start.5 = (bf16[12,5280]{1,0:T(8,128)(2,1)S(1)}, bf16[12,5280]{1,0:T(8,128)(2,1)S(1)}, u32[]{:S(2)}, u32[]{:S(2)}) collective-permute-start(bf16[12,5280]{1,0:T(8,128)(2,1)S(1)} %get-tuple-element.405), channel_id=1, source_target_pairs={{2,0},{3,1},{0,2},{1,3},{6,4},{7,5},{4,6},{5,7},{10,8},{11,9},{8,1... | collective-permute-start | bytes 380168 | tf_op jit(solution)/shard_map/while/body/eval_jaxpr/ppermute | solution.py:13
  550.1 12.2 %collective-permute-start.6 = (bf16[12,5280]{1,0:T(8,128)(2,1)S(1)}, bf16[12,5280]{1,0:T(8,128)(2,1)S(1)}, u32[]{:S(2)}, u32[]{:S(2)}) collective-permute-start(bf16[12,5280]{1,0:T(8,128)(2,1)S(1)} %get-tuple-element.406), channel_id=1, source_target_pairs={{1,0},{2,1},{3,2},{0,3},{5,4},{6,5},{7,6},{4,7},{9,8},{10,9},{11,1... | collective-permute-start | bytes 380168 | tf_op jit(solution)/shard_map/while/body/eval_jaxpr/ppermute | solution.py:13
  573.4 22.5 %collective-permute-start.1 = (bf16[12,5280]{1,0:T(8,128)(2,1)S(1)}, bf16[12,5280]{1,0:T(8,128)(2,1)S(1)}, u32[]{:S(2)}, u32[]{:S(2)}) collective-permute-start(bf16[12,5280]{1,0:T(8,128)(2,1)S(1)} %get-tuple-element.400), channel_id=1, source_target_pairs={{1,0},{2,1},{3,2},{0,3},{5,4},{6,5},{7,6},{4,7},{9,8},{10,9},{11,1... | collective-permute-start | bytes 380168 | tf_op jit(solution)/shard_map/while/body/eval_jaxpr/ppermute | solution.py:13
  582.0 13.9 %collective-permute-start.2 = (bf16[12,5280]{1,0:T(8,128)(2,1)S(1)}, bf16[12,5280]{1,0:T(8,128)(2,1)S(1)}, u32[]{:S(2)}, u32[]{:S(2)}) collective-permute-start(bf16[12,5280]{1,0:T(8,128)(2,1)S(1)} %get-tuple-element.401), channel_id=1, source_target_pairs={{2,0},{3,1},{0,2},{1,3},{6,4},{7,5},{4,6},{5,7},{10,8},{11,9},{8,1... | collective-permute-start | bytes 380168 | tf_op jit(solution)/shard_map/while/body/eval_jaxpr/ppermute | solution.py:13
  585.4 11.7 %collective-permute-start.3 = (bf16[12,5280]{1,0:T(8,128)(2,1)S(1)}, bf16[12,5280]{1,0:T(8,128)(2,1)S(1)}, u32[]{:S(2)}, u32[]{:S(2)}) collective-permute-start(bf16[12,5280]{1,0:T(8,128)(2,1)S(1)} %get-tuple-element.402), channel_id=1, source_target_pairs={{3,0},{0,1},{1,2},{2,3},{7,4},{4,5},{5,6},{6,7},{11,8},{8,9},{9,10... | collective-permute-start | bytes 380168 | tf_op jit(solution)/shard_map/while/body/eval_jaxpr/ppermute | solution.py:13
  606.7 14.3 %collective-permute-start.4 = (bf16[12,5280]{1,0:T(8,128)(2,1)S(1)}, bf16[12,5280]{1,0:T(8,128)(2,1)S(1)}, u32[]{:S(2)}, u32[]{:S(2)}) collective-permute-start(bf16[12,5280]{1,0:T(8,128)(2,1)S(1)} %get-tuple-element.404), channel_id=1, source_target_pairs={{3,0},{0,1},{1,2},{2,3},{7,4},{4,5},{5,6},{6,7},{11,8},{8,9},{9,10... | collective-permute-start | bytes 380168 | tf_op jit(solution)/shard_map/while/body/eval_jaxpr/ppermute | solution.py:13
  609.2 12.2 %collective-permute-start.5 = (bf16[12,5280]{1,0:T(8,128)(2,1)S(1)}, bf16[12,5280]{1,0:T(8,128)(2,1)S(1)}, u32[]{:S(2)}, u32[]{:S(2)}) collective-permute-start(bf16[12,5280]{1,0:T(8,128)(2,1)S(1)} %get-tuple-element.405), channel_id=1, source_target_pairs={{2,0},{3,1},{0,2},{1,3},{6,4},{7,5},{4,6},{5,7},{10,8},{11,9},{8,1... | collective-permute-start | bytes 380168 | tf_op jit(solution)/shard_map/while/body/eval_jaxpr/ppermute | solution.py:13
  610.6 17.1 %collective-permute-start.6 = (bf16[12,5280]{1,0:T(8,128)(2,1)S(1)}, bf16[12,5280]{1,0:T(8,128)(2,1)S(1)}, u32[]{:S(2)}, u32[]{:S(2)}) collective-permute-start(bf16[12,5280]{1,0:T(8,128)(2,1)S(1)} %get-tuple-element.406), channel_id=1, source_target_pairs={{1,0},{2,1},{3,2},{0,3},{5,4},{6,5},{7,6},{4,7},{9,8},{10,9},{11,1... | collective-permute-start | bytes 380168 | tf_op jit(solution)/shard_map/while/body/eval_jaxpr/ppermute | solution.py:13
  638.8 18.6 %collective-permute-start.1 = (bf16[12,5280]{1,0:T(8,128)(2,1)S(1)}, bf16[12,5280]{1,0:T(8,128)(2,1)S(1)}, u32[]{:S(2)}, u32[]{:S(2)}) collective-permute-start(bf16[12,5280]{1,0:T(8,128)(2,1)S(1)} %get-tuple-element.400), channel_id=1, source_target_pairs={{1,0},{2,1},{3,2},{0,3},{5,4},{6,5},{7,6},{4,7},{9,8},{10,9},{11,1... | collective-permute-start | bytes 380168 | tf_op jit(solution)/shard_map/while/body/eval_jaxpr/ppermute | solution.py:13
  643.4 13.9 %collective-permute-start.2 = (bf16[12,5280]{1,0:T(8,128)(2,1)S(1)}, bf16[12,5280]{1,0:T(8,128)(2,1)S(1)}, u32[]{:S(2)}, u32[]{:S(2)}) collective-permute-start(bf16[12,5280]{1,0:T(8,128)(2,1)S(1)} %get-tuple-element.401), channel_id=1, source_target_pairs={{2,0},{3,1},{0,2},{1,3},{6,4},{7,5},{4,6},{5,7},{10,8},{11,9},{8,1... | collective-permute-start | bytes 380168 | tf_op jit(solution)/shard_map/while/body/eval_jaxpr/ppermute | solution.py:13
  669.4 14.8 %collective-permute-start.5 = (bf16[12,5280]{1,0:T(8,128)(2,1)S(1)}, bf16[12,5280]{1,0:T(8,128)(2,1)S(1)}, u32[]{:S(2)}, u32[]{:S(2)}) collective-permute-start(bf16[12,5280]{1,0:T(8,128)(2,1)S(1)} %get-tuple-element.405), channel_id=1, source_target_pairs={{2,0},{3,1},{0,2},{1,3},{6,4},{7,5},{4,6},{5,7},{10,8},{11,9},{8,1... | collective-permute-start | bytes 380168 | tf_op jit(solution)/shard_map/while/body/eval_jaxpr/ppermute | solution.py:13
  673.9 16.0 %collective-permute-start.6 = (bf16[12,5280]{1,0:T(8,128)(2,1)S(1)}, bf16[12,5280]{1,0:T(8,128)(2,1)S(1)}, u32[]{:S(2)}, u32[]{:S(2)}) collective-permute-start(bf16[12,5280]{1,0:T(8,128)(2,1)S(1)} %get-tuple-element.406), channel_id=1, source_target_pairs={{1,0},{2,1},{3,2},{0,3},{5,4},{6,5},{7,6},{4,7},{9,8},{10,9},{11,1... | collective-permute-start | bytes 380168 | tf_op jit(solution)/shard_map/while/body/eval_jaxpr/ppermute | solution.py:13
  701.0 13.8 %collective-permute-start.1 = (bf16[12,5280]{1,0:T(8,128)(2,1)S(1)}, bf16[12,5280]{1,0:T(8,128)(2,1)S(1)}, u32[]{:S(2)}, u32[]{:S(2)}) collective-permute-start(bf16[12,5280]{1,0:T(8,128)(2,1)S(1)} %get-tuple-element.400), channel_id=1, source_target_pairs={{1,0},{2,1},{3,2},{0,3},{5,4},{6,5},{7,6},{4,7},{9,8},{10,9},{11,1... | collective-permute-start | bytes 380168 | tf_op jit(solution)/shard_map/while/body/eval_jaxpr/ppermute | solution.py:13
  706.2 14.0 %collective-permute-start.3 = (bf16[12,5280]{1,0:T(8,128)(2,1)S(1)}, bf16[12,5280]{1,0:T(8,128)(2,1)S(1)}, u32[]{:S(2)}, u32[]{:S(2)}) collective-permute-start(bf16[12,5280]{1,0:T(8,128)(2,1)S(1)} %get-tuple-element.402), channel_id=1, source_target_pairs={{3,0},{0,1},{1,2},{2,3},{7,4},{4,5},{5,6},{6,7},{11,8},{8,9},{9,10... | collective-permute-start | bytes 380168 | tf_op jit(solution)/shard_map/while/body/eval_jaxpr/ppermute | solution.py:13
  732.9 15.7 %collective-permute-start.6 = (bf16[12,5280]{1,0:T(8,128)(2,1)S(1)}, bf16[12,5280]{1,0:T(8,128)(2,1)S(1)}, u32[]{:S(2)}, u32[]{:S(2)}) collective-permute-start(bf16[12,5280]{1,0:T(8,128)(2,1)S(1)} %get-tuple-element.406), channel_id=1, source_target_pairs={{1,0},{2,1},{3,2},{0,3},{5,4},{6,5},{7,6},{4,7},{9,8},{10,9},{11,1... | collective-permute-start | bytes 380168 | tf_op jit(solution)/shard_map/while/body/eval_jaxpr/ppermute | solution.py:13
  759.8 13.2 %collective-permute-start.1 = (bf16[12,5280]{1,0:T(8,128)(2,1)S(1)}, bf16[12,5280]{1,0:T(8,128)(2,1)S(1)}, u32[]{:S(2)}, u32[]{:S(2)}) collective-permute-start(bf16[12,5280]{1,0:T(8,128)(2,1)S(1)} %get-tuple-element.400), channel_id=1, source_target_pairs={{1,0},{2,1},{3,2},{0,3},{5,4},{6,5},{7,6},{4,7},{9,8},{10,9},{11,1... | collective-permute-start | bytes 380168 | tf_op jit(solution)/shard_map/while/body/eval_jaxpr/ppermute | solution.py:13
  760.3 13.4 %collective-permute-start.2 = (bf16[12,5280]{1,0:T(8,128)(2,1)S(1)}, bf16[12,5280]{1,0:T(8,128)(2,1)S(1)}, u32[]{:S(2)}, u32[]{:S(2)}) collective-permute-start(bf16[12,5280]{1,0:T(8,128)(2,1)S(1)} %get-tuple-element.401), channel_id=1, source_target_pairs={{2,0},{3,1},{0,2},{1,3},{6,4},{7,5},{4,6},{5,7},{10,8},{11,9},{8,1... | collective-permute-start | bytes 380168 | tf_op jit(solution)/shard_map/while/body/eval_jaxpr/ppermute | solution.py:13
  764.9 15.2 %collective-permute-start.3 = (bf16[12,5280]{1,0:T(8,128)(2,1)S(1)}, bf16[12,5280]{1,0:T(8,128)(2,1)S(1)}, u32[]{:S(2)}, u32[]{:S(2)}) collective-permute-start(bf16[12,5280]{1,0:T(8,128)(2,1)S(1)} %get-tuple-element.402), channel_id=1, source_target_pairs={{3,0},{0,1},{1,2},{2,3},{7,4},{4,5},{5,6},{6,7},{11,8},{8,9},{9,10... | collective-permute-start | bytes 380168 | tf_op jit(solution)/shard_map/while/body/eval_jaxpr/ppermute | solution.py:13
  789.8 12.0 %collective-permute-start.5 = (bf16[12,5280]{1,0:T(8,128)(2,1)S(1)}, bf16[12,5280]{1,0:T(8,128)(2,1)S(1)}, u32[]{:S(2)}, u32[]{:S(2)}) collective-permute-start(bf16[12,5280]{1,0:T(8,128)(2,1)S(1)} %get-tuple-element.405), channel_id=1, source_target_pairs={{2,0},{3,1},{0,2},{1,3},{6,4},{7,5},{4,6},{5,7},{10,8},{11,9},{8,1... | collective-permute-start | bytes 380168 | tf_op jit(solution)/shard_map/while/body/eval_jaxpr/ppermute | solution.py:13
  791.8 13.1 %collective-permute-start.6 = (bf16[12,5280]{1,0:T(8,128)(2,1)S(1)}, bf16[12,5280]{1,0:T(8,128)(2,1)S(1)}, u32[]{:S(2)}, u32[]{:S(2)}) collective-permute-start(bf16[12,5280]{1,0:T(8,128)(2,1)S(1)} %get-tuple-element.406), channel_id=1, source_target_pairs={{1,0},{2,1},{3,2},{0,3},{5,4},{6,5},{7,6},{4,7},{9,8},{10,9},{11,1... | collective-permute-start | bytes 380168 | tf_op jit(solution)/shard_map/while/body/eval_jaxpr/ppermute | solution.py:13
  843.8 12.9 %collective-permute-start.6 = (bf16[12,5280]{1,0:T(8,128)(2,1)S(1)}, bf16[12,5280]{1,0:T(8,128)(2,1)S(1)}, u32[]{:S(2)}, u32[]{:S(2)}) collective-permute-start(bf16[12,5280]{1,0:T(8,128)(2,1)S(1)} %get-tuple-element.406), channel_id=1, source_target_pairs={{1,0},{2,1},{3,2},{0,3},{5,4},{6,5},{7,6},{4,7},{9,8},{10,9},{11,1... | collective-permute-start | bytes 380168 | tf_op jit(solution)/shard_map/while/body/eval_jaxpr/ppermute | solution.py:13
  (33 other events, 355.7 us)
Sparse Core Ops, SparseCore 0:
  9.5 102.9 all-gather.2
  114.3 95.7 all-gather.4

commit v2 on v1

--- a/solution.py
+++ b/solution.py
@@ -1,7 +1,13 @@
+import functools
+
 import jax
 import jax.numpy as jnp
 from jax import lax
+from jax.experimental import pallas as pl
+from jax.experimental.pallas import tpu as pltpu
 from jax.sharding import PartitionSpec as P
+
+MESH = pl.DeviceIdType.MESH
 
 RECUR = 2
 CAP = 12
@@ -29,13 +35,53 @@
     return result.reshape(extent)
 
 
+def exchange_kernel(direction, src_ref, dst_ref, send_sem, recv_sem):
+    groups = src_ref.shape[0]
+    me = lax.axis_index("expert")
+    place = (lax.axis_index("section"), lax.axis_index("dp"))
+    barrier = pltpu.get_barrier_semaphore()
+    for j in range(1, groups):
+        pl.semaphore_signal(
+            barrier, inc=1, device_id=place + (lax.rem(me + j, groups),), device_id_type=MESH
+        )
+    pl.semaphore_wait(barrier, groups - 1)
+    copies = []
+    for j in range(1, groups):
+        target = lax.rem(me + direction * j + groups, groups)
+        copy = pltpu.make_async_remote_copy(
+            src_ref=src_ref.at[j],
+            dst_ref=dst_ref.at[j],
+            send_sem=send_sem.at[j - 1],
+            recv_sem=recv_sem.at[j - 1],
+            device_id=place + (target,),
+            device_id_type=MESH,
+        )
+        copy.start()
+        copies.append(copy)
+    dst_ref[0] = src_ref[0]
+    for copy in copies:
+        copy.wait()
+
+
+def exchange(buffer, direction, channel):
+    groups = buffer.shape[0]
+    return pl.pallas_call(
+        functools.partial(exchange_kernel, direction),
+        out_shape=jax.ShapeDtypeStruct(buffer.shape, buffer.dtype),
+        in_specs=[pl.BlockSpec(memory_space=pltpu.VMEM)],
+        out_specs=pl.BlockSpec(memory_space=pltpu.VMEM),
+        scratch_shapes=[
+            pltpu.SemaphoreType.DMA((groups - 1,)),
+            pltpu.SemaphoreType.DMA((groups - 1,)),
+        ],
+        compiler_params=pltpu.CompilerParams(collective_id=channel, has_side_effects=True),
+    )(buffer)
+
+
 def whole_round(buffer, w_first, w_second):
-    groups = buffer.shape[0]
-    arrived = jnp.stack([buffer[0]] + [shifted(buffer[j], "expert", j) for j in range(1, groups)])
+    arrived = exchange(buffer, 1, 0)
     processed = expert_rows(arrived, w_first, w_second)
-    return jnp.stack(
-        [processed[0]] + [shifted(processed[j], "expert", groups - j) for j in range(1, groups)]
-    )
+    return exchange(processed, -1, 1)
 
 
 def core_block(current, gain_row, router_rows, w_first, w_second, assign):

time: 877 us -> 924 us (1.054)
  Pallas kernels: 0 us -> 412 us
  waiting for transfers between devices: 477 us -> 240 us
  starting transfers between devices: 164 us -> 3.07 us
  local copies, waits for them, and re-layouts: 67 us -> 111 us
    pallas_call x0 -> x22, Pallas kernels: none -> 412 us  [exchange(): pl.pallas_call(functools.partial(exchange_kernel, direction), out_shape=j...]
    ppermute x76 -> x10, waiting for transfers between devices: 319 us -> 82.7 us  [shifted(): return lax.ppermute(block, axis, route)]
    ppermute x76 -> x10, starting transfers between devices: 164 us -> 3.02 us  [shifted(): return lax.ppermute(block, axis, route)]
    reshape x0 -> x22, local copies, waits for them, and re-layouts: none -> 21.6 us  [the longest x11 10.8 us: core_block(): buffer = jnp.dot(places, normed, preferred_element_type=jnp.float32).asty...]
    reshape x11, local copies, waits for them, and re-layouts: 2.65 us -> 14.7 us  [core_block(): flat_back = returned.reshape(experts * CAP, -1)]
    reshape x11, local copies, waits for them, and re-layouts: 2.66 us -> 14.7 us  [expert_rows(): flat_rows = item_rows.reshape(-1, extent[-1])]
  transfers between devices with their start and end apart: 78 -> 12, of which waited for: 64 -> 12; matrix products, arithmetic and copies ran while one was open for 8% -> 4% of each run, Pallas kernels for 0% -> 2%
where the time goes in v2:
time: 924 us; the launch traced here: 921 us
  Pallas kernels  412 us (45%)
  waiting for transfers between devices  240 us (26%)
  matrix products  116 us (13%)
  local copies, waits for them, and re-layouts  111 us (12%)
  other arithmetic  24.1 us (3%)
  between operations  13.5 us (1%)
    pallas_call x22, Pallas kernels, exchange(): pl.pallas_call(functools.partial(exchange_kernel, direction), out_shape=j...  412 us
    dot_general x11, matrix products, expert_rows(): jnp.dot(hidden, w_second, preferred_element_type=jnp.float32)  104 us
    all_gather x1, waiting for transfers between devices, body(): lax.all_gather(w_down, 'dp', axis=3, tiled=True)  85.9 us
    ppermute x10, waiting for transfers between devices, shifted(): return lax.ppermute(block, axis, route)  82.7 us
    all_gather x1, waiting for transfers between devices, body(): lax.all_gather(w_up, 'dp', axis=2, tiled=True)  71.1 us
    unnamed x10, local copies, waits for them, and re-layouts  52.4 us
  transfers between devices with their start and end apart: 12, of which 12 were waited for; matrix products, arithmetic and copies ran while one was open for 4% of the time, Pallas kernels for 2%

profile of v2, /device:TPU:2, one launch (start us, length us, event | category | flops | bytes accessed | tf_op | source)
XLA Modules:
  0.0 920.5 jit_solution(11411432466070209904)
XLA Ops:
  17.3 22.4 %shard_map.73 = bf16[4,12,5280]{2,1,0:T(8,128)(2,1)} custom-call(bf16[4,12,5280]{2,1,0:T(8,128)(2,1)} %reshape.149.src_ref), custom_call_target="tpu_custom_call" | custom-call | tf_op jit(solution)/shard_map/pallas_call | solution.py:68
  41.3 71.1 %all-gather.3.cloned.1.call-done = bf16[1,1,5280,768]{3,1,0,2:T(2,128)(2,1)} async-done(((bf16[1,1,330,768]{3,1,0,2:T(2,128)(2,1)}), bf16[1,1,5280,768]{3,1,0,2:T(2,128)(2,1)}) %all-gather.3.cloned.1.call-update) | async-done | bytes 8110096 | tf_op jit(solution)/shard_map/all_gather | solution.py:122
  112.4 11.5 %copy.26 = bf16[1,1,5280,768]{3,2,0,1:T(8,128)(2,1)} copy(bf16[1,1,5280,768]{3,1,0,2:T(2,128)(2,1)} %all-gather.3.cloned.1.call-done) | data formatting | bytes 16220160
  123.9 85.9 %all-gather.5.cloned.1.call-done = bf16[1,1,768,5280]{2,1,0,3:T(2,128)(2,1)} async-done(((bf16[1,1,768,330]{2,1,0,3:T(2,128)(2,1)}), bf16[1,1,768,5280]{2,1,0,3:T(2,128)(2,1)}) %all-gather.5.cloned.1.call-update) | async-done | bytes 8110096 | tf_op jit(solution)/shard_map/all_gather | solution.py:123
  209.8 12.2 %fusion.39 = bf16[48,5280]{1,0:T(8,128)(2,1)S(1)} fusion(bf16[1,1,768,5280]{2,1,0,3:T(2,128)(2,1)} %all-gather.5.cloned.1.call-done, bf16[48,5280]{1,0:T(8,128)(2,1)S(1)} %reshape.150, bf16[5280,768]{1,0:T(8,128)(2,1)} %bitcast.70), kind=kOutput, calls=%fused_computation.56 | convolution fusion | flops 779152896 | bytes 17233920 | tf_op jit(solution)/shard_map/dot_general | solution.py:34
  223.0 23.9 %shard_map.74 = bf16[4,12,5280]{2,1,0:T(8,128)(2,1)} custom-call(bf16[4,12,5280]{2,1,0:T(8,128)(2,1)} %reshape.151.src_ref), custom_call_target="tpu_custom_call" | custom-call | tf_op jit(solution)/shard_map/pallas_call | solution.py:68
  248.5 34.5 %copy.18 = bf16[1,1,768,5280]{3,2,0,1:T(8,128)(2,1)} copy(bf16[1,1,768,5280]{2,1,0,3:T(2,128)(2,1)} %all-gather.5.cloned.1.call-done) | data formatting | bytes 16220160
  283.0 629.9 %while.15 = (s32[]{:T(128)}, bf16[32,5280]{1,0:T(8,128)(2,1)S(1)}, s32[]{:T(128)}, pred[]{:T(512)}, bf16[4,32,5280]{2,1,0:T(8,128)(2,1)}, /*index=5*/bf16[4,32,5...) while((s32[]{:T(128)}, bf16[32,5280]{1,0:T(8,128)(2,1)S(1)}, ...), condition=%wide.region_7.8_spmd, body=%wide.region_3.7_spmd.sunk | while | flops 816929280 | bytes 26825484 | solution.py:160
  286.0 8.1 collective-permute-done
  296.9 20.0 %eval_jaxpr.16 = bf16[4,12,5280]{2,1,0:T(8,128)(2,1)} custom-call(bf16[4,12,5280]{2,1,0:T(8,128)(2,1)} %reshape.164.src_ref), custom_call_target="tpu_custom_call" | custom-call | tf_op jit(solution)/shard_map/while/body/eval_jaxpr/pallas_call | solution.py:68
  318.2 9.1 convolution_convert_fusion.6
  328.3 20.2 %eval_jaxpr.17 = bf16[4,12,5280]{2,1,0:T(8,128)(2,1)} custom-call(bf16[4,12,5280]{2,1,0:T(8,128)(2,1)} %reshape.166.src_ref), custom_call_target="tpu_custom_call" | custom-call | tf_op jit(solution)/shard_map/while/body/eval_jaxpr/pallas_call | solution.py:68
  352.5 6.7 collective-permute-done
  361.9 22.6 %eval_jaxpr.16 = bf16[4,12,5280]{2,1,0:T(8,128)(2,1)} custom-call(bf16[4,12,5280]{2,1,0:T(8,128)(2,1)} %reshape.164.src_ref), custom_call_target="tpu_custom_call" | custom-call | tf_op jit(solution)/shard_map/while/body/eval_jaxpr/pallas_call | solution.py:68
  385.8 9.1 convolution_convert_fusion.6
  395.9 19.5 %eval_jaxpr.17 = bf16[4,12,5280]{2,1,0:T(8,128)(2,1)} custom-call(bf16[4,12,5280]{2,1,0:T(8,128)(2,1)} %reshape.166.src_ref), custom_call_target="tpu_custom_call" | custom-call | tf_op jit(solution)/shard_map/while/body/eval_jaxpr/pallas_call | solution.py:68
  419.1 6.9 collective-permute-done
  428.7 22.9 %eval_jaxpr.16 = bf16[4,12,5280]{2,1,0:T(8,128)(2,1)} custom-call(bf16[4,12,5280]{2,1,0:T(8,128)(2,1)} %reshape.164.src_ref), custom_call_target="tpu_custom_call" | custom-call | tf_op jit(solution)/shard_map/while/body/eval_jaxpr/pallas_call | solution.py:68
  452.9 9.1 convolution_convert_fusion.6
  463.0 15.3 %eval_jaxpr.17 = bf16[4,12,5280]{2,1,0:T(8,128)(2,1)} custom-call(bf16[4,12,5280]{2,1,0:T(8,128)(2,1)} %reshape.166.src_ref), custom_call_target="tpu_custom_call" | custom-call | tf_op jit(solution)/shard_map/while/body/eval_jaxpr/pallas_call | solution.py:68
  482.0 6.9 collective-permute-done
  491.7 20.7 %eval_jaxpr.16 = bf16[4,12,5280]{2,1,0:T(8,128)(2,1)} custom-call(bf16[4,12,5280]{2,1,0:T(8,128)(2,1)} %reshape.164.src_ref), custom_call_target="tpu_custom_call" | custom-call | tf_op jit(solution)/shard_map/while/body/eval_jaxpr/pallas_call | solution.py:68
  513.7 9.1 convolution_convert_fusion.6
  523.8 24.8 %eval_jaxpr.17 = bf16[4,12,5280]{2,1,0:T(8,128)(2,1)} custom-call(bf16[4,12,5280]{2,1,0:T(8,128)(2,1)} %reshape.166.src_ref), custom_call_target="tpu_custom_call" | custom-call | tf_op jit(solution)/shard_map/while/body/eval_jaxpr/pallas_call | solution.py:68
  552.2 6.9 collective-permute-done
  561.8 13.7 %eval_jaxpr.16 = bf16[4,12,5280]{2,1,0:T(8,128)(2,1)} custom-call(bf16[4,12,5280]{2,1,0:T(8,128)(2,1)} %reshape.164.src_ref), custom_call_target="tpu_custom_call" | custom-call | tf_op jit(solution)/shard_map/while/body/eval_jaxpr/pallas_call | solution.py:68
  576.9 9.1 convolution_convert_fusion.6
  587.1 13.3 %eval_jaxpr.17 = bf16[4,12,5280]{2,1,0:T(8,128)(2,1)} custom-call(bf16[4,12,5280]{2,1,0:T(8,128)(2,1)} %reshape.166.src_ref), custom_call_target="tpu_custom_call" | custom-call | tf_op jit(solution)/shard_map/while/body/eval_jaxpr/pallas_call | solution.py:68
  604.5 15.2 %collective-permute-done = bf16[32,5280]{1,0:T(8,128)(2,1)S(1)} collective-permute-done((bf16[32,5280]{1,0:T(8,128)(2,1)S(1)}, bf16[32,5280]{1,0:T(8,128)(2,1)S(1)}, u32[]{:S(2)}, u32[]{:S(2)}) %collective-permute-start) | collective-permute-done | bytes 337952 | tf_op jit(solution)/shard_map/while/body/eval_jaxpr/ppermute | solution.py:19
  622.4 15.7 %eval_jaxpr.16 = bf16[4,12,5280]{2,1,0:T(8,128)(2,1)} custom-call(bf16[4,12,5280]{2,1,0:T(8,128)(2,1)} %reshape.164.src_ref), custom_call_target="tpu_custom_call" | custom-call | tf_op jit(solution)/shard_map/while/body/eval_jaxpr/pallas_call | solution.py:68
  639.5 9.1 convolution_convert_fusion.6
  649.6 25.4 %eval_jaxpr.17 = bf16[4,12,5280]{2,1,0:T(8,128)(2,1)} custom-call(bf16[4,12,5280]{2,1,0:T(8,128)(2,1)} %reshape.166.src_ref), custom_call_target="tpu_custom_call" | custom-call | tf_op jit(solution)/shard_map/while/body/eval_jaxpr/pallas_call | solution.py:68
  678.7 11.5 %collective-permute-done = bf16[32,5280]{1,0:T(8,128)(2,1)S(1)} collective-permute-done((bf16[32,5280]{1,0:T(8,128)(2,1)S(1)}, bf16[32,5280]{1,0:T(8,128)(2,1)S(1)}, u32[]{:S(2)}, u32[]{:S(2)}) %collective-permute-start) | collective-permute-done | bytes 337952 | tf_op jit(solution)/shard_map/while/body/eval_jaxpr/ppermute | solution.py:19
  693.0 18.2 %eval_jaxpr.16 = bf16[4,12,5280]{2,1,0:T(8,128)(2,1)} custom-call(bf16[4,12,5280]{2,1,0:T(8,128)(2,1)} %reshape.164.src_ref), custom_call_target="tpu_custom_call" | custom-call | tf_op jit(solution)/shard_map/while/body/eval_jaxpr/pallas_call | solution.py:68
  712.5 9.1 convolution_convert_fusion.6
  722.6 16.2 %eval_jaxpr.17 = bf16[4,12,5280]{2,1,0:T(8,128)(2,1)} custom-call(bf16[4,12,5280]{2,1,0:T(8,128)(2,1)} %reshape.166.src_ref), custom_call_target="tpu_custom_call" | custom-call | tf_op jit(solution)/shard_map/while/body/eval_jaxpr/pallas_call | solution.py:68
  742.5 6.9 collective-permute-done
  752.1 17.3 %eval_jaxpr.16 = bf16[4,12,5280]{2,1,0:T(8,128)(2,1)} custom-call(bf16[4,12,5280]{2,1,0:T(8,128)(2,1)} %reshape.164.src_ref), custom_call_target="tpu_custom_call" | custom-call | tf_op jit(solution)/shard_map/while/body/eval_jaxpr/pallas_call | solution.py:68
  770.7 9.1 convolution_convert_fusion.6
  780.8 21.3 %eval_jaxpr.17 = bf16[4,12,5280]{2,1,0:T(8,128)(2,1)} custom-call(bf16[4,12,5280]{2,1,0:T(8,128)(2,1)} %reshape.166.src_ref), custom_call_target="tpu_custom_call" | custom-call | tf_op jit(solution)/shard_map/while/body/eval_jaxpr/pallas_call | solution.py:68
  805.8 6.9 collective-permute-done
  815.4 17.3 %eval_jaxpr.16 = bf16[4,12,5280]{2,1,0:T(8,128)(2,1)} custom-call(bf16[4,12,5280]{2,1,0:T(8,128)(2,1)} %reshape.164.src_ref), custom_call_target="tpu_custom_call" | custom-call | tf_op jit(solution)/shard_map/while/body/eval_jaxpr/pallas_call | solution.py:68
  834.1 9.1 convolution_convert_fusion.6
  844.2 14.8 %eval_jaxpr.17 = bf16[4,12,5280]{2,1,0:T(8,128)(2,1)} custom-call(bf16[4,12,5280]{2,1,0:T(8,128)(2,1)} %reshape.166.src_ref), custom_call_target="tpu_custom_call" | custom-call | tf_op jit(solution)/shard_map/while/body/eval_jaxpr/pallas_call | solution.py:68
  862.7 6.9 collective-permute-done
  872.3 13.3 %eval_jaxpr.16 = bf16[4,12,5280]{2,1,0:T(8,128)(2,1)} custom-call(bf16[4,12,5280]{2,1,0:T(8,128)(2,1)} %reshape.164.src_ref), custom_call_target="tpu_custom_call" | custom-call | tf_op jit(solution)/shard_map/while/body/eval_jaxpr/pallas_call | solution.py:68
  887.0 9.1 convolution_convert_fusion.6
  897.2 13.8 %eval_jaxpr.17 = bf16[4,12,5280]{2,1,0:T(8,128)(2,1)} custom-call(bf16[4,12,5280]{2,1,0:T(8,128)(2,1)} %reshape.166.src_ref), custom_call_target="tpu_custom_call" | custom-call | tf_op jit(solution)/shard_map/while/body/eval_jaxpr/pallas_call | solution.py:68
  (176 shorter events, 104.2 us)
Async XLA Ops:
  6.5 34.4 %copy-start.2 = (bf16[1,4,5280]{2,1,0:T(4,128)(2,1)S(1)}, bf16[1,4,5280]{2,1,0:T(4,128)(2,1)}, u32[]{:S(2)}) copy-start(bf16[1,4,5280]{2,1,0:T(4,128)(2,1)} %param.13) | copy-start | bytes 126724
  6.5 105.8 %all-gather.3.cloned.1.call-start = ((), (), s32[]{:S(2)}) async-start(), calls=%async_computation | async-start | bytes 17233920 | tf_op jit(solution)/shard_map/all_gather | solution.py:122
  9.4 200.4 %all-gather.5.cloned.1.call-start = ((), (), s32[]{:S(2)}) async-start(), calls=%async_computation.1 | async-start | bytes 17233920 | tf_op jit(solution)/shard_map/all_gather | solution.py:123
  248.5 34.5 %copy-start = (f32[1,5280]{1,0:T(1,128)S(1)}, f32[1,5280]{1,0:T(1,128)}, u32[]{:S(2)}) copy-start(f32[1,5280]{1,0:T(1,128)} %param.12) | copy-start | bytes 63364
  283.0 11.1 %collective-permute-start = (bf16[32,5280]{1,0:T(8,128)(2,1)S(1)}, bf16[32,5280]{1,0:T(8,128)(2,1)S(1)}, u32[]{:S(2)}, u32[]{:S(2)}) collective-permute-start(bf16[32,5280]{1,0:T(8,128)(2,1)S(1)} %get-tuple-element.398), channel_id=1, source_target_pairs={{192,0},{0,64},{64,128},{128,192},{193,1},{1,65},{65,129},{129,193... | collective-permute-start | bytes 1013768 | tf_op jit(solution)/shard_map/while/body/eval_jaxpr/ppermute | solution.py:19
  350.6 8.5 collective-permute-start
  417.4 8.5 collective-permute-start
  480.4 8.5 collective-permute-start
  550.6 8.5 collective-permute-start
  602.3 17.3 %collective-permute-start = (bf16[32,5280]{1,0:T(8,128)(2,1)S(1)}, bf16[32,5280]{1,0:T(8,128)(2,1)S(1)}, u32[]{:S(2)}, u32[]{:S(2)}) collective-permute-start(bf16[32,5280]{1,0:T(8,128)(2,1)S(1)} %get-tuple-element.398), channel_id=1, source_target_pairs={{192,0},{0,64},{64,128},{128,192},{193,1},{1,65},{65,129},{129,193... | collective-permute-start | bytes 1013768 | tf_op jit(solution)/shard_map/while/body/eval_jaxpr/ppermute | solution.py:19
  677.0 13.2 %collective-permute-start = (bf16[32,5280]{1,0:T(8,128)(2,1)S(1)}, bf16[32,5280]{1,0:T(8,128)(2,1)S(1)}, u32[]{:S(2)}, u32[]{:S(2)}) collective-permute-start(bf16[32,5280]{1,0:T(8,128)(2,1)S(1)} %get-tuple-element.398), channel_id=1, source_target_pairs={{192,0},{0,64},{64,128},{128,192},{193,1},{1,65},{65,129},{129,193... | collective-permute-start | bytes 1013768 | tf_op jit(solution)/shard_map/while/body/eval_jaxpr/ppermute | solution.py:19
  740.8 8.5 collective-permute-start
  804.1 8.5 collective-permute-start
  861.0 8.5 collective-permute-start
  912.9 0.7 copy-start.1
Sparse Core Ops, SparseCore 0:
  9.5 102.8 all-gather.2
  114.2 95.5 all-gather.4

commit v3 on v2

--- a/solution.py
+++ b/solution.py
@@ -31,29 +31,48 @@
     hidden = jax.nn.gelu(jnp.dot(flat_rows, w_first, preferred_element_type=jnp.float32)).astype(
         jnp.bfloat16
     )
-    result = jnp.dot(hidden, w_second, preferred_element_type=jnp.float32).astype(jnp.bfloat16)
+    result = lax.dot_general(
+        hidden, w_second, (((1,), (1,)), ((), ())), preferred_element_type=jnp.float32
+    ).astype(jnp.bfloat16)
     return result.reshape(extent)
 
 
-def exchange_kernel(direction, src_ref, dst_ref, send_sem, recv_sem):
+def neighbour(delta):
+    experts = lax.axis_size("expert")
+    dp = lax.axis_index("dp")
+    half = lax.rem(dp // 2, 2)
+    chip = lax.axis_index("expert") * 2 + half
+    target = lax.rem(chip + delta + 2 * experts, 2 * experts)
+    shifted_dp = dp + (lax.rem(target, 2) - half) * 2
+    return (lax.axis_index("section"), shifted_dp, target // 2)
+
+
+def dispatch_delta(group):
+    half = lax.rem(lax.axis_index("dp") // 2, 2)
+    return group * (1 if group == 2 else -1) * (1 - 2 * half)
+
+
+def return_delta(group):
+    half = lax.rem(lax.axis_index("dp") // 2, 2)
+    return group * (2 * half - 1)
+
+
+def exchange_kernel(outgoing, incoming, src_ref, dst_ref, send_sem, recv_sem):
     groups = src_ref.shape[0]
-    me = lax.axis_index("expert")
-    place = (lax.axis_index("section"), lax.axis_index("dp"))
     barrier = pltpu.get_barrier_semaphore()
     for j in range(1, groups):
         pl.semaphore_signal(
-            barrier, inc=1, device_id=place + (lax.rem(me + j, groups),), device_id_type=MESH
+            barrier, inc=1, device_id=neighbour(incoming(j)), device_id_type=MESH
         )
     pl.semaphore_wait(barrier, groups - 1)
     copies = []
     for j in range(1, groups):
-        target = lax.rem(me + direction * j + groups, groups)
         copy = pltpu.make_async_remote_copy(
             src_ref=src_ref.at[j],
             dst_ref=dst_ref.at[j],
             send_sem=send_sem.at[j - 1],
             recv_sem=recv_sem.at[j - 1],
-            device_id=place + (target,),
+            device_id=neighbour(outgoing(j)),
             device_id_type=MESH,
         )
         copy.start()
@@ -63,10 +82,10 @@
         copy.wait()
 
 
-def exchange(buffer, direction, channel):
+def exchange(buffer, outgoing, incoming, channel):
     groups = buffer.shape[0]
     return pl.pallas_call(
-        functools.partial(exchange_kernel, direction),
+        functools.partial(exchange_kernel, outgoing, incoming),
         out_shape=jax.ShapeDtypeStruct(buffer.shape, buffer.dtype),
         in_specs=[pl.BlockSpec(memory_space=pltpu.VMEM)],
         out_specs=pl.BlockSpec(memory_space=pltpu.VMEM),
@@ -78,10 +97,17 @@
     )(buffer)
 
 
+def group_of(assign, experts):
+    relative = jnp.mod(assign - lax.axis_index("expert"), experts)
+    half = lax.rem(lax.axis_index("dp") // 2, 2)
+    swapped = jnp.where((relative == 1) == (half == 0), 2, 1)
+    return jnp.where(relative == 2, 3, jnp.where(relative == 0, 0, swapped))
+
+
 def whole_round(buffer, w_first, w_second):
-    arrived = exchange(buffer, 1, 0)
+    arrived = exchange(buffer, dispatch_delta, return_delta, 0)
     processed = expert_rows(arrived, w_first, w_second)
-    return exchange(processed, -1, 1)
+    return exchange(processed, return_delta, dispatch_delta, 1)
 
 
 def core_block(current, gain_row, router_rows, w_first, w_second, assign):
@@ -98,8 +124,7 @@
     ).astype(jnp.float32)
     counts = jnp.dot(earlier, onehot, preferred_element_type=jnp.float32)
     slot_index = jnp.sum(onehot * counts, axis=-1).astype(jnp.int32)
-    relative = jnp.mod(assign - lax.axis_index("expert"), experts)
-    target = relative * CAP + slot_index
+    target = group_of(assign, experts) * CAP + slot_index
     places = (
         lax.broadcasted_iota(jnp.int32, (experts * CAP, tokens), 0) == target[None, :]
     ).astype(jnp.bfloat16)
@@ -120,7 +145,7 @@
     section_index = lax.axis_index("section")
     up_all, down_all = (
         lax.all_gather(w_up, "dp", axis=2, tiled=True),
-        lax.all_gather(w_down, "dp", axis=3, tiled=True),
+        lax.all_gather(jnp.swapaxes(w_down, 2, 3), "dp", axis=2, tiled=True),
     )
     w_first = up_all[0, 0]
     w_second = down_all[0, 0]

time: 924 us -> 932 us (level); the launches traced: 921 us -> 916 us
  Pallas kernels: 412 us -> 443 us
  local copies, waits for them, and re-layouts: 111 us -> 87.8 us
  waiting for transfers between devices: 240 us -> 217 us
    pallas_call x22, Pallas kernels: 412 us -> 443 us  [exchange(): pl.pallas_call(functools.partial(exchange_kernel, outgoing, incoming), ou...]
    unnamed x10, local copies, waits for them, and re-layouts: 52.4 us -> 29.4 us
    ppermute x10, waiting for transfers between devices: 82.7 us -> 68.3 us  [shifted(): return lax.ppermute(block, axis, route)]
  transfers between devices with their start and end apart: 12 -> 12, of which waited for: 12 -> 12; matrix products, arithmetic and copies ran while one was open for 4% -> 4% of each run, Pallas kernels for 2% -> 3%
where the time goes in v3:
time: 932 us; the launch traced here: 916 us
  Pallas kernels  443 us (48%)
  waiting for transfers between devices  217 us (23%)
  matrix products  121 us (13%)
  local copies, waits for them, and re-layouts  87.8 us (9%)
  other arithmetic  24.2 us (3%)
  between operations  13.6 us (1%)
    pallas_call x22, Pallas kernels, exchange(): pl.pallas_call(functools.partial(exchange_kernel, outgoing, incoming), ou...  443 us
    dot_general x11, matrix products, expert_rows(): lax.dot_general(hidden, w_second, (((1,), (1,)), ((), ())), preferred_ele...  109 us
    all_gather x1, waiting for transfers between devices, body(): lax.all_gather(jnp.swapaxes(w_down, 2, 3), 'dp', axis=2, tiled=True)  85.9 us
    ppermute x10, waiting for transfers between devices, shifted(): return lax.ppermute(block, axis, route)  68.3 us
    all_gather x1, waiting for transfers between devices, body(): lax.all_gather(w_up, 'dp', axis=2, tiled=True)  62.6 us
    unnamed x10, local copies, waits for them, and re-layouts  29.4 us
  transfers between devices with their start and end apart: 12, of which 12 were waited for; matrix products, arithmetic and copies ran while one was open for 4% of the time, Pallas kernels for 3%

profile of v3, /device:TPU:2, one launch (start us, length us, event | category | flops | bytes accessed | tf_op | source)
XLA Modules:
  0.0 915.7 jit_solution(13878870989938404642)
XLA Ops:
  17.3 23.5 %shard_map.73 = bf16[4,12,5280]{2,1,0:T(8,128)(2,1)} custom-call(bf16[4,12,5280]{2,1,0:T(8,128)(2,1)} %reshape.165.src_ref), custom_call_target="tpu_custom_call" | custom-call | tf_op jit(solution)/shard_map/pallas_call | solution.py:87
  42.4 62.6 %all-gather.3.cloned.1.call-done = bf16[1,1,5280,768]{3,1,0,2:T(2,128)(2,1)} async-done(((bf16[1,1,330,768]{3,1,0,2:T(2,128)(2,1)}), bf16[1,1,5280,768]{3,1,0,2:T(2,128)(2,1)}) %all-gather.3.cloned.1.call-update) | async-done | bytes 8110096 | tf_op jit(solution)/shard_map/all_gather | solution.py:147
  105.0 11.5 %copy.18 = bf16[1,1,5280,768]{3,2,0,1:T(8,128)(2,1)} copy(bf16[1,1,5280,768]{3,1,0,2:T(2,128)(2,1)} %all-gather.3.cloned.1.call-done) | data formatting | bytes 16220160
  116.6 85.9 %all-gather.5.cloned.1.call-done = bf16[1,1,5280,768]{3,1,0,2:T(2,128)(2,1)} async-done(((bf16[1,1,330,768]{3,1,0,2:T(2,128)(2,1)}), bf16[1,1,5280,768]{3,1,0,2:T(2,128)(2,1)}) %all-gather.5.cloned.1.call-update) | async-done | bytes 8110096 | tf_op jit(solution)/shard_map/all_gather | solution.py:148
  202.4 11.6 %copy.17 = bf16[1,1,5280,768]{3,2,0,1:T(8,128)(2,1)} copy(bf16[1,1,5280,768]{3,1,0,2:T(2,128)(2,1)} %all-gather.5.cloned.1.call-done) | data formatting | bytes 16220160
  214.0 9.9 %convolution_convert_fusion.2 = bf16[48,5280]{1,0:T(8,128)(2,1)S(1)} fusion(bf16[5280,768]{1,0:T(8,128)(2,1)} %bitcast.73, bf16[48,5280]{1,0:T(8,128)(2,1)S(1)} %reshape.166, bf16[5280,768]{1,0:T(8,128)(2,1)} %bitcast.71), kind=kOutput, calls=%fused_computation.56 | convolution fusion | flops 779152896 | bytes 17233920 | tf_op jit(solution)/shard_map/dot_general | solution.py:34
  224.9 22.2 %shard_map.74 = bf16[4,12,5280]{2,1,0:T(8,128)(2,1)} custom-call(bf16[4,12,5280]{2,1,0:T(8,128)(2,1)} %reshape.167.src_ref), custom_call_target="tpu_custom_call" | custom-call | tf_op jit(solution)/shard_map/pallas_call | solution.py:87
  248.8 659.4 %while.16 = (s32[]{:T(128)}, bf16[32,5280]{1,0:T(8,128)(2,1)S(1)}, s32[]{:T(128)}, pred[]{:T(512)}, bf16[4,32,5280]{2,1,0:T(8,128)(2,1)}, /*index=5*/bf16[4,32,5...) while((s32[]{:T(128)}, bf16[32,5280]{1,0:T(8,128)(2,1)S(1)}, ...), condition=%wide.region_7.8_spmd, body=%wide.region_3.7_spmd.sunk | while | flops 816929536 | bytes 26825756 | solution.py:185
  252.1 7.4 collective-permute-done
  262.5 19.1 %eval_jaxpr.18 = bf16[4,12,5280]{2,1,0:T(8,128)(2,1)} custom-call(bf16[4,12,5280]{2,1,0:T(8,128)(2,1)} %reshape.180.src_ref), custom_call_target="tpu_custom_call" | custom-call | tf_op jit(solution)/shard_map/while/body/eval_jaxpr/pallas_call | solution.py:87
  283.0 9.9 %convolution_convert_fusion.7 = bf16[48,5280]{1,0:T(8,128)(2,1)S(1)} fusion(bf16[5280,768]{1,0:T(8,128)(2,1)} %get-tuple-element.447, bf16[48,5280]{1,0:T(8,128)(2,1)S(1)} %reshape.181, bf16[5280,768]{1,0:T(8,128)(2,1)} %get-tuple-element.446), kind=kOutput, calls=%fused_computation.clone.1 | convolution fusion | flops 779152896 | bytes 17233920 | tf_op jit(solution)/shard_map/while/body/eval_jaxpr/dot_general | solution.py:34
  293.9 20.6 %eval_jaxpr.19 = bf16[4,12,5280]{2,1,0:T(8,128)(2,1)} custom-call(bf16[4,12,5280]{2,1,0:T(8,128)(2,1)} %reshape.182.src_ref), custom_call_target="tpu_custom_call" | custom-call | tf_op jit(solution)/shard_map/while/body/eval_jaxpr/pallas_call | solution.py:87
  318.1 6.7 collective-permute-done
  327.8 21.6 %eval_jaxpr.18 = bf16[4,12,5280]{2,1,0:T(8,128)(2,1)} custom-call(bf16[4,12,5280]{2,1,0:T(8,128)(2,1)} %reshape.180.src_ref), custom_call_target="tpu_custom_call" | custom-call | tf_op jit(solution)/shard_map/while/body/eval_jaxpr/pallas_call | solution.py:87
  350.7 9.9 %convolution_convert_fusion.7 = bf16[48,5280]{1,0:T(8,128)(2,1)S(1)} fusion(bf16[5280,768]{1,0:T(8,128)(2,1)} %get-tuple-element.447, bf16[48,5280]{1,0:T(8,128)(2,1)S(1)} %reshape.181, bf16[5280,768]{1,0:T(8,128)(2,1)} %get-tuple-element.446), kind=kOutput, calls=%fused_computation.clone.1 | convolution fusion | flops 779152896 | bytes 17233920 | tf_op jit(solution)/shard_map/while/body/eval_jaxpr/dot_general | solution.py:34
  361.6 20.7 %eval_jaxpr.19 = bf16[4,12,5280]{2,1,0:T(8,128)(2,1)} custom-call(bf16[4,12,5280]{2,1,0:T(8,128)(2,1)} %reshape.182.src_ref), custom_call_target="tpu_custom_call" | custom-call | tf_op jit(solution)/shard_map/while/body/eval_jaxpr/pallas_call | solution.py:87
  385.7 7.0 collective-permute-done
  395.8 18.1 %eval_jaxpr.18 = bf16[4,12,5280]{2,1,0:T(8,128)(2,1)} custom-call(bf16[4,12,5280]{2,1,0:T(8,128)(2,1)} %reshape.180.src_ref), custom_call_target="tpu_custom_call" | custom-call | tf_op jit(solution)/shard_map/while/body/eval_jaxpr/pallas_call | solution.py:87
  415.2 9.9 %convolution_convert_fusion.7 = bf16[48,5280]{1,0:T(8,128)(2,1)S(1)} fusion(bf16[5280,768]{1,0:T(8,128)(2,1)} %get-tuple-element.447, bf16[48,5280]{1,0:T(8,128)(2,1)S(1)} %reshape.181, bf16[5280,768]{1,0:T(8,128)(2,1)} %get-tuple-element.446), kind=kOutput, calls=%fused_computation.clone.1 | convolution fusion | flops 779152896 | bytes 17233920 | tf_op jit(solution)/shard_map/while/body/eval_jaxpr/dot_general | solution.py:34
  426.1 19.9 %eval_jaxpr.19 = bf16[4,12,5280]{2,1,0:T(8,128)(2,1)} custom-call(bf16[4,12,5280]{2,1,0:T(8,128)(2,1)} %reshape.182.src_ref), custom_call_target="tpu_custom_call" | custom-call | tf_op jit(solution)/shard_map/while/body/eval_jaxpr/pallas_call | solution.py:87
  449.3 6.9 collective-permute-done
  459.3 17.4 %eval_jaxpr.18 = bf16[4,12,5280]{2,1,0:T(8,128)(2,1)} custom-call(bf16[4,12,5280]{2,1,0:T(8,128)(2,1)} %reshape.180.src_ref), custom_call_target="tpu_custom_call" | custom-call | tf_op jit(solution)/shard_map/while/body/eval_jaxpr/pallas_call | solution.py:87
  478.0 9.9 %convolution_convert_fusion.7 = bf16[48,5280]{1,0:T(8,128)(2,1)S(1)} fusion(bf16[5280,768]{1,0:T(8,128)(2,1)} %get-tuple-element.447, bf16[48,5280]{1,0:T(8,128)(2,1)S(1)} %reshape.181, bf16[5280,768]{1,0:T(8,128)(2,1)} %get-tuple-element.446), kind=kOutput, calls=%fused_computation.clone.1 | convolution fusion | flops 779152896 | bytes 17233920 | tf_op jit(solution)/shard_map/while/body/eval_jaxpr/dot_general | solution.py:34
  488.9 19.4 %eval_jaxpr.19 = bf16[4,12,5280]{2,1,0:T(8,128)(2,1)} custom-call(bf16[4,12,5280]{2,1,0:T(8,128)(2,1)} %reshape.182.src_ref), custom_call_target="tpu_custom_call" | custom-call | tf_op jit(solution)/shard_map/while/body/eval_jaxpr/pallas_call | solution.py:87
  513.1 5.5 collective-permute-done
  521.6 19.8 %eval_jaxpr.18 = bf16[4,12,5280]{2,1,0:T(8,128)(2,1)} custom-call(bf16[4,12,5280]{2,1,0:T(8,128)(2,1)} %reshape.180.src_ref), custom_call_target="tpu_custom_call" | custom-call | tf_op jit(solution)/shard_map/while/body/eval_jaxpr/pallas_call | solution.py:87
  542.7 9.9 %convolution_convert_fusion.7 = bf16[48,5280]{1,0:T(8,128)(2,1)S(1)} fusion(bf16[5280,768]{1,0:T(8,128)(2,1)} %get-tuple-element.447, bf16[48,5280]{1,0:T(8,128)(2,1)S(1)} %reshape.181, bf16[5280,768]{1,0:T(8,128)(2,1)} %get-tuple-element.446), kind=kOutput, calls=%fused_computation.clone.1 | convolution fusion | flops 779152896 | bytes 17233920 | tf_op jit(solution)/shard_map/while/body/eval_jaxpr/dot_general | solution.py:34
  553.6 20.7 %eval_jaxpr.19 = bf16[4,12,5280]{2,1,0:T(8,128)(2,1)} custom-call(bf16[4,12,5280]{2,1,0:T(8,128)(2,1)} %reshape.182.src_ref), custom_call_target="tpu_custom_call" | custom-call | tf_op jit(solution)/shard_map/while/body/eval_jaxpr/pallas_call | solution.py:87
  577.9 7.4 collective-permute-done
  588.3 18.5 %eval_jaxpr.18 = bf16[4,12,5280]{2,1,0:T(8,128)(2,1)} custom-call(bf16[4,12,5280]{2,1,0:T(8,128)(2,1)} %reshape.180.src_ref), custom_call_target="tpu_custom_call" | custom-call | tf_op jit(solution)/shard_map/while/body/eval_jaxpr/pallas_call | solution.py:87
  608.1 9.9 %convolution_convert_fusion.7 = bf16[48,5280]{1,0:T(8,128)(2,1)S(1)} fusion(bf16[5280,768]{1,0:T(8,128)(2,1)} %get-tuple-element.447, bf16[48,5280]{1,0:T(8,128)(2,1)S(1)} %reshape.181, bf16[5280,768]{1,0:T(8,128)(2,1)} %get-tuple-element.446), kind=kOutput, calls=%fused_computation.clone.1 | convolution fusion | flops 779152896 | bytes 17233920 | tf_op jit(solution)/shard_map/while/body/eval_jaxpr/dot_general | solution.py:34
  619.0 20.0 %eval_jaxpr.19 = bf16[4,12,5280]{2,1,0:T(8,128)(2,1)} custom-call(bf16[4,12,5280]{2,1,0:T(8,128)(2,1)} %reshape.182.src_ref), custom_call_target="tpu_custom_call" | custom-call | tf_op jit(solution)/shard_map/while/body/eval_jaxpr/pallas_call | solution.py:87
  642.4 7.8 collective-permute-done
  653.2 20.9 %eval_jaxpr.18 = bf16[4,12,5280]{2,1,0:T(8,128)(2,1)} custom-call(bf16[4,12,5280]{2,1,0:T(8,128)(2,1)} %reshape.180.src_ref), custom_call_target="tpu_custom_call" | custom-call | tf_op jit(solution)/shard_map/while/body/eval_jaxpr/pallas_call | solution.py:87
  675.4 9.9 %convolution_convert_fusion.7 = bf16[48,5280]{1,0:T(8,128)(2,1)S(1)} fusion(bf16[5280,768]{1,0:T(8,128)(2,1)} %get-tuple-element.447, bf16[48,5280]{1,0:T(8,128)(2,1)S(1)} %reshape.181, bf16[5280,768]{1,0:T(8,128)(2,1)} %get-tuple-element.446), kind=kOutput, calls=%fused_computation.clone.1 | convolution fusion | flops 779152896 | bytes 17233920 | tf_op jit(solution)/shard_map/while/body/eval_jaxpr/dot_general | solution.py:34
  686.3 19.5 %eval_jaxpr.19 = bf16[4,12,5280]{2,1,0:T(8,128)(2,1)} custom-call(bf16[4,12,5280]{2,1,0:T(8,128)(2,1)} %reshape.182.src_ref), custom_call_target="tpu_custom_call" | custom-call | tf_op jit(solution)/shard_map/while/body/eval_jaxpr/pallas_call | solution.py:87
  709.2 8.9 collective-permute-done
  721.2 18.9 %eval_jaxpr.18 = bf16[4,12,5280]{2,1,0:T(8,128)(2,1)} custom-call(bf16[4,12,5280]{2,1,0:T(8,128)(2,1)} %reshape.180.src_ref), custom_call_target="tpu_custom_call" | custom-call | tf_op jit(solution)/shard_map/while/body/eval_jaxpr/pallas_call | solution.py:87
  741.5 9.9 %convolution_convert_fusion.7 = bf16[48,5280]{1,0:T(8,128)(2,1)S(1)} fusion(bf16[5280,768]{1,0:T(8,128)(2,1)} %get-tuple-element.447, bf16[48,5280]{1,0:T(8,128)(2,1)S(1)} %reshape.181, bf16[5280,768]{1,0:T(8,128)(2,1)} %get-tuple-element.446), kind=kOutput, calls=%fused_computation.clone.1 | convolution fusion | flops 779152896 | bytes 17233920 | tf_op jit(solution)/shard_map/while/body/eval_jaxpr/dot_general | solution.py:34
  752.4 19.7 %eval_jaxpr.19 = bf16[4,12,5280]{2,1,0:T(8,128)(2,1)} custom-call(bf16[4,12,5280]{2,1,0:T(8,128)(2,1)} %reshape.182.src_ref), custom_call_target="tpu_custom_call" | custom-call | tf_op jit(solution)/shard_map/while/body/eval_jaxpr/pallas_call | solution.py:87
  777.3 4.9 collective-permute-done
  785.3 22.9 %eval_jaxpr.18 = bf16[4,12,5280]{2,1,0:T(8,128)(2,1)} custom-call(bf16[4,12,5280]{2,1,0:T(8,128)(2,1)} %reshape.180.src_ref), custom_call_target="tpu_custom_call" | custom-call | tf_op jit(solution)/shard_map/while/body/eval_jaxpr/pallas_call | solution.py:87
  809.6 9.9 %convolution_convert_fusion.7 = bf16[48,5280]{1,0:T(8,128)(2,1)S(1)} fusion(bf16[5280,768]{1,0:T(8,128)(2,1)} %get-tuple-element.447, bf16[48,5280]{1,0:T(8,128)(2,1)S(1)} %reshape.181, bf16[5280,768]{1,0:T(8,128)(2,1)} %get-tuple-element.446), kind=kOutput, calls=%fused_computation.clone.1 | convolution fusion | flops 779152896 | bytes 17233920 | tf_op jit(solution)/shard_map/while/body/eval_jaxpr/dot_general | solution.py:34
  820.6 20.8 %eval_jaxpr.19 = bf16[4,12,5280]{2,1,0:T(8,128)(2,1)} custom-call(bf16[4,12,5280]{2,1,0:T(8,128)(2,1)} %reshape.182.src_ref), custom_call_target="tpu_custom_call" | custom-call | tf_op jit(solution)/shard_map/while/body/eval_jaxpr/pallas_call | solution.py:87
  845.9 6.0 collective-permute-done
  854.9 18.8 %eval_jaxpr.18 = bf16[4,12,5280]{2,1,0:T(8,128)(2,1)} custom-call(bf16[4,12,5280]{2,1,0:T(8,128)(2,1)} %reshape.180.src_ref), custom_call_target="tpu_custom_call" | custom-call | tf_op jit(solution)/shard_map/while/body/eval_jaxpr/pallas_call | solution.py:87
  875.1 9.9 %convolution_convert_fusion.7 = bf16[48,5280]{1,0:T(8,128)(2,1)S(1)} fusion(bf16[5280,768]{1,0:T(8,128)(2,1)} %get-tuple-element.447, bf16[48,5280]{1,0:T(8,128)(2,1)S(1)} %reshape.181, bf16[5280,768]{1,0:T(8,128)(2,1)} %get-tuple-element.446), kind=kOutput, calls=%fused_computation.clone.1 | convolution fusion | flops 779152896 | bytes 17233920 | tf_op jit(solution)/shard_map/while/body/eval_jaxpr/dot_general | solution.py:34
  886.0 20.5 %eval_jaxpr.19 = bf16[4,12,5280]{2,1,0:T(8,128)(2,1)} custom-call(bf16[4,12,5280]{2,1,0:T(8,128)(2,1)} %reshape.182.src_ref), custom_call_target="tpu_custom_call" | custom-call | tf_op jit(solution)/shard_map/while/body/eval_jaxpr/pallas_call | solution.py:87
  (176 shorter events, 108.5 us)
Async XLA Ops:
  6.5 35.6 %copy-start.2 = (bf16[1,4,5280]{2,1,0:T(4,128)(2,1)S(1)}, bf16[1,4,5280]{2,1,0:T(4,128)(2,1)}, u32[]{:S(2)}) copy-start(bf16[1,4,5280]{2,1,0:T(4,128)(2,1)} %param.13) | copy-start | bytes 126724
  6.5 98.5 %all-gather.3.cloned.1.call-start = ((), (), s32[]{:S(2)}) async-start(), calls=%async_computation | async-start | bytes 17233920 | tf_op jit(solution)/shard_map/all_gather | solution.py:147
  9.4 193.1 %all-gather.5.cloned.1.call-start = ((), (), s32[]{:S(2)}) async-start(), calls=%async_computation.1 | async-start | bytes 17233920 | tf_op jit(solution)/shard_map/all_gather | solution.py:148
  214.0 34.8 %copy-start = (f32[1,5280]{1,0:T(1,128)S(1)}, f32[1,5280]{1,0:T(1,128)}, u32[]{:S(2)}) copy-start(f32[1,5280]{1,0:T(1,128)} %param.12) | copy-start | bytes 63364
  249.0 10.5 %collective-permute-start = (bf16[32,5280]{1,0:T(8,128)(2,1)S(1)}, bf16[32,5280]{1,0:T(8,128)(2,1)S(1)}, u32[]{:S(2)}, u32[]{:S(2)}) collective-permute-start(bf16[32,5280]{1,0:T(8,128)(2,1)S(1)} %get-tuple-element.415), channel_id=1, source_target_pairs={{192,0},{0,64},{64,128},{128,192},{193,1},{1,65},{65,129},{129,193... | collective-permute-start | bytes 1013768 | tf_op jit(solution)/shard_map/while/body/eval_jaxpr/ppermute | solution.py:19
  316.2 8.5 collective-permute-start
  384.0 8.7 collective-permute-start
  447.7 8.5 collective-permute-start
  510.0 8.5 collective-permute-start
  576.1 9.2 %collective-permute-start = (bf16[32,5280]{1,0:T(8,128)(2,1)S(1)}, bf16[32,5280]{1,0:T(8,128)(2,1)S(1)}, u32[]{:S(2)}, u32[]{:S(2)}) collective-permute-start(bf16[32,5280]{1,0:T(8,128)(2,1)S(1)} %get-tuple-element.415), channel_id=1, source_target_pairs={{192,0},{0,64},{64,128},{128,192},{193,1},{1,65},{65,129},{129,193... | collective-permute-start | bytes 1013768 | tf_op jit(solution)/shard_map/while/body/eval_jaxpr/ppermute | solution.py:19
  640.7 9.4 %collective-permute-start = (bf16[32,5280]{1,0:T(8,128)(2,1)S(1)}, bf16[32,5280]{1,0:T(8,128)(2,1)S(1)}, u32[]{:S(2)}, u32[]{:S(2)}) collective-permute-start(bf16[32,5280]{1,0:T(8,128)(2,1)S(1)} %get-tuple-element.415), channel_id=1, source_target_pairs={{192,0},{0,64},{64,128},{128,192},{193,1},{1,65},{65,129},{129,193... | collective-permute-start | bytes 1013768 | tf_op jit(solution)/shard_map/while/body/eval_jaxpr/ppermute | solution.py:19
  707.5 10.6 %collective-permute-start = (bf16[32,5280]{1,0:T(8,128)(2,1)S(1)}, bf16[32,5280]{1,0:T(8,128)(2,1)S(1)}, u32[]{:S(2)}, u32[]{:S(2)}) collective-permute-start(bf16[32,5280]{1,0:T(8,128)(2,1)S(1)} %get-tuple-element.415), channel_id=1, source_target_pairs={{192,0},{0,64},{64,128},{128,192},{193,1},{1,65},{65,129},{129,193... | collective-permute-start | bytes 1013768 | tf_op jit(solution)/shard_map/while/body/eval_jaxpr/ppermute | solution.py:19
  773.7 8.5 collective-permute-start
  843.1 8.8 collective-permute-start
  908.2 0.7 copy-start.1
Sparse Core Ops, SparseCore 0:
  9.5 95.4 all-gather.2
  106.9 95.4 all-gather.4

commit v4 on v1

--- a/solution.py
+++ b/solution.py
@@ -25,7 +25,9 @@
     hidden = jax.nn.gelu(jnp.dot(flat_rows, w_first, preferred_element_type=jnp.float32)).astype(
         jnp.bfloat16
     )
-    result = jnp.dot(hidden, w_second, preferred_element_type=jnp.float32).astype(jnp.bfloat16)
+    result = lax.dot_general(
+        hidden, w_second, (((1,), (1,)), ((), ())), preferred_element_type=jnp.float32
+    ).astype(jnp.bfloat16)
     return result.reshape(extent)
 
 
@@ -74,7 +76,7 @@
     section_index = lax.axis_index("section")
     up_all, down_all = (
         lax.all_gather(w_up, "dp", axis=2, tiled=True),
-        lax.all_gather(w_down, "dp", axis=3, tiled=True),
+        lax.all_gather(jnp.swapaxes(w_down, 2, 3), "dp", axis=2, tiled=True),
     )
     w_first = up_all[0, 0]
     w_second = down_all[0, 0]

time: 877 us -> 860 us (0.981); the launches traced: 865 us -> 860 us
  local copies, waits for them, and re-layouts: 67 us -> 44.1 us
    unnamed x10, local copies, waits for them, and re-layouts: 52.4 us -> 29.5 us
  transfers between devices with their start and end apart: 78 -> 78, of which waited for: 64 -> 63; matrix products, arithmetic and copies ran while one was open for 8% -> 4% of each run, Pallas kernels for 0% -> 0%
where the time goes in v4:
time: 860 us
  waiting for transfers between devices  483 us (56%)
  starting transfers between devices  170 us (20%)
  matrix products  121 us (14%)
  local copies, waits for them, and re-layouts  44.1 us (5%)
  other arithmetic  26.9 us (3%)
  between operations  13.5 us (2%)
    ppermute x76, waiting for transfers between devices, shifted(): return lax.ppermute(block, axis, route)  322 us
    ppermute x76, starting transfers between devices, shifted(): return lax.ppermute(block, axis, route)  170 us
    dot_general x11, matrix products, expert_rows(): lax.dot_general(hidden, w_second, (((1,), (1,)), ((), ())), preferred_ele...  109 us
    all_gather x1, waiting for transfers between devices, body(): lax.all_gather(jnp.swapaxes(w_down, 2, 3), 'dp', axis=2, tiled=True)  90.1 us
    all_gather x1, waiting for transfers between devices, body(): lax.all_gather(w_up, 'dp', axis=2, tiled=True)  71.3 us
    unnamed x10, local copies, waits for them, and re-layouts  29.5 us
  transfers between devices with their start and end apart: 78, of which 63 were waited for; matrix products, arithmetic and copies ran while one was open for 4% of the time, Pallas kernels for 0%

profile of v4, /device:TPU:2, one launch (start us, length us, event | category | flops | bytes accessed | tf_op | source)
XLA Modules:
  0.0 859.6 jit_solution(4150578618391267028)
XLA Ops:
  16.4 6.4 collective-permute-start.9
  26.9 10.6 %collective-permute-done.9 = bf16[12,5280]{1,0:T(8,128)(2,1)S(1)} collective-permute-done((bf16[12,5280]{1,0:T(8,128)(2,1)S(1)}, bf16[12,5280]{1,0:T(8,128)(2,1)S(1)}, u32[]{:S(2)}, u32[]{:S(2)}) %collective-permute-start.9) | collective-permute-done | bytes 126752 | tf_op jit(solution)/shard_map/ppermute | solution.py:13
  37.9 71.3 %all-gather.3.cloned.1.call-done = bf16[1,1,5280,768]{3,1,0,2:T(2,128)(2,1)} async-done(((bf16[1,1,330,768]{3,1,0,2:T(2,128)(2,1)}), bf16[1,1,5280,768]{3,1,0,2:T(2,128)(2,1)}) %all-gather.3.cloned.1.call-update) | async-done | bytes 8110096 | tf_op jit(solution)/shard_map/all_gather | solution.py:78
  109.1 11.6 %copy.18 = bf16[1,1,5280,768]{3,2,0,1:T(8,128)(2,1)} copy(bf16[1,1,5280,768]{3,1,0,2:T(2,128)(2,1)} %all-gather.3.cloned.1.call-done) | data formatting | bytes 16220160
  120.7 90.1 %all-gather.5.cloned.1.call-done = bf16[1,1,5280,768]{3,1,0,2:T(2,128)(2,1)} async-done(((bf16[1,1,330,768]{3,1,0,2:T(2,128)(2,1)}), bf16[1,1,5280,768]{3,1,0,2:T(2,128)(2,1)}) %all-gather.5.cloned.1.call-update) | async-done | bytes 8110096 | tf_op jit(solution)/shard_map/all_gather | solution.py:79
  210.8 11.6 %copy.17 = bf16[1,1,5280,768]{3,2,0,1:T(8,128)(2,1)} copy(bf16[1,1,5280,768]{3,1,0,2:T(2,128)(2,1)} %all-gather.5.cloned.1.call-done) | data formatting | bytes 16220160
  222.4 9.9 %convolution_convert_fusion.2 = bf16[48,5280]{1,0:T(8,128)(2,1)S(1)} fusion(bf16[5280,768]{1,0:T(8,128)(2,1)} %bitcast.109, bf16[48,5280]{1,0:T(8,128)(2,1)S(1)} %reshape.183, bf16[5280,768]{1,0:T(8,128)(2,1)} %bitcast.107), kind=kOutput, calls=%fused_computation.58 | convolution fusion | flops 779152896 | bytes 17233920 | tf_op jit(solution)/shard_map/dot_general | solution.py:28
  242.3 8.4 collective-permute-done.11
  256.1 595.9 %while.15 = (s32[]{:T(128)}, bf16[32,5280]{1,0:T(8,128)(2,1)S(1)}, s32[]{:T(128)}, pred[]{:T(512)}, bf16[4,32,5280]{2,1,0:T(8,128)(2,1)}, /*index=5*/bf16[4,32,5...) while((s32[]{:T(128)}, bf16[32,5280]{1,0:T(8,128)(2,1)S(1)}, ...), condition=%wide.region_7.8_spmd, body=%wide.region_3.7_spmd.sunk | while | flops 818449920 | bytes 31894524 | solution.py:116
  259.2 8.2 collective-permute-done
  276.8 6.4 collective-permute-done.1
  288.7 9.9 %convolution_convert_fusion.7 = bf16[48,5280]{1,0:T(8,128)(2,1)S(1)} fusion(bf16[5280,768]{1,0:T(8,128)(2,1)} %get-tuple-element.438, bf16[48,5280]{1,0:T(8,128)(2,1)S(1)} %reshape.194, bf16[5280,768]{1,0:T(8,128)(2,1)} %get-tuple-element.437), kind=kOutput, calls=%fused_computation.clone.1 | convolution fusion | flops 779152896 | bytes 17233920 | tf_op jit(solution)/shard_map/while/body/eval_jaxpr/dot_general | solution.py:28
  308.3 7.2 collective-permute-done.5
  319.4 9.3 %collective-permute-done = bf16[32,5280]{1,0:T(8,128)(2,1)S(1)} collective-permute-done((bf16[32,5280]{1,0:T(8,128)(2,1)S(1)}, bf16[32,5280]{1,0:T(8,128)(2,1)S(1)}, u32[]{:S(2)}, u32[]{:S(2)}) %collective-permute-start) | collective-permute-done | bytes 337952 | tf_op jit(solution)/shard_map/while/body/eval_jaxpr/ppermute | solution.py:13
  337.8 7.6 collective-permute-done.2
  348.0 9.9 %convolution_convert_fusion.7 = bf16[48,5280]{1,0:T(8,128)(2,1)S(1)} fusion(bf16[5280,768]{1,0:T(8,128)(2,1)} %get-tuple-element.438, bf16[48,5280]{1,0:T(8,128)(2,1)S(1)} %reshape.194, bf16[5280,768]{1,0:T(8,128)(2,1)} %get-tuple-element.437), kind=kOutput, calls=%fused_computation.clone.1 | convolution fusion | flops 779152896 | bytes 17233920 | tf_op jit(solution)/shard_map/while/body/eval_jaxpr/dot_general | solution.py:28
  364.6 9.1 %collective-permute-done.4 = bf16[12,5280]{1,0:T(8,128)(2,1)S(1)} collective-permute-done((bf16[12,5280]{1,0:T(8,128)(2,1)S(1)}, bf16[12,5280]{1,0:T(8,128)(2,1)S(1)}, u32[]{:S(2)}, u32[]{:S(2)}) %collective-permute-start.4) | collective-permute-done | bytes 126752 | tf_op jit(solution)/shard_map/while/body/eval_jaxpr/ppermute | solution.py:13
  380.7 6.9 collective-permute-done
  408.7 9.9 %convolution_convert_fusion.7 = bf16[48,5280]{1,0:T(8,128)(2,1)S(1)} fusion(bf16[5280,768]{1,0:T(8,128)(2,1)} %get-tuple-element.438, bf16[48,5280]{1,0:T(8,128)(2,1)S(1)} %reshape.194, bf16[5280,768]{1,0:T(8,128)(2,1)} %get-tuple-element.437), kind=kOutput, calls=%fused_computation.clone.1 | convolution fusion | flops 779152896 | bytes 17233920 | tf_op jit(solution)/shard_map/while/body/eval_jaxpr/dot_general | solution.py:28
  432.9 6.7 collective-permute-done.6
  441.9 6.9 collective-permute-done
  457.1 10.5 %collective-permute-done.1 = bf16[12,5280]{1,0:T(8,128)(2,1)S(1)} collective-permute-done((bf16[12,5280]{1,0:T(8,128)(2,1)S(1)}, bf16[12,5280]{1,0:T(8,128)(2,1)S(1)}, u32[]{:S(2)}, u32[]{:S(2)}) %collective-permute-start.1) | collective-permute-done | bytes 126752 | tf_op jit(solution)/shard_map/while/body/eval_jaxpr/ppermute | solution.py:13
  470.7 9.9 %convolution_convert_fusion.7 = bf16[48,5280]{1,0:T(8,128)(2,1)S(1)} fusion(bf16[5280,768]{1,0:T(8,128)(2,1)} %get-tuple-element.438, bf16[48,5280]{1,0:T(8,128)(2,1)S(1)} %reshape.194, bf16[5280,768]{1,0:T(8,128)(2,1)} %get-tuple-element.437), kind=kOutput, calls=%fused_computation.clone.1 | convolution fusion | flops 779152896 | bytes 17233920 | tf_op jit(solution)/shard_map/while/body/eval_jaxpr/dot_general | solution.py:28
  487.8 5.7 collective-permute-done.4
  499.9 6.9 collective-permute-done
  516.1 6.7 collective-permute-done.1
  525.8 9.9 %convolution_convert_fusion.7 = bf16[48,5280]{1,0:T(8,128)(2,1)S(1)} fusion(bf16[5280,768]{1,0:T(8,128)(2,1)} %get-tuple-element.438, bf16[48,5280]{1,0:T(8,128)(2,1)S(1)} %reshape.194, bf16[5280,768]{1,0:T(8,128)(2,1)} %get-tuple-element.437), kind=kOutput, calls=%fused_computation.clone.1 | convolution fusion | flops 779152896 | bytes 17233920 | tf_op jit(solution)/shard_map/while/body/eval_jaxpr/dot_general | solution.py:28
  557.6 6.1 collective-permute-done
  573.8 11.5 %collective-permute-done.1 = bf16[12,5280]{1,0:T(8,128)(2,1)S(1)} collective-permute-done((bf16[12,5280]{1,0:T(8,128)(2,1)S(1)}, bf16[12,5280]{1,0:T(8,128)(2,1)S(1)}, u32[]{:S(2)}, u32[]{:S(2)}) %collective-permute-start.1) | collective-permute-done | bytes 126752 | tf_op jit(solution)/shard_map/while/body/eval_jaxpr/ppermute | solution.py:13
  585.7 9.9 %convolution_convert_fusion.7 = bf16[48,5280]{1,0:T(8,128)(2,1)S(1)} fusion(bf16[5280,768]{1,0:T(8,128)(2,1)} %get-tuple-element.438, bf16[48,5280]{1,0:T(8,128)(2,1)S(1)} %reshape.194, bf16[5280,768]{1,0:T(8,128)(2,1)} %get-tuple-element.437), kind=kOutput, calls=%fused_computation.clone.1 | convolution fusion | flops 779152896 | bytes 17233920 | tf_op jit(solution)/shard_map/while/body/eval_jaxpr/dot_general | solution.py:28
  602.8 6.7 collective-permute-done.4
  609.4 7.6 collective-permute-done.5
  619.5 6.9 collective-permute-done
  644.7 9.9 %convolution_convert_fusion.7 = bf16[48,5280]{1,0:T(8,128)(2,1)S(1)} fusion(bf16[5280,768]{1,0:T(8,128)(2,1)} %get-tuple-element.438, bf16[48,5280]{1,0:T(8,128)(2,1)S(1)} %reshape.194, bf16[5280,768]{1,0:T(8,128)(2,1)} %get-tuple-element.437), kind=kOutput, calls=%fused_computation.clone.1 | convolution fusion | flops 779152896 | bytes 17233920 | tf_op jit(solution)/shard_map/while/body/eval_jaxpr/dot_general | solution.py:28
  654.7 6.0 collective-permute-start.4
  664.4 6.0 collective-permute-done.4
  670.4 6.6 collective-permute-done.5
  679.4 6.9 collective-permute-done
  704.7 9.9 %convolution_convert_fusion.7 = bf16[48,5280]{1,0:T(8,128)(2,1)S(1)} fusion(bf16[5280,768]{1,0:T(8,128)(2,1)} %get-tuple-element.438, bf16[48,5280]{1,0:T(8,128)(2,1)S(1)} %reshape.194, bf16[5280,768]{1,0:T(8,128)(2,1)} %get-tuple-element.437), kind=kOutput, calls=%fused_computation.clone.1 | convolution fusion | flops 779152896 | bytes 17233920 | tf_op jit(solution)/shard_map/while/body/eval_jaxpr/dot_general | solution.py:28
  727.9 5.4 collective-permute-done.6
  735.7 6.9 collective-permute-done
  752.1 11.6 %collective-permute-done.1 = bf16[12,5280]{1,0:T(8,128)(2,1)S(1)} collective-permute-done((bf16[12,5280]{1,0:T(8,128)(2,1)S(1)}, bf16[12,5280]{1,0:T(8,128)(2,1)S(1)}, u32[]{:S(2)}, u32[]{:S(2)}) %collective-permute-start.1) | collective-permute-done | bytes 126752 | tf_op jit(solution)/shard_map/while/body/eval_jaxpr/ppermute | solution.py:13
  765.6 9.9 %convolution_convert_fusion.7 = bf16[48,5280]{1,0:T(8,128)(2,1)S(1)} fusion(bf16[5280,768]{1,0:T(8,128)(2,1)} %get-tuple-element.438, bf16[48,5280]{1,0:T(8,128)(2,1)S(1)} %reshape.194, bf16[5280,768]{1,0:T(8,128)(2,1)} %get-tuple-element.437), kind=kOutput, calls=%fused_computation.clone.1 | convolution fusion | flops 779152896 | bytes 17233920 | tf_op jit(solution)/shard_map/while/body/eval_jaxpr/dot_general | solution.py:28
  782.3 8.3 collective-permute-done.4
  798.0 6.0 collective-permute-done
  813.6 5.2 collective-permute-done.2
  818.8 6.3 collective-permute-done.3
  825.5 9.9 %convolution_convert_fusion.7 = bf16[48,5280]{1,0:T(8,128)(2,1)S(1)} fusion(bf16[5280,768]{1,0:T(8,128)(2,1)} %get-tuple-element.438, bf16[48,5280]{1,0:T(8,128)(2,1)S(1)} %reshape.194, bf16[5280,768]{1,0:T(8,128)(2,1)} %get-tuple-element.437), kind=kOutput, calls=%fused_computation.clone.1 | convolution fusion | flops 779152896 | bytes 17233920 | tf_op jit(solution)/shard_map/while/body/eval_jaxpr/dot_general | solution.py:28
  (308 shorter events, 314.3 us)
Async XLA Ops:
  6.5 102.6 %all-gather.3.cloned.1.call-start = ((), (), s32[]{:S(2)}) async-start(), calls=%async_computation | async-start | bytes 17233920 | tf_op jit(solution)/shard_map/all_gather | solution.py:78
  9.4 201.4 %all-gather.5.cloned.1.call-start = ((), (), s32[]{:S(2)}) async-start(), calls=%async_computation.1 | async-start | bytes 17233920 | tf_op jit(solution)/shard_map/all_gather | solution.py:79
  16.4 21.1 %collective-permute-start.9 = (bf16[12,5280]{1,0:T(8,128)(2,1)S(1)}, bf16[12,5280]{1,0:T(8,128)(2,1)S(1)}, u32[]{:S(2)}, u32[]{:S(2)}) collective-permute-start(bf16[12,5280]{1,0:T(8,128)(2,1)S(1)} %get-tuple-element.296), channel_id=1, source_target_pairs={{1,0},{2,1},{3,2},{0,3},{5,4},{6,5},{7,6},{4,7},{9,8},{10,9},{11,1... | collective-permute-start | bytes 380168 | tf_op jit(solution)/shard_map/ppermute | solution.py:13
  22.8 14.7 %collective-permute-start.8 = (bf16[12,5280]{1,0:T(8,128)(2,1)S(1)}, bf16[12,5280]{1,0:T(8,128)(2,1)S(1)}, u32[]{:S(2)}, u32[]{:S(2)}) collective-permute-start(bf16[12,5280]{1,0:T(8,128)(2,1)S(1)} %get-tuple-element.297), channel_id=1, source_target_pairs={{2,0},{3,1},{0,2},{1,3},{6,4},{7,5},{4,6},{5,7},{10,8},{11,9},{8,1... | collective-permute-start | bytes 380168 | tf_op jit(solution)/shard_map/ppermute | solution.py:13
  23.8 13.7 %collective-permute-start.7 = (bf16[12,5280]{1,0:T(8,128)(2,1)S(1)}, bf16[12,5280]{1,0:T(8,128)(2,1)S(1)}, u32[]{:S(2)}, u32[]{:S(2)}) collective-permute-start(bf16[12,5280]{1,0:T(8,128)(2,1)S(1)} %get-tuple-element.298), channel_id=1, source_target_pairs={{3,0},{0,1},{1,2},{2,3},{7,4},{4,5},{5,6},{6,7},{11,8},{8,9},{9,10... | collective-permute-start | bytes 380168 | tf_op jit(solution)/shard_map/ppermute | solution.py:13
  235.0 15.7 %collective-permute-start.11 = (bf16[12,5280]{1,0:T(8,128)(2,1)S(1)}, bf16[12,5280]{1,0:T(8,128)(2,1)S(1)}, u32[]{:S(2)}, u32[]{:S(2)}) collective-permute-start(bf16[12,5280]{1,0:T(8,128)(2,1)S(1)} %get-tuple-element.293), channel_id=1, source_target_pairs={{2,0},{3,1},{0,2},{1,3},{6,4},{7,5},{4,6},{5,7},{10,8},{11,9},{8,1... | collective-permute-start | bytes 380168 | tf_op jit(solution)/shard_map/ppermute | solution.py:13
  238.9 16.5 %collective-permute-start.10 = (bf16[12,5280]{1,0:T(8,128)(2,1)S(1)}, bf16[12,5280]{1,0:T(8,128)(2,1)S(1)}, u32[]{:S(2)}, u32[]{:S(2)}) collective-permute-start(bf16[12,5280]{1,0:T(8,128)(2,1)S(1)} %get-tuple-element.294), channel_id=1, source_target_pairs={{1,0},{2,1},{3,2},{0,3},{5,4},{6,5},{7,6},{4,7},{9,8},{10,9},{11,1... | collective-permute-start | bytes 380168 | tf_op jit(solution)/shard_map/ppermute | solution.py:13
  269.3 14.0 %collective-permute-start.1 = (bf16[12,5280]{1,0:T(8,128)(2,1)S(1)}, bf16[12,5280]{1,0:T(8,128)(2,1)S(1)}, u32[]{:S(2)}, u32[]{:S(2)}) collective-permute-start(bf16[12,5280]{1,0:T(8,128)(2,1)S(1)} %get-tuple-element.378), channel_id=1, source_target_pairs={{1,0},{2,1},{3,2},{0,3},{5,4},{6,5},{7,6},{4,7},{9,8},{10,9},{11,1... | collective-permute-start | bytes 380168 | tf_op jit(solution)/shard_map/while/body/eval_jaxpr/ppermute | solution.py:13
  272.6 15.3 %collective-permute-start.2 = (bf16[12,5280]{1,0:T(8,128)(2,1)S(1)}, bf16[12,5280]{1,0:T(8,128)(2,1)S(1)}, u32[]{:S(2)}, u32[]{:S(2)}) collective-permute-start(bf16[12,5280]{1,0:T(8,128)(2,1)S(1)} %get-tuple-element.379), channel_id=1, source_target_pairs={{2,0},{3,1},{0,2},{1,3},{6,4},{7,5},{4,6},{5,7},{10,8},{11,9},{8,1... | collective-permute-start | bytes 380168 | tf_op jit(solution)/shard_map/while/body/eval_jaxpr/ppermute | solution.py:13
  275.4 12.9 %collective-permute-start.3 = (bf16[12,5280]{1,0:T(8,128)(2,1)S(1)}, bf16[12,5280]{1,0:T(8,128)(2,1)S(1)}, u32[]{:S(2)}, u32[]{:S(2)}) collective-permute-start(bf16[12,5280]{1,0:T(8,128)(2,1)S(1)} %get-tuple-element.380), channel_id=1, source_target_pairs={{3,0},{0,1},{1,2},{2,3},{7,4},{4,5},{5,6},{6,7},{11,8},{8,9},{9,10... | collective-permute-start | bytes 380168 | tf_op jit(solution)/shard_map/while/body/eval_jaxpr/ppermute | solution.py:13
  300.7 14.8 %collective-permute-start.5 = (bf16[12,5280]{1,0:T(8,128)(2,1)S(1)}, bf16[12,5280]{1,0:T(8,128)(2,1)S(1)}, u32[]{:S(2)}, u32[]{:S(2)}) collective-permute-start(bf16[12,5280]{1,0:T(8,128)(2,1)S(1)} %get-tuple-element.383), channel_id=1, source_target_pairs={{2,0},{3,1},{0,2},{1,3},{6,4},{7,5},{4,6},{5,7},{10,8},{11,9},{8,1... | collective-permute-start | bytes 380168 | tf_op jit(solution)/shard_map/while/body/eval_jaxpr/ppermute | solution.py:13
  304.6 12.2 %collective-permute-start.6 = (bf16[12,5280]{1,0:T(8,128)(2,1)S(1)}, bf16[12,5280]{1,0:T(8,128)(2,1)S(1)}, u32[]{:S(2)}, u32[]{:S(2)}) collective-permute-start(bf16[12,5280]{1,0:T(8,128)(2,1)S(1)} %get-tuple-element.384), channel_id=1, source_target_pairs={{1,0},{2,1},{3,2},{0,3},{5,4},{6,5},{7,6},{4,7},{9,8},{10,9},{11,1... | collective-permute-start | bytes 380168 | tf_op jit(solution)/shard_map/while/body/eval_jaxpr/ppermute | solution.py:13
  332.4 12.9 %collective-permute-start.2 = (bf16[12,5280]{1,0:T(8,128)(2,1)S(1)}, bf16[12,5280]{1,0:T(8,128)(2,1)S(1)}, u32[]{:S(2)}, u32[]{:S(2)}) collective-permute-start(bf16[12,5280]{1,0:T(8,128)(2,1)S(1)} %get-tuple-element.379), channel_id=1, source_target_pairs={{2,0},{3,1},{0,2},{1,3},{6,4},{7,5},{4,6},{5,7},{10,8},{11,9},{8,1... | collective-permute-start | bytes 380168 | tf_op jit(solution)/shard_map/while/body/eval_jaxpr/ppermute | solution.py:13
  335.1 12.5 %collective-permute-start.3 = (bf16[12,5280]{1,0:T(8,128)(2,1)S(1)}, bf16[12,5280]{1,0:T(8,128)(2,1)S(1)}, u32[]{:S(2)}, u32[]{:S(2)}) collective-permute-start(bf16[12,5280]{1,0:T(8,128)(2,1)S(1)} %get-tuple-element.380), channel_id=1, source_target_pairs={{3,0},{0,1},{1,2},{2,3},{7,4},{4,5},{5,6},{6,7},{11,8},{8,9},{9,10... | collective-permute-start | bytes 380168 | tf_op jit(solution)/shard_map/while/body/eval_jaxpr/ppermute | solution.py:13
  358.0 15.7 %collective-permute-start.4 = (bf16[12,5280]{1,0:T(8,128)(2,1)S(1)}, bf16[12,5280]{1,0:T(8,128)(2,1)S(1)}, u32[]{:S(2)}, u32[]{:S(2)}) collective-permute-start(bf16[12,5280]{1,0:T(8,128)(2,1)S(1)} %get-tuple-element.382), channel_id=1, source_target_pairs={{3,0},{0,1},{1,2},{2,3},{7,4},{4,5},{5,6},{6,7},{11,8},{8,9},{9,10... | collective-permute-start | bytes 380168 | tf_op jit(solution)/shard_map/while/body/eval_jaxpr/ppermute | solution.py:13
  358.9 14.8 %collective-permute-start.5 = (bf16[12,5280]{1,0:T(8,128)(2,1)S(1)}, bf16[12,5280]{1,0:T(8,128)(2,1)S(1)}, u32[]{:S(2)}, u32[]{:S(2)}) collective-permute-start(bf16[12,5280]{1,0:T(8,128)(2,1)S(1)} %get-tuple-element.383), channel_id=1, source_target_pairs={{2,0},{3,1},{0,2},{1,3},{6,4},{7,5},{4,6},{5,7},{10,8},{11,9},{8,1... | collective-permute-start | bytes 380168 | tf_op jit(solution)/shard_map/while/body/eval_jaxpr/ppermute | solution.py:13
  361.6 16.7 %collective-permute-start.6 = (bf16[12,5280]{1,0:T(8,128)(2,1)S(1)}, bf16[12,5280]{1,0:T(8,128)(2,1)S(1)}, u32[]{:S(2)}, u32[]{:S(2)}) collective-permute-start(bf16[12,5280]{1,0:T(8,128)(2,1)S(1)} %get-tuple-element.384), channel_id=1, source_target_pairs={{1,0},{2,1},{3,2},{0,3},{5,4},{6,5},{7,6},{4,7},{9,8},{10,9},{11,1... | collective-permute-start | bytes 380168 | tf_op jit(solution)/shard_map/while/body/eval_jaxpr/ppermute | solution.py:13
  389.4 12.5 %collective-permute-start.1 = (bf16[12,5280]{1,0:T(8,128)(2,1)S(1)}, bf16[12,5280]{1,0:T(8,128)(2,1)S(1)}, u32[]{:S(2)}, u32[]{:S(2)}) collective-permute-start(bf16[12,5280]{1,0:T(8,128)(2,1)S(1)} %get-tuple-element.378), channel_id=1, source_target_pairs={{1,0},{2,1},{3,2},{0,3},{5,4},{6,5},{7,6},{4,7},{9,8},{10,9},{11,1... | collective-permute-start | bytes 380168 | tf_op jit(solution)/shard_map/while/body/eval_jaxpr/ppermute | solution.py:13
  424.7 14.8 %collective-permute-start.6 = (bf16[12,5280]{1,0:T(8,128)(2,1)S(1)}, bf16[12,5280]{1,0:T(8,128)(2,1)S(1)}, u32[]{:S(2)}, u32[]{:S(2)}) collective-permute-start(bf16[12,5280]{1,0:T(8,128)(2,1)S(1)} %get-tuple-element.384), channel_id=1, source_target_pairs={{1,0},{2,1},{3,2},{0,3},{5,4},{6,5},{7,6},{4,7},{9,8},{10,9},{11,1... | collective-permute-start | bytes 380168 | tf_op jit(solution)/shard_map/while/body/eval_jaxpr/ppermute | solution.py:13
  450.7 16.9 %collective-permute-start.1 = (bf16[12,5280]{1,0:T(8,128)(2,1)S(1)}, bf16[12,5280]{1,0:T(8,128)(2,1)S(1)}, u32[]{:S(2)}, u32[]{:S(2)}) collective-permute-start(bf16[12,5280]{1,0:T(8,128)(2,1)S(1)} %get-tuple-element.378), channel_id=1, source_target_pairs={{1,0},{2,1},{3,2},{0,3},{5,4},{6,5},{7,6},{4,7},{9,8},{10,9},{11,1... | collective-permute-start | bytes 380168 | tf_op jit(solution)/shard_map/while/body/eval_jaxpr/ppermute | solution.py:13
  451.3 16.3 %collective-permute-start.2 = (bf16[12,5280]{1,0:T(8,128)(2,1)S(1)}, bf16[12,5280]{1,0:T(8,128)(2,1)S(1)}, u32[]{:S(2)}, u32[]{:S(2)}) collective-permute-start(bf16[12,5280]{1,0:T(8,128)(2,1)S(1)} %get-tuple-element.379), channel_id=1, source_target_pairs={{2,0},{3,1},{0,2},{1,3},{6,4},{7,5},{4,6},{5,7},{10,8},{11,9},{8,1... | collective-permute-start | bytes 380168 | tf_op jit(solution)/shard_map/while/body/eval_jaxpr/ppermute | solution.py:13
  455.3 15.0 %collective-permute-start.3 = (bf16[12,5280]{1,0:T(8,128)(2,1)S(1)}, bf16[12,5280]{1,0:T(8,128)(2,1)S(1)}, u32[]{:S(2)}, u32[]{:S(2)}) collective-permute-start(bf16[12,5280]{1,0:T(8,128)(2,1)S(1)} %get-tuple-element.380), channel_id=1, source_target_pairs={{3,0},{0,1},{1,2},{2,3},{7,4},{4,5},{5,6},{6,7},{11,8},{8,9},{9,10... | collective-permute-start | bytes 380168 | tf_op jit(solution)/shard_map/while/body/eval_jaxpr/ppermute | solution.py:13
  480.6 12.8 %collective-permute-start.4 = (bf16[12,5280]{1,0:T(8,128)(2,1)S(1)}, bf16[12,5280]{1,0:T(8,128)(2,1)S(1)}, u32[]{:S(2)}, u32[]{:S(2)}) collective-permute-start(bf16[12,5280]{1,0:T(8,128)(2,1)S(1)} %get-tuple-element.382), channel_id=1, source_target_pairs={{3,0},{0,1},{1,2},{2,3},{7,4},{4,5},{5,6},{6,7},{11,8},{8,9},{9,10... | collective-permute-start | bytes 380168 | tf_op jit(solution)/shard_map/while/body/eval_jaxpr/ppermute | solution.py:13
  480.8 16.7 %collective-permute-start.5 = (bf16[12,5280]{1,0:T(8,128)(2,1)S(1)}, bf16[12,5280]{1,0:T(8,128)(2,1)S(1)}, u32[]{:S(2)}, u32[]{:S(2)}) collective-permute-start(bf16[12,5280]{1,0:T(8,128)(2,1)S(1)} %get-tuple-element.383), channel_id=1, source_target_pairs={{2,0},{3,1},{0,2},{1,3},{6,4},{7,5},{4,6},{5,7},{10,8},{11,9},{8,1... | collective-permute-start | bytes 380168 | tf_op jit(solution)/shard_map/while/body/eval_jaxpr/ppermute | solution.py:13
  483.9 13.5 %collective-permute-start.6 = (bf16[12,5280]{1,0:T(8,128)(2,1)S(1)}, bf16[12,5280]{1,0:T(8,128)(2,1)S(1)}, u32[]{:S(2)}, u32[]{:S(2)}) collective-permute-start(bf16[12,5280]{1,0:T(8,128)(2,1)S(1)} %get-tuple-element.384), channel_id=1, source_target_pairs={{1,0},{2,1},{3,2},{0,3},{5,4},{6,5},{7,6},{4,7},{9,8},{10,9},{11,1... | collective-permute-start | bytes 380168 | tf_op jit(solution)/shard_map/while/body/eval_jaxpr/ppermute | solution.py:13
  508.6 14.1 %collective-permute-start.1 = (bf16[12,5280]{1,0:T(8,128)(2,1)S(1)}, bf16[12,5280]{1,0:T(8,128)(2,1)S(1)}, u32[]{:S(2)}, u32[]{:S(2)}) collective-permute-start(bf16[12,5280]{1,0:T(8,128)(2,1)S(1)} %get-tuple-element.378), channel_id=1, source_target_pairs={{1,0},{2,1},{3,2},{0,3},{5,4},{6,5},{7,6},{4,7},{9,8},{10,9},{11,1... | collective-permute-start | bytes 380168 | tf_op jit(solution)/shard_map/while/body/eval_jaxpr/ppermute | solution.py:13
  537.7 12.8 %collective-permute-start.5 = (bf16[12,5280]{1,0:T(8,128)(2,1)S(1)}, bf16[12,5280]{1,0:T(8,128)(2,1)S(1)}, u32[]{:S(2)}, u32[]{:S(2)}) collective-permute-start(bf16[12,5280]{1,0:T(8,128)(2,1)S(1)} %get-tuple-element.383), channel_id=1, source_target_pairs={{2,0},{3,1},{0,2},{1,3},{6,4},{7,5},{4,6},{5,7},{10,8},{11,9},{8,1... | collective-permute-start | bytes 380168 | tf_op jit(solution)/shard_map/while/body/eval_jaxpr/ppermute | solution.py:13
  538.9 15.5 %collective-permute-start.6 = (bf16[12,5280]{1,0:T(8,128)(2,1)S(1)}, bf16[12,5280]{1,0:T(8,128)(2,1)S(1)}, u32[]{:S(2)}, u32[]{:S(2)}) collective-permute-start(bf16[12,5280]{1,0:T(8,128)(2,1)S(1)} %get-tuple-element.384), channel_id=1, source_target_pairs={{1,0},{2,1},{3,2},{0,3},{5,4},{6,5},{7,6},{4,7},{9,8},{10,9},{11,1... | collective-permute-start | bytes 380168 | tf_op jit(solution)/shard_map/while/body/eval_jaxpr/ppermute | solution.py:13
  565.6 19.7 %collective-permute-start.1 = (bf16[12,5280]{1,0:T(8,128)(2,1)S(1)}, bf16[12,5280]{1,0:T(8,128)(2,1)S(1)}, u32[]{:S(2)}, u32[]{:S(2)}) collective-permute-start(bf16[12,5280]{1,0:T(8,128)(2,1)S(1)} %get-tuple-element.378), channel_id=1, source_target_pairs={{1,0},{2,1},{3,2},{0,3},{5,4},{6,5},{7,6},{4,7},{9,8},{10,9},{11,1... | collective-permute-start | bytes 380168 | tf_op jit(solution)/shard_map/while/body/eval_jaxpr/ppermute | solution.py:13
  570.2 15.1 %collective-permute-start.2 = (bf16[12,5280]{1,0:T(8,128)(2,1)S(1)}, bf16[12,5280]{1,0:T(8,128)(2,1)S(1)}, u32[]{:S(2)}, u32[]{:S(2)}) collective-permute-start(bf16[12,5280]{1,0:T(8,128)(2,1)S(1)} %get-tuple-element.379), channel_id=1, source_target_pairs={{2,0},{3,1},{0,2},{1,3},{6,4},{7,5},{4,6},{5,7},{10,8},{11,9},{8,1... | collective-permute-start | bytes 380168 | tf_op jit(solution)/shard_map/while/body/eval_jaxpr/ppermute | solution.py:13
  573.0 12.3 %collective-permute-start.3 = (bf16[12,5280]{1,0:T(8,128)(2,1)S(1)}, bf16[12,5280]{1,0:T(8,128)(2,1)S(1)}, u32[]{:S(2)}, u32[]{:S(2)}) collective-permute-start(bf16[12,5280]{1,0:T(8,128)(2,1)S(1)} %get-tuple-element.380), channel_id=1, source_target_pairs={{3,0},{0,1},{1,2},{2,3},{7,4},{4,5},{5,6},{6,7},{11,8},{8,9},{9,10... | collective-permute-start | bytes 380168 | tf_op jit(solution)/shard_map/while/body/eval_jaxpr/ppermute | solution.py:13
  595.7 13.8 %collective-permute-start.4 = (bf16[12,5280]{1,0:T(8,128)(2,1)S(1)}, bf16[12,5280]{1,0:T(8,128)(2,1)S(1)}, u32[]{:S(2)}, u32[]{:S(2)}) collective-permute-start(bf16[12,5280]{1,0:T(8,128)(2,1)S(1)} %get-tuple-element.382), channel_id=1, source_target_pairs={{3,0},{0,1},{1,2},{2,3},{7,4},{4,5},{5,6},{6,7},{11,8},{8,9},{9,10... | collective-permute-start | bytes 380168 | tf_op jit(solution)/shard_map/while/body/eval_jaxpr/ppermute | solution.py:13
  598.6 18.4 %collective-permute-start.5 = (bf16[12,5280]{1,0:T(8,128)(2,1)S(1)}, bf16[12,5280]{1,0:T(8,128)(2,1)S(1)}, u32[]{:S(2)}, u32[]{:S(2)}) collective-permute-start(bf16[12,5280]{1,0:T(8,128)(2,1)S(1)} %get-tuple-element.383), channel_id=1, source_target_pairs={{2,0},{3,1},{0,2},{1,3},{6,4},{7,5},{4,6},{5,7},{10,8},{11,9},{8,1... | collective-permute-start | bytes 380168 | tf_op jit(solution)/shard_map/while/body/eval_jaxpr/ppermute | solution.py:13
  602.7 14.4 %collective-permute-start.6 = (bf16[12,5280]{1,0:T(8,128)(2,1)S(1)}, bf16[12,5280]{1,0:T(8,128)(2,1)S(1)}, u32[]{:S(2)}, u32[]{:S(2)}) collective-permute-start(bf16[12,5280]{1,0:T(8,128)(2,1)S(1)} %get-tuple-element.384), channel_id=1, source_target_pairs={{1,0},{2,1},{3,2},{0,3},{5,4},{6,5},{7,6},{4,7},{9,8},{10,9},{11,1... | collective-permute-start | bytes 380168 | tf_op jit(solution)/shard_map/while/body/eval_jaxpr/ppermute | solution.py:13
  628.7 13.2 %collective-permute-start.2 = (bf16[12,5280]{1,0:T(8,128)(2,1)S(1)}, bf16[12,5280]{1,0:T(8,128)(2,1)S(1)}, u32[]{:S(2)}, u32[]{:S(2)}) collective-permute-start(bf16[12,5280]{1,0:T(8,128)(2,1)S(1)} %get-tuple-element.379), channel_id=1, source_target_pairs={{2,0},{3,1},{0,2},{1,3},{6,4},{7,5},{4,6},{5,7},{10,8},{11,9},{8,1... | collective-permute-start | bytes 380168 | tf_op jit(solution)/shard_map/while/body/eval_jaxpr/ppermute | solution.py:13
  654.7 15.7 %collective-permute-start.4 = (bf16[12,5280]{1,0:T(8,128)(2,1)S(1)}, bf16[12,5280]{1,0:T(8,128)(2,1)S(1)}, u32[]{:S(2)}, u32[]{:S(2)}) collective-permute-start(bf16[12,5280]{1,0:T(8,128)(2,1)S(1)} %get-tuple-element.382), channel_id=1, source_target_pairs={{3,0},{0,1},{1,2},{2,3},{7,4},{4,5},{5,6},{6,7},{11,8},{8,9},{9,10... | collective-permute-start | bytes 380168 | tf_op jit(solution)/shard_map/while/body/eval_jaxpr/ppermute | solution.py:13
  660.7 16.3 %collective-permute-start.5 = (bf16[12,5280]{1,0:T(8,128)(2,1)S(1)}, bf16[12,5280]{1,0:T(8,128)(2,1)S(1)}, u32[]{:S(2)}, u32[]{:S(2)}) collective-permute-start(bf16[12,5280]{1,0:T(8,128)(2,1)S(1)} %get-tuple-element.383), channel_id=1, source_target_pairs={{2,0},{3,1},{0,2},{1,3},{6,4},{7,5},{4,6},{5,7},{10,8},{11,9},{8,1... | collective-permute-start | bytes 380168 | tf_op jit(solution)/shard_map/while/body/eval_jaxpr/ppermute | solution.py:13
  660.7 16.3 %collective-permute-start.6 = (bf16[12,5280]{1,0:T(8,128)(2,1)S(1)}, bf16[12,5280]{1,0:T(8,128)(2,1)S(1)}, u32[]{:S(2)}, u32[]{:S(2)}) collective-permute-start(bf16[12,5280]{1,0:T(8,128)(2,1)S(1)} %get-tuple-element.384), channel_id=1, source_target_pairs={{1,0},{2,1},{3,2},{0,3},{5,4},{6,5},{7,6},{4,7},{9,8},{10,9},{11,1... | collective-permute-start | bytes 380168 | tf_op jit(solution)/shard_map/while/body/eval_jaxpr/ppermute | solution.py:13
  688.1 13.5 %collective-permute-start.1 = (bf16[12,5280]{1,0:T(8,128)(2,1)S(1)}, bf16[12,5280]{1,0:T(8,128)(2,1)S(1)}, u32[]{:S(2)}, u32[]{:S(2)}) collective-permute-start(bf16[12,5280]{1,0:T(8,128)(2,1)S(1)} %get-tuple-element.378), channel_id=1, source_target_pairs={{1,0},{2,1},{3,2},{0,3},{5,4},{6,5},{7,6},{4,7},{9,8},{10,9},{11,1... | collective-permute-start | bytes 380168 | tf_op jit(solution)/shard_map/while/body/eval_jaxpr/ppermute | solution.py:13
  690.5 13.8 %collective-permute-start.2 = (bf16[12,5280]{1,0:T(8,128)(2,1)S(1)}, bf16[12,5280]{1,0:T(8,128)(2,1)S(1)}, u32[]{:S(2)}, u32[]{:S(2)}) collective-permute-start(bf16[12,5280]{1,0:T(8,128)(2,1)S(1)} %get-tuple-element.379), channel_id=1, source_target_pairs={{2,0},{3,1},{0,2},{1,3},{6,4},{7,5},{4,6},{5,7},{10,8},{11,9},{8,1... | collective-permute-start | bytes 380168 | tf_op jit(solution)/shard_map/while/body/eval_jaxpr/ppermute | solution.py:13
  714.7 13.2 %collective-permute-start.4 = (bf16[12,5280]{1,0:T(8,128)(2,1)S(1)}, bf16[12,5280]{1,0:T(8,128)(2,1)S(1)}, u32[]{:S(2)}, u32[]{:S(2)}) collective-permute-start(bf16[12,5280]{1,0:T(8,128)(2,1)S(1)} %get-tuple-element.382), channel_id=1, source_target_pairs={{3,0},{0,1},{1,2},{2,3},{7,4},{4,5},{5,6},{6,7},{11,8},{8,9},{9,10... | collective-permute-start | bytes 380168 | tf_op jit(solution)/shard_map/while/body/eval_jaxpr/ppermute | solution.py:13
  719.5 13.8 %collective-permute-start.6 = (bf16[12,5280]{1,0:T(8,128)(2,1)S(1)}, bf16[12,5280]{1,0:T(8,128)(2,1)S(1)}, u32[]{:S(2)}, u32[]{:S(2)}) collective-permute-start(bf16[12,5280]{1,0:T(8,128)(2,1)S(1)} %get-tuple-element.384), channel_id=1, source_target_pairs={{1,0},{2,1},{3,2},{0,3},{5,4},{6,5},{7,6},{4,7},{9,8},{10,9},{11,1... | collective-permute-start | bytes 380168 | tf_op jit(solution)/shard_map/while/body/eval_jaxpr/ppermute | solution.py:13
  744.4 19.3 %collective-permute-start.1 = (bf16[12,5280]{1,0:T(8,128)(2,1)S(1)}, bf16[12,5280]{1,0:T(8,128)(2,1)S(1)}, u32[]{:S(2)}, u32[]{:S(2)}) collective-permute-start(bf16[12,5280]{1,0:T(8,128)(2,1)S(1)} %get-tuple-element.378), channel_id=1, source_target_pairs={{1,0},{2,1},{3,2},{0,3},{5,4},{6,5},{7,6},{4,7},{9,8},{10,9},{11,1... | collective-permute-start | bytes 380168 | tf_op jit(solution)/shard_map/while/body/eval_jaxpr/ppermute | solution.py:13
  749.4 14.4 %collective-permute-start.2 = (bf16[12,5280]{1,0:T(8,128)(2,1)S(1)}, bf16[12,5280]{1,0:T(8,128)(2,1)S(1)}, u32[]{:S(2)}, u32[]{:S(2)}) collective-permute-start(bf16[12,5280]{1,0:T(8,128)(2,1)S(1)} %get-tuple-element.379), channel_id=1, source_target_pairs={{2,0},{3,1},{0,2},{1,3},{6,4},{7,5},{4,6},{5,7},{10,8},{11,9},{8,1... | collective-permute-start | bytes 380168 | tf_op jit(solution)/shard_map/while/body/eval_jaxpr/ppermute | solution.py:13
  751.6 13.7 %collective-permute-start.3 = (bf16[12,5280]{1,0:T(8,128)(2,1)S(1)}, bf16[12,5280]{1,0:T(8,128)(2,1)S(1)}, u32[]{:S(2)}, u32[]{:S(2)}) collective-permute-start(bf16[12,5280]{1,0:T(8,128)(2,1)S(1)} %get-tuple-element.380), channel_id=1, source_target_pairs={{3,0},{0,1},{1,2},{2,3},{7,4},{4,5},{5,6},{6,7},{11,8},{8,9},{9,10... | collective-permute-start | bytes 380168 | tf_op jit(solution)/shard_map/while/body/eval_jaxpr/ppermute | solution.py:13
  775.6 14.9 %collective-permute-start.4 = (bf16[12,5280]{1,0:T(8,128)(2,1)S(1)}, bf16[12,5280]{1,0:T(8,128)(2,1)S(1)}, u32[]{:S(2)}, u32[]{:S(2)}) collective-permute-start(bf16[12,5280]{1,0:T(8,128)(2,1)S(1)} %get-tuple-element.382), channel_id=1, source_target_pairs={{3,0},{0,1},{1,2},{2,3},{7,4},{4,5},{5,6},{6,7},{11,8},{8,9},{9,10... | collective-permute-start | bytes 380168 | tf_op jit(solution)/shard_map/while/body/eval_jaxpr/ppermute | solution.py:13
  776.1 18.3 %collective-permute-start.5 = (bf16[12,5280]{1,0:T(8,128)(2,1)S(1)}, bf16[12,5280]{1,0:T(8,128)(2,1)S(1)}, u32[]{:S(2)}, u32[]{:S(2)}) collective-permute-start(bf16[12,5280]{1,0:T(8,128)(2,1)S(1)} %get-tuple-element.383), channel_id=1, source_target_pairs={{2,0},{3,1},{0,2},{1,3},{6,4},{7,5},{4,6},{5,7},{10,8},{11,9},{8,1... | collective-permute-start | bytes 380168 | tf_op jit(solution)/shard_map/while/body/eval_jaxpr/ppermute | solution.py:13
  781.3 13.1 %collective-permute-start.6 = (bf16[12,5280]{1,0:T(8,128)(2,1)S(1)}, bf16[12,5280]{1,0:T(8,128)(2,1)S(1)}, u32[]{:S(2)}, u32[]{:S(2)}) collective-permute-start(bf16[12,5280]{1,0:T(8,128)(2,1)S(1)} %get-tuple-element.384), channel_id=1, source_target_pairs={{1,0},{2,1},{3,2},{0,3},{5,4},{6,5},{7,6},{4,7},{9,8},{10,9},{11,1... | collective-permute-start | bytes 380168 | tf_op jit(solution)/shard_map/while/body/eval_jaxpr/ppermute | solution.py:13
  (33 other events, 350.5 us)
Sparse Core Ops, SparseCore 0:
  9.5 99.5 all-gather.2
  111.0 99.7 all-gather.4

commit v5 on v4

--- a/solution.py
+++ b/solution.py
@@ -31,13 +31,15 @@
     return result.reshape(extent)
 
 
-def whole_round(buffer, w_first, w_second):
-    groups = buffer.shape[0]
-    arrived = jnp.stack([buffer[0]] + [shifted(buffer[j], "expert", j) for j in range(1, groups)])
-    processed = expert_rows(arrived, w_first, w_second)
-    return jnp.stack(
-        [processed[0]] + [shifted(processed[j], "expert", groups - j) for j in range(1, groups)]
-    )
+def onward(block, distance):
+    sections = lax.axis_size("section")
+    experts = lax.axis_size("expert")
+    route = [
+        (s * experts + e, ((s + 1) % sections) * experts + (e - distance) % experts)
+        for s in range(sections)
+        for e in range(experts)
+    ]
+    return lax.ppermute(block, ("section", "expert"), route)
 
 
 def core_block(current, gain_row, router_rows, w_first, w_second, assign):
@@ -64,11 +66,23 @@
         .astype(jnp.bfloat16)
         .reshape(experts, CAP, -1)
     )
-    returned = whole_round(buffer, w_first, w_second)
-    flat_back = returned.reshape(experts * CAP, -1)
+    arrived = jnp.stack([buffer[0]] + [shifted(buffer[j], "expert", j) for j in range(1, experts)])
+    processed = expert_rows(arrived, w_first, w_second)
+    back = jnp.stack([onward(processed[j], j) for j in range(experts)])
+    return (
+        shifted(current, "section", 1),
+        shifted(gate_value, "section", 1),
+        shifted(places, "section", 1),
+        back,
+    )
+
+
+def combine(carry, was_live):
+    kept, gate_value, places, back = carry
+    flat_back = back.reshape(-1, back.shape[-1])
     expert_out = jnp.einsum("st,sd->td", places, flat_back, preferred_element_type=jnp.float32)
-    updated = current.astype(jnp.float32) + gate_value[:, None] * expert_out
-    return updated.astype(jnp.bfloat16)
+    updated = (kept.astype(jnp.float32) + gate_value[:, None] * expert_out).astype(jnp.bfloat16)
+    return jnp.where(was_live, updated, kept)
 
 
 def body(init_state, inject, routes, norm_gain, router, w_up, w_down):
@@ -85,14 +99,19 @@
     tokens = init_state.shape[1]
     active_span = sections * RECUR
     total_steps = active_span + sections - 1
+    previous_section = jnp.mod(section_index - 1, sections)
+
+    def live_at(moment, section):
+        offset = moment - section
+        return (offset >= 0) & (offset < active_span)
 
     def advance(moment, hidden_state):
         offset = moment - section_index
-        is_live = (offset >= 0) & (offset < active_span)
+        is_live = live_at(moment, section_index)
         clipped = jnp.clip(offset, 0, active_span - 1)
         loop_round = clipped // sections
         entry_slot = clipped % sections
-        micro_idx = jnp.mod(sections - 2 - entry_slot, sections)
+        micro_idx = jnp.mod(sections - 1 - entry_slot, sections)
         initial = lax.dynamic_index_in_dim(init_state, micro_idx, 0, keepdims=False)
         injected_row = lax.dynamic_index_in_dim(inject, micro_idx, 0, keepdims=False)
         incoming = jnp.where(loop_round == 0, initial, hidden_state)
@@ -104,17 +123,16 @@
         assign = lax.dynamic_slice(
             routes, (loop_round, 0, micro_idx, 0, 0), (1, 1, 1, tokens, 1)
         ).reshape(tokens)
-        result = core_block(current, gain_row, router_rows, w_first, w_second, assign)
-        return jnp.where(is_live, result, hidden_state)
+        return core_block(current, gain_row, router_rows, w_first, w_second, assign)
 
-    def advance_one(moment, hidden_state):
-        arrived = shifted(hidden_state, "section", 1)
+    def advance_one(moment, carry):
+        arrived = combine(carry, live_at(moment - 1, previous_section))
         return advance(moment, arrived)
 
-    hidden_state = jnp.zeros(init_state.shape[1:], jnp.bfloat16)
-    hidden_state = advance(0, hidden_state)
-    hidden_state = lax.fori_loop(1, total_steps, advance_one, hidden_state)
-    return hidden_state[None]
+    carry = advance(0, jnp.zeros(init_state.shape[1:], jnp.bfloat16))
+    carry = lax.fori_loop(1, total_steps, advance_one, carry)
+    final = combine(carry, live_at(total_steps - 1, previous_section))
+    return final[None]
 
 
 def solution(mesh):

time: 860 us -> 893 us (1.038)
  starting transfers between devices: 170 us -> 202 us
  matrix products: 121 us -> 134 us
  other arithmetic: 26.9 us -> 14.2 us
    ppermute x76 -> x66, waiting for transfers between devices: 322 us -> 182 us  [shifted(): return lax.ppermute(block, axis, route)]
    ppermute x0 -> x44, waiting for transfers between devices: none -> 135 us  [onward(): return lax.ppermute(block, ('section', 'expert'), route)]
    ppermute x0 -> x44, starting transfers between devices: none -> 114 us  [onward(): return lax.ppermute(block, ('section', 'expert'), route)]
    ppermute x76 -> x66, starting transfers between devices: 170 us -> 87.9 us  [shifted(): return lax.ppermute(block, axis, route)]
    all_gather x1, waiting for transfers between devices: 71.3 us -> 90.1 us  [body(): lax.all_gather(w_up, 'dp', axis=2, tiled=True)]
    all_gather x1, waiting for transfers between devices: 90.1 us -> 71.3 us  [body(): lax.all_gather(jnp.swapaxes(w_down, 2, 3), 'dp', axis=2, tiled=True)]
    reduce_sum x11 -> x1, other arithmetic: 15.2 us -> 1.36 us  [normalize(): jnp.mean(as_float * as_float, axis=-1, keepdims=True) + 1e-05]
    dot_general x11, matrix products: 3.51 us -> 16.6 us  [combine(): jnp.einsum('st,sd->td', places, flat_back, preferred_element_type=jnp.flo...]
  transfers between devices with their start and end apart: 78 -> 112, of which waited for: 63 -> 67; matrix products, arithmetic and copies ran while one was open for 4% -> 17% of each run, Pallas kernels for 0% -> 0%
where the time goes in v5:
time: 893 us; the launch traced here: 887 us
  waiting for transfers between devices  479 us (54%)
  starting transfers between devices  202 us (23%)
  matrix products  134 us (15%)
  local copies, waits for them, and re-layouts  43.3 us (5%)
  other arithmetic  14.2 us (2%)
  between operations  13.5 us (2%)
    ppermute x66, waiting for transfers between devices, shifted(): return lax.ppermute(block, axis, route)  182 us
    ppermute x44, waiting for transfers between devices, onward(): return lax.ppermute(block, ('section', 'expert'), route)  135 us
    ppermute x44, starting transfers between devices, onward(): return lax.ppermute(block, ('section', 'expert'), route)  114 us
    dot_general x11, matrix products, expert_rows(): lax.dot_general(hidden, w_second, (((1,), (1,)), ((), ())), preferred_ele...  108 us
    all_gather x1, waiting for transfers between devices, body(): lax.all_gather(w_up, 'dp', axis=2, tiled=True)  90.1 us
    ppermute x66, starting transfers between devices, shifted(): return lax.ppermute(block, axis, route)  87.9 us
    all_gather x1, waiting for transfers between devices, body(): lax.all_gather(jnp.swapaxes(w_down, 2, 3), 'dp', axis=2, tiled=True)  71.3 us
    unnamed x8, local copies, waits for them, and re-layouts  28.7 us
  transfers between devices with their start and end apart: 112, of which 67 were waited for; matrix products, arithmetic and copies ran while one was open for 17% of the time, Pallas kernels for 0%

profile of v5, /device:TPU:2, one launch (start us, length us, event | category | flops | bytes accessed | tf_op | source)
XLA Modules:
  0.0 886.7 jit_solution(5299198411770663404)
XLA Ops:
  16.4 6.4 collective-permute-start.15
  26.9 10.6 %collective-permute-done.15 = bf16[12,5280]{1,0:T(8,128)(2,1)S(1)} collective-permute-done((bf16[12,5280]{1,0:T(8,128)(2,1)S(1)}, bf16[12,5280]{1,0:T(8,128)(2,1)S(1)}, u32[]{:S(2)}, u32[]{:S(2)}) %collective-permute-start.15) | collective-permute-done | bytes 126752 | tf_op jit(solution)/shard_map/ppermute | solution.py:13
  37.9 71.3 %all-gather.5.cloned.1.call-done = bf16[1,1,5280,768]{3,1,0,2:T(2,128)(2,1)} async-done(((bf16[1,1,330,768]{3,1,0,2:T(2,128)(2,1)}), bf16[1,1,5280,768]{3,1,0,2:T(2,128)(2,1)}) %all-gather.5.cloned.1.call-update) | async-done | bytes 8110096 | tf_op jit(solution)/shard_map/all_gather | solution.py:93
  109.1 11.6 %copy.17 = bf16[1,1,5280,768]{3,2,0,1:T(8,128)(2,1)} copy(bf16[1,1,5280,768]{3,1,0,2:T(2,128)(2,1)} %all-gather.5.cloned.1.call-done) | data formatting | bytes 16220160
  120.7 90.1 %all-gather.3.cloned.1.call-done = bf16[1,1,5280,768]{3,1,0,2:T(2,128)(2,1)} async-done(((bf16[1,1,330,768]{3,1,0,2:T(2,128)(2,1)}), bf16[1,1,5280,768]{3,1,0,2:T(2,128)(2,1)}) %all-gather.3.cloned.1.call-update) | async-done | bytes 8110096 | tf_op jit(solution)/shard_map/all_gather | solution.py:92
  210.8 11.6 %copy.18 = bf16[1,1,5280,768]{3,2,0,1:T(8,128)(2,1)} copy(bf16[1,1,5280,768]{3,1,0,2:T(2,128)(2,1)} %all-gather.3.cloned.1.call-done) | data formatting | bytes 16220160
  222.4 9.9 %convolution_convert_fusion.2 = bf16[48,5280]{1,0:T(8,128)(2,1)S(1)} fusion(bf16[5280,768]{1,0:T(8,128)(2,1)} %bitcast.99, bf16[48,5280]{1,0:T(8,128)(2,1)S(1)} %reshape.179, bf16[5280,768]{1,0:T(8,128)(2,1)} %bitcast.101), kind=kOutput, calls=%fused_computation.57 | convolution fusion | flops 779152896 | bytes 17233920 | tf_op jit(solution)/shard_map/dot_general | solution.py:28
  248.2 5.3 collective-permute-done.18
  258.7 6.6 collective-permute-done.11
  265.4 613.0 %while.24 = (s32[]{:T(128)}, bf16[32,5280]{1,0:T(8,128)(2,1)S(1)}, f32[32]{0:T(128)S(1)}, bf16[48,32]{1,0:T(8,128)(2,1)S(1)}, bf16[4,12,5280]{2,1,0:T(8,128)(2,1...) while((s32[]{:T(128)}, bf16[32,5280]{1,0:T(8,128)(2,1)S(1)}, ...), condition=%wide.region_7.8_spmd, body=%wide.region_3.7_spmd.sunk | while | flops 818451392 | bytes 31412924 | solution.py:133
  276.8 6.5 collective-permute-done.4
  287.8 9.9 %convolution_convert_fusion.7 = bf16[48,5280]{1,0:T(8,128)(2,1)S(1)} fusion(bf16[5280,768]{1,0:T(8,128)(2,1)} %get-tuple-element.726, bf16[48,5280]{1,0:T(8,128)(2,1)S(1)} %reshape.190, bf16[5280,768]{1,0:T(8,128)(2,1)} %get-tuple-element.725), kind=kOutput, calls=%fused_computation.clone.1 | convolution fusion | flops 779152896 | bytes 17233920 | tf_op jit(solution)/shard_map/while/body/eval_jaxpr/dot_general | solution.py:28
  301.9 5.8 collective-permute-start.8
  308.5 8.9 %collective-permute-done.6 = bf16[12,5280]{1,0:T(8,128)(2,1)S(1)} collective-permute-done((bf16[12,5280]{1,0:T(8,128)(2,1)S(1)}, bf16[12,5280]{1,0:T(8,128)(2,1)S(1)}, u32[]{:S(2)}, u32[]{:S(2)}) %collective-permute-start.6) | collective-permute-done | bytes 126752 | tf_op jit(solution)/shard_map/while/body/eval_jaxpr/ppermute | solution.py:42
  321.6 5.3 collective-permute-done.1
  338.1 9.2 %collective-permute-done.4 = bf16[12,5280]{1,0:T(8,128)(2,1)S(1)} collective-permute-done((bf16[12,5280]{1,0:T(8,128)(2,1)S(1)}, bf16[12,5280]{1,0:T(8,128)(2,1)S(1)}, u32[]{:S(2)}, u32[]{:S(2)}) %collective-permute-start.4) | collective-permute-done | bytes 126752 | tf_op jit(solution)/shard_map/while/body/eval_jaxpr/ppermute | solution.py:13
  349.2 9.9 %convolution_convert_fusion.7 = bf16[48,5280]{1,0:T(8,128)(2,1)S(1)} fusion(bf16[5280,768]{1,0:T(8,128)(2,1)} %get-tuple-element.726, bf16[48,5280]{1,0:T(8,128)(2,1)S(1)} %reshape.190, bf16[5280,768]{1,0:T(8,128)(2,1)} %get-tuple-element.725), kind=kOutput, calls=%fused_computation.clone.1 | convolution fusion | flops 779152896 | bytes 17233920 | tf_op jit(solution)/shard_map/while/body/eval_jaxpr/dot_general | solution.py:28
  363.8 5.3 collective-permute-start.8
  370.2 8.7 collective-permute-done.6
  399.4 9.2 %collective-permute-done.4 = bf16[12,5280]{1,0:T(8,128)(2,1)S(1)} collective-permute-done((bf16[12,5280]{1,0:T(8,128)(2,1)S(1)}, bf16[12,5280]{1,0:T(8,128)(2,1)S(1)}, u32[]{:S(2)}, u32[]{:S(2)}) %collective-permute-start.4) | collective-permute-done | bytes 126752 | tf_op jit(solution)/shard_map/while/body/eval_jaxpr/ppermute | solution.py:13
  410.6 9.9 %convolution_convert_fusion.7 = bf16[48,5280]{1,0:T(8,128)(2,1)S(1)} fusion(bf16[5280,768]{1,0:T(8,128)(2,1)} %get-tuple-element.726, bf16[48,5280]{1,0:T(8,128)(2,1)S(1)} %reshape.190, bf16[5280,768]{1,0:T(8,128)(2,1)} %get-tuple-element.725), kind=kOutput, calls=%fused_computation.clone.1 | convolution fusion | flops 779152896 | bytes 17233920 | tf_op jit(solution)/shard_map/while/body/eval_jaxpr/dot_general | solution.py:28
  425.1 5.3 collective-permute-start.8
  432.1 7.9 collective-permute-done.6
  444.6 5.1 collective-permute-done.1
  460.8 9.2 %collective-permute-done.4 = bf16[12,5280]{1,0:T(8,128)(2,1)S(1)} collective-permute-done((bf16[12,5280]{1,0:T(8,128)(2,1)S(1)}, bf16[12,5280]{1,0:T(8,128)(2,1)S(1)}, u32[]{:S(2)}, u32[]{:S(2)}) %collective-permute-start.4) | collective-permute-done | bytes 126752 | tf_op jit(solution)/shard_map/while/body/eval_jaxpr/ppermute | solution.py:13
  471.8 9.9 %convolution_convert_fusion.7 = bf16[48,5280]{1,0:T(8,128)(2,1)S(1)} fusion(bf16[5280,768]{1,0:T(8,128)(2,1)} %get-tuple-element.726, bf16[48,5280]{1,0:T(8,128)(2,1)S(1)} %reshape.190, bf16[5280,768]{1,0:T(8,128)(2,1)} %get-tuple-element.725), kind=kOutput, calls=%fused_computation.clone.1 | convolution fusion | flops 779152896 | bytes 17233920 | tf_op jit(solution)/shard_map/while/body/eval_jaxpr/dot_general | solution.py:28
  486.5 5.0 collective-permute-start.8
  493.3 7.8 collective-permute-done.6
  522.1 9.2 %collective-permute-done.4 = bf16[12,5280]{1,0:T(8,128)(2,1)S(1)} collective-permute-done((bf16[12,5280]{1,0:T(8,128)(2,1)S(1)}, bf16[12,5280]{1,0:T(8,128)(2,1)S(1)}, u32[]{:S(2)}, u32[]{:S(2)}) %collective-permute-start.4) | collective-permute-done | bytes 126752 | tf_op jit(solution)/shard_map/while/body/eval_jaxpr/ppermute | solution.py:13
  533.1 9.9 %convolution_convert_fusion.7 = bf16[48,5280]{1,0:T(8,128)(2,1)S(1)} fusion(bf16[5280,768]{1,0:T(8,128)(2,1)} %get-tuple-element.726, bf16[48,5280]{1,0:T(8,128)(2,1)S(1)} %reshape.190, bf16[5280,768]{1,0:T(8,128)(2,1)} %get-tuple-element.725), kind=kOutput, calls=%fused_computation.clone.1 | convolution fusion | flops 779152896 | bytes 17233920 | tf_op jit(solution)/shard_map/while/body/eval_jaxpr/dot_general | solution.py:28
  554.6 7.6 collective-permute-done.6
  583.4 9.2 %collective-permute-done.4 = bf16[12,5280]{1,0:T(8,128)(2,1)S(1)} collective-permute-done((bf16[12,5280]{1,0:T(8,128)(2,1)S(1)}, bf16[12,5280]{1,0:T(8,128)(2,1)S(1)}, u32[]{:S(2)}, u32[]{:S(2)}) %collective-permute-start.4) | collective-permute-done | bytes 126752 | tf_op jit(solution)/shard_map/while/body/eval_jaxpr/ppermute | solution.py:13
  594.3 9.9 %convolution_convert_fusion.7 = bf16[48,5280]{1,0:T(8,128)(2,1)S(1)} fusion(bf16[5280,768]{1,0:T(8,128)(2,1)} %get-tuple-element.726, bf16[48,5280]{1,0:T(8,128)(2,1)S(1)} %reshape.190, bf16[5280,768]{1,0:T(8,128)(2,1)} %get-tuple-element.725), kind=kOutput, calls=%fused_computation.clone.1 | convolution fusion | flops 779152896 | bytes 17233920 | tf_op jit(solution)/shard_map/while/body/eval_jaxpr/dot_general | solution.py:28
  615.9 7.6 collective-permute-done.6
  644.6 9.2 %collective-permute-done.4 = bf16[12,5280]{1,0:T(8,128)(2,1)S(1)} collective-permute-done((bf16[12,5280]{1,0:T(8,128)(2,1)S(1)}, bf16[12,5280]{1,0:T(8,128)(2,1)S(1)}, u32[]{:S(2)}, u32[]{:S(2)}) %collective-permute-start.4) | collective-permute-done | bytes 126752 | tf_op jit(solution)/shard_map/while/body/eval_jaxpr/ppermute | solution.py:13
  655.6 9.9 %convolution_convert_fusion.7 = bf16[48,5280]{1,0:T(8,128)(2,1)S(1)} fusion(bf16[5280,768]{1,0:T(8,128)(2,1)} %get-tuple-element.726, bf16[48,5280]{1,0:T(8,128)(2,1)S(1)} %reshape.190, bf16[5280,768]{1,0:T(8,128)(2,1)} %get-tuple-element.725), kind=kOutput, calls=%fused_computation.clone.1 | convolution fusion | flops 779152896 | bytes 17233920 | tf_op jit(solution)/shard_map/while/body/eval_jaxpr/dot_general | solution.py:28
  677.1 7.7 collective-permute-done.6
  705.9 9.2 %collective-permute-done.4 = bf16[12,5280]{1,0:T(8,128)(2,1)S(1)} collective-permute-done((bf16[12,5280]{1,0:T(8,128)(2,1)S(1)}, bf16[12,5280]{1,0:T(8,128)(2,1)S(1)}, u32[]{:S(2)}, u32[]{:S(2)}) %collective-permute-start.4) | collective-permute-done | bytes 126752 | tf_op jit(solution)/shard_map/while/body/eval_jaxpr/ppermute | solution.py:13
  716.9 9.9 %convolution_convert_fusion.7 = bf16[48,5280]{1,0:T(8,128)(2,1)S(1)} fusion(bf16[5280,768]{1,0:T(8,128)(2,1)} %get-tuple-element.726, bf16[48,5280]{1,0:T(8,128)(2,1)S(1)} %reshape.190, bf16[5280,768]{1,0:T(8,128)(2,1)} %get-tuple-element.725), kind=kOutput, calls=%fused_computation.clone.1 | convolution fusion | flops 779152896 | bytes 17233920 | tf_op jit(solution)/shard_map/while/body/eval_jaxpr/dot_general | solution.py:28
  731.6 5.0 collective-permute-start.8
  738.4 7.7 collective-permute-done.6
  767.2 9.2 %collective-permute-done.4 = bf16[12,5280]{1,0:T(8,128)(2,1)S(1)} collective-permute-done((bf16[12,5280]{1,0:T(8,128)(2,1)S(1)}, bf16[12,5280]{1,0:T(8,128)(2,1)S(1)}, u32[]{:S(2)}, u32[]{:S(2)}) %collective-permute-start.4) | collective-permute-done | bytes 126752 | tf_op jit(solution)/shard_map/while/body/eval_jaxpr/ppermute | solution.py:13
  778.1 9.9 %convolution_convert_fusion.7 = bf16[48,5280]{1,0:T(8,128)(2,1)S(1)} fusion(bf16[5280,768]{1,0:T(8,128)(2,1)} %get-tuple-element.726, bf16[48,5280]{1,0:T(8,128)(2,1)S(1)} %reshape.190, bf16[5280,768]{1,0:T(8,128)(2,1)} %get-tuple-element.725), kind=kOutput, calls=%fused_computation.clone.1 | convolution fusion | flops 779152896 | bytes 17233920 | tf_op jit(solution)/shard_map/while/body/eval_jaxpr/dot_general | solution.py:28
  792.8 5.0 collective-permute-start.8
  799.6 7.7 collective-permute-done.6
  828.4 9.2 %collective-permute-done.4 = bf16[12,5280]{1,0:T(8,128)(2,1)S(1)} collective-permute-done((bf16[12,5280]{1,0:T(8,128)(2,1)S(1)}, bf16[12,5280]{1,0:T(8,128)(2,1)S(1)}, u32[]{:S(2)}, u32[]{:S(2)}) %collective-permute-start.4) | collective-permute-done | bytes 126752 | tf_op jit(solution)/shard_map/while/body/eval_jaxpr/ppermute | solution.py:13
  839.4 9.9 %convolution_convert_fusion.7 = bf16[48,5280]{1,0:T(8,128)(2,1)S(1)} fusion(bf16[5280,768]{1,0:T(8,128)(2,1)} %get-tuple-element.726, bf16[48,5280]{1,0:T(8,128)(2,1)S(1)} %reshape.190, bf16[5280,768]{1,0:T(8,128)(2,1)} %get-tuple-element.725), kind=kOutput, calls=%fused_computation.clone.1 | convolution fusion | flops 779152896 | bytes 17233920 | tf_op jit(solution)/shard_map/while/body/eval_jaxpr/dot_general | solution.py:28
  860.9 7.7 collective-permute-done.6
  (386 shorter events, 340.1 us)
Async XLA Ops:
  6.5 102.6 %all-gather.5.cloned.1.call-start = ((), (), s32[]{:S(2)}) async-start(), calls=%async_computation.1 | async-start | bytes 17233920 | tf_op jit(solution)/shard_map/all_gather | solution.py:93
  9.4 201.4 %all-gather.3.cloned.1.call-start = ((), (), s32[]{:S(2)}) async-start(), calls=%async_computation | async-start | bytes 17233920 | tf_op jit(solution)/shard_map/all_gather | solution.py:92
  16.4 21.1 %collective-permute-start.15 = (bf16[12,5280]{1,0:T(8,128)(2,1)S(1)}, bf16[12,5280]{1,0:T(8,128)(2,1)S(1)}, u32[]{:S(2)}, u32[]{:S(2)}) collective-permute-start(bf16[12,5280]{1,0:T(8,128)(2,1)S(1)} %get-tuple-element.548), channel_id=1, source_target_pairs={{1,0},{2,1},{3,2},{0,3},{5,4},{6,5},{7,6},{4,7},{9,8},{10,9},{11,1... | collective-permute-start | bytes 380168 | tf_op jit(solution)/shard_map/ppermute | solution.py:13
  245.3 20.2 %collective-permute-start.10 = (bf16[32,5280]{1,0:T(8,128)(2,1)S(1)}, bf16[32,5280]{1,0:T(8,128)(2,1)S(1)}, u32[]{:S(2)}, u32[]{:S(2)}) collective-permute-start(bf16[32,5280]{1,0:T(8,128)(2,1)S(1)} %bitcast.111), channel_id=1, source_target_pairs={{192,0},{0,64},{64,128},{128,192},{193,1},{1,65},{65,129},{129,193... | collective-permute-start | bytes 1013768 | tf_op jit(solution)/shard_map/ppermute | solution.py:13
  246.8 18.6 %collective-permute-start.11 = (f32[32]{0:T(128)S(1)}, f32[32]{0:T(128)S(1)}, u32[]{:S(2)}, u32[]{:S(2)}) collective-permute-start(f32[32]{0:T(128)S(1)} %add_divide_fusion.1), channel_id=1, source_target_pairs={{192,0},{0,64},{64,128},{128,192},{193,1},{1,65},{65,129},{129,193... | collective-permute-start | bytes 392 | tf_op jit(solution)/shard_map/ppermute | solution.py:13
  266.9 41.1 %collective-permute-start.2 = (bf16[48,32]{1,0:T(8,128)(2,1)S(1)}, bf16[48,32]{1,0:T(8,128)(2,1)S(1)}, u32[]{:S(2)}, u32[]{:S(2)}) collective-permute-start(bf16[48,32]{1,0:T(8,128)(2,1)S(1)} %fusion.126), channel_id=1, source_target_pairs={{192,0},{0,64},{64,128},{128,192},{193,1},{1,65},{65,129},{129,193... | collective-permute-start | bytes 9224 | tf_op jit(solution)/shard_map/while/body/eval_jaxpr/ppermute | solution.py:13
  297.8 19.7 %collective-permute-start.6 = (bf16[12,5280]{1,0:T(8,128)(2,1)S(1)}, bf16[12,5280]{1,0:T(8,128)(2,1)S(1)}, u32[]{:S(2)}, u32[]{:S(2)}) collective-permute-start(bf16[12,5280]{1,0:T(8,128)(2,1)S(1)} %get-tuple-element.658), channel_id=1, source_target_pairs={{0,65},{1,66},{2,67},{3,64},{64,129},{65,130},{66,131},{67,128},{1... | collective-permute-start | bytes 380168 | tf_op jit(solution)/shard_map/while/body/eval_jaxpr/ppermute | solution.py:42
  298.2 19.3 %collective-permute-start.7 = (bf16[12,5280]{1,0:T(8,128)(2,1)S(1)}, bf16[12,5280]{1,0:T(8,128)(2,1)S(1)}, u32[]{:S(2)}, u32[]{:S(2)}) collective-permute-start(bf16[12,5280]{1,0:T(8,128)(2,1)S(1)} %get-tuple-element.659), channel_id=1, source_target_pairs={{0,66},{1,67},{2,64},{3,65},{64,130},{65,131},{66,128},{67,129},{1... | collective-permute-start | bytes 380168 | tf_op jit(solution)/shard_map/while/body/eval_jaxpr/ppermute | solution.py:42
  301.9 19.5 %collective-permute-start.8 = (bf16[12,5280]{1,0:T(8,128)(2,1)S(1)}, bf16[12,5280]{1,0:T(8,128)(2,1)S(1)}, u32[]{:S(2)}, u32[]{:S(2)}) collective-permute-start(bf16[12,5280]{1,0:T(8,128)(2,1)S(1)} %get-tuple-element.660), channel_id=1, source_target_pairs={{0,67},{1,64},{2,65},{3,66},{64,131},{65,128},{66,129},{67,130},{1... | collective-permute-start | bytes 380168 | tf_op jit(solution)/shard_map/while/body/eval_jaxpr/ppermute | solution.py:42
  308.1 18.8 %collective-permute-start = (bf16[32,5280]{1,0:T(8,128)(2,1)S(1)}, bf16[32,5280]{1,0:T(8,128)(2,1)S(1)}, u32[]{:S(2)}, u32[]{:S(2)}) collective-permute-start(bf16[32,5280]{1,0:T(8,128)(2,1)S(1)} %get-tuple-element.652), channel_id=1, source_target_pairs={{192,0},{0,64},{64,128},{128,192},{193,1},{1,65},{65,129},{129,193... | collective-permute-start | bytes 1013768 | tf_op jit(solution)/shard_map/while/body/eval_jaxpr/ppermute | solution.py:13
  328.4 41.0 %collective-permute-start.2 = (bf16[48,32]{1,0:T(8,128)(2,1)S(1)}, bf16[48,32]{1,0:T(8,128)(2,1)S(1)}, u32[]{:S(2)}, u32[]{:S(2)}) collective-permute-start(bf16[48,32]{1,0:T(8,128)(2,1)S(1)} %fusion.126), channel_id=1, source_target_pairs={{192,0},{0,64},{64,128},{128,192},{193,1},{1,65},{65,129},{129,193... | collective-permute-start | bytes 9224 | tf_op jit(solution)/shard_map/while/body/eval_jaxpr/ppermute | solution.py:13
  359.1 19.8 %collective-permute-start.6 = (bf16[12,5280]{1,0:T(8,128)(2,1)S(1)}, bf16[12,5280]{1,0:T(8,128)(2,1)S(1)}, u32[]{:S(2)}, u32[]{:S(2)}) collective-permute-start(bf16[12,5280]{1,0:T(8,128)(2,1)S(1)} %get-tuple-element.658), channel_id=1, source_target_pairs={{0,65},{1,66},{2,67},{3,64},{64,129},{65,130},{66,131},{67,128},{1... | collective-permute-start | bytes 380168 | tf_op jit(solution)/shard_map/while/body/eval_jaxpr/ppermute | solution.py:42
  359.7 19.3 %collective-permute-start.7 = (bf16[12,5280]{1,0:T(8,128)(2,1)S(1)}, bf16[12,5280]{1,0:T(8,128)(2,1)S(1)}, u32[]{:S(2)}, u32[]{:S(2)}) collective-permute-start(bf16[12,5280]{1,0:T(8,128)(2,1)S(1)} %get-tuple-element.659), channel_id=1, source_target_pairs={{0,66},{1,67},{2,64},{3,65},{64,130},{65,131},{66,128},{67,129},{1... | collective-permute-start | bytes 380168 | tf_op jit(solution)/shard_map/while/body/eval_jaxpr/ppermute | solution.py:42
  363.8 19.4 %collective-permute-start.8 = (bf16[12,5280]{1,0:T(8,128)(2,1)S(1)}, bf16[12,5280]{1,0:T(8,128)(2,1)S(1)}, u32[]{:S(2)}, u32[]{:S(2)}) collective-permute-start(bf16[12,5280]{1,0:T(8,128)(2,1)S(1)} %get-tuple-element.660), channel_id=1, source_target_pairs={{0,67},{1,64},{2,65},{3,66},{64,131},{65,128},{66,129},{67,130},{1... | collective-permute-start | bytes 380168 | tf_op jit(solution)/shard_map/while/body/eval_jaxpr/ppermute | solution.py:42
  369.4 18.8 %collective-permute-start = (bf16[32,5280]{1,0:T(8,128)(2,1)S(1)}, bf16[32,5280]{1,0:T(8,128)(2,1)S(1)}, u32[]{:S(2)}, u32[]{:S(2)}) collective-permute-start(bf16[32,5280]{1,0:T(8,128)(2,1)S(1)} %get-tuple-element.652), channel_id=1, source_target_pairs={{192,0},{0,64},{64,128},{128,192},{193,1},{1,65},{65,129},{129,193... | collective-permute-start | bytes 1013768 | tf_op jit(solution)/shard_map/while/body/eval_jaxpr/ppermute | solution.py:13
  389.7 41.0 %collective-permute-start.2 = (bf16[48,32]{1,0:T(8,128)(2,1)S(1)}, bf16[48,32]{1,0:T(8,128)(2,1)S(1)}, u32[]{:S(2)}, u32[]{:S(2)}) collective-permute-start(bf16[48,32]{1,0:T(8,128)(2,1)S(1)} %fusion.126), channel_id=1, source_target_pairs={{192,0},{0,64},{64,128},{128,192},{193,1},{1,65},{65,129},{129,193... | collective-permute-start | bytes 9224 | tf_op jit(solution)/shard_map/while/body/eval_jaxpr/ppermute | solution.py:13
  420.6 19.4 %collective-permute-start.6 = (bf16[12,5280]{1,0:T(8,128)(2,1)S(1)}, bf16[12,5280]{1,0:T(8,128)(2,1)S(1)}, u32[]{:S(2)}, u32[]{:S(2)}) collective-permute-start(bf16[12,5280]{1,0:T(8,128)(2,1)S(1)} %get-tuple-element.658), channel_id=1, source_target_pairs={{0,65},{1,66},{2,67},{3,64},{64,129},{65,130},{66,131},{67,128},{1... | collective-permute-start | bytes 380168 | tf_op jit(solution)/shard_map/while/body/eval_jaxpr/ppermute | solution.py:42
  421.3 18.6 %collective-permute-start.7 = (bf16[12,5280]{1,0:T(8,128)(2,1)S(1)}, bf16[12,5280]{1,0:T(8,128)(2,1)S(1)}, u32[]{:S(2)}, u32[]{:S(2)}) collective-permute-start(bf16[12,5280]{1,0:T(8,128)(2,1)S(1)} %get-tuple-element.659), channel_id=1, source_target_pairs={{0,66},{1,67},{2,64},{3,65},{64,130},{65,131},{66,128},{67,129},{1... | collective-permute-start | bytes 380168 | tf_op jit(solution)/shard_map/while/body/eval_jaxpr/ppermute | solution.py:42
  425.1 19.3 %collective-permute-start.8 = (bf16[12,5280]{1,0:T(8,128)(2,1)S(1)}, bf16[12,5280]{1,0:T(8,128)(2,1)S(1)}, u32[]{:S(2)}, u32[]{:S(2)}) collective-permute-start(bf16[12,5280]{1,0:T(8,128)(2,1)S(1)} %get-tuple-element.660), channel_id=1, source_target_pairs={{0,67},{1,64},{2,65},{3,66},{64,131},{65,128},{66,129},{67,130},{1... | collective-permute-start | bytes 380168 | tf_op jit(solution)/shard_map/while/body/eval_jaxpr/ppermute | solution.py:42
  430.7 18.9 %collective-permute-start = (bf16[32,5280]{1,0:T(8,128)(2,1)S(1)}, bf16[32,5280]{1,0:T(8,128)(2,1)S(1)}, u32[]{:S(2)}, u32[]{:S(2)}) collective-permute-start(bf16[32,5280]{1,0:T(8,128)(2,1)S(1)} %get-tuple-element.652), channel_id=1, source_target_pairs={{192,0},{0,64},{64,128},{128,192},{193,1},{1,65},{65,129},{129,193... | collective-permute-start | bytes 1013768 | tf_op jit(solution)/shard_map/while/body/eval_jaxpr/ppermute | solution.py:13
  451.1 40.8 %collective-permute-start.2 = (bf16[48,32]{1,0:T(8,128)(2,1)S(1)}, bf16[48,32]{1,0:T(8,128)(2,1)S(1)}, u32[]{:S(2)}, u32[]{:S(2)}) collective-permute-start(bf16[48,32]{1,0:T(8,128)(2,1)S(1)} %fusion.126), channel_id=1, source_target_pairs={{192,0},{0,64},{64,128},{128,192},{193,1},{1,65},{65,129},{129,193... | collective-permute-start | bytes 9224 | tf_op jit(solution)/shard_map/while/body/eval_jaxpr/ppermute | solution.py:13
  481.8 19.3 %collective-permute-start.6 = (bf16[12,5280]{1,0:T(8,128)(2,1)S(1)}, bf16[12,5280]{1,0:T(8,128)(2,1)S(1)}, u32[]{:S(2)}, u32[]{:S(2)}) collective-permute-start(bf16[12,5280]{1,0:T(8,128)(2,1)S(1)} %get-tuple-element.658), channel_id=1, source_target_pairs={{0,65},{1,66},{2,67},{3,64},{64,129},{65,130},{66,131},{67,128},{1... | collective-permute-start | bytes 380168 | tf_op jit(solution)/shard_map/while/body/eval_jaxpr/ppermute | solution.py:42
  486.5 19.3 %collective-permute-start.8 = (bf16[12,5280]{1,0:T(8,128)(2,1)S(1)}, bf16[12,5280]{1,0:T(8,128)(2,1)S(1)}, u32[]{:S(2)}, u32[]{:S(2)}) collective-permute-start(bf16[12,5280]{1,0:T(8,128)(2,1)S(1)} %get-tuple-element.660), channel_id=1, source_target_pairs={{0,67},{1,64},{2,65},{3,66},{64,131},{65,128},{66,129},{67,130},{1... | collective-permute-start | bytes 380168 | tf_op jit(solution)/shard_map/while/body/eval_jaxpr/ppermute | solution.py:42
  491.9 19.0 %collective-permute-start = (bf16[32,5280]{1,0:T(8,128)(2,1)S(1)}, bf16[32,5280]{1,0:T(8,128)(2,1)S(1)}, u32[]{:S(2)}, u32[]{:S(2)}) collective-permute-start(bf16[32,5280]{1,0:T(8,128)(2,1)S(1)} %get-tuple-element.652), channel_id=1, source_target_pairs={{192,0},{0,64},{64,128},{128,192},{193,1},{1,65},{65,129},{129,193... | collective-permute-start | bytes 1013768 | tf_op jit(solution)/shard_map/while/body/eval_jaxpr/ppermute | solution.py:13
  512.4 40.8 %collective-permute-start.2 = (bf16[48,32]{1,0:T(8,128)(2,1)S(1)}, bf16[48,32]{1,0:T(8,128)(2,1)S(1)}, u32[]{:S(2)}, u32[]{:S(2)}) collective-permute-start(bf16[48,32]{1,0:T(8,128)(2,1)S(1)} %fusion.126), channel_id=1, source_target_pairs={{192,0},{0,64},{64,128},{128,192},{193,1},{1,65},{65,129},{129,193... | collective-permute-start | bytes 9224 | tf_op jit(solution)/shard_map/while/body/eval_jaxpr/ppermute | solution.py:13
  543.0 19.2 %collective-permute-start.6 = (bf16[12,5280]{1,0:T(8,128)(2,1)S(1)}, bf16[12,5280]{1,0:T(8,128)(2,1)S(1)}, u32[]{:S(2)}, u32[]{:S(2)}) collective-permute-start(bf16[12,5280]{1,0:T(8,128)(2,1)S(1)} %get-tuple-element.658), channel_id=1, source_target_pairs={{0,65},{1,66},{2,67},{3,64},{64,129},{65,130},{66,131},{67,128},{1... | collective-permute-start | bytes 380168 | tf_op jit(solution)/shard_map/while/body/eval_jaxpr/ppermute | solution.py:42
  547.8 19.3 %collective-permute-start.8 = (bf16[12,5280]{1,0:T(8,128)(2,1)S(1)}, bf16[12,5280]{1,0:T(8,128)(2,1)S(1)}, u32[]{:S(2)}, u32[]{:S(2)}) collective-permute-start(bf16[12,5280]{1,0:T(8,128)(2,1)S(1)} %get-tuple-element.660), channel_id=1, source_target_pairs={{0,67},{1,64},{2,65},{3,66},{64,131},{65,128},{66,129},{67,130},{1... | collective-permute-start | bytes 380168 | tf_op jit(solution)/shard_map/while/body/eval_jaxpr/ppermute | solution.py:42
  553.2 19.0 %collective-permute-start = (bf16[32,5280]{1,0:T(8,128)(2,1)S(1)}, bf16[32,5280]{1,0:T(8,128)(2,1)S(1)}, u32[]{:S(2)}, u32[]{:S(2)}) collective-permute-start(bf16[32,5280]{1,0:T(8,128)(2,1)S(1)} %get-tuple-element.652), channel_id=1, source_target_pairs={{192,0},{0,64},{64,128},{128,192},{193,1},{1,65},{65,129},{129,193... | collective-permute-start | bytes 1013768 | tf_op jit(solution)/shard_map/while/body/eval_jaxpr/ppermute | solution.py:13
  573.6 40.8 %collective-permute-start.2 = (bf16[48,32]{1,0:T(8,128)(2,1)S(1)}, bf16[48,32]{1,0:T(8,128)(2,1)S(1)}, u32[]{:S(2)}, u32[]{:S(2)}) collective-permute-start(bf16[48,32]{1,0:T(8,128)(2,1)S(1)} %fusion.126), channel_id=1, source_target_pairs={{192,0},{0,64},{64,128},{128,192},{193,1},{1,65},{65,129},{129,193... | collective-permute-start | bytes 9224 | tf_op jit(solution)/shard_map/while/body/eval_jaxpr/ppermute | solution.py:13
  604.3 19.2 %collective-permute-start.6 = (bf16[12,5280]{1,0:T(8,128)(2,1)S(1)}, bf16[12,5280]{1,0:T(8,128)(2,1)S(1)}, u32[]{:S(2)}, u32[]{:S(2)}) collective-permute-start(bf16[12,5280]{1,0:T(8,128)(2,1)S(1)} %get-tuple-element.658), channel_id=1, source_target_pairs={{0,65},{1,66},{2,67},{3,64},{64,129},{65,130},{66,131},{67,128},{1... | collective-permute-start | bytes 380168 | tf_op jit(solution)/shard_map/while/body/eval_jaxpr/ppermute | solution.py:42
  609.0 19.3 %collective-permute-start.8 = (bf16[12,5280]{1,0:T(8,128)(2,1)S(1)}, bf16[12,5280]{1,0:T(8,128)(2,1)S(1)}, u32[]{:S(2)}, u32[]{:S(2)}) collective-permute-start(bf16[12,5280]{1,0:T(8,128)(2,1)S(1)} %get-tuple-element.660), channel_id=1, source_target_pairs={{0,67},{1,64},{2,65},{3,66},{64,131},{65,128},{66,129},{67,130},{1... | collective-permute-start | bytes 380168 | tf_op jit(solution)/shard_map/while/body/eval_jaxpr/ppermute | solution.py:42
  614.4 19.0 %collective-permute-start = (bf16[32,5280]{1,0:T(8,128)(2,1)S(1)}, bf16[32,5280]{1,0:T(8,128)(2,1)S(1)}, u32[]{:S(2)}, u32[]{:S(2)}) collective-permute-start(bf16[32,5280]{1,0:T(8,128)(2,1)S(1)} %get-tuple-element.652), channel_id=1, source_target_pairs={{192,0},{0,64},{64,128},{128,192},{193,1},{1,65},{65,129},{129,193... | collective-permute-start | bytes 1013768 | tf_op jit(solution)/shard_map/while/body/eval_jaxpr/ppermute | solution.py:13
  634.9 40.8 %collective-permute-start.2 = (bf16[48,32]{1,0:T(8,128)(2,1)S(1)}, bf16[48,32]{1,0:T(8,128)(2,1)S(1)}, u32[]{:S(2)}, u32[]{:S(2)}) collective-permute-start(bf16[48,32]{1,0:T(8,128)(2,1)S(1)} %fusion.126), channel_id=1, source_target_pairs={{192,0},{0,64},{64,128},{128,192},{193,1},{1,65},{65,129},{129,193... | collective-permute-start | bytes 9224 | tf_op jit(solution)/shard_map/while/body/eval_jaxpr/ppermute | solution.py:13
  665.6 19.2 %collective-permute-start.6 = (bf16[12,5280]{1,0:T(8,128)(2,1)S(1)}, bf16[12,5280]{1,0:T(8,128)(2,1)S(1)}, u32[]{:S(2)}, u32[]{:S(2)}) collective-permute-start(bf16[12,5280]{1,0:T(8,128)(2,1)S(1)} %get-tuple-element.658), channel_id=1, source_target_pairs={{0,65},{1,66},{2,67},{3,64},{64,129},{65,130},{66,131},{67,128},{1... | collective-permute-start | bytes 380168 | tf_op jit(solution)/shard_map/while/body/eval_jaxpr/ppermute | solution.py:42
  670.3 19.3 %collective-permute-start.8 = (bf16[12,5280]{1,0:T(8,128)(2,1)S(1)}, bf16[12,5280]{1,0:T(8,128)(2,1)S(1)}, u32[]{:S(2)}, u32[]{:S(2)}) collective-permute-start(bf16[12,5280]{1,0:T(8,128)(2,1)S(1)} %get-tuple-element.660), channel_id=1, source_target_pairs={{0,67},{1,64},{2,65},{3,66},{64,131},{65,128},{66,129},{67,130},{1... | collective-permute-start | bytes 380168 | tf_op jit(solution)/shard_map/while/body/eval_jaxpr/ppermute | solution.py:42
  675.7 19.0 %collective-permute-start = (bf16[32,5280]{1,0:T(8,128)(2,1)S(1)}, bf16[32,5280]{1,0:T(8,128)(2,1)S(1)}, u32[]{:S(2)}, u32[]{:S(2)}) collective-permute-start(bf16[32,5280]{1,0:T(8,128)(2,1)S(1)} %get-tuple-element.652), channel_id=1, source_target_pairs={{192,0},{0,64},{64,128},{128,192},{193,1},{1,65},{65,129},{129,193... | collective-permute-start | bytes 1013768 | tf_op jit(solution)/shard_map/while/body/eval_jaxpr/ppermute | solution.py:13
  696.1 40.8 %collective-permute-start.2 = (bf16[48,32]{1,0:T(8,128)(2,1)S(1)}, bf16[48,32]{1,0:T(8,128)(2,1)S(1)}, u32[]{:S(2)}, u32[]{:S(2)}) collective-permute-start(bf16[48,32]{1,0:T(8,128)(2,1)S(1)} %fusion.126), channel_id=1, source_target_pairs={{192,0},{0,64},{64,128},{128,192},{193,1},{1,65},{65,129},{129,193... | collective-permute-start | bytes 9224 | tf_op jit(solution)/shard_map/while/body/eval_jaxpr/ppermute | solution.py:13
  726.8 19.2 %collective-permute-start.6 = (bf16[12,5280]{1,0:T(8,128)(2,1)S(1)}, bf16[12,5280]{1,0:T(8,128)(2,1)S(1)}, u32[]{:S(2)}, u32[]{:S(2)}) collective-permute-start(bf16[12,5280]{1,0:T(8,128)(2,1)S(1)} %get-tuple-element.658), channel_id=1, source_target_pairs={{0,65},{1,66},{2,67},{3,64},{64,129},{65,130},{66,131},{67,128},{1... | collective-permute-start | bytes 380168 | tf_op jit(solution)/shard_map/while/body/eval_jaxpr/ppermute | solution.py:42
  731.6 19.3 %collective-permute-start.8 = (bf16[12,5280]{1,0:T(8,128)(2,1)S(1)}, bf16[12,5280]{1,0:T(8,128)(2,1)S(1)}, u32[]{:S(2)}, u32[]{:S(2)}) collective-permute-start(bf16[12,5280]{1,0:T(8,128)(2,1)S(1)} %get-tuple-element.660), channel_id=1, source_target_pairs={{0,67},{1,64},{2,65},{3,66},{64,131},{65,128},{66,129},{67,130},{1... | collective-permute-start | bytes 380168 | tf_op jit(solution)/shard_map/while/body/eval_jaxpr/ppermute | solution.py:42
  736.9 19.0 %collective-permute-start = (bf16[32,5280]{1,0:T(8,128)(2,1)S(1)}, bf16[32,5280]{1,0:T(8,128)(2,1)S(1)}, u32[]{:S(2)}, u32[]{:S(2)}) collective-permute-start(bf16[32,5280]{1,0:T(8,128)(2,1)S(1)} %get-tuple-element.652), channel_id=1, source_target_pairs={{192,0},{0,64},{64,128},{128,192},{193,1},{1,65},{65,129},{129,193... | collective-permute-start | bytes 1013768 | tf_op jit(solution)/shard_map/while/body/eval_jaxpr/ppermute | solution.py:13
  757.4 40.8 %collective-permute-start.2 = (bf16[48,32]{1,0:T(8,128)(2,1)S(1)}, bf16[48,32]{1,0:T(8,128)(2,1)S(1)}, u32[]{:S(2)}, u32[]{:S(2)}) collective-permute-start(bf16[48,32]{1,0:T(8,128)(2,1)S(1)} %fusion.126), channel_id=1, source_target_pairs={{192,0},{0,64},{64,128},{128,192},{193,1},{1,65},{65,129},{129,193... | collective-permute-start | bytes 9224 | tf_op jit(solution)/shard_map/while/body/eval_jaxpr/ppermute | solution.py:13
  788.1 19.2 %collective-permute-start.6 = (bf16[12,5280]{1,0:T(8,128)(2,1)S(1)}, bf16[12,5280]{1,0:T(8,128)(2,1)S(1)}, u32[]{:S(2)}, u32[]{:S(2)}) collective-permute-start(bf16[12,5280]{1,0:T(8,128)(2,1)S(1)} %get-tuple-element.658), channel_id=1, source_target_pairs={{0,65},{1,66},{2,67},{3,64},{64,129},{65,130},{66,131},{67,128},{1... | collective-permute-start | bytes 380168 | tf_op jit(solution)/shard_map/while/body/eval_jaxpr/ppermute | solution.py:42
  792.8 19.3 %collective-permute-start.8 = (bf16[12,5280]{1,0:T(8,128)(2,1)S(1)}, bf16[12,5280]{1,0:T(8,128)(2,1)S(1)}, u32[]{:S(2)}, u32[]{:S(2)}) collective-permute-start(bf16[12,5280]{1,0:T(8,128)(2,1)S(1)} %get-tuple-element.660), channel_id=1, source_target_pairs={{0,67},{1,64},{2,65},{3,66},{64,131},{65,128},{66,129},{67,130},{1... | collective-permute-start | bytes 380168 | tf_op jit(solution)/shard_map/while/body/eval_jaxpr/ppermute | solution.py:42
  798.2 19.0 %collective-permute-start = (bf16[32,5280]{1,0:T(8,128)(2,1)S(1)}, bf16[32,5280]{1,0:T(8,128)(2,1)S(1)}, u32[]{:S(2)}, u32[]{:S(2)}) collective-permute-start(bf16[32,5280]{1,0:T(8,128)(2,1)S(1)} %get-tuple-element.652), channel_id=1, source_target_pairs={{192,0},{0,64},{64,128},{128,192},{193,1},{1,65},{65,129},{129,193... | collective-permute-start | bytes 1013768 | tf_op jit(solution)/shard_map/while/body/eval_jaxpr/ppermute | solution.py:13
  818.7 40.8 %collective-permute-start.2 = (bf16[48,32]{1,0:T(8,128)(2,1)S(1)}, bf16[48,32]{1,0:T(8,128)(2,1)S(1)}, u32[]{:S(2)}, u32[]{:S(2)}) collective-permute-start(bf16[48,32]{1,0:T(8,128)(2,1)S(1)} %fusion.126), channel_id=1, source_target_pairs={{192,0},{0,64},{64,128},{128,192},{193,1},{1,65},{65,129},{129,193... | collective-permute-start | bytes 9224 | tf_op jit(solution)/shard_map/while/body/eval_jaxpr/ppermute | solution.py:13
  849.4 19.2 %collective-permute-start.6 = (bf16[12,5280]{1,0:T(8,128)(2,1)S(1)}, bf16[12,5280]{1,0:T(8,128)(2,1)S(1)}, u32[]{:S(2)}, u32[]{:S(2)}) collective-permute-start(bf16[12,5280]{1,0:T(8,128)(2,1)S(1)} %get-tuple-element.658), channel_id=1, source_target_pairs={{0,65},{1,66},{2,67},{3,64},{64,129},{65,130},{66,131},{67,128},{1... | collective-permute-start | bytes 380168 | tf_op jit(solution)/shard_map/while/body/eval_jaxpr/ppermute | solution.py:42
  854.1 19.3 %collective-permute-start.8 = (bf16[12,5280]{1,0:T(8,128)(2,1)S(1)}, bf16[12,5280]{1,0:T(8,128)(2,1)S(1)}, u32[]{:S(2)}, u32[]{:S(2)}) collective-permute-start(bf16[12,5280]{1,0:T(8,128)(2,1)S(1)} %get-tuple-element.660), channel_id=1, source_target_pairs={{0,67},{1,64},{2,65},{3,66},{64,131},{65,128},{66,129},{67,130},{1... | collective-permute-start | bytes 380168 | tf_op jit(solution)/shard_map/while/body/eval_jaxpr/ppermute | solution.py:42
  859.5 19.0 %collective-permute-start = (bf16[32,5280]{1,0:T(8,128)(2,1)S(1)}, bf16[32,5280]{1,0:T(8,128)(2,1)S(1)}, u32[]{:S(2)}, u32[]{:S(2)}) collective-permute-start(bf16[32,5280]{1,0:T(8,128)(2,1)S(1)} %get-tuple-element.652), channel_id=1, source_target_pairs={{192,0},{0,64},{64,128},{128,192},{193,1},{1,65},{65,129},{129,193... | collective-permute-start | bytes 1013768 | tf_op jit(solution)/shard_map/while/body/eval_jaxpr/ppermute | solution.py:13
  (66 other events, 879.8 us)
Sparse Core Ops, SparseCore 0:
  9.5 99.5 all-gather.4
  111.0 99.7 all-gather.2

commit v6 on v2

--- a/solution.py
+++ b/solution.py
@@ -8,6 +8,7 @@
 from jax.sharding import PartitionSpec as P
 
 MESH = pl.DeviceIdType.MESH
+SLAB = 16
 
 RECUR = 2
 CAP = 12
@@ -31,7 +32,9 @@
     hidden = jax.nn.gelu(jnp.dot(flat_rows, w_first, preferred_element_type=jnp.float32)).astype(
         jnp.bfloat16
     )
-    result = jnp.dot(hidden, w_second, preferred_element_type=jnp.float32).astype(jnp.bfloat16)
+    result = lax.dot_general(
+        hidden, w_second, (((1,), (1,)), ((), ())), preferred_element_type=jnp.float32
+    ).astype(jnp.bfloat16)
     return result.reshape(extent)
 
 
@@ -47,13 +50,12 @@
     pl.semaphore_wait(barrier, groups - 1)
     copies = []
     for j in range(1, groups):
-        target = lax.rem(me + direction * j + groups, groups)
         copy = pltpu.make_async_remote_copy(
             src_ref=src_ref.at[j],
             dst_ref=dst_ref.at[j],
             send_sem=send_sem.at[j - 1],
             recv_sem=recv_sem.at[j - 1],
-            device_id=place + (target,),
+            device_id=place + (lax.rem(me + direction * j + groups, groups),),
             device_id_type=MESH,
         )
         copy.start()
@@ -99,17 +101,17 @@
     counts = jnp.dot(earlier, onehot, preferred_element_type=jnp.float32)
     slot_index = jnp.sum(onehot * counts, axis=-1).astype(jnp.int32)
     relative = jnp.mod(assign - lax.axis_index("expert"), experts)
-    target = relative * CAP + slot_index
+    target = relative * SLAB + slot_index
     places = (
-        lax.broadcasted_iota(jnp.int32, (experts * CAP, tokens), 0) == target[None, :]
+        lax.broadcasted_iota(jnp.int32, (experts * SLAB, tokens), 0) == target[None, :]
     ).astype(jnp.bfloat16)
     buffer = (
         jnp.dot(places, normed, preferred_element_type=jnp.float32)
         .astype(jnp.bfloat16)
-        .reshape(experts, CAP, -1)
+        .reshape(experts, SLAB, -1)
     )
     returned = whole_round(buffer, w_first, w_second)
-    flat_back = returned.reshape(experts * CAP, -1)
+    flat_back = returned.reshape(experts * SLAB, -1)
     expert_out = jnp.einsum("st,sd->td", places, flat_back, preferred_element_type=jnp.float32)
     updated = current.astype(jnp.float32) + gate_value[:, None] * expert_out
     return updated.astype(jnp.bfloat16)
@@ -120,7 +122,7 @@
     section_index = lax.axis_index("section")
     up_all, down_all = (
         lax.all_gather(w_up, "dp", axis=2, tiled=True),
-        lax.all_gather(w_down, "dp", axis=3, tiled=True),
+        lax.all_gather(jnp.swapaxes(w_down, 2, 3), "dp", axis=2, tiled=True),
     )
     w_first = up_all[0, 0]
     w_second = down_all[0, 0]

time: 924 us -> 910 us (0.985)
  local copies, waits for them, and re-layouts: 111 us -> 36.7 us
  matrix products: 116 us -> 157 us
  Pallas kernels: 412 us -> 425 us
    reshape x44 -> x0, local copies, waits for them, and re-layouts: 51.1 us -> none  [the longest x11 14.7 us: core_block(): flat_back = returned.reshape(experts * CAP, -1)]
    unnamed x10 -> x12, local copies, waits for them, and re-layouts: 52.4 us -> 29.4 us
    dot_general x11, matrix products: 104 us -> 122 us  [expert_rows(): lax.dot_general(hidden, w_second, (((1,), (1,)), ((), ())), preferred_ele...]
    pallas_call x22, Pallas kernels: 412 us -> 425 us  [exchange(): pl.pallas_call(functools.partial(exchange_kernel, direction), out_shape=j...]
    dot_general x11, matrix products: 3.65 us -> 15.6 us  [core_block(): jnp.einsum('st,sd->td', places, flat_back, preferred_element_type=jnp.flo...]
    dot_general x11, matrix products: 4.04 us -> 14.5 us  [core_block(): jnp.dot(places, normed, preferred_element_type=jnp.float32)]
where the time goes in v6:
time: 910 us; the launch traced here: 904 us
  Pallas kernels  425 us (47%)
  waiting for transfers between devices  237 us (26%)
  matrix products  157 us (17%)
  local copies, waits for them, and re-layouts  36.7 us (4%)
  other arithmetic  24.1 us (3%)
  between operations  13.5 us (1%)
  starting transfers between devices  10.3 us (1%)
    pallas_call x22, Pallas kernels, exchange(): pl.pallas_call(functools.partial(exchange_kernel, direction), out_shape=j...  425 us
    dot_general x11, matrix products, expert_rows(): lax.dot_general(hidden, w_second, (((1,), (1,)), ((), ())), preferred_ele...  122 us
    all_gather x1, waiting for transfers between devices, body(): lax.all_gather(jnp.swapaxes(w_down, 2, 3), 'dp', axis=2, tiled=True)  85.9 us
    ppermute x10, waiting for transfers between devices, shifted(): return lax.ppermute(block, axis, route)  78.6 us
    all_gather x1, waiting for transfers between devices, body(): lax.all_gather(w_up, 'dp', axis=2, tiled=True)  72.5 us
    unnamed x12, local copies, waits for them, and re-layouts  29.4 us
  transfers between devices with their start and end apart: 12, of which 12 were waited for; matrix products, arithmetic and copies ran while one was open for 4% of the time, Pallas kernels for 2%

profile of v6, /device:TPU:2, one launch (start us, length us, event | category | flops | bytes accessed | tf_op | source)
XLA Modules:
  0.0 904.5 jit_solution(7077250033732590156)
XLA Ops:
  17.2 22.3 %shard_map.73 = bf16[4,16,5280]{2,1,0:T(8,128)(2,1)} custom-call(bf16[4,16,5280]{2,1,0:T(8,128)(2,1)} %bitcast.99), custom_call_target="tpu_custom_call" | custom-call | tf_op jit(solution)/shard_map/pallas_call | solution.py:70
  39.8 72.5 %all-gather.3.cloned.1.call-done = bf16[1,1,5280,768]{3,1,0,2:T(2,128)(2,1)} async-done(((bf16[1,1,330,768]{3,1,0,2:T(2,128)(2,1)}), bf16[1,1,5280,768]{3,1,0,2:T(2,128)(2,1)}) %all-gather.3.cloned.1.call-update) | async-done | bytes 8110096 | tf_op jit(solution)/shard_map/all_gather | solution.py:124
  112.4 11.5 %copy.18 = bf16[1,1,5280,768]{3,2,0,1:T(8,128)(2,1)} copy(bf16[1,1,5280,768]{3,1,0,2:T(2,128)(2,1)} %all-gather.3.cloned.1.call-done) | data formatting | bytes 16220160
  123.9 85.9 %all-gather.5.cloned.1.call-done = bf16[1,1,5280,768]{3,1,0,2:T(2,128)(2,1)} async-done(((bf16[1,1,330,768]{3,1,0,2:T(2,128)(2,1)}), bf16[1,1,5280,768]{3,1,0,2:T(2,128)(2,1)}) %all-gather.5.cloned.1.call-update) | async-done | bytes 8110096 | tf_op jit(solution)/shard_map/all_gather | solution.py:125
  209.8 11.6 %copy.17 = bf16[1,1,5280,768]{3,2,0,1:T(8,128)(2,1)} copy(bf16[1,1,5280,768]{3,1,0,2:T(2,128)(2,1)} %all-gather.5.cloned.1.call-done) | data formatting | bytes 16220160
  221.4 10.9 %convolution_convert_fusion.3 = bf16[64,5280]{1,0:T(8,128)(2,1)} fusion(bf16[5280,768]{1,0:T(8,128)(2,1)} %bitcast.89, bf16[64,5280]{1,0:T(8,128)(2,1)S(1)} %bitcast.96, bf16[5280,768]{1,0:T(8,128)(2,1)} %bitcast.87), kind=kOutput, calls=%fused_computation.55 | convolution fusion | flops 1038870528 | bytes 17571840 | tf_op jit(solution)/shard_map/dot_general | solution.py:35
  232.3 23.9 %shard_map.74 = bf16[4,16,5280]{2,1,0:T(8,128)(2,1)} custom-call(bf16[4,16,5280]{2,1,0:T(8,128)(2,1)} %bitcast.97), custom_call_target="tpu_custom_call" | custom-call | tf_op jit(solution)/shard_map/pallas_call | solution.py:70
  257.7 639.2 %while.15 = (s32[]{:T(128)}, bf16[32,5280]{1,0:T(8,128)(2,1)S(1)}, s32[]{:T(128)}, pred[]{:T(512)}, bf16[4,32,5280]{2,1,0:T(8,128)(2,1)}, /*index=5*/bf16[4,32,5...) while((s32[]{:T(128)}, bf16[32,5280]{1,0:T(8,128)(2,1)S(1)}, ...), condition=%wide.region_7.8_spmd, body=%wide.region_3.7_spmd.sunk | while | flops 1087545856 | bytes 23446284 | solution.py:162
  260.8 8.1 collective-permute-done
  271.9 19.8 %eval_jaxpr.16 = bf16[4,16,5280]{2,1,0:T(8,128)(2,1)} custom-call(bf16[4,16,5280]{2,1,0:T(8,128)(2,1)} %bitcast.94), custom_call_target="tpu_custom_call" | custom-call | tf_op jit(solution)/shard_map/while/body/eval_jaxpr/pallas_call | solution.py:70
  291.7 11.2 %convolution_convert_fusion.7 = bf16[64,5280]{1,0:T(8,128)(2,1)} fusion(bf16[5280,768]{1,0:T(8,128)(2,1)} %get-tuple-element.406, bf16[64,5280]{1,0:T(8,128)(2,1)} %bitcast.91, bf16[5280,768]{1,0:T(8,128)(2,1)} %get-tuple-element.405), kind=kOutput, calls=%fused_computation.1.clone.1 | convolution fusion | flops 1038870528 | bytes 17571840 | tf_op jit(solution)/shard_map/while/body/eval_jaxpr/dot_general | solution.py:35
  302.8 20.3 %eval_jaxpr.17 = bf16[4,16,5280]{2,1,0:T(8,128)(2,1)} custom-call(bf16[4,16,5280]{2,1,0:T(8,128)(2,1)} %bitcast.92), custom_call_target="tpu_custom_call" | custom-call | tf_op jit(solution)/shard_map/while/body/eval_jaxpr/pallas_call | solution.py:70
  336.2 22.5 %eval_jaxpr.16 = bf16[4,16,5280]{2,1,0:T(8,128)(2,1)} custom-call(bf16[4,16,5280]{2,1,0:T(8,128)(2,1)} %bitcast.94), custom_call_target="tpu_custom_call" | custom-call | tf_op jit(solution)/shard_map/while/body/eval_jaxpr/pallas_call | solution.py:70
  358.7 11.2 %convolution_convert_fusion.7 = bf16[64,5280]{1,0:T(8,128)(2,1)} fusion(bf16[5280,768]{1,0:T(8,128)(2,1)} %get-tuple-element.406, bf16[64,5280]{1,0:T(8,128)(2,1)} %bitcast.91, bf16[5280,768]{1,0:T(8,128)(2,1)} %get-tuple-element.405), kind=kOutput, calls=%fused_computation.1.clone.1 | convolution fusion | flops 1038870528 | bytes 17571840 | tf_op jit(solution)/shard_map/while/body/eval_jaxpr/dot_general | solution.py:35
  369.8 19.5 %eval_jaxpr.17 = bf16[4,16,5280]{2,1,0:T(8,128)(2,1)} custom-call(bf16[4,16,5280]{2,1,0:T(8,128)(2,1)} %bitcast.92), custom_call_target="tpu_custom_call" | custom-call | tf_op jit(solution)/shard_map/while/body/eval_jaxpr/pallas_call | solution.py:70
  392.4 6.9 collective-permute-done
  402.3 22.5 %eval_jaxpr.16 = bf16[4,16,5280]{2,1,0:T(8,128)(2,1)} custom-call(bf16[4,16,5280]{2,1,0:T(8,128)(2,1)} %bitcast.94), custom_call_target="tpu_custom_call" | custom-call | tf_op jit(solution)/shard_map/while/body/eval_jaxpr/pallas_call | solution.py:70
  424.8 11.2 %convolution_convert_fusion.7 = bf16[64,5280]{1,0:T(8,128)(2,1)} fusion(bf16[5280,768]{1,0:T(8,128)(2,1)} %get-tuple-element.406, bf16[64,5280]{1,0:T(8,128)(2,1)} %bitcast.91, bf16[5280,768]{1,0:T(8,128)(2,1)} %get-tuple-element.405), kind=kOutput, calls=%fused_computation.1.clone.1 | convolution fusion | flops 1038870528 | bytes 17571840 | tf_op jit(solution)/shard_map/while/body/eval_jaxpr/dot_general | solution.py:35
  435.9 17.1 %eval_jaxpr.17 = bf16[4,16,5280]{2,1,0:T(8,128)(2,1)} custom-call(bf16[4,16,5280]{2,1,0:T(8,128)(2,1)} %bitcast.92), custom_call_target="tpu_custom_call" | custom-call | tf_op jit(solution)/shard_map/while/body/eval_jaxpr/pallas_call | solution.py:70
  456.2 6.9 collective-permute-done
  466.1 16.3 %eval_jaxpr.16 = bf16[4,16,5280]{2,1,0:T(8,128)(2,1)} custom-call(bf16[4,16,5280]{2,1,0:T(8,128)(2,1)} %bitcast.94), custom_call_target="tpu_custom_call" | custom-call | tf_op jit(solution)/shard_map/while/body/eval_jaxpr/pallas_call | solution.py:70
  482.4 11.2 %convolution_convert_fusion.7 = bf16[64,5280]{1,0:T(8,128)(2,1)} fusion(bf16[5280,768]{1,0:T(8,128)(2,1)} %get-tuple-element.406, bf16[64,5280]{1,0:T(8,128)(2,1)} %bitcast.91, bf16[5280,768]{1,0:T(8,128)(2,1)} %get-tuple-element.405), kind=kOutput, calls=%fused_computation.1.clone.1 | convolution fusion | flops 1038870528 | bytes 17571840 | tf_op jit(solution)/shard_map/while/body/eval_jaxpr/dot_general | solution.py:35
  493.6 27.6 %eval_jaxpr.17 = bf16[4,16,5280]{2,1,0:T(8,128)(2,1)} custom-call(bf16[4,16,5280]{2,1,0:T(8,128)(2,1)} %bitcast.92), custom_call_target="tpu_custom_call" | custom-call | tf_op jit(solution)/shard_map/while/body/eval_jaxpr/pallas_call | solution.py:70
  524.3 6.9 collective-permute-done
  534.2 18.0 %eval_jaxpr.16 = bf16[4,16,5280]{2,1,0:T(8,128)(2,1)} custom-call(bf16[4,16,5280]{2,1,0:T(8,128)(2,1)} %bitcast.94), custom_call_target="tpu_custom_call" | custom-call | tf_op jit(solution)/shard_map/while/body/eval_jaxpr/pallas_call | solution.py:70
  552.2 11.2 %convolution_convert_fusion.7 = bf16[64,5280]{1,0:T(8,128)(2,1)} fusion(bf16[5280,768]{1,0:T(8,128)(2,1)} %get-tuple-element.406, bf16[64,5280]{1,0:T(8,128)(2,1)} %bitcast.91, bf16[5280,768]{1,0:T(8,128)(2,1)} %get-tuple-element.405), kind=kOutput, calls=%fused_computation.1.clone.1 | convolution fusion | flops 1038870528 | bytes 17571840 | tf_op jit(solution)/shard_map/while/body/eval_jaxpr/dot_general | solution.py:35
  563.3 22.1 %eval_jaxpr.17 = bf16[4,16,5280]{2,1,0:T(8,128)(2,1)} custom-call(bf16[4,16,5280]{2,1,0:T(8,128)(2,1)} %bitcast.92), custom_call_target="tpu_custom_call" | custom-call | tf_op jit(solution)/shard_map/while/body/eval_jaxpr/pallas_call | solution.py:70
  588.5 9.6 %collective-permute-done = bf16[32,5280]{1,0:T(8,128)(2,1)S(1)} collective-permute-done((bf16[32,5280]{1,0:T(8,128)(2,1)S(1)}, bf16[32,5280]{1,0:T(8,128)(2,1)S(1)}, u32[]{:S(2)}, u32[]{:S(2)}) %collective-permute-start) | collective-permute-done | bytes 337952 | tf_op jit(solution)/shard_map/while/body/eval_jaxpr/ppermute | solution.py:20
  601.2 18.7 %eval_jaxpr.16 = bf16[4,16,5280]{2,1,0:T(8,128)(2,1)} custom-call(bf16[4,16,5280]{2,1,0:T(8,128)(2,1)} %bitcast.94), custom_call_target="tpu_custom_call" | custom-call | tf_op jit(solution)/shard_map/while/body/eval_jaxpr/pallas_call | solution.py:70
  619.9 11.2 %convolution_convert_fusion.7 = bf16[64,5280]{1,0:T(8,128)(2,1)} fusion(bf16[5280,768]{1,0:T(8,128)(2,1)} %get-tuple-element.406, bf16[64,5280]{1,0:T(8,128)(2,1)} %bitcast.91, bf16[5280,768]{1,0:T(8,128)(2,1)} %get-tuple-element.405), kind=kOutput, calls=%fused_computation.1.clone.1 | convolution fusion | flops 1038870528 | bytes 17571840 | tf_op jit(solution)/shard_map/while/body/eval_jaxpr/dot_general | solution.py:35
  631.0 17.9 %eval_jaxpr.17 = bf16[4,16,5280]{2,1,0:T(8,128)(2,1)} custom-call(bf16[4,16,5280]{2,1,0:T(8,128)(2,1)} %bitcast.92), custom_call_target="tpu_custom_call" | custom-call | tf_op jit(solution)/shard_map/while/body/eval_jaxpr/pallas_call | solution.py:70
  652.1 8.1 collective-permute-done
  663.2 18.8 %eval_jaxpr.16 = bf16[4,16,5280]{2,1,0:T(8,128)(2,1)} custom-call(bf16[4,16,5280]{2,1,0:T(8,128)(2,1)} %bitcast.94), custom_call_target="tpu_custom_call" | custom-call | tf_op jit(solution)/shard_map/while/body/eval_jaxpr/pallas_call | solution.py:70
  682.0 11.2 %convolution_convert_fusion.7 = bf16[64,5280]{1,0:T(8,128)(2,1)} fusion(bf16[5280,768]{1,0:T(8,128)(2,1)} %get-tuple-element.406, bf16[64,5280]{1,0:T(8,128)(2,1)} %bitcast.91, bf16[5280,768]{1,0:T(8,128)(2,1)} %get-tuple-element.405), kind=kOutput, calls=%fused_computation.1.clone.1 | convolution fusion | flops 1038870528 | bytes 17571840 | tf_op jit(solution)/shard_map/while/body/eval_jaxpr/dot_general | solution.py:35
  693.1 18.8 %eval_jaxpr.17 = bf16[4,16,5280]{2,1,0:T(8,128)(2,1)} custom-call(bf16[4,16,5280]{2,1,0:T(8,128)(2,1)} %bitcast.92), custom_call_target="tpu_custom_call" | custom-call | tf_op jit(solution)/shard_map/while/body/eval_jaxpr/pallas_call | solution.py:70
  715.1 6.9 collective-permute-done
  725.0 14.5 %eval_jaxpr.16 = bf16[4,16,5280]{2,1,0:T(8,128)(2,1)} custom-call(bf16[4,16,5280]{2,1,0:T(8,128)(2,1)} %bitcast.94), custom_call_target="tpu_custom_call" | custom-call | tf_op jit(solution)/shard_map/while/body/eval_jaxpr/pallas_call | solution.py:70
  739.5 11.2 %convolution_convert_fusion.7 = bf16[64,5280]{1,0:T(8,128)(2,1)} fusion(bf16[5280,768]{1,0:T(8,128)(2,1)} %get-tuple-element.406, bf16[64,5280]{1,0:T(8,128)(2,1)} %bitcast.91, bf16[5280,768]{1,0:T(8,128)(2,1)} %get-tuple-element.405), kind=kOutput, calls=%fused_computation.1.clone.1 | convolution fusion | flops 1038870528 | bytes 17571840 | tf_op jit(solution)/shard_map/while/body/eval_jaxpr/dot_general | solution.py:35
  750.6 14.5 %eval_jaxpr.17 = bf16[4,16,5280]{2,1,0:T(8,128)(2,1)} custom-call(bf16[4,16,5280]{2,1,0:T(8,128)(2,1)} %bitcast.92), custom_call_target="tpu_custom_call" | custom-call | tf_op jit(solution)/shard_map/while/body/eval_jaxpr/pallas_call | solution.py:70
  766.6 7.8 collective-permute-start
  775.9 11.8 %collective-permute-done = bf16[32,5280]{1,0:T(8,128)(2,1)S(1)} collective-permute-done((bf16[32,5280]{1,0:T(8,128)(2,1)S(1)}, bf16[32,5280]{1,0:T(8,128)(2,1)S(1)}, u32[]{:S(2)}, u32[]{:S(2)}) %collective-permute-start) | collective-permute-done | bytes 337952 | tf_op jit(solution)/shard_map/while/body/eval_jaxpr/ppermute | solution.py:20
  790.7 16.4 %eval_jaxpr.16 = bf16[4,16,5280]{2,1,0:T(8,128)(2,1)} custom-call(bf16[4,16,5280]{2,1,0:T(8,128)(2,1)} %bitcast.94), custom_call_target="tpu_custom_call" | custom-call | tf_op jit(solution)/shard_map/while/body/eval_jaxpr/pallas_call | solution.py:70
  807.1 11.2 %convolution_convert_fusion.7 = bf16[64,5280]{1,0:T(8,128)(2,1)} fusion(bf16[5280,768]{1,0:T(8,128)(2,1)} %get-tuple-element.406, bf16[64,5280]{1,0:T(8,128)(2,1)} %bitcast.91, bf16[5280,768]{1,0:T(8,128)(2,1)} %get-tuple-element.405), kind=kOutput, calls=%fused_computation.1.clone.1 | convolution fusion | flops 1038870528 | bytes 17571840 | tf_op jit(solution)/shard_map/while/body/eval_jaxpr/dot_general | solution.py:35
  818.3 24.4 %eval_jaxpr.17 = bf16[4,16,5280]{2,1,0:T(8,128)(2,1)} custom-call(bf16[4,16,5280]{2,1,0:T(8,128)(2,1)} %bitcast.92), custom_call_target="tpu_custom_call" | custom-call | tf_op jit(solution)/shard_map/while/body/eval_jaxpr/pallas_call | solution.py:70
  845.8 6.9 collective-permute-done
  855.7 15.4 %eval_jaxpr.16 = bf16[4,16,5280]{2,1,0:T(8,128)(2,1)} custom-call(bf16[4,16,5280]{2,1,0:T(8,128)(2,1)} %bitcast.94), custom_call_target="tpu_custom_call" | custom-call | tf_op jit(solution)/shard_map/while/body/eval_jaxpr/pallas_call | solution.py:70
  871.1 11.1 %convolution_convert_fusion.7 = bf16[64,5280]{1,0:T(8,128)(2,1)} fusion(bf16[5280,768]{1,0:T(8,128)(2,1)} %get-tuple-element.406, bf16[64,5280]{1,0:T(8,128)(2,1)} %bitcast.91, bf16[5280,768]{1,0:T(8,128)(2,1)} %get-tuple-element.405), kind=kOutput, calls=%fused_computation.1.clone.1 | convolution fusion | flops 1038870528 | bytes 17571840 | tf_op jit(solution)/shard_map/while/body/eval_jaxpr/dot_general | solution.py:35
  882.3 13.2 %eval_jaxpr.17 = bf16[4,16,5280]{2,1,0:T(8,128)(2,1)} custom-call(bf16[4,16,5280]{2,1,0:T(8,128)(2,1)} %bitcast.92), custom_call_target="tpu_custom_call" | custom-call | tf_op jit(solution)/shard_map/while/body/eval_jaxpr/pallas_call | solution.py:70
  (134 shorter events, 81.8 us)
Async XLA Ops:
  6.5 33.0 %copy-start.3 = (bf16[1,4,5280]{2,1,0:T(4,128)(2,1)S(1)}, bf16[1,4,5280]{2,1,0:T(4,128)(2,1)}, u32[]{:S(2)}) copy-start(bf16[1,4,5280]{2,1,0:T(4,128)(2,1)} %param.13) | copy-start | bytes 126724
  6.5 105.8 %all-gather.3.cloned.1.call-start = ((), (), s32[]{:S(2)}) async-start(), calls=%async_computation | async-start | bytes 17233920 | tf_op jit(solution)/shard_map/all_gather | solution.py:124
  9.4 200.4 %all-gather.5.cloned.1.call-start = ((), (), s32[]{:S(2)}) async-start(), calls=%async_computation.1 | async-start | bytes 17233920 | tf_op jit(solution)/shard_map/all_gather | solution.py:125
  123.9 97.5 %copy-start = (bf16[4,16,5280]{2,1,0:T(8,128)(2,1)S(1)}, bf16[4,16,5280]{2,1,0:T(8,128)(2,1)}, u32[]{:S(2)}) copy-start(bf16[4,16,5280]{2,1,0:T(8,128)(2,1)} %shard_map.73) | copy-start | bytes 2027524
  221.4 36.3 %copy-start.1 = (f32[1,5280]{1,0:T(1,128)S(1)}, f32[1,5280]{1,0:T(1,128)}, u32[]{:S(2)}) copy-start(f32[1,5280]{1,0:T(1,128)} %param.12) | copy-start | bytes 63364
  257.7 11.2 %collective-permute-start = (bf16[32,5280]{1,0:T(8,128)(2,1)S(1)}, bf16[32,5280]{1,0:T(8,128)(2,1)S(1)}, u32[]{:S(2)}, u32[]{:S(2)}) collective-permute-start(bf16[32,5280]{1,0:T(8,128)(2,1)S(1)} %get-tuple-element.376), channel_id=1, source_target_pairs={{192,0},{0,64},{64,128},{128,192},{193,1},{1,65},{65,129},{129,193... | collective-permute-start | bytes 1013768 | tf_op jit(solution)/shard_map/while/body/eval_jaxpr/ppermute | solution.py:20
  324.6 8.5 collective-permute-start
  390.7 8.5 collective-permute-start
  454.5 8.5 collective-permute-start
  522.6 8.5 collective-permute-start
  586.8 11.3 %collective-permute-start = (bf16[32,5280]{1,0:T(8,128)(2,1)S(1)}, bf16[32,5280]{1,0:T(8,128)(2,1)S(1)}, u32[]{:S(2)}, u32[]{:S(2)}) collective-permute-start(bf16[32,5280]{1,0:T(8,128)(2,1)S(1)} %get-tuple-element.376), channel_id=1, source_target_pairs={{192,0},{0,64},{64,128},{128,192},{193,1},{1,65},{65,129},{129,193... | collective-permute-start | bytes 1013768 | tf_op jit(solution)/shard_map/while/body/eval_jaxpr/ppermute | solution.py:20
  650.4 9.8 %collective-permute-start = (bf16[32,5280]{1,0:T(8,128)(2,1)S(1)}, bf16[32,5280]{1,0:T(8,128)(2,1)S(1)}, u32[]{:S(2)}, u32[]{:S(2)}) collective-permute-start(bf16[32,5280]{1,0:T(8,128)(2,1)S(1)} %get-tuple-element.376), channel_id=1, source_target_pairs={{192,0},{0,64},{64,128},{128,192},{193,1},{1,65},{65,129},{129,193... | collective-permute-start | bytes 1013768 | tf_op jit(solution)/shard_map/while/body/eval_jaxpr/ppermute | solution.py:20
  713.4 8.5 collective-permute-start
  766.6 21.1 %collective-permute-start = (bf16[32,5280]{1,0:T(8,128)(2,1)S(1)}, bf16[32,5280]{1,0:T(8,128)(2,1)S(1)}, u32[]{:S(2)}, u32[]{:S(2)}) collective-permute-start(bf16[32,5280]{1,0:T(8,128)(2,1)S(1)} %get-tuple-element.376), channel_id=1, source_target_pairs={{192,0},{0,64},{64,128},{128,192},{193,1},{1,65},{65,129},{129,193... | collective-permute-start | bytes 1013768 | tf_op jit(solution)/shard_map/while/body/eval_jaxpr/ppermute | solution.py:20
  844.1 8.5 collective-permute-start
  896.9 0.7 copy-start.2
Sparse Core Ops, SparseCore 0:
  9.5 102.8 all-gather.2
  114.2 95.5 all-gather.4

commit v7 on v4

--- a/solution.py
+++ b/solution.py
@@ -1,7 +1,13 @@
+import functools
+
 import jax
 import jax.numpy as jnp
 from jax import lax
+from jax.experimental import pallas as pl
+from jax.experimental.pallas import tpu as pltpu
 from jax.sharding import PartitionSpec as P
+
+CHUNK = 256
 
 RECUR = 2
 CAP = 12
@@ -19,15 +25,48 @@
     return (as_float * inv_rms * gain_row).astype(jnp.bfloat16)
 
 
+def mlp_kernel(rows_ref, up_ref, down_ref, out_ref, total_ref):
+    step = pl.program_id(0)
+
+    @pl.when(step == 0)
+    def _():
+        total_ref[...] = jnp.zeros_like(total_ref)
+
+    hidden = jax.nn.gelu(
+        jnp.dot(rows_ref[...], up_ref[...], preferred_element_type=jnp.float32)
+    ).astype(jnp.bfloat16)
+    total_ref[...] += lax.dot_general(
+        hidden, down_ref[...], (((1,), (1,)), ((), ())), preferred_element_type=jnp.float32
+    )
+
+    @pl.when(step == pl.num_programs(0) - 1)
+    def _():
+        out_ref[...] = total_ref[...].astype(out_ref.dtype)
+
+
 def expert_rows(item_rows, w_first, w_second):
     extent = item_rows.shape
     flat_rows = item_rows.reshape(-1, extent[-1])
-    hidden = jax.nn.gelu(jnp.dot(flat_rows, w_first, preferred_element_type=jnp.float32)).astype(
-        jnp.bfloat16
-    )
-    result = lax.dot_general(
-        hidden, w_second, (((1,), (1,)), ((), ())), preferred_element_type=jnp.float32
-    ).astype(jnp.bfloat16)
+    count, width = flat_rows.shape
+    inner = w_first.shape[1]
+    result = pl.pallas_call(
+        mlp_kernel,
+        out_shape=jax.ShapeDtypeStruct((count, width), jnp.bfloat16),
+        grid=(inner // CHUNK,),
+        in_specs=[
+            pl.BlockSpec((count, width), lambda k: (0, 0)),
+            pl.BlockSpec((width, CHUNK), lambda k: (0, k)),
+            pl.BlockSpec((width, CHUNK), lambda k: (0, k)),
+        ],
+        out_specs=pl.BlockSpec((count, width), lambda k: (0, 0)),
+        scratch_shapes=[pltpu.VMEM((count, width), jnp.float32)],
+        compiler_params=pltpu.CompilerParams(dimension_semantics=("arbitrary",)),
+        cost_estimate=pl.CostEstimate(
+            flops=4 * count * width * inner,
+            bytes_accessed=2 * (2 * width * inner + 2 * count * width),
+            transcendentals=count * inner,
+        ),
+    )(flat_rows, w_first, w_second)
     return result.reshape(extent)
 
 

time: 860 us -> 886 us (1.030); the launches traced: 860 us -> 876 us
  Pallas kernels: 0 us -> 112 us
  matrix products: 121 us -> 20.2 us
  local copies, waits for them, and re-layouts: 44.1 us -> 57.1 us
  other arithmetic: 26.9 us -> 17.9 us
    pallas_call x0 -> x11, Pallas kernels: none -> 112 us  [expert_rows(): pl.pallas_call(mlp_kernel, out_shape=jax.ShapeDtypeStruct((count, width),...]
    dot_general x11 -> x0, matrix products: 109 us -> none  [expert_rows(): lax.dot_general(hidden, w_second, (((1,), (1,)), ((), ())), preferred_ele...]
    slice x11, local copies, waits for them, and re-layouts: 1 us -> 14.1 us  [whole_round(): processed[0]]
    reshape x11, local copies, waits for them, and re-layouts: 2.66 us -> 11.6 us  [expert_rows(): flat_rows = item_rows.reshape(-1, extent[-1])]
    unnamed x10 -> x14, local copies, waits for them, and re-layouts: 29.5 us -> 27.8 us
  transfers between devices with their start and end apart: 78 -> 78, of which waited for: 63 -> 62; matrix products, arithmetic and copies ran while one was open for 4% -> 2% of each run, Pallas kernels for 0% -> 0%
where the time goes in v7:
time: 886 us; the launch traced here: 876 us
  waiting for transfers between devices  480 us (54%)
  starting transfers between devices  174 us (20%)
  Pallas kernels  112 us (13%)
  local copies, waits for them, and re-layouts  57.1 us (6%)
  matrix products  20.2 us (2%)
  other arithmetic  17.9 us (2%)
  between operations  13.6 us (2%)
    ppermute x76, waiting for transfers between devices, shifted(): return lax.ppermute(block, axis, route)  320 us
    ppermute x76, starting transfers between devices, shifted(): return lax.ppermute(block, axis, route)  174 us
    pallas_call x11, Pallas kernels, expert_rows(): pl.pallas_call(mlp_kernel, out_shape=jax.ShapeDtypeStruct((count, width),...  112 us
    all_gather x1, waiting for transfers between devices, body(): lax.all_gather(jnp.swapaxes(w_down, 2, 3), 'dp', axis=2, tiled=True)  90.1 us
    all_gather x1, waiting for transfers between devices, body(): lax.all_gather(w_up, 'dp', axis=2, tiled=True)  70.4 us
    unnamed x14, local copies, waits for them, and re-layouts  27.8 us
  transfers between devices with their start and end apart: 78, of which 62 were waited for; matrix products, arithmetic and copies ran while one was open for 2% of the time, Pallas kernels for 0%

profile of v7, /device:TPU:2, one launch (start us, length us, event | category | flops | bytes accessed | tf_op | source)
XLA Modules:
  0.0 875.9 jit_solution(11299799329871163291)
XLA Ops:
  13.4 6.4 collective-permute-start.9
  23.8 10.6 %collective-permute-done.9 = bf16[12,5280]{1,0:T(8,128)(2,1)S(1)} collective-permute-done((bf16[12,5280]{1,0:T(8,128)(2,1)S(1)}, bf16[12,5280]{1,0:T(8,128)(2,1)S(1)}, u32[]{:S(2)}, u32[]{:S(2)}) %collective-permute-start.9) | collective-permute-done | bytes 126752 | tf_op jit(solution)/shard_map/ppermute | solution.py:19
  35.7 70.4 %all-gather.3.cloned.1.call-done = bf16[1,1,5280,768]{3,1,0,2:T(2,128)(2,1)} async-done(((bf16[1,1,330,768]{3,1,0,2:T(2,128)(2,1)}), bf16[1,1,5280,768]{3,1,0,2:T(2,128)(2,1)}) %all-gather.3.cloned.1.call-update) | async-done | bytes 8110096 | tf_op jit(solution)/shard_map/all_gather | solution.py:117
  106.1 11.6 %copy.18 = bf16[1,1,5280,768]{3,2,0,1:T(8,128)(2,1)} copy(bf16[1,1,5280,768]{3,1,0,2:T(2,128)(2,1)} %all-gather.3.cloned.1.call-done) | data formatting | bytes 16220160
  117.7 90.1 %all-gather.5.cloned.1.call-done = bf16[1,1,5280,768]{3,1,0,2:T(2,128)(2,1)} async-done(((bf16[1,1,330,768]{3,1,0,2:T(2,128)(2,1)}), bf16[1,1,5280,768]{3,1,0,2:T(2,128)(2,1)}) %all-gather.5.cloned.1.call-update) | async-done | bytes 8110096 | tf_op jit(solution)/shard_map/all_gather | solution.py:118
  207.8 11.6 %copy.17 = bf16[1,1,5280,768]{3,2,0,1:T(8,128)(2,1)} copy(bf16[1,1,5280,768]{3,1,0,2:T(2,128)(2,1)} %all-gather.5.cloned.1.call-done) | data formatting | bytes 16220160
  219.3 10.1 %shard_map.73 = bf16[48,5280]{1,0:T(8,128)(2,1)} custom-call(bf16[48,5280]{1,0:T(8,128)(2,1)} %reshape.176.rows_ref, bf16[5280,768]{1,0:T(8,128)(2,1)} %bitcast.95, bf16[5280,768]{1,0:T(8,128)(2,1)} %bitcast.97), custom_call_target="tpu_custom_call" | custom-call | flops 778567680 | bytes 17233920 | tf_op jit(solution)/shard_map/pallas_call | solution.py:52
  240.7 8.4 collective-permute-done.11
  255.3 613.8 %while.15 = (s32[]{:T(128)}, bf16[32,5280]{1,0:T(8,128)(2,1)}, s32[]{:T(128)}, pred[]{:T(512)}, bf16[4,32,5280]{2,1,0:T(8,128)(2,1)}, /*index=5*/bf16[4,32,5280]...) while((s32[]{:T(128)}, bf16[32,5280]{1,0:T(8,128)(2,1)}, ...), condition=%wide.region_7.8_spmd, body=%wide.region_3.7_spmd.sunk | while | flops 817864704 | bytes 31894524 | solution.py:155
  257.0 9.7 %collective-permute-done = bf16[32,5280]{1,0:T(8,128)(2,1)S(1)} collective-permute-done((bf16[32,5280]{1,0:T(8,128)(2,1)}, bf16[32,5280]{1,0:T(8,128)(2,1)S(1)}, u32[]{:S(2)}, u32[]{:S(2)}) %collective-permute-start) | collective-permute-done | bytes 337952 | tf_op jit(solution)/shard_map/while/body/eval_jaxpr/ppermute | solution.py:19
  276.0 6.5 collective-permute-done.1
  288.6 10.2 %eval_jaxpr.8 = bf16[48,5280]{1,0:T(8,128)(2,1)} custom-call(bf16[48,5280]{1,0:T(8,128)(2,1)} %reshape.187.rows_ref, bf16[5280,768]{1,0:T(8,128)(2,1)} %get-tuple-element.433.up_ref, bf16[5280,768]{1,0:T(8,128)(2,1)} %get-tuple-element.434.down_ref), custom_call_target="tpu_custom_call" | custom-call | flops 778567680 | bytes 17233920 | tf_op jit(solution)/shard_map/while/body/eval_jaxpr/pallas_call | solution.py:52
  309.7 7.3 collective-permute-done.5
  320.5 10.8 %collective-permute-done = bf16[32,5280]{1,0:T(8,128)(2,1)S(1)} collective-permute-done((bf16[32,5280]{1,0:T(8,128)(2,1)}, bf16[32,5280]{1,0:T(8,128)(2,1)S(1)}, u32[]{:S(2)}, u32[]{:S(2)}) %collective-permute-start) | collective-permute-done | bytes 337952 | tf_op jit(solution)/shard_map/while/body/eval_jaxpr/ppermute | solution.py:19
  342.4 5.6 collective-permute-done.2
  351.9 10.2 %eval_jaxpr.8 = bf16[48,5280]{1,0:T(8,128)(2,1)} custom-call(bf16[48,5280]{1,0:T(8,128)(2,1)} %reshape.187.rows_ref, bf16[5280,768]{1,0:T(8,128)(2,1)} %get-tuple-element.433.up_ref, bf16[5280,768]{1,0:T(8,128)(2,1)} %get-tuple-element.434.down_ref), custom_call_target="tpu_custom_call" | custom-call | flops 778567680 | bytes 17233920 | tf_op jit(solution)/shard_map/while/body/eval_jaxpr/pallas_call | solution.py:52
  369.7 9.8 %collective-permute-done.4 = bf16[12,5280]{1,0:T(8,128)(2,1)S(1)} collective-permute-done((bf16[12,5280]{1,0:T(8,128)(2,1)S(1)}, bf16[12,5280]{1,0:T(8,128)(2,1)S(1)}, u32[]{:S(2)}, u32[]{:S(2)}) %collective-permute-start.4) | collective-permute-done | bytes 126752 | tf_op jit(solution)/shard_map/while/body/eval_jaxpr/ppermute | solution.py:19
  381.2 8.4 collective-permute-done
  391.4 6.3 collective-permute-start.1
  397.7 5.9 collective-permute-start.2
  404.7 9.7 %collective-permute-done.2 = bf16[12,5280]{1,0:T(8,128)(2,1)S(1)} collective-permute-done((bf16[12,5280]{1,0:T(8,128)(2,1)S(1)}, bf16[12,5280]{1,0:T(8,128)(2,1)S(1)}, u32[]{:S(2)}, u32[]{:S(2)}) %collective-permute-start.2) | collective-permute-done | bytes 126752 | tf_op jit(solution)/shard_map/while/body/eval_jaxpr/ppermute | solution.py:19
  415.6 10.2 %eval_jaxpr.8 = bf16[48,5280]{1,0:T(8,128)(2,1)} custom-call(bf16[48,5280]{1,0:T(8,128)(2,1)} %reshape.187.rows_ref, bf16[5280,768]{1,0:T(8,128)(2,1)} %get-tuple-element.433.up_ref, bf16[5280,768]{1,0:T(8,128)(2,1)} %get-tuple-element.434.down_ref), custom_call_target="tpu_custom_call" | custom-call | flops 778567680 | bytes 17233920 | tf_op jit(solution)/shard_map/while/body/eval_jaxpr/pallas_call | solution.py:52
  445.9 8.4 collective-permute-done
  465.2 9.2 %collective-permute-done.1 = bf16[12,5280]{1,0:T(8,128)(2,1)S(1)} collective-permute-done((bf16[12,5280]{1,0:T(8,128)(2,1)S(1)}, bf16[12,5280]{1,0:T(8,128)(2,1)S(1)}, u32[]{:S(2)}, u32[]{:S(2)}) %collective-permute-start.1) | collective-permute-done | bytes 126752 | tf_op jit(solution)/shard_map/while/body/eval_jaxpr/ppermute | solution.py:19
  475.6 10.2 %eval_jaxpr.8 = bf16[48,5280]{1,0:T(8,128)(2,1)} custom-call(bf16[48,5280]{1,0:T(8,128)(2,1)} %reshape.187.rows_ref, bf16[5280,768]{1,0:T(8,128)(2,1)} %get-tuple-element.433.up_ref, bf16[5280,768]{1,0:T(8,128)(2,1)} %get-tuple-element.434.down_ref), custom_call_target="tpu_custom_call" | custom-call | flops 778567680 | bytes 17233920 | tf_op jit(solution)/shard_map/while/body/eval_jaxpr/pallas_call | solution.py:52
  498.4 6.4 collective-permute-done.5
  508.2 8.4 collective-permute-done
  524.6 9.5 %collective-permute-done.1 = bf16[12,5280]{1,0:T(8,128)(2,1)S(1)} collective-permute-done((bf16[12,5280]{1,0:T(8,128)(2,1)S(1)}, bf16[12,5280]{1,0:T(8,128)(2,1)S(1)}, u32[]{:S(2)}, u32[]{:S(2)}) %collective-permute-start.1) | collective-permute-done | bytes 126752 | tf_op jit(solution)/shard_map/while/body/eval_jaxpr/ppermute | solution.py:19
  536.4 10.2 %eval_jaxpr.8 = bf16[48,5280]{1,0:T(8,128)(2,1)} custom-call(bf16[48,5280]{1,0:T(8,128)(2,1)} %reshape.187.rows_ref, bf16[5280,768]{1,0:T(8,128)(2,1)} %get-tuple-element.433.up_ref, bf16[5280,768]{1,0:T(8,128)(2,1)} %get-tuple-element.434.down_ref), custom_call_target="tpu_custom_call" | custom-call | flops 778567680 | bytes 17233920 | tf_op jit(solution)/shard_map/while/body/eval_jaxpr/pallas_call | solution.py:52
  555.5 8.3 collective-permute-done.5
  565.5 8.4 collective-permute-done
  581.5 7.4 collective-permute-done.1
  594.5 10.2 %eval_jaxpr.8 = bf16[48,5280]{1,0:T(8,128)(2,1)} custom-call(bf16[48,5280]{1,0:T(8,128)(2,1)} %reshape.187.rows_ref, bf16[5280,768]{1,0:T(8,128)(2,1)} %get-tuple-element.433.up_ref, bf16[5280,768]{1,0:T(8,128)(2,1)} %get-tuple-element.434.down_ref), custom_call_target="tpu_custom_call" | custom-call | flops 778567680 | bytes 17233920 | tf_op jit(solution)/shard_map/while/body/eval_jaxpr/pallas_call | solution.py:52
  625.2 8.4 collective-permute-done
  642.8 8.4 collective-permute-done.2
  654.9 10.2 %eval_jaxpr.8 = bf16[48,5280]{1,0:T(8,128)(2,1)} custom-call(bf16[48,5280]{1,0:T(8,128)(2,1)} %reshape.187.rows_ref, bf16[5280,768]{1,0:T(8,128)(2,1)} %get-tuple-element.433.up_ref, bf16[5280,768]{1,0:T(8,128)(2,1)} %get-tuple-element.434.down_ref), custom_call_target="tpu_custom_call" | custom-call | flops 778567680 | bytes 17233920 | tf_op jit(solution)/shard_map/while/body/eval_jaxpr/pallas_call | solution.py:52
  682.7 8.4 collective-permute-done
  695.6 11.5 %collective-permute-start.2 = (bf16[12,5280]{1,0:T(8,128)(2,1)S(1)}, bf16[12,5280]{1,0:T(8,128)(2,1)S(1)}, u32[]{:S(2)}, u32[]{:S(2)}) collective-permute-start(bf16[12,5280]{1,0:T(8,128)(2,1)S(1)} %get-tuple-element.375), channel_id=1, source_target_pairs={{2,0},{3,1},{0,2},{1,3},{6,4},{7,5},{4,6},{5,7},{10,8},{11,9},{8,1... | collective-permute-start | bytes 380168 | tf_op jit(solution)/shard_map/while/body/eval_jaxpr/ppermute | solution.py:19
  712.4 5.8 collective-permute-done.3
  719.3 10.2 %eval_jaxpr.8 = bf16[48,5280]{1,0:T(8,128)(2,1)} custom-call(bf16[48,5280]{1,0:T(8,128)(2,1)} %reshape.187.rows_ref, bf16[5280,768]{1,0:T(8,128)(2,1)} %get-tuple-element.433.up_ref, bf16[5280,768]{1,0:T(8,128)(2,1)} %get-tuple-element.434.down_ref), custom_call_target="tpu_custom_call" | custom-call | flops 778567680 | bytes 17233920 | tf_op jit(solution)/shard_map/while/body/eval_jaxpr/pallas_call | solution.py:52
  743.3 5.2 collective-permute-done.5
  754.2 7.3 collective-permute-done
  770.0 11.2 %collective-permute-done.1 = bf16[12,5280]{1,0:T(8,128)(2,1)S(1)} collective-permute-done((bf16[12,5280]{1,0:T(8,128)(2,1)S(1)}, bf16[12,5280]{1,0:T(8,128)(2,1)S(1)}, u32[]{:S(2)}, u32[]{:S(2)}) %collective-permute-start.1) | collective-permute-done | bytes 126752 | tf_op jit(solution)/shard_map/while/body/eval_jaxpr/ppermute | solution.py:19
  782.4 10.2 %eval_jaxpr.8 = bf16[48,5280]{1,0:T(8,128)(2,1)} custom-call(bf16[48,5280]{1,0:T(8,128)(2,1)} %reshape.187.rows_ref, bf16[5280,768]{1,0:T(8,128)(2,1)} %get-tuple-element.433.up_ref, bf16[5280,768]{1,0:T(8,128)(2,1)} %get-tuple-element.434.down_ref), custom_call_target="tpu_custom_call" | custom-call | flops 778567680 | bytes 17233920 | tf_op jit(solution)/shard_map/while/body/eval_jaxpr/pallas_call | solution.py:52
  804.8 8.1 collective-permute-done.5
  814.5 8.4 collective-permute-done
  831.2 5.2 collective-permute-done.1
  841.3 10.2 %eval_jaxpr.8 = bf16[48,5280]{1,0:T(8,128)(2,1)} custom-call(bf16[48,5280]{1,0:T(8,128)(2,1)} %reshape.187.rows_ref, bf16[5280,768]{1,0:T(8,128)(2,1)} %get-tuple-element.433.up_ref, bf16[5280,768]{1,0:T(8,128)(2,1)} %get-tuple-element.434.down_ref), custom_call_target="tpu_custom_call" | custom-call | flops 778567680 | bytes 17233920 | tf_op jit(solution)/shard_map/while/body/eval_jaxpr/pallas_call | solution.py:52
  (312 shorter events, 306.7 us)
Async XLA Ops:
  6.5 99.6 %all-gather.3.cloned.1.call-start = ((), (), s32[]{:S(2)}) async-start(), calls=%async_computation | async-start | bytes 17233920 | tf_op jit(solution)/shard_map/all_gather | solution.py:117
  9.5 198.3 %all-gather.5.cloned.1.call-start = ((), (), s32[]{:S(2)}) async-start(), calls=%async_computation.1 | async-start | bytes 17233920 | tf_op jit(solution)/shard_map/all_gather | solution.py:118
  13.4 21.1 %collective-permute-start.9 = (bf16[12,5280]{1,0:T(8,128)(2,1)S(1)}, bf16[12,5280]{1,0:T(8,128)(2,1)S(1)}, u32[]{:S(2)}, u32[]{:S(2)}) collective-permute-start(bf16[12,5280]{1,0:T(8,128)(2,1)S(1)} %get-tuple-element.292), channel_id=1, source_target_pairs={{1,0},{2,1},{3,2},{0,3},{5,4},{6,5},{7,6},{4,7},{9,8},{10,9},{11,1... | collective-permute-start | bytes 380168 | tf_op jit(solution)/shard_map/ppermute | solution.py:19
  19.7 14.7 %collective-permute-start.8 = (bf16[12,5280]{1,0:T(8,128)(2,1)S(1)}, bf16[12,5280]{1,0:T(8,128)(2,1)S(1)}, u32[]{:S(2)}, u32[]{:S(2)}) collective-permute-start(bf16[12,5280]{1,0:T(8,128)(2,1)S(1)} %get-tuple-element.293), channel_id=1, source_target_pairs={{2,0},{3,1},{0,2},{1,3},{6,4},{7,5},{4,6},{5,7},{10,8},{11,9},{8,1... | collective-permute-start | bytes 380168 | tf_op jit(solution)/shard_map/ppermute | solution.py:19
  20.7 13.7 %collective-permute-start.7 = (bf16[12,5280]{1,0:T(8,128)(2,1)S(1)}, bf16[12,5280]{1,0:T(8,128)(2,1)S(1)}, u32[]{:S(2)}, u32[]{:S(2)}) collective-permute-start(bf16[12,5280]{1,0:T(8,128)(2,1)S(1)} %get-tuple-element.294), channel_id=1, source_target_pairs={{3,0},{0,1},{1,2},{2,3},{7,4},{4,5},{5,6},{6,7},{11,8},{8,9},{9,10... | collective-permute-start | bytes 380168 | tf_op jit(solution)/shard_map/ppermute | solution.py:19
  233.4 15.7 %collective-permute-start.11 = (bf16[12,5280]{1,0:T(8,128)(2,1)S(1)}, bf16[12,5280]{1,0:T(8,128)(2,1)S(1)}, u32[]{:S(2)}, u32[]{:S(2)}) collective-permute-start(bf16[12,5280]{1,0:T(8,128)(2,1)S(1)} %get-tuple-element.289), channel_id=1, source_target_pairs={{2,0},{3,1},{0,2},{1,3},{6,4},{7,5},{4,6},{5,7},{10,8},{11,9},{8,1... | collective-permute-start | bytes 380168 | tf_op jit(solution)/shard_map/ppermute | solution.py:19
  237.3 16.5 %collective-permute-start.10 = (bf16[12,5280]{1,0:T(8,128)(2,1)S(1)}, bf16[12,5280]{1,0:T(8,128)(2,1)S(1)}, u32[]{:S(2)}, u32[]{:S(2)}) collective-permute-start(bf16[12,5280]{1,0:T(8,128)(2,1)S(1)} %get-tuple-element.290), channel_id=1, source_target_pairs={{1,0},{2,1},{3,2},{0,3},{5,4},{6,5},{7,6},{4,7},{9,8},{10,9},{11,1... | collective-permute-start | bytes 380168 | tf_op jit(solution)/shard_map/ppermute | solution.py:19
  268.4 14.0 %collective-permute-start.1 = (bf16[12,5280]{1,0:T(8,128)(2,1)S(1)}, bf16[12,5280]{1,0:T(8,128)(2,1)S(1)}, u32[]{:S(2)}, u32[]{:S(2)}) collective-permute-start(bf16[12,5280]{1,0:T(8,128)(2,1)S(1)} %get-tuple-element.374), channel_id=1, source_target_pairs={{1,0},{2,1},{3,2},{0,3},{5,4},{6,5},{7,6},{4,7},{9,8},{10,9},{11,1... | collective-permute-start | bytes 380168 | tf_op jit(solution)/shard_map/while/body/eval_jaxpr/ppermute | solution.py:19
  271.8 15.3 %collective-permute-start.2 = (bf16[12,5280]{1,0:T(8,128)(2,1)S(1)}, bf16[12,5280]{1,0:T(8,128)(2,1)S(1)}, u32[]{:S(2)}, u32[]{:S(2)}) collective-permute-start(bf16[12,5280]{1,0:T(8,128)(2,1)S(1)} %get-tuple-element.375), channel_id=1, source_target_pairs={{2,0},{3,1},{0,2},{1,3},{6,4},{7,5},{4,6},{5,7},{10,8},{11,9},{8,1... | collective-permute-start | bytes 380168 | tf_op jit(solution)/shard_map/while/body/eval_jaxpr/ppermute | solution.py:19
  274.6 12.9 %collective-permute-start.3 = (bf16[12,5280]{1,0:T(8,128)(2,1)S(1)}, bf16[12,5280]{1,0:T(8,128)(2,1)S(1)}, u32[]{:S(2)}, u32[]{:S(2)}) collective-permute-start(bf16[12,5280]{1,0:T(8,128)(2,1)S(1)} %get-tuple-element.376), channel_id=1, source_target_pairs={{3,0},{0,1},{1,2},{2,3},{7,4},{4,5},{5,6},{6,7},{11,8},{8,9},{9,10... | collective-permute-start | bytes 380168 | tf_op jit(solution)/shard_map/while/body/eval_jaxpr/ppermute | solution.py:19
  302.1 14.9 %collective-permute-start.5 = (bf16[12,5280]{1,0:T(8,128)(2,1)S(1)}, bf16[12,5280]{1,0:T(8,128)(2,1)S(1)}, u32[]{:S(2)}, u32[]{:S(2)}) collective-permute-start(bf16[12,5280]{1,0:T(8,128)(2,1)S(1)} %get-tuple-element.379), channel_id=1, source_target_pairs={{2,0},{3,1},{0,2},{1,3},{6,4},{7,5},{4,6},{5,7},{10,8},{11,9},{8,1... | collective-permute-start | bytes 380168 | tf_op jit(solution)/shard_map/while/body/eval_jaxpr/ppermute | solution.py:19
  306.0 12.5 %collective-permute-start.6 = (bf16[12,5280]{1,0:T(8,128)(2,1)S(1)}, bf16[12,5280]{1,0:T(8,128)(2,1)S(1)}, u32[]{:S(2)}, u32[]{:S(2)}) collective-permute-start(bf16[12,5280]{1,0:T(8,128)(2,1)S(1)} %get-tuple-element.380), channel_id=1, source_target_pairs={{1,0},{2,1},{3,2},{0,3},{5,4},{6,5},{7,6},{4,7},{9,8},{10,9},{11,1... | collective-permute-start | bytes 380168 | tf_op jit(solution)/shard_map/while/body/eval_jaxpr/ppermute | solution.py:19
  334.6 13.4 %collective-permute-start.2 = (bf16[12,5280]{1,0:T(8,128)(2,1)S(1)}, bf16[12,5280]{1,0:T(8,128)(2,1)S(1)}, u32[]{:S(2)}, u32[]{:S(2)}) collective-permute-start(bf16[12,5280]{1,0:T(8,128)(2,1)S(1)} %get-tuple-element.375), channel_id=1, source_target_pairs={{2,0},{3,1},{0,2},{1,3},{6,4},{7,5},{4,6},{5,7},{10,8},{11,9},{8,1... | collective-permute-start | bytes 380168 | tf_op jit(solution)/shard_map/while/body/eval_jaxpr/ppermute | solution.py:19
  337.4 13.3 %collective-permute-start.3 = (bf16[12,5280]{1,0:T(8,128)(2,1)S(1)}, bf16[12,5280]{1,0:T(8,128)(2,1)S(1)}, u32[]{:S(2)}, u32[]{:S(2)}) collective-permute-start(bf16[12,5280]{1,0:T(8,128)(2,1)S(1)} %get-tuple-element.376), channel_id=1, source_target_pairs={{3,0},{0,1},{1,2},{2,3},{7,4},{4,5},{5,6},{6,7},{11,8},{8,9},{9,10... | collective-permute-start | bytes 380168 | tf_op jit(solution)/shard_map/while/body/eval_jaxpr/ppermute | solution.py:19
  363.4 16.1 %collective-permute-start.4 = (bf16[12,5280]{1,0:T(8,128)(2,1)S(1)}, bf16[12,5280]{1,0:T(8,128)(2,1)S(1)}, u32[]{:S(2)}, u32[]{:S(2)}) collective-permute-start(bf16[12,5280]{1,0:T(8,128)(2,1)S(1)} %get-tuple-element.378), channel_id=1, source_target_pairs={{3,0},{0,1},{1,2},{2,3},{7,4},{4,5},{5,6},{6,7},{11,8},{8,9},{9,10... | collective-permute-start | bytes 380168 | tf_op jit(solution)/shard_map/while/body/eval_jaxpr/ppermute | solution.py:19
  364.3 15.3 %collective-permute-start.5 = (bf16[12,5280]{1,0:T(8,128)(2,1)S(1)}, bf16[12,5280]{1,0:T(8,128)(2,1)S(1)}, u32[]{:S(2)}, u32[]{:S(2)}) collective-permute-start(bf16[12,5280]{1,0:T(8,128)(2,1)S(1)} %get-tuple-element.379), channel_id=1, source_target_pairs={{2,0},{3,1},{0,2},{1,3},{6,4},{7,5},{4,6},{5,7},{10,8},{11,9},{8,1... | collective-permute-start | bytes 380168 | tf_op jit(solution)/shard_map/while/body/eval_jaxpr/ppermute | solution.py:19
  366.6 12.9 %collective-permute-start.6 = (bf16[12,5280]{1,0:T(8,128)(2,1)S(1)}, bf16[12,5280]{1,0:T(8,128)(2,1)S(1)}, u32[]{:S(2)}, u32[]{:S(2)}) collective-permute-start(bf16[12,5280]{1,0:T(8,128)(2,1)S(1)} %get-tuple-element.380), channel_id=1, source_target_pairs={{1,0},{2,1},{3,2},{0,3},{5,4},{6,5},{7,6},{4,7},{9,8},{10,9},{11,1... | collective-permute-start | bytes 380168 | tf_op jit(solution)/shard_map/while/body/eval_jaxpr/ppermute | solution.py:19
  391.4 13.3 %collective-permute-start.1 = (bf16[12,5280]{1,0:T(8,128)(2,1)S(1)}, bf16[12,5280]{1,0:T(8,128)(2,1)S(1)}, u32[]{:S(2)}, u32[]{:S(2)}) collective-permute-start(bf16[12,5280]{1,0:T(8,128)(2,1)S(1)} %get-tuple-element.374), channel_id=1, source_target_pairs={{1,0},{2,1},{3,2},{0,3},{5,4},{6,5},{7,6},{4,7},{9,8},{10,9},{11,1... | collective-permute-start | bytes 380168 | tf_op jit(solution)/shard_map/while/body/eval_jaxpr/ppermute | solution.py:19
  397.7 16.7 %collective-permute-start.2 = (bf16[12,5280]{1,0:T(8,128)(2,1)S(1)}, bf16[12,5280]{1,0:T(8,128)(2,1)S(1)}, u32[]{:S(2)}, u32[]{:S(2)}) collective-permute-start(bf16[12,5280]{1,0:T(8,128)(2,1)S(1)} %get-tuple-element.375), channel_id=1, source_target_pairs={{2,0},{3,1},{0,2},{1,3},{6,4},{7,5},{4,6},{5,7},{10,8},{11,9},{8,1... | collective-permute-start | bytes 380168 | tf_op jit(solution)/shard_map/while/body/eval_jaxpr/ppermute | solution.py:19
  432.0 12.3 %collective-permute-start.6 = (bf16[12,5280]{1,0:T(8,128)(2,1)S(1)}, bf16[12,5280]{1,0:T(8,128)(2,1)S(1)}, u32[]{:S(2)}, u32[]{:S(2)}) collective-permute-start(bf16[12,5280]{1,0:T(8,128)(2,1)S(1)} %get-tuple-element.380), channel_id=1, source_target_pairs={{1,0},{2,1},{3,2},{0,3},{5,4},{6,5},{7,6},{4,7},{9,8},{10,9},{11,1... | collective-permute-start | bytes 380168 | tf_op jit(solution)/shard_map/while/body/eval_jaxpr/ppermute | solution.py:19
  456.1 18.3 %collective-permute-start.1 = (bf16[12,5280]{1,0:T(8,128)(2,1)S(1)}, bf16[12,5280]{1,0:T(8,128)(2,1)S(1)}, u32[]{:S(2)}, u32[]{:S(2)}) collective-permute-start(bf16[12,5280]{1,0:T(8,128)(2,1)S(1)} %get-tuple-element.374), channel_id=1, source_target_pairs={{1,0},{2,1},{3,2},{0,3},{5,4},{6,5},{7,6},{4,7},{9,8},{10,9},{11,1... | collective-permute-start | bytes 380168 | tf_op jit(solution)/shard_map/while/body/eval_jaxpr/ppermute | solution.py:19
  460.5 13.8 %collective-permute-start.2 = (bf16[12,5280]{1,0:T(8,128)(2,1)S(1)}, bf16[12,5280]{1,0:T(8,128)(2,1)S(1)}, u32[]{:S(2)}, u32[]{:S(2)}) collective-permute-start(bf16[12,5280]{1,0:T(8,128)(2,1)S(1)} %get-tuple-element.375), channel_id=1, source_target_pairs={{2,0},{3,1},{0,2},{1,3},{6,4},{7,5},{4,6},{5,7},{10,8},{11,9},{8,1... | collective-permute-start | bytes 380168 | tf_op jit(solution)/shard_map/while/body/eval_jaxpr/ppermute | solution.py:19
  462.1 12.3 %collective-permute-start.3 = (bf16[12,5280]{1,0:T(8,128)(2,1)S(1)}, bf16[12,5280]{1,0:T(8,128)(2,1)S(1)}, u32[]{:S(2)}, u32[]{:S(2)}) collective-permute-start(bf16[12,5280]{1,0:T(8,128)(2,1)S(1)} %get-tuple-element.376), channel_id=1, source_target_pairs={{3,0},{0,1},{1,2},{2,3},{7,4},{4,5},{5,6},{6,7},{11,8},{8,9},{9,10... | collective-permute-start | bytes 380168 | tf_op jit(solution)/shard_map/while/body/eval_jaxpr/ppermute | solution.py:19
  489.7 15.0 %collective-permute-start.5 = (bf16[12,5280]{1,0:T(8,128)(2,1)S(1)}, bf16[12,5280]{1,0:T(8,128)(2,1)S(1)}, u32[]{:S(2)}, u32[]{:S(2)}) collective-permute-start(bf16[12,5280]{1,0:T(8,128)(2,1)S(1)} %get-tuple-element.379), channel_id=1, source_target_pairs={{2,0},{3,1},{0,2},{1,3},{6,4},{7,5},{4,6},{5,7},{10,8},{11,9},{8,1... | collective-permute-start | bytes 380168 | tf_op jit(solution)/shard_map/while/body/eval_jaxpr/ppermute | solution.py:19
  494.1 12.5 %collective-permute-start.6 = (bf16[12,5280]{1,0:T(8,128)(2,1)S(1)}, bf16[12,5280]{1,0:T(8,128)(2,1)S(1)}, u32[]{:S(2)}, u32[]{:S(2)}) collective-permute-start(bf16[12,5280]{1,0:T(8,128)(2,1)S(1)} %get-tuple-element.380), channel_id=1, source_target_pairs={{1,0},{2,1},{3,2},{0,3},{5,4},{6,5},{7,6},{4,7},{9,8},{10,9},{11,1... | collective-permute-start | bytes 380168 | tf_op jit(solution)/shard_map/while/body/eval_jaxpr/ppermute | solution.py:19
  518.4 15.7 %collective-permute-start.1 = (bf16[12,5280]{1,0:T(8,128)(2,1)S(1)}, bf16[12,5280]{1,0:T(8,128)(2,1)S(1)}, u32[]{:S(2)}, u32[]{:S(2)}) collective-permute-start(bf16[12,5280]{1,0:T(8,128)(2,1)S(1)} %get-tuple-element.374), channel_id=1, source_target_pairs={{1,0},{2,1},{3,2},{0,3},{5,4},{6,5},{7,6},{4,7},{9,8},{10,9},{11,1... | collective-permute-start | bytes 380168 | tf_op jit(solution)/shard_map/while/body/eval_jaxpr/ppermute | solution.py:19
  519.1 15.0 %collective-permute-start.2 = (bf16[12,5280]{1,0:T(8,128)(2,1)S(1)}, bf16[12,5280]{1,0:T(8,128)(2,1)S(1)}, u32[]{:S(2)}, u32[]{:S(2)}) collective-permute-start(bf16[12,5280]{1,0:T(8,128)(2,1)S(1)} %get-tuple-element.375), channel_id=1, source_target_pairs={{2,0},{3,1},{0,2},{1,3},{6,4},{7,5},{4,6},{5,7},{10,8},{11,9},{8,1... | collective-permute-start | bytes 380168 | tf_op jit(solution)/shard_map/while/body/eval_jaxpr/ppermute | solution.py:19
  521.6 13.6 %collective-permute-start.3 = (bf16[12,5280]{1,0:T(8,128)(2,1)S(1)}, bf16[12,5280]{1,0:T(8,128)(2,1)S(1)}, u32[]{:S(2)}, u32[]{:S(2)}) collective-permute-start(bf16[12,5280]{1,0:T(8,128)(2,1)S(1)} %get-tuple-element.376), channel_id=1, source_target_pairs={{3,0},{0,1},{1,2},{2,3},{7,4},{4,5},{5,6},{6,7},{11,8},{8,9},{9,10... | collective-permute-start | bytes 380168 | tf_op jit(solution)/shard_map/while/body/eval_jaxpr/ppermute | solution.py:19
  549.0 14.8 %collective-permute-start.5 = (bf16[12,5280]{1,0:T(8,128)(2,1)S(1)}, bf16[12,5280]{1,0:T(8,128)(2,1)S(1)}, u32[]{:S(2)}, u32[]{:S(2)}) collective-permute-start(bf16[12,5280]{1,0:T(8,128)(2,1)S(1)} %get-tuple-element.379), channel_id=1, source_target_pairs={{2,0},{3,1},{0,2},{1,3},{6,4},{7,5},{4,6},{5,7},{10,8},{11,9},{8,1... | collective-permute-start | bytes 380168 | tf_op jit(solution)/shard_map/while/body/eval_jaxpr/ppermute | solution.py:19
  575.7 13.2 %collective-permute-start.1 = (bf16[12,5280]{1,0:T(8,128)(2,1)S(1)}, bf16[12,5280]{1,0:T(8,128)(2,1)S(1)}, u32[]{:S(2)}, u32[]{:S(2)}) collective-permute-start(bf16[12,5280]{1,0:T(8,128)(2,1)S(1)} %get-tuple-element.374), channel_id=1, source_target_pairs={{1,0},{2,1},{3,2},{0,3},{5,4},{6,5},{7,6},{4,7},{9,8},{10,9},{11,1... | collective-permute-start | bytes 380168 | tf_op jit(solution)/shard_map/while/body/eval_jaxpr/ppermute | solution.py:19
  577.6 14.9 %collective-permute-start.2 = (bf16[12,5280]{1,0:T(8,128)(2,1)S(1)}, bf16[12,5280]{1,0:T(8,128)(2,1)S(1)}, u32[]{:S(2)}, u32[]{:S(2)}) collective-permute-start(bf16[12,5280]{1,0:T(8,128)(2,1)S(1)} %get-tuple-element.375), channel_id=1, source_target_pairs={{2,0},{3,1},{0,2},{1,3},{6,4},{7,5},{4,6},{5,7},{10,8},{11,9},{8,1... | collective-permute-start | bytes 380168 | tf_op jit(solution)/shard_map/while/body/eval_jaxpr/ppermute | solution.py:19
  580.6 12.8 %collective-permute-start.3 = (bf16[12,5280]{1,0:T(8,128)(2,1)S(1)}, bf16[12,5280]{1,0:T(8,128)(2,1)S(1)}, u32[]{:S(2)}, u32[]{:S(2)}) collective-permute-start(bf16[12,5280]{1,0:T(8,128)(2,1)S(1)} %get-tuple-element.376), channel_id=1, source_target_pairs={{3,0},{0,1},{1,2},{2,3},{7,4},{4,5},{5,6},{6,7},{11,8},{8,9},{9,10... | collective-permute-start | bytes 380168 | tf_op jit(solution)/shard_map/while/body/eval_jaxpr/ppermute | solution.py:19
  606.0 12.9 %collective-permute-start.4 = (bf16[12,5280]{1,0:T(8,128)(2,1)S(1)}, bf16[12,5280]{1,0:T(8,128)(2,1)S(1)}, u32[]{:S(2)}, u32[]{:S(2)}) collective-permute-start(bf16[12,5280]{1,0:T(8,128)(2,1)S(1)} %get-tuple-element.378), channel_id=1, source_target_pairs={{3,0},{0,1},{1,2},{2,3},{7,4},{4,5},{5,6},{6,7},{11,8},{8,9},{9,10... | collective-permute-start | bytes 380168 | tf_op jit(solution)/shard_map/while/body/eval_jaxpr/ppermute | solution.py:19
  608.3 15.2 %collective-permute-start.5 = (bf16[12,5280]{1,0:T(8,128)(2,1)S(1)}, bf16[12,5280]{1,0:T(8,128)(2,1)S(1)}, u32[]{:S(2)}, u32[]{:S(2)}) collective-permute-start(bf16[12,5280]{1,0:T(8,128)(2,1)S(1)} %get-tuple-element.379), channel_id=1, source_target_pairs={{2,0},{3,1},{0,2},{1,3},{6,4},{7,5},{4,6},{5,7},{10,8},{11,9},{8,1... | collective-permute-start | bytes 380168 | tf_op jit(solution)/shard_map/while/body/eval_jaxpr/ppermute | solution.py:19
  637.9 13.3 %collective-permute-start.2 = (bf16[12,5280]{1,0:T(8,128)(2,1)S(1)}, bf16[12,5280]{1,0:T(8,128)(2,1)S(1)}, u32[]{:S(2)}, u32[]{:S(2)}) collective-permute-start(bf16[12,5280]{1,0:T(8,128)(2,1)S(1)} %get-tuple-element.375), channel_id=1, source_target_pairs={{2,0},{3,1},{0,2},{1,3},{6,4},{7,5},{4,6},{5,7},{10,8},{11,9},{8,1... | collective-permute-start | bytes 380168 | tf_op jit(solution)/shard_map/while/body/eval_jaxpr/ppermute | solution.py:19
  667.1 13.9 %collective-permute-start.5 = (bf16[12,5280]{1,0:T(8,128)(2,1)S(1)}, bf16[12,5280]{1,0:T(8,128)(2,1)S(1)}, u32[]{:S(2)}, u32[]{:S(2)}) collective-permute-start(bf16[12,5280]{1,0:T(8,128)(2,1)S(1)} %get-tuple-element.379), channel_id=1, source_target_pairs={{2,0},{3,1},{0,2},{1,3},{6,4},{7,5},{4,6},{5,7},{10,8},{11,9},{8,1... | collective-permute-start | bytes 380168 | tf_op jit(solution)/shard_map/while/body/eval_jaxpr/ppermute | solution.py:19
  669.4 11.6 %collective-permute-start.6 = (bf16[12,5280]{1,0:T(8,128)(2,1)S(1)}, bf16[12,5280]{1,0:T(8,128)(2,1)S(1)}, u32[]{:S(2)}, u32[]{:S(2)}) collective-permute-start(bf16[12,5280]{1,0:T(8,128)(2,1)S(1)} %get-tuple-element.380), channel_id=1, source_target_pairs={{1,0},{2,1},{3,2},{0,3},{5,4},{6,5},{7,6},{4,7},{9,8},{10,9},{11,1... | collective-permute-start | bytes 380168 | tf_op jit(solution)/shard_map/while/body/eval_jaxpr/ppermute | solution.py:19
  692.9 15.9 %collective-permute-start.1 = (bf16[12,5280]{1,0:T(8,128)(2,1)S(1)}, bf16[12,5280]{1,0:T(8,128)(2,1)S(1)}, u32[]{:S(2)}, u32[]{:S(2)}) collective-permute-start(bf16[12,5280]{1,0:T(8,128)(2,1)S(1)} %get-tuple-element.374), channel_id=1, source_target_pairs={{1,0},{2,1},{3,2},{0,3},{5,4},{6,5},{7,6},{4,7},{9,8},{10,9},{11,1... | collective-permute-start | bytes 380168 | tf_op jit(solution)/shard_map/while/body/eval_jaxpr/ppermute | solution.py:19
  695.6 16.8 %collective-permute-start.2 = (bf16[12,5280]{1,0:T(8,128)(2,1)S(1)}, bf16[12,5280]{1,0:T(8,128)(2,1)S(1)}, u32[]{:S(2)}, u32[]{:S(2)}) collective-permute-start(bf16[12,5280]{1,0:T(8,128)(2,1)S(1)} %get-tuple-element.375), channel_id=1, source_target_pairs={{2,0},{3,1},{0,2},{1,3},{6,4},{7,5},{4,6},{5,7},{10,8},{11,9},{8,1... | collective-permute-start | bytes 380168 | tf_op jit(solution)/shard_map/while/body/eval_jaxpr/ppermute | solution.py:19
  730.8 12.5 %collective-permute-start.4 = (bf16[12,5280]{1,0:T(8,128)(2,1)S(1)}, bf16[12,5280]{1,0:T(8,128)(2,1)S(1)}, u32[]{:S(2)}, u32[]{:S(2)}) collective-permute-start(bf16[12,5280]{1,0:T(8,128)(2,1)S(1)} %get-tuple-element.378), channel_id=1, source_target_pairs={{3,0},{0,1},{1,2},{2,3},{7,4},{4,5},{5,6},{6,7},{11,8},{8,9},{9,10... | collective-permute-start | bytes 380168 | tf_op jit(solution)/shard_map/while/body/eval_jaxpr/ppermute | solution.py:19
  734.7 13.8 %collective-permute-start.5 = (bf16[12,5280]{1,0:T(8,128)(2,1)S(1)}, bf16[12,5280]{1,0:T(8,128)(2,1)S(1)}, u32[]{:S(2)}, u32[]{:S(2)}) collective-permute-start(bf16[12,5280]{1,0:T(8,128)(2,1)S(1)} %get-tuple-element.379), channel_id=1, source_target_pairs={{2,0},{3,1},{0,2},{1,3},{6,4},{7,5},{4,6},{5,7},{10,8},{11,9},{8,1... | collective-permute-start | bytes 380168 | tf_op jit(solution)/shard_map/while/body/eval_jaxpr/ppermute | solution.py:19
  734.7 16.7 %collective-permute-start.6 = (bf16[12,5280]{1,0:T(8,128)(2,1)S(1)}, bf16[12,5280]{1,0:T(8,128)(2,1)S(1)}, u32[]{:S(2)}, u32[]{:S(2)}) collective-permute-start(bf16[12,5280]{1,0:T(8,128)(2,1)S(1)} %get-tuple-element.380), channel_id=1, source_target_pairs={{1,0},{2,1},{3,2},{0,3},{5,4},{6,5},{7,6},{4,7},{9,8},{10,9},{11,1... | collective-permute-start | bytes 380168 | tf_op jit(solution)/shard_map/while/body/eval_jaxpr/ppermute | solution.py:19
  763.3 17.9 %collective-permute-start.1 = (bf16[12,5280]{1,0:T(8,128)(2,1)S(1)}, bf16[12,5280]{1,0:T(8,128)(2,1)S(1)}, u32[]{:S(2)}, u32[]{:S(2)}) collective-permute-start(bf16[12,5280]{1,0:T(8,128)(2,1)S(1)} %get-tuple-element.374), channel_id=1, source_target_pairs={{1,0},{2,1},{3,2},{0,3},{5,4},{6,5},{7,6},{4,7},{9,8},{10,9},{11,1... | collective-permute-start | bytes 380168 | tf_op jit(solution)/shard_map/while/body/eval_jaxpr/ppermute | solution.py:19
  764.9 16.3 %collective-permute-start.2 = (bf16[12,5280]{1,0:T(8,128)(2,1)S(1)}, bf16[12,5280]{1,0:T(8,128)(2,1)S(1)}, u32[]{:S(2)}, u32[]{:S(2)}) collective-permute-start(bf16[12,5280]{1,0:T(8,128)(2,1)S(1)} %get-tuple-element.375), channel_id=1, source_target_pairs={{2,0},{3,1},{0,2},{1,3},{6,4},{7,5},{4,6},{5,7},{10,8},{11,9},{8,1... | collective-permute-start | bytes 380168 | tf_op jit(solution)/shard_map/while/body/eval_jaxpr/ppermute | solution.py:19
  767.9 13.3 %collective-permute-start.3 = (bf16[12,5280]{1,0:T(8,128)(2,1)S(1)}, bf16[12,5280]{1,0:T(8,128)(2,1)S(1)}, u32[]{:S(2)}, u32[]{:S(2)}) collective-permute-start(bf16[12,5280]{1,0:T(8,128)(2,1)S(1)} %get-tuple-element.376), channel_id=1, source_target_pairs={{3,0},{0,1},{1,2},{2,3},{7,4},{4,5},{5,6},{6,7},{11,8},{8,9},{9,10... | collective-permute-start | bytes 380168 | tf_op jit(solution)/shard_map/while/body/eval_jaxpr/ppermute | solution.py:19
  794.8 18.1 %collective-permute-start.5 = (bf16[12,5280]{1,0:T(8,128)(2,1)S(1)}, bf16[12,5280]{1,0:T(8,128)(2,1)S(1)}, u32[]{:S(2)}, u32[]{:S(2)}) collective-permute-start(bf16[12,5280]{1,0:T(8,128)(2,1)S(1)} %get-tuple-element.379), channel_id=1, source_target_pairs={{2,0},{3,1},{0,2},{1,3},{6,4},{7,5},{4,6},{5,7},{10,8},{11,9},{8,1... | collective-permute-start | bytes 380168 | tf_op jit(solution)/shard_map/while/body/eval_jaxpr/ppermute | solution.py:19
  798.3 14.6 %collective-permute-start.6 = (bf16[12,5280]{1,0:T(8,128)(2,1)S(1)}, bf16[12,5280]{1,0:T(8,128)(2,1)S(1)}, u32[]{:S(2)}, u32[]{:S(2)}) collective-permute-start(bf16[12,5280]{1,0:T(8,128)(2,1)S(1)} %get-tuple-element.380), channel_id=1, source_target_pairs={{1,0},{2,1},{3,2},{0,3},{5,4},{6,5},{7,6},{4,7},{9,8},{10,9},{11,1... | collective-permute-start | bytes 380168 | tf_op jit(solution)/shard_map/while/body/eval_jaxpr/ppermute | solution.py:19
  826.6 12.3 %collective-permute-start.2 = (bf16[12,5280]{1,0:T(8,128)(2,1)S(1)}, bf16[12,5280]{1,0:T(8,128)(2,1)S(1)}, u32[]{:S(2)}, u32[]{:S(2)}) collective-permute-start(bf16[12,5280]{1,0:T(8,128)(2,1)S(1)} %get-tuple-element.375), channel_id=1, source_target_pairs={{2,0},{3,1},{0,2},{1,3},{6,4},{7,5},{4,6},{5,7},{10,8},{11,9},{8,1... | collective-permute-start | bytes 380168 | tf_op jit(solution)/shard_map/while/body/eval_jaxpr/ppermute | solution.py:19
  (35 other events, 316.9 us)
Sparse Core Ops, SparseCore 0:
  9.6 96.5 all-gather.2
  108.0 99.7 all-gather.4

commit v8 on v4

--- a/solution.py
+++ b/solution.py
@@ -11,6 +11,22 @@
     devices = range(lax.axis_size(axis))
     route = [((i - distance) % len(devices), i) for i in devices]
     return lax.ppermute(block, axis, route)
+
+
+def doubling_gather(piece, axis):
+    count = lax.axis_size(axis)
+    me = lax.axis_index(axis)
+    held = piece
+    bit = count // 2
+    while bit >= 1:
+        theirs = lax.ppermute(held, axis, [(i, i ^ bit) for i in range(count)])
+        upper = (me & bit) != 0
+        held = jnp.stack([jnp.where(upper, theirs, held), jnp.where(upper, held, theirs)])
+        bit //= 2
+    rank = held.ndim - piece.ndim
+    order = tuple(reversed(range(rank))) + tuple(range(rank, held.ndim))
+    held = jnp.transpose(held, order)
+    return held.reshape((count * piece.shape[0],) + piece.shape[1:])
 
 
 def normalize(current, gain_row):
@@ -74,12 +90,9 @@
 def body(init_state, inject, routes, norm_gain, router, w_up, w_down):
     sections = lax.axis_size("section")
     section_index = lax.axis_index("section")
-    up_all, down_all = (
-        lax.all_gather(w_up, "dp", axis=2, tiled=True),
-        lax.all_gather(jnp.swapaxes(w_down, 2, 3), "dp", axis=2, tiled=True),
-    )
+    up_all = lax.all_gather(w_up, "dp", axis=2, tiled=True)
     w_first = up_all[0, 0]
-    w_second = down_all[0, 0]
+    w_second = doubling_gather(jnp.swapaxes(w_down[0, 0], 0, 1), "dp")
     gain_row = norm_gain[0]
     router_rows = router[0]
     tokens = init_state.shape[1]

time: 860 us -> 891 us (1.036)
  the two profiles are of different devices: /device:TPU:2 before, /device:TPU:8 now
where the time goes in v8:
time: 891 us; the launch traced here: 890 us
  waiting for transfers between devices  473 us (53%)
  starting transfers between devices  186 us (21%)
  matrix products  130 us (15%)
  local copies, waits for them, and re-layouts  49.7 us (6%)
  other arithmetic  37.5 us (4%)
  between operations  13.6 us (2%)
    ppermute x76, waiting for transfers between devices, shifted(): return lax.ppermute(block, axis, route)  332 us
    ppermute x76, starting transfers between devices, shifted(): return lax.ppermute(block, axis, route)  179 us
    ppermute x4, waiting for transfers between devices, doubling_gather(): theirs = lax.ppermute(held, axis, [(i, i ^ bit) for i in range(count)])  141 us
    dot_general x11, matrix products, expert_rows(): lax.dot_general(hidden, w_second, (((1,), (1,)), ((), ())), preferred_ele...  108 us
  transfers between devices with their start and end apart: 81, of which 68 were waited for; matrix products, arithmetic and copies ran while one was open for 6% of the time, Pallas kernels for 0%

profile of v8, /device:TPU:8, one launch (start us, length us, event | category | flops | bytes accessed | tf_op | source)
XLA Modules:
  0.0 889.8 jit_solution(9642467629341904121)
XLA Ops:
  12.5 12.2 %collective-permute-done.10 = bf16[330,768]{1,0:T(8,128)(2,1)S(1)} collective-permute-done((bf16[330,768]{1,0:T(8,128)(2,1)}, bf16[330,768]{1,0:T(8,128)(2,1)S(1)}, u32[]{:S(2)}, u32[]{:S(2)}) %collective-permute-start.10) | collective-permute-done | bytes 506912 | tf_op jit(solution)/shard_map/ppermute | solution.py:22
  28.3 44.8 %collective-permute-done.11 = bf16[2,330,768]{2,0,1:T(2,128)(2,1)S(1)} collective-permute-done((bf16[2,330,768]{2,0,1:T(2,128)(2,1)S(1)}, bf16[2,330,768]{2,0,1:T(2,128)(2,1)S(1)}, u32[]{:S(2)}, u32[]{:S(2)}) %collective-permute-start.11) | collective-permute-done | bytes 1013792 | tf_op jit(solution)/shard_map/ppermute | solution.py:22
  78.0 83.5 %collective-permute-done.12 = bf16[2,2,330,768]{3,1,2,0:T(2,128)(2,1)} collective-permute-done((bf16[2,2,330,768]{3,1,2,0:T(2,128)(2,1)S(1)}, bf16[2,2,330,768]{3,1,2,0:T(2,128)(2,1)}, u32[]{:S(2)}, u32[]{:S(2)}) %collective-permute-start.12) | collective-permute-done | bytes 2027552 | tf_op jit(solution)/shard_map/ppermute | solution.py:22
  204.1 7.4 maximum_bitcast_fusion
  211.5 7.2 copy.23
  218.7 7.7 reshape.187
  226.4 11.6 %copy.32 = bf16[1,1,5280,768]{3,2,0,1:T(8,128)(2,1)} copy(bf16[1,1,5280,768]{3,1,0,2:T(2,128)(2,1)} %all-gather.2.cloned.1.call-done) | data formatting | bytes 16220160
  238.1 9.9 %convolution_convert_fusion.2 = bf16[48,5280]{1,0:T(8,128)(2,1)S(1)} fusion(bf16[5280,768]{1,0:T(8,128)(2,1)} %reshape.187, bf16[48,5280]{1,0:T(8,128)(2,1)S(1)} %copy-done.5, bf16[5280,768]{1,0:T(8,128)(2,1)} %bitcast.124), kind=kOutput, calls=%fused_computation.58 | convolution fusion | flops 779152896 | bytes 17233920 | tf_op jit(solution)/shard_map/dot_general | solution.py:44
  263.6 7.7 collective-permute-done.14
  272.7 610.3 %while.15 = (s32[]{:T(128)}, bf16[32,5280]{1,0:T(8,128)(2,1)}, s32[]{:T(128)}, pred[]{:T(512)}, bf16[4,32,5280]{2,1,0:T(8,128)(2,1)}, /*index=5*/bf16[4,32,5280]...) while((s32[]{:T(128)}, bf16[32,5280]{1,0:T(8,128)(2,1)}, ...), condition=%wide.region_7.8_spmd, body=%wide.region_3.7_spmd.sunk | while | flops 818449920 | bytes 31894524 | solution.py:129
  290.2 10.5 %collective-permute-done.1 = bf16[12,5280]{1,0:T(8,128)(2,1)S(1)} collective-permute-done((bf16[12,5280]{1,0:T(8,128)(2,1)S(1)}, bf16[12,5280]{1,0:T(8,128)(2,1)S(1)}, u32[]{:S(2)}, u32[]{:S(2)}) %collective-permute-start.1) | collective-permute-done | bytes 126752 | tf_op jit(solution)/shard_map/while/body/eval_jaxpr/ppermute | solution.py:13
  301.1 9.9 %convolution_convert_fusion.7 = bf16[48,5280]{1,0:T(8,128)(2,1)S(1)} fusion(bf16[5280,768]{1,0:T(8,128)(2,1)} %get-tuple-element.446, bf16[48,5280]{1,0:T(8,128)(2,1)S(1)} %reshape.198, bf16[5280,768]{1,0:T(8,128)(2,1)} %get-tuple-element.445), kind=kOutput, calls=%fused_computation.clone.1 | convolution fusion | flops 779152896 | bytes 17233920 | tf_op jit(solution)/shard_map/while/body/eval_jaxpr/dot_general | solution.py:44
  311.2 7.6 collective-permute-start.5
  327.1 6.7 collective-permute-done.6
  351.3 10.2 %collective-permute-done.1 = bf16[12,5280]{1,0:T(8,128)(2,1)S(1)} collective-permute-done((bf16[12,5280]{1,0:T(8,128)(2,1)S(1)}, bf16[12,5280]{1,0:T(8,128)(2,1)S(1)}, u32[]{:S(2)}, u32[]{:S(2)}) %collective-permute-start.1) | collective-permute-done | bytes 126752 | tf_op jit(solution)/shard_map/while/body/eval_jaxpr/ppermute | solution.py:13
  364.6 9.9 %convolution_convert_fusion.7 = bf16[48,5280]{1,0:T(8,128)(2,1)S(1)} fusion(bf16[5280,768]{1,0:T(8,128)(2,1)} %get-tuple-element.446, bf16[48,5280]{1,0:T(8,128)(2,1)S(1)} %reshape.198, bf16[5280,768]{1,0:T(8,128)(2,1)} %get-tuple-element.445), kind=kOutput, calls=%fused_computation.clone.1 | convolution fusion | flops 779152896 | bytes 17233920 | tf_op jit(solution)/shard_map/while/body/eval_jaxpr/dot_general | solution.py:44
  375.2 6.3 collective-permute-start.5
  383.7 6.6 collective-permute-done.5
  392.3 7.2 collective-permute-start
  399.8 7.2 collective-permute-done
  414.4 9.4 %collective-permute-done.1 = bf16[12,5280]{1,0:T(8,128)(2,1)S(1)} collective-permute-done((bf16[12,5280]{1,0:T(8,128)(2,1)S(1)}, bf16[12,5280]{1,0:T(8,128)(2,1)S(1)}, u32[]{:S(2)}, u32[]{:S(2)}) %collective-permute-start.1) | collective-permute-done | bytes 126752 | tf_op jit(solution)/shard_map/while/body/eval_jaxpr/ppermute | solution.py:13
  424.4 9.9 %convolution_convert_fusion.7 = bf16[48,5280]{1,0:T(8,128)(2,1)S(1)} fusion(bf16[5280,768]{1,0:T(8,128)(2,1)} %get-tuple-element.446, bf16[48,5280]{1,0:T(8,128)(2,1)S(1)} %reshape.198, bf16[5280,768]{1,0:T(8,128)(2,1)} %get-tuple-element.445), kind=kOutput, calls=%fused_computation.clone.1 | convolution fusion | flops 779152896 | bytes 17233920 | tf_op jit(solution)/shard_map/while/body/eval_jaxpr/dot_general | solution.py:44
  449.4 7.8 collective-permute-done.6
  458.8 7.2 collective-permute-done
  475.2 7.3 collective-permute-done.1
  488.2 9.9 %convolution_convert_fusion.7 = bf16[48,5280]{1,0:T(8,128)(2,1)S(1)} fusion(bf16[5280,768]{1,0:T(8,128)(2,1)} %get-tuple-element.446, bf16[48,5280]{1,0:T(8,128)(2,1)S(1)} %reshape.198, bf16[5280,768]{1,0:T(8,128)(2,1)} %get-tuple-element.445), kind=kOutput, calls=%fused_computation.clone.1 | convolution fusion | flops 779152896 | bytes 17233920 | tf_op jit(solution)/shard_map/while/body/eval_jaxpr/dot_general | solution.py:44
  505.2 9.1 %collective-permute-done.4 = bf16[12,5280]{1,0:T(8,128)(2,1)S(1)} collective-permute-done((bf16[12,5280]{1,0:T(8,128)(2,1)S(1)}, bf16[12,5280]{1,0:T(8,128)(2,1)S(1)}, u32[]{:S(2)}, u32[]{:S(2)}) %collective-permute-start.4) | collective-permute-done | bytes 126752 | tf_op jit(solution)/shard_map/while/body/eval_jaxpr/ppermute | solution.py:13
  519.4 9.4 %collective-permute-done = bf16[32,5280]{1,0:T(8,128)(2,1)S(1)} collective-permute-done((bf16[32,5280]{1,0:T(8,128)(2,1)}, bf16[32,5280]{1,0:T(8,128)(2,1)S(1)}, u32[]{:S(2)}, u32[]{:S(2)}) %collective-permute-start) | collective-permute-done | bytes 337952 | tf_op jit(solution)/shard_map/while/body/eval_jaxpr/ppermute | solution.py:13
  537.1 8.4 collective-permute-done.1
  548.9 9.9 %convolution_convert_fusion.7 = bf16[48,5280]{1,0:T(8,128)(2,1)S(1)} fusion(bf16[5280,768]{1,0:T(8,128)(2,1)} %get-tuple-element.446, bf16[48,5280]{1,0:T(8,128)(2,1)S(1)} %reshape.198, bf16[5280,768]{1,0:T(8,128)(2,1)} %get-tuple-element.445), kind=kOutput, calls=%fused_computation.clone.1 | convolution fusion | flops 779152896 | bytes 17233920 | tf_op jit(solution)/shard_map/while/body/eval_jaxpr/dot_general | solution.py:44
  580.9 7.9 collective-permute-done
  607.4 9.9 %convolution_convert_fusion.7 = bf16[48,5280]{1,0:T(8,128)(2,1)S(1)} fusion(bf16[5280,768]{1,0:T(8,128)(2,1)} %get-tuple-element.446, bf16[48,5280]{1,0:T(8,128)(2,1)S(1)} %reshape.198, bf16[5280,768]{1,0:T(8,128)(2,1)} %get-tuple-element.445), kind=kOutput, calls=%fused_computation.clone.1 | convolution fusion | flops 779152896 | bytes 17233920 | tf_op jit(solution)/shard_map/while/body/eval_jaxpr/dot_general | solution.py:44
  626.8 6.4 collective-permute-done.5
  633.2 6.3 collective-permute-done.6
  641.2 7.2 collective-permute-done
  657.9 9.5 %collective-permute-done.1 = bf16[12,5280]{1,0:T(8,128)(2,1)S(1)} collective-permute-done((bf16[12,5280]{1,0:T(8,128)(2,1)S(1)}, bf16[12,5280]{1,0:T(8,128)(2,1)S(1)}, u32[]{:S(2)}, u32[]{:S(2)}) %collective-permute-start.1) | collective-permute-done | bytes 126752 | tf_op jit(solution)/shard_map/while/body/eval_jaxpr/ppermute | solution.py:13
  667.8 9.9 %convolution_convert_fusion.7 = bf16[48,5280]{1,0:T(8,128)(2,1)S(1)} fusion(bf16[5280,768]{1,0:T(8,128)(2,1)} %get-tuple-element.446, bf16[48,5280]{1,0:T(8,128)(2,1)S(1)} %reshape.198, bf16[5280,768]{1,0:T(8,128)(2,1)} %get-tuple-element.445), kind=kOutput, calls=%fused_computation.clone.1 | convolution fusion | flops 779152896 | bytes 17233920 | tf_op jit(solution)/shard_map/while/body/eval_jaxpr/dot_general | solution.py:44
  677.9 7.0 collective-permute-start.5
  688.8 9.1 %collective-permute-done.5 = bf16[12,5280]{1,0:T(8,128)(2,1)S(1)} collective-permute-done((bf16[12,5280]{1,0:T(8,128)(2,1)S(1)}, bf16[12,5280]{1,0:T(8,128)(2,1)S(1)}, u32[]{:S(2)}, u32[]{:S(2)}) %collective-permute-start.5) | collective-permute-done | bytes 126752 | tf_op jit(solution)/shard_map/while/body/eval_jaxpr/ppermute | solution.py:13
  701.4 10.6 %collective-permute-done = bf16[32,5280]{1,0:T(8,128)(2,1)S(1)} collective-permute-done((bf16[32,5280]{1,0:T(8,128)(2,1)}, bf16[32,5280]{1,0:T(8,128)(2,1)S(1)}, u32[]{:S(2)}, u32[]{:S(2)}) %collective-permute-start) | collective-permute-done | bytes 337952 | tf_op jit(solution)/shard_map/while/body/eval_jaxpr/ppermute | solution.py:13
  732.5 9.9 %convolution_convert_fusion.7 = bf16[48,5280]{1,0:T(8,128)(2,1)S(1)} fusion(bf16[5280,768]{1,0:T(8,128)(2,1)} %get-tuple-element.446, bf16[48,5280]{1,0:T(8,128)(2,1)S(1)} %reshape.198, bf16[5280,768]{1,0:T(8,128)(2,1)} %get-tuple-element.445), kind=kOutput, calls=%fused_computation.clone.1 | convolution fusion | flops 779152896 | bytes 17233920 | tf_op jit(solution)/shard_map/while/body/eval_jaxpr/dot_general | solution.py:44
  764.4 7.6 collective-permute-done
  782.3 9.3 %collective-permute-done.2 = bf16[12,5280]{1,0:T(8,128)(2,1)S(1)} collective-permute-done((bf16[12,5280]{1,0:T(8,128)(2,1)S(1)}, bf16[12,5280]{1,0:T(8,128)(2,1)S(1)}, u32[]{:S(2)}, u32[]{:S(2)}) %collective-permute-start.2) | collective-permute-done | bytes 126752 | tf_op jit(solution)/shard_map/while/body/eval_jaxpr/ppermute | solution.py:13
  792.2 9.9 %convolution_convert_fusion.7 = bf16[48,5280]{1,0:T(8,128)(2,1)S(1)} fusion(bf16[5280,768]{1,0:T(8,128)(2,1)} %get-tuple-element.446, bf16[48,5280]{1,0:T(8,128)(2,1)S(1)} %reshape.198, bf16[5280,768]{1,0:T(8,128)(2,1)} %get-tuple-element.445), kind=kOutput, calls=%fused_computation.clone.1 | convolution fusion | flops 779152896 | bytes 17233920 | tf_op jit(solution)/shard_map/while/body/eval_jaxpr/dot_general | solution.py:44
  815.8 7.7 collective-permute-done.6
  842.4 10.4 %collective-permute-done.1 = bf16[12,5280]{1,0:T(8,128)(2,1)S(1)} collective-permute-done((bf16[12,5280]{1,0:T(8,128)(2,1)S(1)}, bf16[12,5280]{1,0:T(8,128)(2,1)S(1)}, u32[]{:S(2)}, u32[]{:S(2)}) %collective-permute-start.1) | collective-permute-done | bytes 126752 | tf_op jit(solution)/shard_map/while/body/eval_jaxpr/ppermute | solution.py:13
  853.2 9.9 %convolution_convert_fusion.7 = bf16[48,5280]{1,0:T(8,128)(2,1)S(1)} fusion(bf16[5280,768]{1,0:T(8,128)(2,1)} %get-tuple-element.446, bf16[48,5280]{1,0:T(8,128)(2,1)S(1)} %reshape.198, bf16[5280,768]{1,0:T(8,128)(2,1)} %get-tuple-element.445), kind=kOutput, calls=%fused_computation.clone.1 | convolution fusion | flops 779152896 | bytes 17233920 | tf_op jit(solution)/shard_map/while/body/eval_jaxpr/dot_general | solution.py:44
  863.3 6.9 collective-permute-start.5
  (336 shorter events, 357.7 us)
Async XLA Ops:
  6.5 219.9 %all-gather.2.cloned.1.call-start = ((), (), s32[]{:S(2)}) async-start(), calls=%async_computation | async-start | bytes 17233920 | tf_op jit(solution)/shard_map/all_gather | solution.py:93
  9.3 15.3 %collective-permute-start.10 = (bf16[330,768]{1,0:T(8,128)(2,1)}, bf16[330,768]{1,0:T(8,128)(2,1)S(1)}, u32[]{:S(2)}, u32[]{:S(2)}) collective-permute-start(bf16[330,768]{1,0:T(8,128)(2,1)} %bitcast.132), channel_id=1, source_target_pairs={{0,32},{4,36},{8,40},{12,44},{16,48},{20,52},{24,56},{28,60},{32,0... | collective-permute-start | bytes 1520648 | tf_op jit(solution)/shard_map/ppermute | solution.py:22
  26.7 46.4 %collective-permute-start.11 = (bf16[2,330,768]{2,0,1:T(2,128)(2,1)S(1)}, bf16[2,330,768]{2,0,1:T(2,128)(2,1)S(1)}, u32[]{:S(2)}, u32[]{:S(2)}) collective-permute-start(bf16[2,330,768]{2,0,1:T(2,128)(2,1)S(1)} %copy.14), channel_id=1, source_target_pairs={{0,16},{4,20},{8,24},{12,28},{16,0},{20,4},{24,8},{28,12},{32,48},... | collective-permute-start | bytes 3041288 | tf_op jit(solution)/shard_map/ppermute | solution.py:22
  76.0 85.5 %collective-permute-start.12 = (bf16[2,2,330,768]{3,1,2,0:T(2,128)(2,1)S(1)}, bf16[2,2,330,768]{3,1,2,0:T(2,128)(2,1)}, u32[]{:S(2)}, u32[]{:S(2)}) collective-permute-start(bf16[2,2,330,768]{3,1,2,0:T(2,128)(2,1)S(1)} %copy.17), channel_id=1, source_target_pairs={{0,8},{4,12},{8,0},{12,4},{16,24},{20,28},{24,16},{28,20},{32,40},... | collective-permute-start | bytes 6082568 | tf_op jit(solution)/shard_map/ppermute | solution.py:22
  170.7 27.4 %collective-permute-start.13 = (bf16[2,2,2,330,768]{4,2,3,1,0:T(2,128)(2,1)}, bf16[2,2,2,330,768]{4,2,3,1,0:T(2,128)(2,1)}, u32[]{:S(2)}, u32[]{:S(2)}) collective-permute-start(bf16[2,2,2,330,768]{4,2,3,1,0:T(2,128)(2,1)} %copy.20), channel_id=1, source_target_pairs={{0,4},{4,0},{8,12},{12,8},{16,20},{20,16},{24,28},{28,24},{32,36},... | collective-permute-start | bytes 12165128 | tf_op jit(solution)/shard_map/ppermute | solution.py:22
  174.0 14.3 %collective-permute-start.9 = (bf16[12,5280]{1,0:T(8,128)(2,1)}, bf16[12,5280]{1,0:T(8,128)(2,1)}, u32[]{:S(2)}, u32[]{:S(2)}) collective-permute-start(bf16[12,5280]{1,0:T(8,128)(2,1)} %get-tuple-element.304), channel_id=1, source_target_pairs={{1,0},{2,1},{3,2},{0,3},{5,4},{6,5},{7,6},{4,7},{9,8},{10,9},{11,1... | collective-permute-start | bytes 380168 | tf_op jit(solution)/shard_map/ppermute | solution.py:13
  178.5 15.3 %collective-permute-start.8 = (bf16[12,5280]{1,0:T(8,128)(2,1)}, bf16[12,5280]{1,0:T(8,128)(2,1)}, u32[]{:S(2)}, u32[]{:S(2)}) collective-permute-start(bf16[12,5280]{1,0:T(8,128)(2,1)} %get-tuple-element.305), channel_id=1, source_target_pairs={{2,0},{3,1},{0,2},{1,3},{6,4},{7,5},{4,6},{5,7},{10,8},{11,9},{8,1... | collective-permute-start | bytes 380168 | tf_op jit(solution)/shard_map/ppermute | solution.py:13
  180.4 13.4 %collective-permute-start.7 = (bf16[12,5280]{1,0:T(8,128)(2,1)}, bf16[12,5280]{1,0:T(8,128)(2,1)}, u32[]{:S(2)}, u32[]{:S(2)}) collective-permute-start(bf16[12,5280]{1,0:T(8,128)(2,1)} %get-tuple-element.306), channel_id=1, source_target_pairs={{3,0},{0,1},{1,2},{2,3},{7,4},{4,5},{5,6},{6,7},{11,8},{8,9},{9,10... | collective-permute-start | bytes 380168 | tf_op jit(solution)/shard_map/ppermute | solution.py:13
  250.4 13.2 %collective-permute-start.15 = (bf16[12,5280]{1,0:T(8,128)(2,1)S(1)}, bf16[12,5280]{1,0:T(8,128)(2,1)S(1)}, u32[]{:S(2)}, u32[]{:S(2)}) collective-permute-start(bf16[12,5280]{1,0:T(8,128)(2,1)S(1)} %get-tuple-element.301), channel_id=1, source_target_pairs={{2,0},{3,1},{0,2},{1,3},{6,4},{7,5},{4,6},{5,7},{10,8},{11,9},{8,1... | collective-permute-start | bytes 380168 | tf_op jit(solution)/shard_map/ppermute | solution.py:13
  254.6 16.7 %collective-permute-start.14 = (bf16[12,5280]{1,0:T(8,128)(2,1)S(1)}, bf16[12,5280]{1,0:T(8,128)(2,1)S(1)}, u32[]{:S(2)}, u32[]{:S(2)}) collective-permute-start(bf16[12,5280]{1,0:T(8,128)(2,1)S(1)} %get-tuple-element.302), channel_id=1, source_target_pairs={{1,0},{2,1},{3,2},{0,3},{5,4},{6,5},{7,6},{4,7},{9,8},{10,9},{11,1... | collective-permute-start | bytes 380168 | tf_op jit(solution)/shard_map/ppermute | solution.py:13
  282.5 18.3 %collective-permute-start.1 = (bf16[12,5280]{1,0:T(8,128)(2,1)S(1)}, bf16[12,5280]{1,0:T(8,128)(2,1)S(1)}, u32[]{:S(2)}, u32[]{:S(2)}) collective-permute-start(bf16[12,5280]{1,0:T(8,128)(2,1)S(1)} %get-tuple-element.386), channel_id=1, source_target_pairs={{1,0},{2,1},{3,2},{0,3},{5,4},{6,5},{7,6},{4,7},{9,8},{10,9},{11,1... | collective-permute-start | bytes 380168 | tf_op jit(solution)/shard_map/while/body/eval_jaxpr/ppermute | solution.py:13
  287.0 13.7 %collective-permute-start.2 = (bf16[12,5280]{1,0:T(8,128)(2,1)S(1)}, bf16[12,5280]{1,0:T(8,128)(2,1)S(1)}, u32[]{:S(2)}, u32[]{:S(2)}) collective-permute-start(bf16[12,5280]{1,0:T(8,128)(2,1)S(1)} %get-tuple-element.387), channel_id=1, source_target_pairs={{2,0},{3,1},{0,2},{1,3},{6,4},{7,5},{4,6},{5,7},{10,8},{11,9},{8,1... | collective-permute-start | bytes 380168 | tf_op jit(solution)/shard_map/while/body/eval_jaxpr/ppermute | solution.py:13
  287.8 13.0 %collective-permute-start.3 = (bf16[12,5280]{1,0:T(8,128)(2,1)S(1)}, bf16[12,5280]{1,0:T(8,128)(2,1)S(1)}, u32[]{:S(2)}, u32[]{:S(2)}) collective-permute-start(bf16[12,5280]{1,0:T(8,128)(2,1)S(1)} %get-tuple-element.388), channel_id=1, source_target_pairs={{3,0},{0,1},{1,2},{2,3},{7,4},{4,5},{5,6},{6,7},{11,8},{8,9},{9,10... | collective-permute-start | bytes 380168 | tf_op jit(solution)/shard_map/while/body/eval_jaxpr/ppermute | solution.py:13
  311.2 15.9 %collective-permute-start.5 = (bf16[12,5280]{1,0:T(8,128)(2,1)S(1)}, bf16[12,5280]{1,0:T(8,128)(2,1)S(1)}, u32[]{:S(2)}, u32[]{:S(2)}) collective-permute-start(bf16[12,5280]{1,0:T(8,128)(2,1)S(1)} %get-tuple-element.391), channel_id=1, source_target_pairs={{2,0},{3,1},{0,2},{1,3},{6,4},{7,5},{4,6},{5,7},{10,8},{11,9},{8,1... | collective-permute-start | bytes 380168 | tf_op jit(solution)/shard_map/while/body/eval_jaxpr/ppermute | solution.py:13
  318.8 15.0 %collective-permute-start.6 = (bf16[12,5280]{1,0:T(8,128)(2,1)S(1)}, bf16[12,5280]{1,0:T(8,128)(2,1)S(1)}, u32[]{:S(2)}, u32[]{:S(2)}) collective-permute-start(bf16[12,5280]{1,0:T(8,128)(2,1)S(1)} %get-tuple-element.392), channel_id=1, source_target_pairs={{1,0},{2,1},{3,2},{0,3},{5,4},{6,5},{7,6},{4,7},{9,8},{10,9},{11,1... | collective-permute-start | bytes 380168 | tf_op jit(solution)/shard_map/while/body/eval_jaxpr/ppermute | solution.py:13
  344.5 17.1 %collective-permute-start.1 = (bf16[12,5280]{1,0:T(8,128)(2,1)S(1)}, bf16[12,5280]{1,0:T(8,128)(2,1)S(1)}, u32[]{:S(2)}, u32[]{:S(2)}) collective-permute-start(bf16[12,5280]{1,0:T(8,128)(2,1)S(1)} %get-tuple-element.386), channel_id=1, source_target_pairs={{1,0},{2,1},{3,2},{0,3},{5,4},{6,5},{7,6},{4,7},{9,8},{10,9},{11,1... | collective-permute-start | bytes 380168 | tf_op jit(solution)/shard_map/while/body/eval_jaxpr/ppermute | solution.py:13
  348.6 14.1 %collective-permute-start.2 = (bf16[12,5280]{1,0:T(8,128)(2,1)S(1)}, bf16[12,5280]{1,0:T(8,128)(2,1)S(1)}, u32[]{:S(2)}, u32[]{:S(2)}) collective-permute-start(bf16[12,5280]{1,0:T(8,128)(2,1)S(1)} %get-tuple-element.387), channel_id=1, source_target_pairs={{2,0},{3,1},{0,2},{1,3},{6,4},{7,5},{4,6},{5,7},{10,8},{11,9},{8,1... | collective-permute-start | bytes 380168 | tf_op jit(solution)/shard_map/while/body/eval_jaxpr/ppermute | solution.py:13
  349.3 14.9 %collective-permute-start.3 = (bf16[12,5280]{1,0:T(8,128)(2,1)S(1)}, bf16[12,5280]{1,0:T(8,128)(2,1)S(1)}, u32[]{:S(2)}, u32[]{:S(2)}) collective-permute-start(bf16[12,5280]{1,0:T(8,128)(2,1)S(1)} %get-tuple-element.388), channel_id=1, source_target_pairs={{3,0},{0,1},{1,2},{2,3},{7,4},{4,5},{5,6},{6,7},{11,8},{8,9},{9,10... | collective-permute-start | bytes 380168 | tf_op jit(solution)/shard_map/while/body/eval_jaxpr/ppermute | solution.py:13
  375.2 15.1 %collective-permute-start.5 = (bf16[12,5280]{1,0:T(8,128)(2,1)S(1)}, bf16[12,5280]{1,0:T(8,128)(2,1)S(1)}, u32[]{:S(2)}, u32[]{:S(2)}) collective-permute-start(bf16[12,5280]{1,0:T(8,128)(2,1)S(1)} %get-tuple-element.391), channel_id=1, source_target_pairs={{2,0},{3,1},{0,2},{1,3},{6,4},{7,5},{4,6},{5,7},{10,8},{11,9},{8,1... | collective-permute-start | bytes 380168 | tf_op jit(solution)/shard_map/while/body/eval_jaxpr/ppermute | solution.py:13
  392.3 14.7 %collective-permute-start = (bf16[32,5280]{1,0:T(8,128)(2,1)}, bf16[32,5280]{1,0:T(8,128)(2,1)S(1)}, u32[]{:S(2)}, u32[]{:S(2)}) collective-permute-start(bf16[32,5280]{1,0:T(8,128)(2,1)} %get-tuple-element.416), channel_id=1, source_target_pairs={{192,0},{0,64},{64,128},{128,192},{193,1},{1,65},{65,129},{129,193... | collective-permute-start | bytes 1013768 | tf_op jit(solution)/shard_map/while/body/eval_jaxpr/ppermute | solution.py:13
  408.8 15.0 %collective-permute-start.1 = (bf16[12,5280]{1,0:T(8,128)(2,1)S(1)}, bf16[12,5280]{1,0:T(8,128)(2,1)S(1)}, u32[]{:S(2)}, u32[]{:S(2)}) collective-permute-start(bf16[12,5280]{1,0:T(8,128)(2,1)S(1)} %get-tuple-element.386), channel_id=1, source_target_pairs={{1,0},{2,1},{3,2},{0,3},{5,4},{6,5},{7,6},{4,7},{9,8},{10,9},{11,1... | collective-permute-start | bytes 380168 | tf_op jit(solution)/shard_map/while/body/eval_jaxpr/ppermute | solution.py:13
  409.4 14.4 %collective-permute-start.2 = (bf16[12,5280]{1,0:T(8,128)(2,1)S(1)}, bf16[12,5280]{1,0:T(8,128)(2,1)S(1)}, u32[]{:S(2)}, u32[]{:S(2)}) collective-permute-start(bf16[12,5280]{1,0:T(8,128)(2,1)S(1)} %get-tuple-element.387), channel_id=1, source_target_pairs={{2,0},{3,1},{0,2},{1,3},{6,4},{7,5},{4,6},{5,7},{10,8},{11,9},{8,1... | collective-permute-start | bytes 380168 | tf_op jit(solution)/shard_map/while/body/eval_jaxpr/ppermute | solution.py:13
  436.4 13.0 %collective-permute-start.5 = (bf16[12,5280]{1,0:T(8,128)(2,1)S(1)}, bf16[12,5280]{1,0:T(8,128)(2,1)S(1)}, u32[]{:S(2)}, u32[]{:S(2)}) collective-permute-start(bf16[12,5280]{1,0:T(8,128)(2,1)S(1)} %get-tuple-element.391), channel_id=1, source_target_pairs={{2,0},{3,1},{0,2},{1,3},{6,4},{7,5},{4,6},{5,7},{10,8},{11,9},{8,1... | collective-permute-start | bytes 380168 | tf_op jit(solution)/shard_map/while/body/eval_jaxpr/ppermute | solution.py:13
  438.2 19.0 %collective-permute-start.6 = (bf16[12,5280]{1,0:T(8,128)(2,1)S(1)}, bf16[12,5280]{1,0:T(8,128)(2,1)S(1)}, u32[]{:S(2)}, u32[]{:S(2)}) collective-permute-start(bf16[12,5280]{1,0:T(8,128)(2,1)S(1)} %get-tuple-element.392), channel_id=1, source_target_pairs={{1,0},{2,1},{3,2},{0,3},{5,4},{6,5},{7,6},{4,7},{9,8},{10,9},{11,1... | collective-permute-start | bytes 380168 | tf_op jit(solution)/shard_map/while/body/eval_jaxpr/ppermute | solution.py:13
  467.8 14.7 %collective-permute-start.1 = (bf16[12,5280]{1,0:T(8,128)(2,1)S(1)}, bf16[12,5280]{1,0:T(8,128)(2,1)S(1)}, u32[]{:S(2)}, u32[]{:S(2)}) collective-permute-start(bf16[12,5280]{1,0:T(8,128)(2,1)S(1)} %get-tuple-element.386), channel_id=1, source_target_pairs={{1,0},{2,1},{3,2},{0,3},{5,4},{6,5},{7,6},{4,7},{9,8},{10,9},{11,1... | collective-permute-start | bytes 380168 | tf_op jit(solution)/shard_map/while/body/eval_jaxpr/ppermute | solution.py:13
  474.9 12.9 %collective-permute-start.3 = (bf16[12,5280]{1,0:T(8,128)(2,1)S(1)}, bf16[12,5280]{1,0:T(8,128)(2,1)S(1)}, u32[]{:S(2)}, u32[]{:S(2)}) collective-permute-start(bf16[12,5280]{1,0:T(8,128)(2,1)S(1)} %get-tuple-element.388), channel_id=1, source_target_pairs={{3,0},{0,1},{1,2},{2,3},{7,4},{4,5},{5,6},{6,7},{11,8},{8,9},{9,10... | collective-permute-start | bytes 380168 | tf_op jit(solution)/shard_map/while/body/eval_jaxpr/ppermute | solution.py:13
  498.2 16.1 %collective-permute-start.4 = (bf16[12,5280]{1,0:T(8,128)(2,1)S(1)}, bf16[12,5280]{1,0:T(8,128)(2,1)S(1)}, u32[]{:S(2)}, u32[]{:S(2)}) collective-permute-start(bf16[12,5280]{1,0:T(8,128)(2,1)S(1)} %get-tuple-element.390), channel_id=1, source_target_pairs={{3,0},{0,1},{1,2},{2,3},{7,4},{4,5},{5,6},{6,7},{11,8},{8,9},{9,10... | collective-permute-start | bytes 380168 | tf_op jit(solution)/shard_map/while/body/eval_jaxpr/ppermute | solution.py:13
  498.3 16.0 %collective-permute-start.5 = (bf16[12,5280]{1,0:T(8,128)(2,1)S(1)}, bf16[12,5280]{1,0:T(8,128)(2,1)S(1)}, u32[]{:S(2)}, u32[]{:S(2)}) collective-permute-start(bf16[12,5280]{1,0:T(8,128)(2,1)S(1)} %get-tuple-element.391), channel_id=1, source_target_pairs={{2,0},{3,1},{0,2},{1,3},{6,4},{7,5},{4,6},{5,7},{10,8},{11,9},{8,1... | collective-permute-start | bytes 380168 | tf_op jit(solution)/shard_map/while/body/eval_jaxpr/ppermute | solution.py:13
  501.2 16.6 %collective-permute-start.6 = (bf16[12,5280]{1,0:T(8,128)(2,1)S(1)}, bf16[12,5280]{1,0:T(8,128)(2,1)S(1)}, u32[]{:S(2)}, u32[]{:S(2)}) collective-permute-start(bf16[12,5280]{1,0:T(8,128)(2,1)S(1)} %get-tuple-element.392), channel_id=1, source_target_pairs={{1,0},{2,1},{3,2},{0,3},{5,4},{6,5},{7,6},{4,7},{9,8},{10,9},{11,1... | collective-permute-start | bytes 380168 | tf_op jit(solution)/shard_map/while/body/eval_jaxpr/ppermute | solution.py:13
  530.6 15.0 %collective-permute-start.1 = (bf16[12,5280]{1,0:T(8,128)(2,1)S(1)}, bf16[12,5280]{1,0:T(8,128)(2,1)S(1)}, u32[]{:S(2)}, u32[]{:S(2)}) collective-permute-start(bf16[12,5280]{1,0:T(8,128)(2,1)S(1)} %get-tuple-element.386), channel_id=1, source_target_pairs={{1,0},{2,1},{3,2},{0,3},{5,4},{6,5},{7,6},{4,7},{9,8},{10,9},{11,1... | collective-permute-start | bytes 380168 | tf_op jit(solution)/shard_map/while/body/eval_jaxpr/ppermute | solution.py:13
  532.8 14.4 %collective-permute-start.2 = (bf16[12,5280]{1,0:T(8,128)(2,1)S(1)}, bf16[12,5280]{1,0:T(8,128)(2,1)S(1)}, u32[]{:S(2)}, u32[]{:S(2)}) collective-permute-start(bf16[12,5280]{1,0:T(8,128)(2,1)S(1)} %get-tuple-element.387), channel_id=1, source_target_pairs={{2,0},{3,1},{0,2},{1,3},{6,4},{7,5},{4,6},{5,7},{10,8},{11,9},{8,1... | collective-permute-start | bytes 380168 | tf_op jit(solution)/shard_map/while/body/eval_jaxpr/ppermute | solution.py:13
  558.9 13.6 %collective-permute-start.4 = (bf16[12,5280]{1,0:T(8,128)(2,1)S(1)}, bf16[12,5280]{1,0:T(8,128)(2,1)S(1)}, u32[]{:S(2)}, u32[]{:S(2)}) collective-permute-start(bf16[12,5280]{1,0:T(8,128)(2,1)S(1)} %get-tuple-element.390), channel_id=1, source_target_pairs={{3,0},{0,1},{1,2},{2,3},{7,4},{4,5},{5,6},{6,7},{11,8},{8,9},{9,10... | collective-permute-start | bytes 380168 | tf_op jit(solution)/shard_map/while/body/eval_jaxpr/ppermute | solution.py:13
  561.3 16.7 %collective-permute-start.5 = (bf16[12,5280]{1,0:T(8,128)(2,1)S(1)}, bf16[12,5280]{1,0:T(8,128)(2,1)S(1)}, u32[]{:S(2)}, u32[]{:S(2)}) collective-permute-start(bf16[12,5280]{1,0:T(8,128)(2,1)S(1)} %get-tuple-element.391), channel_id=1, source_target_pairs={{2,0},{3,1},{0,2},{1,3},{6,4},{7,5},{4,6},{5,7},{10,8},{11,9},{8,1... | collective-permute-start | bytes 380168 | tf_op jit(solution)/shard_map/while/body/eval_jaxpr/ppermute | solution.py:13
  564.1 14.7 %collective-permute-start.6 = (bf16[12,5280]{1,0:T(8,128)(2,1)S(1)}, bf16[12,5280]{1,0:T(8,128)(2,1)S(1)}, u32[]{:S(2)}, u32[]{:S(2)}) collective-permute-start(bf16[12,5280]{1,0:T(8,128)(2,1)S(1)} %get-tuple-element.392), channel_id=1, source_target_pairs={{1,0},{2,1},{3,2},{0,3},{5,4},{6,5},{7,6},{4,7},{9,8},{10,9},{11,1... | collective-permute-start | bytes 380168 | tf_op jit(solution)/shard_map/while/body/eval_jaxpr/ppermute | solution.py:13
  594.3 12.6 %collective-permute-start.2 = (bf16[12,5280]{1,0:T(8,128)(2,1)S(1)}, bf16[12,5280]{1,0:T(8,128)(2,1)S(1)}, u32[]{:S(2)}, u32[]{:S(2)}) collective-permute-start(bf16[12,5280]{1,0:T(8,128)(2,1)S(1)} %get-tuple-element.387), channel_id=1, source_target_pairs={{2,0},{3,1},{0,2},{1,3},{6,4},{7,5},{4,6},{5,7},{10,8},{11,9},{8,1... | collective-permute-start | bytes 380168 | tf_op jit(solution)/shard_map/while/body/eval_jaxpr/ppermute | solution.py:13
  617.4 15.8 %collective-permute-start.5 = (bf16[12,5280]{1,0:T(8,128)(2,1)S(1)}, bf16[12,5280]{1,0:T(8,128)(2,1)S(1)}, u32[]{:S(2)}, u32[]{:S(2)}) collective-permute-start(bf16[12,5280]{1,0:T(8,128)(2,1)S(1)} %get-tuple-element.391), channel_id=1, source_target_pairs={{2,0},{3,1},{0,2},{1,3},{6,4},{7,5},{4,6},{5,7},{10,8},{11,9},{8,1... | collective-permute-start | bytes 380168 | tf_op jit(solution)/shard_map/while/body/eval_jaxpr/ppermute | solution.py:13
  622.1 17.4 %collective-permute-start.6 = (bf16[12,5280]{1,0:T(8,128)(2,1)S(1)}, bf16[12,5280]{1,0:T(8,128)(2,1)S(1)}, u32[]{:S(2)}, u32[]{:S(2)}) collective-permute-start(bf16[12,5280]{1,0:T(8,128)(2,1)S(1)} %get-tuple-element.392), channel_id=1, source_target_pairs={{1,0},{2,1},{3,2},{0,3},{5,4},{6,5},{7,6},{4,7},{9,8},{10,9},{11,1... | collective-permute-start | bytes 380168 | tf_op jit(solution)/shard_map/while/body/eval_jaxpr/ppermute | solution.py:13
  650.1 17.2 %collective-permute-start.1 = (bf16[12,5280]{1,0:T(8,128)(2,1)S(1)}, bf16[12,5280]{1,0:T(8,128)(2,1)S(1)}, u32[]{:S(2)}, u32[]{:S(2)}) collective-permute-start(bf16[12,5280]{1,0:T(8,128)(2,1)S(1)} %get-tuple-element.386), channel_id=1, source_target_pairs={{1,0},{2,1},{3,2},{0,3},{5,4},{6,5},{7,6},{4,7},{9,8},{10,9},{11,1... | collective-permute-start | bytes 380168 | tf_op jit(solution)/shard_map/while/body/eval_jaxpr/ppermute | solution.py:13
  653.3 14.1 %collective-permute-start.2 = (bf16[12,5280]{1,0:T(8,128)(2,1)S(1)}, bf16[12,5280]{1,0:T(8,128)(2,1)S(1)}, u32[]{:S(2)}, u32[]{:S(2)}) collective-permute-start(bf16[12,5280]{1,0:T(8,128)(2,1)S(1)} %get-tuple-element.387), channel_id=1, source_target_pairs={{2,0},{3,1},{0,2},{1,3},{6,4},{7,5},{4,6},{5,7},{10,8},{11,9},{8,1... | collective-permute-start | bytes 380168 | tf_op jit(solution)/shard_map/while/body/eval_jaxpr/ppermute | solution.py:13
  677.9 20.0 %collective-permute-start.5 = (bf16[12,5280]{1,0:T(8,128)(2,1)S(1)}, bf16[12,5280]{1,0:T(8,128)(2,1)S(1)}, u32[]{:S(2)}, u32[]{:S(2)}) collective-permute-start(bf16[12,5280]{1,0:T(8,128)(2,1)S(1)} %get-tuple-element.391), channel_id=1, source_target_pairs={{2,0},{3,1},{0,2},{1,3},{6,4},{7,5},{4,6},{5,7},{10,8},{11,9},{8,1... | collective-permute-start | bytes 380168 | tf_op jit(solution)/shard_map/while/body/eval_jaxpr/ppermute | solution.py:13
  684.9 14.8 %collective-permute-start.6 = (bf16[12,5280]{1,0:T(8,128)(2,1)S(1)}, bf16[12,5280]{1,0:T(8,128)(2,1)S(1)}, u32[]{:S(2)}, u32[]{:S(2)}) collective-permute-start(bf16[12,5280]{1,0:T(8,128)(2,1)S(1)} %get-tuple-element.392), channel_id=1, source_target_pairs={{1,0},{2,1},{3,2},{0,3},{5,4},{6,5},{7,6},{4,7},{9,8},{10,9},{11,1... | collective-permute-start | bytes 380168 | tf_op jit(solution)/shard_map/while/body/eval_jaxpr/ppermute | solution.py:13
  716.3 14.7 %collective-permute-start.2 = (bf16[12,5280]{1,0:T(8,128)(2,1)S(1)}, bf16[12,5280]{1,0:T(8,128)(2,1)S(1)}, u32[]{:S(2)}, u32[]{:S(2)}) collective-permute-start(bf16[12,5280]{1,0:T(8,128)(2,1)S(1)} %get-tuple-element.387), channel_id=1, source_target_pairs={{2,0},{3,1},{0,2},{1,3},{6,4},{7,5},{4,6},{5,7},{10,8},{11,9},{8,1... | collective-permute-start | bytes 380168 | tf_op jit(solution)/shard_map/while/body/eval_jaxpr/ppermute | solution.py:13
  777.5 14.1 %collective-permute-start.2 = (bf16[12,5280]{1,0:T(8,128)(2,1)S(1)}, bf16[12,5280]{1,0:T(8,128)(2,1)S(1)}, u32[]{:S(2)}, u32[]{:S(2)}) collective-permute-start(bf16[12,5280]{1,0:T(8,128)(2,1)S(1)} %get-tuple-element.387), channel_id=1, source_target_pairs={{2,0},{3,1},{0,2},{1,3},{6,4},{7,5},{4,6},{5,7},{10,8},{11,9},{8,1... | collective-permute-start | bytes 380168 | tf_op jit(solution)/shard_map/while/body/eval_jaxpr/ppermute | solution.py:13
  807.2 16.3 %collective-permute-start.6 = (bf16[12,5280]{1,0:T(8,128)(2,1)S(1)}, bf16[12,5280]{1,0:T(8,128)(2,1)S(1)}, u32[]{:S(2)}, u32[]{:S(2)}) collective-permute-start(bf16[12,5280]{1,0:T(8,128)(2,1)S(1)} %get-tuple-element.392), channel_id=1, source_target_pairs={{1,0},{2,1},{3,2},{0,3},{5,4},{6,5},{7,6},{4,7},{9,8},{10,9},{11,1... | collective-permute-start | bytes 380168 | tf_op jit(solution)/shard_map/while/body/eval_jaxpr/ppermute | solution.py:13
  835.0 17.8 %collective-permute-start.1 = (bf16[12,5280]{1,0:T(8,128)(2,1)S(1)}, bf16[12,5280]{1,0:T(8,128)(2,1)S(1)}, u32[]{:S(2)}, u32[]{:S(2)}) collective-permute-start(bf16[12,5280]{1,0:T(8,128)(2,1)S(1)} %get-tuple-element.386), channel_id=1, source_target_pairs={{1,0},{2,1},{3,2},{0,3},{5,4},{6,5},{7,6},{4,7},{9,8},{10,9},{11,1... | collective-permute-start | bytes 380168 | tf_op jit(solution)/shard_map/while/body/eval_jaxpr/ppermute | solution.py:13
  839.7 13.2 %collective-permute-start.2 = (bf16[12,5280]{1,0:T(8,128)(2,1)S(1)}, bf16[12,5280]{1,0:T(8,128)(2,1)S(1)}, u32[]{:S(2)}, u32[]{:S(2)}) collective-permute-start(bf16[12,5280]{1,0:T(8,128)(2,1)S(1)} %get-tuple-element.387), channel_id=1, source_target_pairs={{2,0},{3,1},{0,2},{1,3},{6,4},{7,5},{4,6},{5,7},{10,8},{11,9},{8,1... | collective-permute-start | bytes 380168 | tf_op jit(solution)/shard_map/while/body/eval_jaxpr/ppermute | solution.py:13
  839.7 13.2 %collective-permute-start.3 = (bf16[12,5280]{1,0:T(8,128)(2,1)S(1)}, bf16[12,5280]{1,0:T(8,128)(2,1)S(1)}, u32[]{:S(2)}, u32[]{:S(2)}) collective-permute-start(bf16[12,5280]{1,0:T(8,128)(2,1)S(1)} %get-tuple-element.388), channel_id=1, source_target_pairs={{3,0},{0,1},{1,2},{2,3},{7,4},{4,5},{5,6},{6,7},{11,8},{8,9},{9,10... | collective-permute-start | bytes 380168 | tf_op jit(solution)/shard_map/while/body/eval_jaxpr/ppermute | solution.py:13
  863.3 15.9 %collective-permute-start.5 = (bf16[12,5280]{1,0:T(8,128)(2,1)S(1)}, bf16[12,5280]{1,0:T(8,128)(2,1)S(1)}, u32[]{:S(2)}, u32[]{:S(2)}) collective-permute-start(bf16[12,5280]{1,0:T(8,128)(2,1)S(1)} %get-tuple-element.391), channel_id=1, source_target_pairs={{2,0},{3,1},{0,2},{1,3},{6,4},{7,5},{4,6},{5,7},{10,8},{11,9},{8,1... | collective-permute-start | bytes 380168 | tf_op jit(solution)/shard_map/while/body/eval_jaxpr/ppermute | solution.py:13
  (42 other events, 409.1 us)
Sparse Core Ops, SparseCore 0:
  9.5 151.3 all-gather.1

commit v9 on v5

--- a/solution.py
+++ b/solution.py
@@ -42,7 +42,7 @@
     return lax.ppermute(block, ("section", "expert"), route)
 
 
-def core_block(current, gain_row, router_rows, w_first, w_second, assign):
+def front(current, gain_row, router_rows, assign):
     tokens = current.shape[0]
     experts = router_rows.shape[0]
     normed = normalize(current, gain_row)
@@ -61,6 +61,12 @@
     places = (
         lax.broadcasted_iota(jnp.int32, (experts * CAP, tokens), 0) == target[None, :]
     ).astype(jnp.bfloat16)
+    return normed, gate_value, places
+
+
+def core_block(current, gain_row, router_rows, w_first, w_second, assign):
+    experts = router_rows.shape[0]
+    normed, _, places = front(current, gain_row, router_rows, assign)
     buffer = (
         jnp.dot(places, normed, preferred_element_type=jnp.float32)
         .astype(jnp.bfloat16)
@@ -68,21 +74,8 @@
     )
     arrived = jnp.stack([buffer[0]] + [shifted(buffer[j], "expert", j) for j in range(1, experts)])
     processed = expert_rows(arrived, w_first, w_second)
-    back = jnp.stack([onward(processed[j], j) for j in range(experts)])
-    return (
-        shifted(current, "section", 1),
-        shifted(gate_value, "section", 1),
-        shifted(places, "section", 1),
-        back,
-    )
-
-
-def combine(carry, was_live):
-    kept, gate_value, places, back = carry
-    flat_back = back.reshape(-1, back.shape[-1])
-    expert_out = jnp.einsum("st,sd->td", places, flat_back, preferred_element_type=jnp.float32)
-    updated = (kept.astype(jnp.float32) + gate_value[:, None] * expert_out).astype(jnp.bfloat16)
-    return jnp.where(was_live, updated, kept)
+    packed = onward(jnp.concatenate([processed[0], current]), 0)
+    return (packed,) + tuple(onward(processed[j], j) for j in range(1, experts))
 
 
 def body(init_state, inject, routes, norm_gain, router, w_up, w_down):
@@ -92,10 +85,11 @@
         lax.all_gather(w_up, "dp", axis=2, tiled=True),
         lax.all_gather(jnp.swapaxes(w_down, 2, 3), "dp", axis=2, tiled=True),
     )
+    gains = lax.all_gather(norm_gain, "section", axis=0, tiled=True)
+    routers = lax.all_gather(router, "section", axis=0, tiled=True)
+    all_routes = lax.all_gather(routes, "section", axis=1, tiled=True)
     w_first = up_all[0, 0]
     w_second = down_all[0, 0]
-    gain_row = norm_gain[0]
-    router_rows = router[0]
     tokens = init_state.shape[1]
     active_span = sections * RECUR
     total_steps = active_span + sections - 1
@@ -105,13 +99,34 @@
         offset = moment - section
         return (offset >= 0) & (offset < active_span)
 
+    def schedule(moment, section):
+        clipped = jnp.clip(moment - section, 0, active_span - 1)
+        loop_round = clipped // sections
+        micro_idx = jnp.mod(sections - 1 - clipped % sections, sections)
+        assign = lax.dynamic_slice(
+            all_routes, (loop_round, section, micro_idx, 0, 0), (1, 1, 1, tokens, 1)
+        ).reshape(tokens)
+        return loop_round, micro_idx, assign
+
+    def combine(moment, carry):
+        packed, *rest = carry
+        slots = packed.shape[0] - tokens
+        kept = packed[slots:]
+        _, _, assign = schedule(moment - 1, previous_section)
+        _, gate_value, places = front(
+            kept,
+            lax.dynamic_index_in_dim(gains, previous_section, 0, keepdims=False),
+            lax.dynamic_index_in_dim(routers, previous_section, 0, keepdims=False),
+            assign,
+        )
+        flat_back = jnp.concatenate([packed[:slots]] + list(rest))
+        expert_out = jnp.einsum("st,sd->td", places, flat_back, preferred_element_type=jnp.float32)
+        updated = (kept.astype(jnp.float32) + gate_value[:, None] * expert_out).astype(jnp.bfloat16)
+        return jnp.where(live_at(moment - 1, previous_section), updated, kept)
+
     def advance(moment, hidden_state):
-        offset = moment - section_index
         is_live = live_at(moment, section_index)
-        clipped = jnp.clip(offset, 0, active_span - 1)
-        loop_round = clipped // sections
-        entry_slot = clipped % sections
-        micro_idx = jnp.mod(sections - 1 - entry_slot, sections)
+        loop_round, micro_idx, assign = schedule(moment, section_index)
         initial = lax.dynamic_index_in_dim(init_state, micro_idx, 0, keepdims=False)
         injected_row = lax.dynamic_index_in_dim(inject, micro_idx, 0, keepdims=False)
         incoming = jnp.where(loop_round == 0, initial, hidden_state)
@@ -120,19 +135,16 @@
         )
         entering = is_live & (section_index == 0)
         current = jnp.where(entering, injected, hidden_state)
-        assign = lax.dynamic_slice(
-            routes, (loop_round, 0, micro_idx, 0, 0), (1, 1, 1, tokens, 1)
-        ).reshape(tokens)
+        gain_row = lax.dynamic_index_in_dim(gains, section_index, 0, keepdims=False)
+        router_rows = lax.dynamic_index_in_dim(routers, section_index, 0, keepdims=False)
         return core_block(current, gain_row, router_rows, w_first, w_second, assign)
 
     def advance_one(moment, carry):
-        arrived = combine(carry, live_at(moment - 1, previous_section))
-        return advance(moment, arrived)
+        return advance(moment, combine(moment, carry))
 
     carry = advance(0, jnp.zeros(init_state.shape[1:], jnp.bfloat16))
     carry = lax.fori_loop(1, total_steps, advance_one, carry)
-    final = combine(carry, live_at(total_steps - 1, previous_section))
-    return final[None]
+    return combine(total_steps, carry)[None]
 
 
 def solution(mesh):

time: 893 us -> 825 us (0.924)
  waiting for transfers between devices: 479 us -> 371 us
  blocking collectives: 0 us -> 35.6 us
  starting transfers between devices: 202 us -> 214 us
  local copies, waits for them, and re-layouts: 43.3 us -> 33.8 us
    ppermute x66 -> x33, waiting for transfers between devices: 182 us -> 94.1 us  [shifted(): return lax.ppermute(block, axis, route)]
    all_gather x0 -> x3, blocking collectives: none -> 35.6 us  [the longest x1 12.1 us: body(): gains = lax.all_gather(norm_gain, 'section', axis=0, tiled=True)]
    all_gather x1, waiting for transfers between devices: 71.3 us -> 50.4 us  [body(): lax.all_gather(jnp.swapaxes(w_down, 2, 3), 'dp', axis=2, tiled=True)]
    ppermute x44, starting transfers between devices: 114 us -> 124 us  [onward(): return lax.ppermute(block, ('section', 'expert'), route)]
    ppermute x66 -> x33, starting transfers between devices: 87.9 us -> 89.3 us  [shifted(): return lax.ppermute(block, axis, route)]
    unnamed x8 -> x6, local copies, waits for them, and re-layouts: 28.7 us -> 28.7 us
  transfers between devices with their start and end apart: 112 -> 79, of which waited for: 67 -> 57; matrix products, arithmetic and copies ran while one was open for 17% -> 2% of each run, Pallas kernels for 0% -> 0%
where the time goes in v9:
time: 825 us; the launch traced here: 815 us
  waiting for transfers between devices  371 us (45%)
  starting transfers between devices  214 us (26%)
  matrix products  138 us (17%)
  blocking collectives  35.6 us (4%)
  local copies, waits for them, and re-layouts  33.8 us (4%)
  between operations  13.6 us (2%)
  other arithmetic  8.43 us (1%)
    ppermute x44, waiting for transfers between devices, onward(): return lax.ppermute(block, ('section', 'expert'), route)  138 us
    ppermute x44, starting transfers between devices, onward(): return lax.ppermute(block, ('section', 'expert'), route)  124 us
    dot_general x11, matrix products, expert_rows(): lax.dot_general(hidden, w_second, (((1,), (1,)), ((), ())), preferred_ele...  109 us
    ppermute x33, waiting for transfers between devices, shifted(): return lax.ppermute(block, axis, route)  94.1 us
    ppermute x33, starting transfers between devices, shifted(): return lax.ppermute(block, axis, route)  89.3 us
    all_gather x1, waiting for transfers between devices, body(): lax.all_gather(w_up, 'dp', axis=2, tiled=True)  88.2 us
    all_gather x1, waiting for transfers between devices, body(): lax.all_gather(jnp.swapaxes(w_down, 2, 3), 'dp', axis=2, tiled=True)  50.4 us
    unnamed x6, local copies, waits for them, and re-layouts  28.7 us
  transfers between devices with their start and end apart: 79, of which 57 were waited for; matrix products, arithmetic and copies ran while one was open for 2% of the time, Pallas kernels for 0%

profile of v9, /device:TPU:2, one launch (start us, length us, event | category | flops | bytes accessed | tf_op | source)
XLA Modules:
  0.0 815.3 jit_solution(16317242064303067431)
XLA Ops:
  12.3 11.4 %all_gather.15 = s32[2,4,4,32,1]{3,4,2,1,0:T(1,128)S(1)} all-gather(s32[2,1,4,32,1]{3,4,2,1,0:T(1,128)} %param.11), channel_id=1, replica_groups=mesh['section'=4,'dp'=16,'expert'=4] {'section'}, dimensions={1}, use_global_device_ids=true | all-gather | bytes 5120 | tf_op jit(solution)/shard_map/all_gather | solution.py:90
  23.7 12.1 %all-gather = f32[4,1,5280]{2,1,0:T(1,128)S(1)} all-gather(f32[1,1,5280]{2,1,0:T(1,128)} %bitcast.85), channel_id=1, replica_groups=mesh['section'=4,'dp'=16,'expert'=4] {'section'}, dimensions={0}, use_global_device_ids=true | all-gather | bytes 105600 | tf_op jit(solution)/shard_map/all_gather | solution.py:88
  49.5 12.1 %all_gather.19 = bf16[4,4,5280]{2,1,0:T(4,128)(2,1)S(1)} all-gather(bf16[1,4,5280]{2,1,0:T(4,128)(2,1)S(1)} %copy-done), channel_id=1, replica_groups=mesh['section'=4,'dp'=16,'expert'=4] {'section'}, dimensions={0}, use_global_device_ids=true | all-gather | bytes 211200 | tf_op jit(solution)/shard_map/all_gather | solution.py:89
  62.0 50.4 %all-gather.6.cloned.1.call-done = bf16[1,1,5280,768]{3,1,0,2:T(2,128)(2,1)} async-done(((bf16[1,1,330,768]{3,1,0,2:T(2,128)(2,1)}), bf16[1,1,5280,768]{3,1,0,2:T(2,128)(2,1)}) %all-gather.6.cloned.1.call-update) | async-done | bytes 8110096 | tf_op jit(solution)/shard_map/all_gather | solution.py:86
  112.4 11.5 %copy.17 = bf16[1,1,5280,768]{3,2,0,1:T(8,128)(2,1)} copy(bf16[1,1,5280,768]{3,1,0,2:T(2,128)(2,1)} %all-gather.6.cloned.1.call-done) | data formatting | bytes 16220160
  123.9 88.2 %all-gather.4.cloned.1.call-done = bf16[1,1,5280,768]{3,1,0,2:T(2,128)(2,1)} async-done(((bf16[1,1,330,768]{3,1,0,2:T(2,128)(2,1)}), bf16[1,1,5280,768]{3,1,0,2:T(2,128)(2,1)}) %all-gather.4.cloned.1.call-update) | async-done | bytes 8110096 | tf_op jit(solution)/shard_map/all_gather | solution.py:85
  212.1 11.6 %copy.18 = bf16[1,1,5280,768]{3,2,0,1:T(8,128)(2,1)} copy(bf16[1,1,5280,768]{3,1,0,2:T(2,128)(2,1)} %all-gather.4.cloned.1.call-done) | data formatting | bytes 16220160
  223.7 9.9 %convolution_convert_fusion.2 = bf16[48,5280]{1,0:T(8,128)(2,1)S(1)} fusion(bf16[5280,768]{1,0:T(8,128)(2,1)} %bitcast.74, bf16[48,5280]{1,0:T(8,128)(2,1)S(1)} %reshape.243, bf16[5280,768]{1,0:T(8,128)(2,1)} %bitcast.76), kind=kOutput, calls=%fused_computation.90 | convolution fusion | flops 779152896 | bytes 17233920 | tf_op jit(solution)/shard_map/dot_general | solution.py:28
  245.9 9.7 %collective-permute-done.11 = bf16[12,5280]{1,0:T(8,128)(2,1)S(1)} collective-permute-done((bf16[12,5280]{1,0:T(8,128)(2,1)S(1)}, bf16[12,5280]{1,0:T(8,128)(2,1)S(1)}, u32[]{:S(2)}, u32[]{:S(2)}) %collective-permute-start.11) | collective-permute-done | bytes 126752 | tf_op jit(solution)/shard_map/ppermute | solution.py:42
  260.2 546.5 %while.24 = (s32[]{:T(128)}, bf16[44,5280]{1,0:T(8,128)(2,1)S(1)}, bf16[12,5280]{1,0:T(8,128)(2,1)S(1)}, bf16[12,5280]{1,0:T(8,128)(2,1)S(1)}, bf16[12,5280]{1,0...) while((s32[]{:T(128)}, bf16[44,5280]{1,0:T(8,128)(2,1)S(1)}, ...), condition=%wide.region_8.9_spmd, body=%wide.region_2.8_spmd.sunk | while | flops 821163456 | bytes 30935848 | solution.py:146
  272.3 7.5 collective-permute-done
  282.0 9.9 %convolution_convert_fusion.7 = bf16[48,5280]{1,0:T(8,128)(2,1)S(1)} fusion(bf16[5280,768]{1,0:T(8,128)(2,1)} %get-tuple-element.841, bf16[48,5280]{1,0:T(8,128)(2,1)S(1)} %reshape.259, bf16[5280,768]{1,0:T(8,128)(2,1)} %get-tuple-element.840), kind=kOutput, calls=%fused_computation.clone.1 | convolution fusion | flops 779152896 | bytes 17233920 | tf_op jit(solution)/shard_map/while/body/eval_jaxpr/dot_general | solution.py:28
  328.0 9.0 %collective-permute-done.1 = bf16[12,5280]{1,0:T(8,128)(2,1)S(1)} collective-permute-done((bf16[12,5280]{1,0:T(8,128)(2,1)S(1)}, bf16[12,5280]{1,0:T(8,128)(2,1)S(1)}, u32[]{:S(2)}, u32[]{:S(2)}) %collective-permute-start.1) | collective-permute-done | bytes 126752 | tf_op jit(solution)/shard_map/while/body/eval_jaxpr/ppermute | solution.py:13
  338.6 9.9 %convolution_convert_fusion.7 = bf16[48,5280]{1,0:T(8,128)(2,1)S(1)} fusion(bf16[5280,768]{1,0:T(8,128)(2,1)} %get-tuple-element.841, bf16[48,5280]{1,0:T(8,128)(2,1)S(1)} %reshape.259, bf16[5280,768]{1,0:T(8,128)(2,1)} %get-tuple-element.840), kind=kOutput, calls=%fused_computation.clone.1 | convolution fusion | flops 779152896 | bytes 17233920 | tf_op jit(solution)/shard_map/while/body/eval_jaxpr/dot_general | solution.py:28
  358.7 7.8 collective-permute-done.5
  368.8 5.8 collective-permute-done.3
  384.2 7.7 collective-permute-done.1
  395.3 9.9 %convolution_convert_fusion.7 = bf16[48,5280]{1,0:T(8,128)(2,1)S(1)} fusion(bf16[5280,768]{1,0:T(8,128)(2,1)} %get-tuple-element.841, bf16[48,5280]{1,0:T(8,128)(2,1)S(1)} %reshape.259, bf16[5280,768]{1,0:T(8,128)(2,1)} %get-tuple-element.840), kind=kOutput, calls=%fused_computation.clone.1 | convolution fusion | flops 779152896 | bytes 17233920 | tf_op jit(solution)/shard_map/while/body/eval_jaxpr/dot_general | solution.py:28
  405.7 9.5 %collective-permute-start.5 = (bf16[12,5280]{1,0:T(8,128)(2,1)S(1)}, bf16[12,5280]{1,0:T(8,128)(2,1)S(1)}, u32[]{:S(2)}, u32[]{:S(2)}) collective-permute-start(bf16[12,5280]{1,0:T(8,128)(2,1)S(1)} %get-tuple-element.766), channel_id=1, source_target_pairs={{0,66},{1,67},{2,64},{3,65},{64,130},{65,131},{66,128},{67,129},{1... | collective-permute-start | bytes 380168 | tf_op jit(solution)/shard_map/while/body/eval_jaxpr/ppermute | solution.py:42
  415.1 11.2 %collective-permute-done.4 = bf16[12,5280]{1,0:T(8,128)(2,1)S(1)} collective-permute-done((bf16[12,5280]{1,0:T(8,128)(2,1)S(1)}, bf16[12,5280]{1,0:T(8,128)(2,1)S(1)}, u32[]{:S(2)}, u32[]{:S(2)}) %collective-permute-start.4) | collective-permute-done | bytes 126752 | tf_op jit(solution)/shard_map/while/body/eval_jaxpr/ppermute | solution.py:42
  434.9 6.0 collective-permute-start.1
  440.8 7.3 collective-permute-done.1
  450.4 9.9 %convolution_convert_fusion.7 = bf16[48,5280]{1,0:T(8,128)(2,1)S(1)} fusion(bf16[5280,768]{1,0:T(8,128)(2,1)} %get-tuple-element.841, bf16[48,5280]{1,0:T(8,128)(2,1)S(1)} %reshape.259, bf16[5280,768]{1,0:T(8,128)(2,1)} %get-tuple-element.840), kind=kOutput, calls=%fused_computation.clone.1 | convolution fusion | flops 779152896 | bytes 17233920 | tf_op jit(solution)/shard_map/while/body/eval_jaxpr/dot_general | solution.py:28
  461.0 9.9 %collective-permute-start.5 = (bf16[12,5280]{1,0:T(8,128)(2,1)S(1)}, bf16[12,5280]{1,0:T(8,128)(2,1)S(1)}, u32[]{:S(2)}, u32[]{:S(2)}) collective-permute-start(bf16[12,5280]{1,0:T(8,128)(2,1)S(1)} %get-tuple-element.766), channel_id=1, source_target_pairs={{0,66},{1,67},{2,64},{3,65},{64,130},{65,131},{66,128},{67,129},{1... | collective-permute-start | bytes 380168 | tf_op jit(solution)/shard_map/while/body/eval_jaxpr/ppermute | solution.py:42
  471.2 5.5 collective-permute-done.5
  493.1 10.2 %collective-permute-done.1 = bf16[12,5280]{1,0:T(8,128)(2,1)S(1)} collective-permute-done((bf16[12,5280]{1,0:T(8,128)(2,1)S(1)}, bf16[12,5280]{1,0:T(8,128)(2,1)S(1)}, u32[]{:S(2)}, u32[]{:S(2)}) %collective-permute-start.1) | collective-permute-done | bytes 126752 | tf_op jit(solution)/shard_map/while/body/eval_jaxpr/ppermute | solution.py:13
  503.7 9.9 %convolution_convert_fusion.7 = bf16[48,5280]{1,0:T(8,128)(2,1)S(1)} fusion(bf16[5280,768]{1,0:T(8,128)(2,1)} %get-tuple-element.841, bf16[48,5280]{1,0:T(8,128)(2,1)S(1)} %reshape.259, bf16[5280,768]{1,0:T(8,128)(2,1)} %get-tuple-element.840), kind=kOutput, calls=%fused_computation.clone.1 | convolution fusion | flops 779152896 | bytes 17233920 | tf_op jit(solution)/shard_map/while/body/eval_jaxpr/dot_general | solution.py:28
  519.2 6.9 collective-permute-start.6
  526.1 7.0 collective-permute-done.4
  538.0 6.3 collective-permute-start
  547.2 7.9 collective-permute-done.1
  556.4 9.9 %convolution_convert_fusion.7 = bf16[48,5280]{1,0:T(8,128)(2,1)S(1)} fusion(bf16[5280,768]{1,0:T(8,128)(2,1)} %get-tuple-element.841, bf16[48,5280]{1,0:T(8,128)(2,1)S(1)} %reshape.259, bf16[5280,768]{1,0:T(8,128)(2,1)} %get-tuple-element.840), kind=kOutput, calls=%fused_computation.clone.1 | convolution fusion | flops 779152896 | bytes 17233920 | tf_op jit(solution)/shard_map/while/body/eval_jaxpr/dot_general | solution.py:28
  571.1 5.5 collective-permute-start.6
  576.6 6.3 collective-permute-done.5
  583.8 5.8 collective-permute-done.3
  609.8 9.9 %convolution_convert_fusion.7 = bf16[48,5280]{1,0:T(8,128)(2,1)S(1)} fusion(bf16[5280,768]{1,0:T(8,128)(2,1)} %get-tuple-element.841, bf16[48,5280]{1,0:T(8,128)(2,1)S(1)} %reshape.259, bf16[5280,768]{1,0:T(8,128)(2,1)} %get-tuple-element.840), kind=kOutput, calls=%fused_computation.clone.1 | convolution fusion | flops 779152896 | bytes 17233920 | tf_op jit(solution)/shard_map/while/body/eval_jaxpr/dot_general | solution.py:28
  621.2 7.4 collective-permute-start.5
  631.0 8.9 %collective-permute-done.4 = bf16[12,5280]{1,0:T(8,128)(2,1)S(1)} collective-permute-done((bf16[12,5280]{1,0:T(8,128)(2,1)S(1)}, bf16[12,5280]{1,0:T(8,128)(2,1)S(1)}, u32[]{:S(2)}, u32[]{:S(2)}) %collective-permute-start.4) | collective-permute-done | bytes 126752 | tf_op jit(solution)/shard_map/while/body/eval_jaxpr/ppermute | solution.py:42
  646.6 6.0 collective-permute-start.1
  664.3 9.9 %convolution_convert_fusion.7 = bf16[48,5280]{1,0:T(8,128)(2,1)S(1)} fusion(bf16[5280,768]{1,0:T(8,128)(2,1)} %get-tuple-element.841, bf16[48,5280]{1,0:T(8,128)(2,1)S(1)} %reshape.259, bf16[5280,768]{1,0:T(8,128)(2,1)} %get-tuple-element.840), kind=kOutput, calls=%fused_computation.clone.1 | convolution fusion | flops 779152896 | bytes 17233920 | tf_op jit(solution)/shard_map/while/body/eval_jaxpr/dot_general | solution.py:28
  674.8 8.1 collective-permute-start.5
  688.3 7.2 collective-permute-done.4
  701.2 5.8 collective-permute-start.1
  718.6 9.9 %convolution_convert_fusion.7 = bf16[48,5280]{1,0:T(8,128)(2,1)S(1)} fusion(bf16[5280,768]{1,0:T(8,128)(2,1)} %get-tuple-element.841, bf16[48,5280]{1,0:T(8,128)(2,1)S(1)} %reshape.259, bf16[5280,768]{1,0:T(8,128)(2,1)} %get-tuple-element.840), kind=kOutput, calls=%fused_computation.clone.1 | convolution fusion | flops 779152896 | bytes 17233920 | tf_op jit(solution)/shard_map/while/body/eval_jaxpr/dot_general | solution.py:28
  730.8 6.4 collective-permute-start.5
  772.2 9.9 %convolution_convert_fusion.7 = bf16[48,5280]{1,0:T(8,128)(2,1)S(1)} fusion(bf16[5280,768]{1,0:T(8,128)(2,1)} %get-tuple-element.841, bf16[48,5280]{1,0:T(8,128)(2,1)S(1)} %reshape.259, bf16[5280,768]{1,0:T(8,128)(2,1)} %get-tuple-element.840), kind=kOutput, calls=%fused_computation.clone.1 | convolution fusion | flops 779152896 | bytes 17233920 | tf_op jit(solution)/shard_map/while/body/eval_jaxpr/dot_general | solution.py:28
  792.6 5.8 collective-permute-done.5
  800.5 6.3 collective-permute-done.3
  (344 shorter events, 279.2 us)
Async XLA Ops:
  6.5 105.8 %all-gather.6.cloned.1.call-start = ((), (), s32[]{:S(2)}) async-start(), calls=%async_computation.1 | async-start | bytes 17233920 | tf_op jit(solution)/shard_map/all_gather | solution.py:86
  9.4 202.7 %all-gather.4.cloned.1.call-start = ((), (), s32[]{:S(2)}) async-start(), calls=%async_computation | async-start | bytes 17233920 | tf_op jit(solution)/shard_map/all_gather | solution.py:85
  38.0 23.5 %collective-permute-start.7 = (bf16[12,5280]{1,0:T(8,128)(2,1)S(1)}, bf16[12,5280]{1,0:T(8,128)(2,1)S(1)}, u32[]{:S(2)}, u32[]{:S(2)}) collective-permute-start(bf16[12,5280]{1,0:T(8,128)(2,1)S(1)} %get-tuple-element.626), channel_id=1, source_target_pairs={{3,0},{0,1},{1,2},{2,3},{7,4},{4,5},{5,6},{6,7},{11,8},{8,9},{9,10... | collective-permute-start | bytes 380168 | tf_op jit(solution)/shard_map/ppermute | solution.py:13
  41.4 20.2 %collective-permute-start.8 = (bf16[12,5280]{1,0:T(8,128)(2,1)S(1)}, bf16[12,5280]{1,0:T(8,128)(2,1)S(1)}, u32[]{:S(2)}, u32[]{:S(2)}) collective-permute-start(bf16[12,5280]{1,0:T(8,128)(2,1)S(1)} %get-tuple-element.625), channel_id=1, source_target_pairs={{2,0},{3,1},{0,2},{1,3},{6,4},{7,5},{4,6},{5,7},{10,8},{11,9},{8,1... | collective-permute-start | bytes 380168 | tf_op jit(solution)/shard_map/ppermute | solution.py:13
  46.8 14.8 %collective-permute-start.9 = (bf16[12,5280]{1,0:T(8,128)(2,1)S(1)}, bf16[12,5280]{1,0:T(8,128)(2,1)S(1)}, u32[]{:S(2)}, u32[]{:S(2)}) collective-permute-start(bf16[12,5280]{1,0:T(8,128)(2,1)S(1)} %get-tuple-element.624), channel_id=1, source_target_pairs={{1,0},{2,1},{3,2},{0,3},{5,4},{6,5},{7,6},{4,7},{9,8},{10,9},{11,1... | collective-permute-start | bytes 380168 | tf_op jit(solution)/shard_map/ppermute | solution.py:13
  233.8 26.4 %collective-permute-start.10 = (bf16[44,5280]{1,0:T(8,128)(2,1)S(1)}, bf16[44,5280]{1,0:T(8,128)(2,1)S(1)}, u32[]{:S(2)}, u32[]{:S(2)}) collective-permute-start(bf16[44,5280]{1,0:T(8,128)(2,1)S(1)} %pad_maximum_fusion.3), channel_id=1, source_target_pairs={{0,64},{1,65},{2,66},{3,67},{64,128},{65,129},{66,130},{67,131},{1... | collective-permute-start | bytes 1393928 | tf_op jit(solution)/shard_map/ppermute | solution.py:42
  235.7 19.9 %collective-permute-start.11 = (bf16[12,5280]{1,0:T(8,128)(2,1)S(1)}, bf16[12,5280]{1,0:T(8,128)(2,1)S(1)}, u32[]{:S(2)}, u32[]{:S(2)}) collective-permute-start(bf16[12,5280]{1,0:T(8,128)(2,1)S(1)} %get-tuple-element.621), channel_id=1, source_target_pairs={{0,67},{1,64},{2,65},{3,66},{64,131},{65,128},{66,129},{67,130},{1... | collective-permute-start | bytes 380168 | tf_op jit(solution)/shard_map/ppermute | solution.py:42
  240.8 17.2 %collective-permute-start.12 = (bf16[12,5280]{1,0:T(8,128)(2,1)S(1)}, bf16[12,5280]{1,0:T(8,128)(2,1)S(1)}, u32[]{:S(2)}, u32[]{:S(2)}) collective-permute-start(bf16[12,5280]{1,0:T(8,128)(2,1)S(1)} %get-tuple-element.620), channel_id=1, source_target_pairs={{0,66},{1,67},{2,64},{3,65},{64,130},{65,131},{66,128},{67,129},{1... | collective-permute-start | bytes 380168 | tf_op jit(solution)/shard_map/ppermute | solution.py:42
  243.4 14.7 %collective-permute-start.13 = (bf16[12,5280]{1,0:T(8,128)(2,1)S(1)}, bf16[12,5280]{1,0:T(8,128)(2,1)S(1)}, u32[]{:S(2)}, u32[]{:S(2)}) collective-permute-start(bf16[12,5280]{1,0:T(8,128)(2,1)S(1)} %get-tuple-element.619), channel_id=1, source_target_pairs={{0,65},{1,66},{2,67},{3,64},{64,129},{65,130},{66,131},{67,128},{1... | collective-permute-start | bytes 380168 | tf_op jit(solution)/shard_map/ppermute | solution.py:42
  263.5 16.2 %collective-permute-start = (bf16[12,5280]{1,0:T(8,128)(2,1)S(1)}, bf16[12,5280]{1,0:T(8,128)(2,1)S(1)}, u32[]{:S(2)}, u32[]{:S(2)}) collective-permute-start(bf16[12,5280]{1,0:T(8,128)(2,1)S(1)} %get-tuple-element.760), channel_id=1, source_target_pairs={{1,0},{2,1},{3,2},{0,3},{5,4},{6,5},{7,6},{4,7},{9,8},{10,9},{11,1... | collective-permute-start | bytes 380168 | tf_op jit(solution)/shard_map/while/body/eval_jaxpr/ppermute | solution.py:13
  267.7 13.9 %collective-permute-start.1 = (bf16[12,5280]{1,0:T(8,128)(2,1)S(1)}, bf16[12,5280]{1,0:T(8,128)(2,1)S(1)}, u32[]{:S(2)}, u32[]{:S(2)}) collective-permute-start(bf16[12,5280]{1,0:T(8,128)(2,1)S(1)} %get-tuple-element.761), channel_id=1, source_target_pairs={{2,0},{3,1},{0,2},{1,3},{6,4},{7,5},{4,6},{5,7},{10,8},{11,9},{8,1... | collective-permute-start | bytes 380168 | tf_op jit(solution)/shard_map/while/body/eval_jaxpr/ppermute | solution.py:13
  292.1 24.6 %collective-permute-start.3 = (bf16[44,5280]{1,0:T(8,128)(2,1)S(1)}, bf16[44,5280]{1,0:T(8,128)(2,1)S(1)}, u32[]{:S(2)}, u32[]{:S(2)}) collective-permute-start(bf16[44,5280]{1,0:T(8,128)(2,1)S(1)} %pad_maximum_fusion.7), channel_id=1, source_target_pairs={{0,64},{1,65},{2,66},{3,67},{64,128},{65,129},{66,130},{67,131},{1... | collective-permute-start | bytes 1393928 | tf_op jit(solution)/shard_map/while/body/eval_jaxpr/ppermute | solution.py:42
  292.3 14.5 %collective-permute-start.4 = (bf16[12,5280]{1,0:T(8,128)(2,1)S(1)}, bf16[12,5280]{1,0:T(8,128)(2,1)S(1)}, u32[]{:S(2)}, u32[]{:S(2)}) collective-permute-start(bf16[12,5280]{1,0:T(8,128)(2,1)S(1)} %get-tuple-element.765), channel_id=1, source_target_pairs={{0,67},{1,64},{2,65},{3,66},{64,131},{65,128},{66,129},{67,130},{1... | collective-permute-start | bytes 380168 | tf_op jit(solution)/shard_map/while/body/eval_jaxpr/ppermute | solution.py:42
  297.0 14.3 %collective-permute-start.5 = (bf16[12,5280]{1,0:T(8,128)(2,1)S(1)}, bf16[12,5280]{1,0:T(8,128)(2,1)S(1)}, u32[]{:S(2)}, u32[]{:S(2)}) collective-permute-start(bf16[12,5280]{1,0:T(8,128)(2,1)S(1)} %get-tuple-element.766), channel_id=1, source_target_pairs={{0,66},{1,67},{2,64},{3,65},{64,130},{65,131},{66,128},{67,129},{1... | collective-permute-start | bytes 380168 | tf_op jit(solution)/shard_map/while/body/eval_jaxpr/ppermute | solution.py:42
  324.2 12.8 %collective-permute-start.1 = (bf16[12,5280]{1,0:T(8,128)(2,1)S(1)}, bf16[12,5280]{1,0:T(8,128)(2,1)S(1)}, u32[]{:S(2)}, u32[]{:S(2)}) collective-permute-start(bf16[12,5280]{1,0:T(8,128)(2,1)S(1)} %get-tuple-element.761), channel_id=1, source_target_pairs={{2,0},{3,1},{0,2},{1,3},{6,4},{7,5},{4,6},{5,7},{10,8},{11,9},{8,1... | collective-permute-start | bytes 380168 | tf_op jit(solution)/shard_map/while/body/eval_jaxpr/ppermute | solution.py:13
  348.8 25.8 %collective-permute-start.3 = (bf16[44,5280]{1,0:T(8,128)(2,1)S(1)}, bf16[44,5280]{1,0:T(8,128)(2,1)S(1)}, u32[]{:S(2)}, u32[]{:S(2)}) collective-permute-start(bf16[44,5280]{1,0:T(8,128)(2,1)S(1)} %pad_maximum_fusion.7), channel_id=1, source_target_pairs={{0,64},{1,65},{2,66},{3,67},{64,128},{65,129},{66,130},{67,131},{1... | collective-permute-start | bytes 1393928 | tf_op jit(solution)/shard_map/while/body/eval_jaxpr/ppermute | solution.py:42
  351.0 15.5 %collective-permute-start.5 = (bf16[12,5280]{1,0:T(8,128)(2,1)S(1)}, bf16[12,5280]{1,0:T(8,128)(2,1)S(1)}, u32[]{:S(2)}, u32[]{:S(2)}) collective-permute-start(bf16[12,5280]{1,0:T(8,128)(2,1)S(1)} %get-tuple-element.766), channel_id=1, source_target_pairs={{0,66},{1,67},{2,64},{3,65},{64,130},{65,131},{66,128},{67,129},{1... | collective-permute-start | bytes 380168 | tf_op jit(solution)/shard_map/while/body/eval_jaxpr/ppermute | solution.py:42
  354.4 14.4 %collective-permute-start.6 = (bf16[12,5280]{1,0:T(8,128)(2,1)S(1)}, bf16[12,5280]{1,0:T(8,128)(2,1)S(1)}, u32[]{:S(2)}, u32[]{:S(2)}) collective-permute-start(bf16[12,5280]{1,0:T(8,128)(2,1)S(1)} %get-tuple-element.767), channel_id=1, source_target_pairs={{0,65},{1,66},{2,67},{3,64},{64,129},{65,130},{66,131},{67,128},{1... | collective-permute-start | bytes 380168 | tf_op jit(solution)/shard_map/while/body/eval_jaxpr/ppermute | solution.py:42
  378.6 13.3 %collective-permute-start.1 = (bf16[12,5280]{1,0:T(8,128)(2,1)S(1)}, bf16[12,5280]{1,0:T(8,128)(2,1)S(1)}, u32[]{:S(2)}, u32[]{:S(2)}) collective-permute-start(bf16[12,5280]{1,0:T(8,128)(2,1)S(1)} %get-tuple-element.761), channel_id=1, source_target_pairs={{2,0},{3,1},{0,2},{1,3},{6,4},{7,5},{4,6},{5,7},{10,8},{11,9},{8,1... | collective-permute-start | bytes 380168 | tf_op jit(solution)/shard_map/while/body/eval_jaxpr/ppermute | solution.py:13
  405.5 25.0 %collective-permute-start.3 = (bf16[44,5280]{1,0:T(8,128)(2,1)S(1)}, bf16[44,5280]{1,0:T(8,128)(2,1)S(1)}, u32[]{:S(2)}, u32[]{:S(2)}) collective-permute-start(bf16[44,5280]{1,0:T(8,128)(2,1)S(1)} %pad_maximum_fusion.7), channel_id=1, source_target_pairs={{0,64},{1,65},{2,66},{3,67},{64,128},{65,129},{66,130},{67,131},{1... | collective-permute-start | bytes 1393928 | tf_op jit(solution)/shard_map/while/body/eval_jaxpr/ppermute | solution.py:42
  405.6 20.8 %collective-permute-start.4 = (bf16[12,5280]{1,0:T(8,128)(2,1)S(1)}, bf16[12,5280]{1,0:T(8,128)(2,1)S(1)}, u32[]{:S(2)}, u32[]{:S(2)}) collective-permute-start(bf16[12,5280]{1,0:T(8,128)(2,1)S(1)} %get-tuple-element.765), channel_id=1, source_target_pairs={{0,67},{1,64},{2,65},{3,66},{64,131},{65,128},{66,129},{67,130},{1... | collective-permute-start | bytes 380168 | tf_op jit(solution)/shard_map/while/body/eval_jaxpr/ppermute | solution.py:42
  405.7 20.7 %collective-permute-start.5 = (bf16[12,5280]{1,0:T(8,128)(2,1)S(1)}, bf16[12,5280]{1,0:T(8,128)(2,1)S(1)}, u32[]{:S(2)}, u32[]{:S(2)}) collective-permute-start(bf16[12,5280]{1,0:T(8,128)(2,1)S(1)} %get-tuple-element.766), channel_id=1, source_target_pairs={{0,66},{1,67},{2,64},{3,65},{64,130},{65,131},{66,128},{67,129},{1... | collective-permute-start | bytes 380168 | tf_op jit(solution)/shard_map/while/body/eval_jaxpr/ppermute | solution.py:42
  415.1 12.9 %collective-permute-start.6 = (bf16[12,5280]{1,0:T(8,128)(2,1)S(1)}, bf16[12,5280]{1,0:T(8,128)(2,1)S(1)}, u32[]{:S(2)}, u32[]{:S(2)}) collective-permute-start(bf16[12,5280]{1,0:T(8,128)(2,1)S(1)} %get-tuple-element.767), channel_id=1, source_target_pairs={{0,65},{1,66},{2,67},{3,64},{64,129},{65,130},{66,131},{67,128},{1... | collective-permute-start | bytes 380168 | tf_op jit(solution)/shard_map/while/body/eval_jaxpr/ppermute | solution.py:42
  434.9 13.3 %collective-permute-start.1 = (bf16[12,5280]{1,0:T(8,128)(2,1)S(1)}, bf16[12,5280]{1,0:T(8,128)(2,1)S(1)}, u32[]{:S(2)}, u32[]{:S(2)}) collective-permute-start(bf16[12,5280]{1,0:T(8,128)(2,1)S(1)} %get-tuple-element.761), channel_id=1, source_target_pairs={{2,0},{3,1},{0,2},{1,3},{6,4},{7,5},{4,6},{5,7},{10,8},{11,9},{8,1... | collective-permute-start | bytes 380168 | tf_op jit(solution)/shard_map/while/body/eval_jaxpr/ppermute | solution.py:13
  460.6 22.6 %collective-permute-start.3 = (bf16[44,5280]{1,0:T(8,128)(2,1)S(1)}, bf16[44,5280]{1,0:T(8,128)(2,1)S(1)}, u32[]{:S(2)}, u32[]{:S(2)}) collective-permute-start(bf16[44,5280]{1,0:T(8,128)(2,1)S(1)} %pad_maximum_fusion.7), channel_id=1, source_target_pairs={{0,64},{1,65},{2,66},{3,67},{64,128},{65,129},{66,130},{67,131},{1... | collective-permute-start | bytes 1393928 | tf_op jit(solution)/shard_map/while/body/eval_jaxpr/ppermute | solution.py:42
  461.0 15.8 %collective-permute-start.5 = (bf16[12,5280]{1,0:T(8,128)(2,1)S(1)}, bf16[12,5280]{1,0:T(8,128)(2,1)S(1)}, u32[]{:S(2)}, u32[]{:S(2)}) collective-permute-start(bf16[12,5280]{1,0:T(8,128)(2,1)S(1)} %get-tuple-element.766), channel_id=1, source_target_pairs={{0,66},{1,67},{2,64},{3,65},{64,130},{65,131},{66,128},{67,129},{1... | collective-permute-start | bytes 380168 | tf_op jit(solution)/shard_map/while/body/eval_jaxpr/ppermute | solution.py:42
  490.2 13.1 %collective-permute-start.1 = (bf16[12,5280]{1,0:T(8,128)(2,1)S(1)}, bf16[12,5280]{1,0:T(8,128)(2,1)S(1)}, u32[]{:S(2)}, u32[]{:S(2)}) collective-permute-start(bf16[12,5280]{1,0:T(8,128)(2,1)S(1)} %get-tuple-element.761), channel_id=1, source_target_pairs={{2,0},{3,1},{0,2},{1,3},{6,4},{7,5},{4,6},{5,7},{10,8},{11,9},{8,1... | collective-permute-start | bytes 380168 | tf_op jit(solution)/shard_map/while/body/eval_jaxpr/ppermute | solution.py:13
  490.2 13.1 %collective-permute-start.2 = (bf16[12,5280]{1,0:T(8,128)(2,1)S(1)}, bf16[12,5280]{1,0:T(8,128)(2,1)S(1)}, u32[]{:S(2)}, u32[]{:S(2)}) collective-permute-start(bf16[12,5280]{1,0:T(8,128)(2,1)S(1)} %get-tuple-element.762), channel_id=1, source_target_pairs={{3,0},{0,1},{1,2},{2,3},{7,4},{4,5},{5,6},{6,7},{11,8},{8,9},{9,10... | collective-permute-start | bytes 380168 | tf_op jit(solution)/shard_map/while/body/eval_jaxpr/ppermute | solution.py:13
  513.8 20.9 %collective-permute-start.3 = (bf16[44,5280]{1,0:T(8,128)(2,1)S(1)}, bf16[44,5280]{1,0:T(8,128)(2,1)S(1)}, u32[]{:S(2)}, u32[]{:S(2)}) collective-permute-start(bf16[44,5280]{1,0:T(8,128)(2,1)S(1)} %pad_maximum_fusion.7), channel_id=1, source_target_pairs={{0,64},{1,65},{2,66},{3,67},{64,128},{65,129},{66,130},{67,131},{1... | collective-permute-start | bytes 1393928 | tf_op jit(solution)/shard_map/while/body/eval_jaxpr/ppermute | solution.py:42
  513.9 19.2 %collective-permute-start.4 = (bf16[12,5280]{1,0:T(8,128)(2,1)S(1)}, bf16[12,5280]{1,0:T(8,128)(2,1)S(1)}, u32[]{:S(2)}, u32[]{:S(2)}) collective-permute-start(bf16[12,5280]{1,0:T(8,128)(2,1)S(1)} %get-tuple-element.765), channel_id=1, source_target_pairs={{0,67},{1,64},{2,65},{3,66},{64,131},{65,128},{66,129},{67,130},{1... | collective-permute-start | bytes 380168 | tf_op jit(solution)/shard_map/while/body/eval_jaxpr/ppermute | solution.py:42
  519.1 14.0 %collective-permute-start.5 = (bf16[12,5280]{1,0:T(8,128)(2,1)S(1)}, bf16[12,5280]{1,0:T(8,128)(2,1)S(1)}, u32[]{:S(2)}, u32[]{:S(2)}) collective-permute-start(bf16[12,5280]{1,0:T(8,128)(2,1)S(1)} %get-tuple-element.766), channel_id=1, source_target_pairs={{0,66},{1,67},{2,64},{3,65},{64,130},{65,131},{66,128},{67,129},{1... | collective-permute-start | bytes 380168 | tf_op jit(solution)/shard_map/while/body/eval_jaxpr/ppermute | solution.py:42
  519.2 13.9 %collective-permute-start.6 = (bf16[12,5280]{1,0:T(8,128)(2,1)S(1)}, bf16[12,5280]{1,0:T(8,128)(2,1)S(1)}, u32[]{:S(2)}, u32[]{:S(2)}) collective-permute-start(bf16[12,5280]{1,0:T(8,128)(2,1)S(1)} %get-tuple-element.767), channel_id=1, source_target_pairs={{0,65},{1,66},{2,67},{3,64},{64,129},{65,130},{66,131},{67,128},{1... | collective-permute-start | bytes 380168 | tf_op jit(solution)/shard_map/while/body/eval_jaxpr/ppermute | solution.py:42
  566.6 22.9 %collective-permute-start.3 = (bf16[44,5280]{1,0:T(8,128)(2,1)S(1)}, bf16[44,5280]{1,0:T(8,128)(2,1)S(1)}, u32[]{:S(2)}, u32[]{:S(2)}) collective-permute-start(bf16[44,5280]{1,0:T(8,128)(2,1)S(1)} %pad_maximum_fusion.7), channel_id=1, source_target_pairs={{0,64},{1,65},{2,66},{3,67},{64,128},{65,129},{66,130},{67,131},{1... | collective-permute-start | bytes 1393928 | tf_op jit(solution)/shard_map/while/body/eval_jaxpr/ppermute | solution.py:42
  568.5 14.4 %collective-permute-start.5 = (bf16[12,5280]{1,0:T(8,128)(2,1)S(1)}, bf16[12,5280]{1,0:T(8,128)(2,1)S(1)}, u32[]{:S(2)}, u32[]{:S(2)}) collective-permute-start(bf16[12,5280]{1,0:T(8,128)(2,1)S(1)} %get-tuple-element.766), channel_id=1, source_target_pairs={{0,66},{1,67},{2,64},{3,65},{64,130},{65,131},{66,128},{67,129},{1... | collective-permute-start | bytes 380168 | tf_op jit(solution)/shard_map/while/body/eval_jaxpr/ppermute | solution.py:42
  571.1 12.7 %collective-permute-start.6 = (bf16[12,5280]{1,0:T(8,128)(2,1)S(1)}, bf16[12,5280]{1,0:T(8,128)(2,1)S(1)}, u32[]{:S(2)}, u32[]{:S(2)}) collective-permute-start(bf16[12,5280]{1,0:T(8,128)(2,1)S(1)} %get-tuple-element.767), channel_id=1, source_target_pairs={{0,65},{1,66},{2,67},{3,64},{64,129},{65,130},{66,131},{67,128},{1... | collective-permute-start | bytes 380168 | tf_op jit(solution)/shard_map/while/body/eval_jaxpr/ppermute | solution.py:42
  620.0 23.3 %collective-permute-start.3 = (bf16[44,5280]{1,0:T(8,128)(2,1)S(1)}, bf16[44,5280]{1,0:T(8,128)(2,1)S(1)}, u32[]{:S(2)}, u32[]{:S(2)}) collective-permute-start(bf16[44,5280]{1,0:T(8,128)(2,1)S(1)} %pad_maximum_fusion.7), channel_id=1, source_target_pairs={{0,64},{1,65},{2,66},{3,67},{64,128},{65,129},{66,130},{67,131},{1... | collective-permute-start | bytes 1393928 | tf_op jit(solution)/shard_map/while/body/eval_jaxpr/ppermute | solution.py:42
  621.2 18.6 %collective-permute-start.4 = (bf16[12,5280]{1,0:T(8,128)(2,1)S(1)}, bf16[12,5280]{1,0:T(8,128)(2,1)S(1)}, u32[]{:S(2)}, u32[]{:S(2)}) collective-permute-start(bf16[12,5280]{1,0:T(8,128)(2,1)S(1)} %get-tuple-element.765), channel_id=1, source_target_pairs={{0,67},{1,64},{2,65},{3,66},{64,131},{65,128},{66,129},{67,130},{1... | collective-permute-start | bytes 380168 | tf_op jit(solution)/shard_map/while/body/eval_jaxpr/ppermute | solution.py:42
  621.2 18.6 %collective-permute-start.5 = (bf16[12,5280]{1,0:T(8,128)(2,1)S(1)}, bf16[12,5280]{1,0:T(8,128)(2,1)S(1)}, u32[]{:S(2)}, u32[]{:S(2)}) collective-permute-start(bf16[12,5280]{1,0:T(8,128)(2,1)S(1)} %get-tuple-element.766), channel_id=1, source_target_pairs={{0,66},{1,67},{2,64},{3,65},{64,130},{65,131},{66,128},{67,129},{1... | collective-permute-start | bytes 380168 | tf_op jit(solution)/shard_map/while/body/eval_jaxpr/ppermute | solution.py:42
  646.6 13.1 %collective-permute-start.1 = (bf16[12,5280]{1,0:T(8,128)(2,1)S(1)}, bf16[12,5280]{1,0:T(8,128)(2,1)S(1)}, u32[]{:S(2)}, u32[]{:S(2)}) collective-permute-start(bf16[12,5280]{1,0:T(8,128)(2,1)S(1)} %get-tuple-element.761), channel_id=1, source_target_pairs={{2,0},{3,1},{0,2},{1,3},{6,4},{7,5},{4,6},{5,7},{10,8},{11,9},{8,1... | collective-permute-start | bytes 380168 | tf_op jit(solution)/shard_map/while/body/eval_jaxpr/ppermute | solution.py:13
  674.4 23.3 %collective-permute-start.3 = (bf16[44,5280]{1,0:T(8,128)(2,1)S(1)}, bf16[44,5280]{1,0:T(8,128)(2,1)S(1)}, u32[]{:S(2)}, u32[]{:S(2)}) collective-permute-start(bf16[44,5280]{1,0:T(8,128)(2,1)S(1)} %pad_maximum_fusion.7), channel_id=1, source_target_pairs={{0,64},{1,65},{2,66},{3,67},{64,128},{65,129},{66,130},{67,131},{1... | collective-permute-start | bytes 1393928 | tf_op jit(solution)/shard_map/while/body/eval_jaxpr/ppermute | solution.py:42
  674.5 21.0 %collective-permute-start.4 = (bf16[12,5280]{1,0:T(8,128)(2,1)S(1)}, bf16[12,5280]{1,0:T(8,128)(2,1)S(1)}, u32[]{:S(2)}, u32[]{:S(2)}) collective-permute-start(bf16[12,5280]{1,0:T(8,128)(2,1)S(1)} %get-tuple-element.765), channel_id=1, source_target_pairs={{0,67},{1,64},{2,65},{3,66},{64,131},{65,128},{66,129},{67,130},{1... | collective-permute-start | bytes 380168 | tf_op jit(solution)/shard_map/while/body/eval_jaxpr/ppermute | solution.py:42
  674.8 20.7 %collective-permute-start.5 = (bf16[12,5280]{1,0:T(8,128)(2,1)S(1)}, bf16[12,5280]{1,0:T(8,128)(2,1)S(1)}, u32[]{:S(2)}, u32[]{:S(2)}) collective-permute-start(bf16[12,5280]{1,0:T(8,128)(2,1)S(1)} %get-tuple-element.766), channel_id=1, source_target_pairs={{0,66},{1,67},{2,64},{3,65},{64,130},{65,131},{66,128},{67,129},{1... | collective-permute-start | bytes 380168 | tf_op jit(solution)/shard_map/while/body/eval_jaxpr/ppermute | solution.py:42
  701.2 12.9 %collective-permute-start.1 = (bf16[12,5280]{1,0:T(8,128)(2,1)S(1)}, bf16[12,5280]{1,0:T(8,128)(2,1)S(1)}, u32[]{:S(2)}, u32[]{:S(2)}) collective-permute-start(bf16[12,5280]{1,0:T(8,128)(2,1)S(1)} %get-tuple-element.761), channel_id=1, source_target_pairs={{2,0},{3,1},{0,2},{1,3},{6,4},{7,5},{4,6},{5,7},{10,8},{11,9},{8,1... | collective-permute-start | bytes 380168 | tf_op jit(solution)/shard_map/while/body/eval_jaxpr/ppermute | solution.py:13
  728.8 23.5 %collective-permute-start.3 = (bf16[44,5280]{1,0:T(8,128)(2,1)S(1)}, bf16[44,5280]{1,0:T(8,128)(2,1)S(1)}, u32[]{:S(2)}, u32[]{:S(2)}) collective-permute-start(bf16[44,5280]{1,0:T(8,128)(2,1)S(1)} %pad_maximum_fusion.7), channel_id=1, source_target_pairs={{0,64},{1,65},{2,66},{3,67},{64,128},{65,129},{66,130},{67,131},{1... | collective-permute-start | bytes 1393928 | tf_op jit(solution)/shard_map/while/body/eval_jaxpr/ppermute | solution.py:42
  730.8 13.0 %collective-permute-start.5 = (bf16[12,5280]{1,0:T(8,128)(2,1)S(1)}, bf16[12,5280]{1,0:T(8,128)(2,1)S(1)}, u32[]{:S(2)}, u32[]{:S(2)}) collective-permute-start(bf16[12,5280]{1,0:T(8,128)(2,1)S(1)} %get-tuple-element.766), channel_id=1, source_target_pairs={{0,66},{1,67},{2,64},{3,65},{64,130},{65,131},{66,128},{67,129},{1... | collective-permute-start | bytes 380168 | tf_op jit(solution)/shard_map/while/body/eval_jaxpr/ppermute | solution.py:42
  782.4 24.4 %collective-permute-start.3 = (bf16[44,5280]{1,0:T(8,128)(2,1)S(1)}, bf16[44,5280]{1,0:T(8,128)(2,1)S(1)}, u32[]{:S(2)}, u32[]{:S(2)}) collective-permute-start(bf16[44,5280]{1,0:T(8,128)(2,1)S(1)} %pad_maximum_fusion.7), channel_id=1, source_target_pairs={{0,64},{1,65},{2,66},{3,67},{64,128},{65,129},{66,130},{67,131},{1... | collective-permute-start | bytes 1393928 | tf_op jit(solution)/shard_map/while/body/eval_jaxpr/ppermute | solution.py:42
  783.0 15.4 %collective-permute-start.5 = (bf16[12,5280]{1,0:T(8,128)(2,1)S(1)}, bf16[12,5280]{1,0:T(8,128)(2,1)S(1)}, u32[]{:S(2)}, u32[]{:S(2)}) collective-permute-start(bf16[12,5280]{1,0:T(8,128)(2,1)S(1)} %get-tuple-element.766), channel_id=1, source_target_pairs={{0,66},{1,67},{2,64},{3,65},{64,130},{65,131},{66,128},{67,129},{1... | collective-permute-start | bytes 380168 | tf_op jit(solution)/shard_map/while/body/eval_jaxpr/ppermute | solution.py:42
  787.4 13.1 %collective-permute-start.6 = (bf16[12,5280]{1,0:T(8,128)(2,1)S(1)}, bf16[12,5280]{1,0:T(8,128)(2,1)S(1)}, u32[]{:S(2)}, u32[]{:S(2)}) collective-permute-start(bf16[12,5280]{1,0:T(8,128)(2,1)S(1)} %get-tuple-element.767), channel_id=1, source_target_pairs={{0,65},{1,66},{2,67},{3,64},{64,129},{65,130},{66,131},{67,128},{1... | collective-permute-start | bytes 380168 | tf_op jit(solution)/shard_map/while/body/eval_jaxpr/ppermute | solution.py:42
  (32 other events, 353.6 us)
Sparse Core Ops, SparseCore 0:
  9.5 102.8 all-gather.5
  114.2 97.8 all-gather.3

commit v10 on v9

--- a/solution.py
+++ b/solution.py
@@ -81,15 +81,14 @@
 def body(init_state, inject, routes, norm_gain, router, w_up, w_down):
     sections = lax.axis_size("section")
     section_index = lax.axis_index("section")
-    up_all, down_all = (
-        lax.all_gather(w_up, "dp", axis=2, tiled=True),
-        lax.all_gather(jnp.swapaxes(w_down, 2, 3), "dp", axis=2, tiled=True),
-    )
+    rows = w_up.shape[2]
+    pieces = jnp.concatenate([w_up[0, 0], jnp.swapaxes(w_down[0, 0], 0, 1)], axis=0)
+    both = lax.all_gather(pieces, "dp", axis=0, tiled=False)
     gains = lax.all_gather(norm_gain, "section", axis=0, tiled=True)
     routers = lax.all_gather(router, "section", axis=0, tiled=True)
     all_routes = lax.all_gather(routes, "section", axis=1, tiled=True)
-    w_first = up_all[0, 0]
-    w_second = down_all[0, 0]
+    w_first = both[:, :rows].reshape(-1, both.shape[-1])
+    w_second = both[:, rows:].reshape(-1, both.shape[-1])
     tokens = init_state.shape[1]
     active_span = sections * RECUR
     total_steps = active_span + sections - 1

time: 825 us -> 747 us (0.905)
  the two profiles are of different devices: /device:TPU:2 before, /device:TPU:32 now
where the time goes in v10:
time: 747 us; the launch traced here: 746 us
  waiting for transfers between devices  339 us (45%)
  starting transfers between devices  176 us (24%)
  matrix products  137 us (18%)
  blocking collectives  35.8 us (5%)
  local copies, waits for them, and re-layouts  32 us (4%)
  between operations  13.6 us (2%)
  other arithmetic  10.8 us (1%)
    ppermute x44, waiting for transfers between devices, onward(): return lax.ppermute(block, ('section', 'expert'), route)  178 us
    dot_general x11, matrix products, expert_rows(): lax.dot_general(hidden, w_second, (((1,), (1,)), ((), ())), preferred_ele...  108 us
    ppermute x33, waiting for transfers between devices, shifted(): return lax.ppermute(block, axis, route)  106 us
    ppermute x44, starting transfers between devices, onward(): return lax.ppermute(block, ('section', 'expert'), route)  102 us
    ppermute x33, starting transfers between devices, shifted(): return lax.ppermute(block, axis, route)  73.7 us
    all_gather x1, waiting for transfers between devices, body(): both = lax.all_gather(pieces, 'dp', axis=0, tiled=False)  55.6 us
    dot_general x11, matrix products, combine(): jnp.einsum('st,sd->td', places, flat_back, preferred_element_type=jnp.flo...  18.4 us
  transfers between devices with their start and end apart: 78, of which 63 were waited for; matrix products, arithmetic and copies ran while one was open for 0% of the time, Pallas kernels for 0%

profile of v10, /device:TPU:32, one launch (start us, length us, event | category | flops | bytes accessed | tf_op | source)
XLA Modules:
  0.0 746.2 jit_solution(6726393407540657621)
XLA Ops:
  9.0 11.4 %all_gather.15 = s32[2,4,4,32,1]{3,4,2,1,0:T(1,128)S(1)} all-gather(s32[2,1,4,32,1]{3,4,2,1,0:T(1,128)} %param.11), channel_id=1, replica_groups=mesh['section'=4,'dp'=16,'expert'=4] {'section'}, dimensions={1}, use_global_device_ids=true | all-gather | bytes 5120 | tf_op jit(solution)/shard_map/all_gather | solution.py:89
  20.4 12.1 %all-gather.1 = f32[4,1,5280]{2,1,0:T(1,128)S(1)} all-gather(f32[1,1,5280]{2,1,0:T(1,128)} %bitcast.79), channel_id=1, replica_groups=mesh['section'=4,'dp'=16,'expert'=4] {'section'}, dimensions={0}, use_global_device_ids=true | all-gather | bytes 105600 | tf_op jit(solution)/shard_map/all_gather | solution.py:87
  34.7 5.5 collective-permute-start.9
  44.1 12.3 %all_gather.19 = bf16[4,4,5280]{2,1,0:T(4,128)(2,1)S(1)} all-gather(bf16[1,4,5280]{2,1,0:T(4,128)(2,1)} %param.13), channel_id=1, replica_groups=mesh['section'=4,'dp'=16,'expert'=4] {'section'}, dimensions={0}, use_global_device_ids=true | all-gather | bytes 211200 | tf_op jit(solution)/shard_map/all_gather | solution.py:88
  61.6 55.6 %all-gather.5.cloned.1.call-done = bf16[16,660,768]{2,1,0:T(8,128)(2,1)} async-done(((bf16[1,660,768]{2,1,0:T(8,128)(2,1)}), bf16[16,660,768]{2,1,0:T(8,128)(2,1)}) %all-gather.5.cloned.1.call-update) | async-done | bytes 16220176 | tf_op jit(solution)/shard_map/all_gather | solution.py:86
  117.2 11.6 %fusion.123 = (bf16[16,330,768]{2,1,0:T(8,128)(2,1)}, bf16[16,330,768]{2,1,0:T(8,128)(2,1)}) fusion(bf16[16,660,768]{2,1,0:T(8,128)(2,1)} %all-gather.5.cloned.1.call-done), kind=kLoop, calls=%fused_computation.183 | loop fusion | bytes 32440320 | tf_op jit(solution)/shard_map/slice | solution.py:90
  128.7 7.6 %reshape.251 = bf16[5280,768]{1,0:T(8,128)(2,1)} reshape(bf16[16,330,768]{2,1,0:T(8,128)(2,1)} %get-tuple-element.620) | data formatting | bytes 16220160 | tf_op jit(solution)/shard_map/reshape | solution.py:91
  136.4 7.6 %reshape.250 = bf16[5280,768]{1,0:T(8,128)(2,1)} reshape(bf16[16,330,768]{2,1,0:T(8,128)(2,1)} %get-tuple-element.619) | data formatting | bytes 16220160 | tf_op jit(solution)/shard_map/reshape | solution.py:90
  144.0 9.9 %convolution_convert_fusion.2 = bf16[48,5280]{1,0:T(8,128)(2,1)S(1)} fusion(bf16[5280,768]{1,0:T(8,128)(2,1)} %reshape.251, bf16[48,5280]{1,0:T(8,128)(2,1)S(1)} %reshape.249, bf16[5280,768]{1,0:T(8,128)(2,1)} %reshape.250), kind=kOutput, calls=%fused_computation.88 | convolution fusion | flops 779152896 | bytes 17233920 | tf_op jit(solution)/shard_map/dot_general | solution.py:28
  156.1 5.0 collective-permute-start.11
  171.2 8.2 %collective-permute-done.12 = bf16[12,5280]{1,0:T(8,128)(2,1)S(1)} collective-permute-done((bf16[12,5280]{1,0:T(8,128)(2,1)S(1)}, bf16[12,5280]{1,0:T(8,128)(2,1)S(1)}, u32[]{:S(2)}, u32[]{:S(2)}) %collective-permute-start.12) | collective-permute-done | bytes 126752 | tf_op jit(solution)/shard_map/ppermute | solution.py:42
  182.2 555.5 %while.24 = (s32[]{:T(128)}, bf16[44,5280]{1,0:T(8,128)(2,1)S(1)}, bf16[12,5280]{1,0:T(8,128)(2,1)S(1)}, bf16[12,5280]{1,0:T(8,128)(2,1)S(1)}, bf16[12,5280]{1,0...) while((s32[]{:T(128)}, bf16[44,5280]{1,0:T(8,128)(2,1)S(1)}, ...), condition=%wide.region_8.9_spmd, body=%wide.region_2.8_spmd.sunk | while | flops 821163456 | bytes 30935856 | solution.py:145
  197.5 7.6 %collective-permute-done.1 = bf16[12,5280]{1,0:T(8,128)(2,1)S(1)} collective-permute-done((bf16[12,5280]{1,0:T(8,128)(2,1)S(1)}, bf16[12,5280]{1,0:T(8,128)(2,1)S(1)}, u32[]{:S(2)}, u32[]{:S(2)}) %collective-permute-start.1) | collective-permute-done | bytes 126752 | tf_op jit(solution)/shard_map/while/body/eval_jaxpr/ppermute | solution.py:13
  206.7 9.9 %convolution_convert_fusion.7 = bf16[48,5280]{1,0:T(8,128)(2,1)S(1)} fusion(bf16[5280,768]{1,0:T(8,128)(2,1)} %get-tuple-element.843, bf16[48,5280]{1,0:T(8,128)(2,1)S(1)} %reshape.271, bf16[5280,768]{1,0:T(8,128)(2,1)} %get-tuple-element.842), kind=kOutput, calls=%fused_computation.clone.1 | convolution fusion | flops 779152896 | bytes 17233920 | tf_op jit(solution)/shard_map/while/body/eval_jaxpr/dot_general | solution.py:28
  237.7 5.0 collective-permute-done.3
  254.7 7.8 %collective-permute-done.1 = bf16[12,5280]{1,0:T(8,128)(2,1)S(1)} collective-permute-done((bf16[12,5280]{1,0:T(8,128)(2,1)S(1)}, bf16[12,5280]{1,0:T(8,128)(2,1)S(1)}, u32[]{:S(2)}, u32[]{:S(2)}) %collective-permute-start.1) | collective-permute-done | bytes 126752 | tf_op jit(solution)/shard_map/while/body/eval_jaxpr/ppermute | solution.py:13
  263.4 9.9 %convolution_convert_fusion.7 = bf16[48,5280]{1,0:T(8,128)(2,1)S(1)} fusion(bf16[5280,768]{1,0:T(8,128)(2,1)} %get-tuple-element.843, bf16[48,5280]{1,0:T(8,128)(2,1)S(1)} %reshape.271, bf16[5280,768]{1,0:T(8,128)(2,1)} %get-tuple-element.842), kind=kOutput, calls=%fused_computation.clone.1 | convolution fusion | flops 779152896 | bytes 17233920 | tf_op jit(solution)/shard_map/while/body/eval_jaxpr/dot_general | solution.py:28
  285.9 10.3 %collective-permute-done.5 = bf16[12,5280]{1,0:T(8,128)(2,1)S(1)} collective-permute-done((bf16[12,5280]{1,0:T(8,128)(2,1)S(1)}, bf16[12,5280]{1,0:T(8,128)(2,1)S(1)}, u32[]{:S(2)}, u32[]{:S(2)}) %collective-permute-start.5) | collective-permute-done | bytes 126752 | tf_op jit(solution)/shard_map/while/body/eval_jaxpr/ppermute | solution.py:42
  312.5 7.1 collective-permute-done.1
  320.0 9.9 %convolution_convert_fusion.7 = bf16[48,5280]{1,0:T(8,128)(2,1)S(1)} fusion(bf16[5280,768]{1,0:T(8,128)(2,1)} %get-tuple-element.843, bf16[48,5280]{1,0:T(8,128)(2,1)S(1)} %reshape.271, bf16[5280,768]{1,0:T(8,128)(2,1)} %get-tuple-element.842), kind=kOutput, calls=%fused_computation.clone.1 | convolution fusion | flops 779152896 | bytes 17233920 | tf_op jit(solution)/shard_map/while/body/eval_jaxpr/dot_general | solution.py:28
  341.0 9.9 %collective-permute-done.5 = bf16[12,5280]{1,0:T(8,128)(2,1)S(1)} collective-permute-done((bf16[12,5280]{1,0:T(8,128)(2,1)S(1)}, bf16[12,5280]{1,0:T(8,128)(2,1)S(1)}, u32[]{:S(2)}, u32[]{:S(2)}) %collective-permute-start.5) | collective-permute-done | bytes 126752 | tf_op jit(solution)/shard_map/while/body/eval_jaxpr/ppermute | solution.py:42
  367.8 6.5 collective-permute-done.1
  375.2 9.9 %convolution_convert_fusion.7 = bf16[48,5280]{1,0:T(8,128)(2,1)S(1)} fusion(bf16[5280,768]{1,0:T(8,128)(2,1)} %get-tuple-element.843, bf16[48,5280]{1,0:T(8,128)(2,1)S(1)} %reshape.271, bf16[5280,768]{1,0:T(8,128)(2,1)} %get-tuple-element.842), kind=kOutput, calls=%fused_computation.clone.1 | convolution fusion | flops 779152896 | bytes 17233920 | tf_op jit(solution)/shard_map/while/body/eval_jaxpr/dot_general | solution.py:28
  387.6 6.9 collective-permute-start.6
  396.2 8.4 %collective-permute-done.5 = bf16[12,5280]{1,0:T(8,128)(2,1)S(1)} collective-permute-done((bf16[12,5280]{1,0:T(8,128)(2,1)S(1)}, bf16[12,5280]{1,0:T(8,128)(2,1)S(1)}, u32[]{:S(2)}, u32[]{:S(2)}) %collective-permute-start.5) | collective-permute-done | bytes 126752 | tf_op jit(solution)/shard_map/while/body/eval_jaxpr/ppermute | solution.py:42
  404.6 6.7 collective-permute-done.3
  420.3 6.3 collective-permute-done
  427.4 9.9 %convolution_convert_fusion.7 = bf16[48,5280]{1,0:T(8,128)(2,1)S(1)} fusion(bf16[5280,768]{1,0:T(8,128)(2,1)} %get-tuple-element.843, bf16[48,5280]{1,0:T(8,128)(2,1)S(1)} %reshape.271, bf16[5280,768]{1,0:T(8,128)(2,1)} %get-tuple-element.842), kind=kOutput, calls=%fused_computation.clone.1 | convolution fusion | flops 779152896 | bytes 17233920 | tf_op jit(solution)/shard_map/while/body/eval_jaxpr/dot_general | solution.py:28
  445.7 5.0 collective-permute-done.4
  450.8 12.3 %collective-permute-done.5 = bf16[12,5280]{1,0:T(8,128)(2,1)S(1)} collective-permute-done((bf16[12,5280]{1,0:T(8,128)(2,1)S(1)}, bf16[12,5280]{1,0:T(8,128)(2,1)S(1)}, u32[]{:S(2)}, u32[]{:S(2)}) %collective-permute-start.5) | collective-permute-done | bytes 126752 | tf_op jit(solution)/shard_map/while/body/eval_jaxpr/ppermute | solution.py:42
  478.0 7.8 %collective-permute-done.1 = bf16[12,5280]{1,0:T(8,128)(2,1)S(1)} collective-permute-done((bf16[12,5280]{1,0:T(8,128)(2,1)S(1)}, bf16[12,5280]{1,0:T(8,128)(2,1)S(1)}, u32[]{:S(2)}, u32[]{:S(2)}) %collective-permute-start.1) | collective-permute-done | bytes 126752 | tf_op jit(solution)/shard_map/while/body/eval_jaxpr/ppermute | solution.py:13
  488.0 9.9 %convolution_convert_fusion.7 = bf16[48,5280]{1,0:T(8,128)(2,1)S(1)} fusion(bf16[5280,768]{1,0:T(8,128)(2,1)} %get-tuple-element.843, bf16[48,5280]{1,0:T(8,128)(2,1)S(1)} %reshape.271, bf16[5280,768]{1,0:T(8,128)(2,1)} %get-tuple-element.842), kind=kOutput, calls=%fused_computation.clone.1 | convolution fusion | flops 779152896 | bytes 17233920 | tf_op jit(solution)/shard_map/while/body/eval_jaxpr/dot_general | solution.py:28
  498.3 6.7 collective-permute-start.6
  532.0 7.5 collective-permute-done.2
  539.9 9.9 %convolution_convert_fusion.7 = bf16[48,5280]{1,0:T(8,128)(2,1)S(1)} fusion(bf16[5280,768]{1,0:T(8,128)(2,1)} %get-tuple-element.843, bf16[48,5280]{1,0:T(8,128)(2,1)S(1)} %reshape.271, bf16[5280,768]{1,0:T(8,128)(2,1)} %get-tuple-element.842), kind=kOutput, calls=%fused_computation.clone.1 | convolution fusion | flops 779152896 | bytes 17233920 | tf_op jit(solution)/shard_map/while/body/eval_jaxpr/dot_general | solution.py:28
  559.4 10.7 %collective-permute-done.5 = bf16[12,5280]{1,0:T(8,128)(2,1)S(1)} collective-permute-done((bf16[12,5280]{1,0:T(8,128)(2,1)S(1)}, bf16[12,5280]{1,0:T(8,128)(2,1)S(1)}, u32[]{:S(2)}, u32[]{:S(2)}) %collective-permute-start.5) | collective-permute-done | bytes 126752 | tf_op jit(solution)/shard_map/while/body/eval_jaxpr/ppermute | solution.py:42
  585.0 5.4 collective-permute-done.1
  590.8 9.9 %convolution_convert_fusion.7 = bf16[48,5280]{1,0:T(8,128)(2,1)S(1)} fusion(bf16[5280,768]{1,0:T(8,128)(2,1)} %get-tuple-element.843, bf16[48,5280]{1,0:T(8,128)(2,1)S(1)} %reshape.271, bf16[5280,768]{1,0:T(8,128)(2,1)} %get-tuple-element.842), kind=kOutput, calls=%fused_computation.clone.1 | convolution fusion | flops 779152896 | bytes 17233920 | tf_op jit(solution)/shard_map/while/body/eval_jaxpr/dot_general | solution.py:28
  607.3 6.5 collective-permute-start.5
  616.9 7.9 %collective-permute-done.5 = bf16[12,5280]{1,0:T(8,128)(2,1)S(1)} collective-permute-done((bf16[12,5280]{1,0:T(8,128)(2,1)S(1)}, bf16[12,5280]{1,0:T(8,128)(2,1)S(1)}, u32[]{:S(2)}, u32[]{:S(2)}) %collective-permute-start.5) | collective-permute-done | bytes 126752 | tf_op jit(solution)/shard_map/while/body/eval_jaxpr/ppermute | solution.py:42
  624.8 9.3 %collective-permute-done.6 = bf16[12,5280]{1,0:T(8,128)(2,1)S(1)} collective-permute-done((bf16[12,5280]{1,0:T(8,128)(2,1)S(1)}, bf16[12,5280]{1,0:T(8,128)(2,1)S(1)}, u32[]{:S(2)}, u32[]{:S(2)}) %collective-permute-start.6) | collective-permute-done | bytes 126752 | tf_op jit(solution)/shard_map/while/body/eval_jaxpr/ppermute | solution.py:42
  649.3 9.9 %convolution_convert_fusion.7 = bf16[48,5280]{1,0:T(8,128)(2,1)S(1)} fusion(bf16[5280,768]{1,0:T(8,128)(2,1)} %get-tuple-element.843, bf16[48,5280]{1,0:T(8,128)(2,1)S(1)} %reshape.271, bf16[5280,768]{1,0:T(8,128)(2,1)} %get-tuple-element.842), kind=kOutput, calls=%fused_computation.clone.1 | convolution fusion | flops 779152896 | bytes 17233920 | tf_op jit(solution)/shard_map/while/body/eval_jaxpr/dot_general | solution.py:28
  659.5 5.0 collective-permute-start.4
  668.7 11.2 %collective-permute-done.5 = bf16[12,5280]{1,0:T(8,128)(2,1)S(1)} collective-permute-done((bf16[12,5280]{1,0:T(8,128)(2,1)S(1)}, bf16[12,5280]{1,0:T(8,128)(2,1)S(1)}, u32[]{:S(2)}, u32[]{:S(2)}) %collective-permute-start.5) | collective-permute-done | bytes 126752 | tf_op jit(solution)/shard_map/while/body/eval_jaxpr/ppermute | solution.py:42
  692.8 9.5 %collective-permute-done.1 = bf16[12,5280]{1,0:T(8,128)(2,1)S(1)} collective-permute-done((bf16[12,5280]{1,0:T(8,128)(2,1)S(1)}, bf16[12,5280]{1,0:T(8,128)(2,1)S(1)}, u32[]{:S(2)}, u32[]{:S(2)}) %collective-permute-start.1) | collective-permute-done | bytes 126752 | tf_op jit(solution)/shard_map/while/body/eval_jaxpr/ppermute | solution.py:13
  702.7 9.9 %convolution_convert_fusion.7 = bf16[48,5280]{1,0:T(8,128)(2,1)S(1)} fusion(bf16[5280,768]{1,0:T(8,128)(2,1)} %get-tuple-element.843, bf16[48,5280]{1,0:T(8,128)(2,1)S(1)} %reshape.271, bf16[5280,768]{1,0:T(8,128)(2,1)} %get-tuple-element.842), kind=kOutput, calls=%fused_computation.clone.1 | convolution fusion | flops 779152896 | bytes 17233920 | tf_op jit(solution)/shard_map/while/body/eval_jaxpr/dot_general | solution.py:28
  713.4 5.7 collective-permute-start.5
  730.0 7.7 %collective-permute-done.3 = bf16[44,5280]{1,0:T(8,128)(2,1)S(1)} collective-permute-done((bf16[44,5280]{1,0:T(8,128)(2,1)S(1)}, bf16[44,5280]{1,0:T(8,128)(2,1)S(1)}, u32[]{:S(2)}, u32[]{:S(2)}) %collective-permute-start.3) | collective-permute-done | bytes 464672 | tf_op jit(solution)/shard_map/while/body/eval_jaxpr/ppermute | solution.py:42
  (339 shorter events, 284.8 us)
Async XLA Ops:
  6.5 110.6 %all-gather.5.cloned.1.call-start = ((), (), s32[]{:S(2)}) async-start(), calls=%async_computation | async-start | bytes 17338368 | tf_op jit(solution)/shard_map/all_gather | solution.py:86
  34.7 21.7 %collective-permute-start.9 = (bf16[12,5280]{1,0:T(8,128)(2,1)S(1)}, bf16[12,5280]{1,0:T(8,128)(2,1)S(1)}, u32[]{:S(2)}, u32[]{:S(2)}) collective-permute-start(bf16[12,5280]{1,0:T(8,128)(2,1)S(1)} %get-tuple-element.626), channel_id=1, source_target_pairs={{1,0},{2,1},{3,2},{0,3},{5,4},{6,5},{7,6},{4,7},{9,8},{10,9},{11,1... | collective-permute-start | bytes 380168 | tf_op jit(solution)/shard_map/ppermute | solution.py:13
  40.2 21.0 %collective-permute-start.8 = (bf16[12,5280]{1,0:T(8,128)(2,1)S(1)}, bf16[12,5280]{1,0:T(8,128)(2,1)S(1)}, u32[]{:S(2)}, u32[]{:S(2)}) collective-permute-start(bf16[12,5280]{1,0:T(8,128)(2,1)S(1)} %get-tuple-element.627), channel_id=1, source_target_pairs={{2,0},{3,1},{0,2},{1,3},{6,4},{7,5},{4,6},{5,7},{10,8},{11,9},{8,1... | collective-permute-start | bytes 380168 | tf_op jit(solution)/shard_map/ppermute | solution.py:13
  41.6 19.6 %collective-permute-start.7 = (bf16[12,5280]{1,0:T(8,128)(2,1)S(1)}, bf16[12,5280]{1,0:T(8,128)(2,1)S(1)}, u32[]{:S(2)}, u32[]{:S(2)}) collective-permute-start(bf16[12,5280]{1,0:T(8,128)(2,1)S(1)} %get-tuple-element.628), channel_id=1, source_target_pairs={{3,0},{0,1},{1,2},{2,3},{7,4},{4,5},{5,6},{6,7},{11,8},{8,9},{9,10... | collective-permute-start | bytes 380168 | tf_op jit(solution)/shard_map/ppermute | solution.py:13
  154.1 28.1 %collective-permute-start.10 = (bf16[44,5280]{1,0:T(8,128)(2,1)S(1)}, bf16[44,5280]{1,0:T(8,128)(2,1)S(1)}, u32[]{:S(2)}, u32[]{:S(2)}) collective-permute-start(bf16[44,5280]{1,0:T(8,128)(2,1)S(1)} %pad_maximum_fusion.3), channel_id=1, source_target_pairs={{0,64},{1,65},{2,66},{3,67},{64,128},{65,129},{66,130},{67,131},{1... | collective-permute-start | bytes 1393928 | tf_op jit(solution)/shard_map/ppermute | solution.py:42
  156.1 15.1 %collective-permute-start.11 = (bf16[12,5280]{1,0:T(8,128)(2,1)S(1)}, bf16[12,5280]{1,0:T(8,128)(2,1)S(1)}, u32[]{:S(2)}, u32[]{:S(2)}) collective-permute-start(bf16[12,5280]{1,0:T(8,128)(2,1)S(1)} %get-tuple-element.623), channel_id=1, source_target_pairs={{0,67},{1,64},{2,65},{3,66},{64,131},{65,128},{66,129},{67,130},{1... | collective-permute-start | bytes 380168 | tf_op jit(solution)/shard_map/ppermute | solution.py:42
  161.1 18.3 %collective-permute-start.12 = (bf16[12,5280]{1,0:T(8,128)(2,1)S(1)}, bf16[12,5280]{1,0:T(8,128)(2,1)S(1)}, u32[]{:S(2)}, u32[]{:S(2)}) collective-permute-start(bf16[12,5280]{1,0:T(8,128)(2,1)S(1)} %get-tuple-element.622), channel_id=1, source_target_pairs={{0,66},{1,67},{2,64},{3,65},{64,130},{65,131},{66,128},{67,129},{1... | collective-permute-start | bytes 380168 | tf_op jit(solution)/shard_map/ppermute | solution.py:42
  163.7 18.5 %collective-permute-start.13 = (bf16[12,5280]{1,0:T(8,128)(2,1)S(1)}, bf16[12,5280]{1,0:T(8,128)(2,1)S(1)}, u32[]{:S(2)}, u32[]{:S(2)}) collective-permute-start(bf16[12,5280]{1,0:T(8,128)(2,1)S(1)} %get-tuple-element.621), channel_id=1, source_target_pairs={{0,65},{1,66},{2,67},{3,64},{64,129},{65,130},{66,131},{67,128},{1... | collective-permute-start | bytes 380168 | tf_op jit(solution)/shard_map/ppermute | solution.py:42
  188.2 16.8 %collective-permute-start.1 = (bf16[12,5280]{1,0:T(8,128)(2,1)S(1)}, bf16[12,5280]{1,0:T(8,128)(2,1)S(1)}, u32[]{:S(2)}, u32[]{:S(2)}) collective-permute-start(bf16[12,5280]{1,0:T(8,128)(2,1)S(1)} %get-tuple-element.763), channel_id=1, source_target_pairs={{2,0},{3,1},{0,2},{1,3},{6,4},{7,5},{4,6},{5,7},{10,8},{11,9},{8,1... | collective-permute-start | bytes 380168 | tf_op jit(solution)/shard_map/while/body/eval_jaxpr/ppermute | solution.py:13
  191.4 14.9 %collective-permute-start.2 = (bf16[12,5280]{1,0:T(8,128)(2,1)S(1)}, bf16[12,5280]{1,0:T(8,128)(2,1)S(1)}, u32[]{:S(2)}, u32[]{:S(2)}) collective-permute-start(bf16[12,5280]{1,0:T(8,128)(2,1)S(1)} %get-tuple-element.764), channel_id=1, source_target_pairs={{3,0},{0,1},{1,2},{2,3},{7,4},{4,5},{5,6},{6,7},{11,8},{8,9},{9,10... | collective-permute-start | bytes 380168 | tf_op jit(solution)/shard_map/while/body/eval_jaxpr/ppermute | solution.py:13
  216.8 26.0 %collective-permute-start.3 = (bf16[44,5280]{1,0:T(8,128)(2,1)S(1)}, bf16[44,5280]{1,0:T(8,128)(2,1)S(1)}, u32[]{:S(2)}, u32[]{:S(2)}) collective-permute-start(bf16[44,5280]{1,0:T(8,128)(2,1)S(1)} %pad_maximum_fusion.7), channel_id=1, source_target_pairs={{0,64},{1,65},{2,66},{3,67},{64,128},{65,129},{66,130},{67,131},{1... | collective-permute-start | bytes 1393928 | tf_op jit(solution)/shard_map/while/body/eval_jaxpr/ppermute | solution.py:42
  224.5 13.2 %collective-permute-start.6 = (bf16[12,5280]{1,0:T(8,128)(2,1)S(1)}, bf16[12,5280]{1,0:T(8,128)(2,1)S(1)}, u32[]{:S(2)}, u32[]{:S(2)}) collective-permute-start(bf16[12,5280]{1,0:T(8,128)(2,1)S(1)} %get-tuple-element.769), channel_id=1, source_target_pairs={{0,65},{1,66},{2,67},{3,64},{64,129},{65,130},{66,131},{67,128},{1... | collective-permute-start | bytes 380168 | tf_op jit(solution)/shard_map/while/body/eval_jaxpr/ppermute | solution.py:42
  249.3 13.3 %collective-permute-start.1 = (bf16[12,5280]{1,0:T(8,128)(2,1)S(1)}, bf16[12,5280]{1,0:T(8,128)(2,1)S(1)}, u32[]{:S(2)}, u32[]{:S(2)}) collective-permute-start(bf16[12,5280]{1,0:T(8,128)(2,1)S(1)} %get-tuple-element.763), channel_id=1, source_target_pairs={{2,0},{3,1},{0,2},{1,3},{6,4},{7,5},{4,6},{5,7},{10,8},{11,9},{8,1... | collective-permute-start | bytes 380168 | tf_op jit(solution)/shard_map/while/body/eval_jaxpr/ppermute | solution.py:13
  273.5 26.0 %collective-permute-start.3 = (bf16[44,5280]{1,0:T(8,128)(2,1)S(1)}, bf16[44,5280]{1,0:T(8,128)(2,1)S(1)}, u32[]{:S(2)}, u32[]{:S(2)}) collective-permute-start(bf16[44,5280]{1,0:T(8,128)(2,1)S(1)} %pad_maximum_fusion.7), channel_id=1, source_target_pairs={{0,64},{1,65},{2,66},{3,67},{64,128},{65,129},{66,130},{67,131},{1... | collective-permute-start | bytes 1393928 | tf_op jit(solution)/shard_map/while/body/eval_jaxpr/ppermute | solution.py:42
  276.8 19.4 %collective-permute-start.5 = (bf16[12,5280]{1,0:T(8,128)(2,1)S(1)}, bf16[12,5280]{1,0:T(8,128)(2,1)S(1)}, u32[]{:S(2)}, u32[]{:S(2)}) collective-permute-start(bf16[12,5280]{1,0:T(8,128)(2,1)S(1)} %get-tuple-element.768), channel_id=1, source_target_pairs={{0,66},{1,67},{2,64},{3,65},{64,130},{65,131},{66,128},{67,129},{1... | collective-permute-start | bytes 380168 | tf_op jit(solution)/shard_map/while/body/eval_jaxpr/ppermute | solution.py:42
  280.2 16.5 %collective-permute-start.6 = (bf16[12,5280]{1,0:T(8,128)(2,1)S(1)}, bf16[12,5280]{1,0:T(8,128)(2,1)S(1)}, u32[]{:S(2)}, u32[]{:S(2)}) collective-permute-start(bf16[12,5280]{1,0:T(8,128)(2,1)S(1)} %get-tuple-element.769), channel_id=1, source_target_pairs={{0,65},{1,66},{2,67},{3,64},{64,129},{65,130},{66,131},{67,128},{1... | collective-permute-start | bytes 380168 | tf_op jit(solution)/shard_map/while/body/eval_jaxpr/ppermute | solution.py:42
  304.2 15.5 %collective-permute-start.1 = (bf16[12,5280]{1,0:T(8,128)(2,1)S(1)}, bf16[12,5280]{1,0:T(8,128)(2,1)S(1)}, u32[]{:S(2)}, u32[]{:S(2)}) collective-permute-start(bf16[12,5280]{1,0:T(8,128)(2,1)S(1)} %get-tuple-element.763), channel_id=1, source_target_pairs={{2,0},{3,1},{0,2},{1,3},{6,4},{7,5},{4,6},{5,7},{10,8},{11,9},{8,1... | collective-permute-start | bytes 380168 | tf_op jit(solution)/shard_map/while/body/eval_jaxpr/ppermute | solution.py:13
  330.1 25.6 %collective-permute-start.3 = (bf16[44,5280]{1,0:T(8,128)(2,1)S(1)}, bf16[44,5280]{1,0:T(8,128)(2,1)S(1)}, u32[]{:S(2)}, u32[]{:S(2)}) collective-permute-start(bf16[44,5280]{1,0:T(8,128)(2,1)S(1)} %pad_maximum_fusion.7), channel_id=1, source_target_pairs={{0,64},{1,65},{2,66},{3,67},{64,128},{65,129},{66,130},{67,131},{1... | collective-permute-start | bytes 1393928 | tf_op jit(solution)/shard_map/while/body/eval_jaxpr/ppermute | solution.py:42
  330.4 20.6 %collective-permute-start.5 = (bf16[12,5280]{1,0:T(8,128)(2,1)S(1)}, bf16[12,5280]{1,0:T(8,128)(2,1)S(1)}, u32[]{:S(2)}, u32[]{:S(2)}) collective-permute-start(bf16[12,5280]{1,0:T(8,128)(2,1)S(1)} %get-tuple-element.768), channel_id=1, source_target_pairs={{0,66},{1,67},{2,64},{3,65},{64,130},{65,131},{66,128},{67,129},{1... | collective-permute-start | bytes 380168 | tf_op jit(solution)/shard_map/while/body/eval_jaxpr/ppermute | solution.py:42
  334.0 17.7 %collective-permute-start.6 = (bf16[12,5280]{1,0:T(8,128)(2,1)S(1)}, bf16[12,5280]{1,0:T(8,128)(2,1)S(1)}, u32[]{:S(2)}, u32[]{:S(2)}) collective-permute-start(bf16[12,5280]{1,0:T(8,128)(2,1)S(1)} %get-tuple-element.769), channel_id=1, source_target_pairs={{0,65},{1,66},{2,67},{3,64},{64,129},{65,130},{66,131},{67,128},{1... | collective-permute-start | bytes 380168 | tf_op jit(solution)/shard_map/while/body/eval_jaxpr/ppermute | solution.py:42
  359.9 14.4 %collective-permute-start.1 = (bf16[12,5280]{1,0:T(8,128)(2,1)S(1)}, bf16[12,5280]{1,0:T(8,128)(2,1)S(1)}, u32[]{:S(2)}, u32[]{:S(2)}) collective-permute-start(bf16[12,5280]{1,0:T(8,128)(2,1)S(1)} %get-tuple-element.763), channel_id=1, source_target_pairs={{2,0},{3,1},{0,2},{1,3},{6,4},{7,5},{4,6},{5,7},{10,8},{11,9},{8,1... | collective-permute-start | bytes 380168 | tf_op jit(solution)/shard_map/while/body/eval_jaxpr/ppermute | solution.py:13
  385.3 26.0 %collective-permute-start.3 = (bf16[44,5280]{1,0:T(8,128)(2,1)S(1)}, bf16[44,5280]{1,0:T(8,128)(2,1)S(1)}, u32[]{:S(2)}, u32[]{:S(2)}) collective-permute-start(bf16[44,5280]{1,0:T(8,128)(2,1)S(1)} %pad_maximum_fusion.7), channel_id=1, source_target_pairs={{0,64},{1,65},{2,66},{3,67},{64,128},{65,129},{66,130},{67,131},{1... | collective-permute-start | bytes 1393928 | tf_op jit(solution)/shard_map/while/body/eval_jaxpr/ppermute | solution.py:42
  385.5 19.1 %collective-permute-start.5 = (bf16[12,5280]{1,0:T(8,128)(2,1)S(1)}, bf16[12,5280]{1,0:T(8,128)(2,1)S(1)}, u32[]{:S(2)}, u32[]{:S(2)}) collective-permute-start(bf16[12,5280]{1,0:T(8,128)(2,1)S(1)} %get-tuple-element.768), channel_id=1, source_target_pairs={{0,66},{1,67},{2,64},{3,65},{64,130},{65,131},{66,128},{67,129},{1... | collective-permute-start | bytes 380168 | tf_op jit(solution)/shard_map/while/body/eval_jaxpr/ppermute | solution.py:42
  387.6 16.9 %collective-permute-start.6 = (bf16[12,5280]{1,0:T(8,128)(2,1)S(1)}, bf16[12,5280]{1,0:T(8,128)(2,1)S(1)}, u32[]{:S(2)}, u32[]{:S(2)}) collective-permute-start(bf16[12,5280]{1,0:T(8,128)(2,1)S(1)} %get-tuple-element.769), channel_id=1, source_target_pairs={{0,65},{1,66},{2,67},{3,64},{64,129},{65,130},{66,131},{67,128},{1... | collective-permute-start | bytes 380168 | tf_op jit(solution)/shard_map/while/body/eval_jaxpr/ppermute | solution.py:42
  437.5 26.8 %collective-permute-start.3 = (bf16[44,5280]{1,0:T(8,128)(2,1)S(1)}, bf16[44,5280]{1,0:T(8,128)(2,1)S(1)}, u32[]{:S(2)}, u32[]{:S(2)}) collective-permute-start(bf16[44,5280]{1,0:T(8,128)(2,1)S(1)} %pad_maximum_fusion.7), channel_id=1, source_target_pairs={{0,64},{1,65},{2,66},{3,67},{64,128},{65,129},{66,130},{67,131},{1... | collective-permute-start | bytes 1393928 | tf_op jit(solution)/shard_map/while/body/eval_jaxpr/ppermute | solution.py:42
  437.6 13.2 %collective-permute-start.4 = (bf16[12,5280]{1,0:T(8,128)(2,1)S(1)}, bf16[12,5280]{1,0:T(8,128)(2,1)S(1)}, u32[]{:S(2)}, u32[]{:S(2)}) collective-permute-start(bf16[12,5280]{1,0:T(8,128)(2,1)S(1)} %get-tuple-element.767), channel_id=1, source_target_pairs={{0,67},{1,64},{2,65},{3,66},{64,131},{65,128},{66,129},{67,130},{1... | collective-permute-start | bytes 380168 | tf_op jit(solution)/shard_map/while/body/eval_jaxpr/ppermute | solution.py:42
  441.6 21.5 %collective-permute-start.5 = (bf16[12,5280]{1,0:T(8,128)(2,1)S(1)}, bf16[12,5280]{1,0:T(8,128)(2,1)S(1)}, u32[]{:S(2)}, u32[]{:S(2)}) collective-permute-start(bf16[12,5280]{1,0:T(8,128)(2,1)S(1)} %get-tuple-element.768), channel_id=1, source_target_pairs={{0,66},{1,67},{2,64},{3,65},{64,130},{65,131},{66,128},{67,129},{1... | collective-permute-start | bytes 380168 | tf_op jit(solution)/shard_map/while/body/eval_jaxpr/ppermute | solution.py:42
  444.5 19.8 %collective-permute-start.6 = (bf16[12,5280]{1,0:T(8,128)(2,1)S(1)}, bf16[12,5280]{1,0:T(8,128)(2,1)S(1)}, u32[]{:S(2)}, u32[]{:S(2)}) collective-permute-start(bf16[12,5280]{1,0:T(8,128)(2,1)S(1)} %get-tuple-element.769), channel_id=1, source_target_pairs={{0,65},{1,66},{2,67},{3,64},{64,129},{65,130},{66,131},{67,128},{1... | collective-permute-start | bytes 380168 | tf_op jit(solution)/shard_map/while/body/eval_jaxpr/ppermute | solution.py:42
  469.8 15.9 %collective-permute-start.1 = (bf16[12,5280]{1,0:T(8,128)(2,1)S(1)}, bf16[12,5280]{1,0:T(8,128)(2,1)S(1)}, u32[]{:S(2)}, u32[]{:S(2)}) collective-permute-start(bf16[12,5280]{1,0:T(8,128)(2,1)S(1)} %get-tuple-element.763), channel_id=1, source_target_pairs={{2,0},{3,1},{0,2},{1,3},{6,4},{7,5},{4,6},{5,7},{10,8},{11,9},{8,1... | collective-permute-start | bytes 380168 | tf_op jit(solution)/shard_map/while/body/eval_jaxpr/ppermute | solution.py:13
  474.6 13.0 %collective-permute-start.2 = (bf16[12,5280]{1,0:T(8,128)(2,1)S(1)}, bf16[12,5280]{1,0:T(8,128)(2,1)S(1)}, u32[]{:S(2)}, u32[]{:S(2)}) collective-permute-start(bf16[12,5280]{1,0:T(8,128)(2,1)S(1)} %get-tuple-element.764), channel_id=1, source_target_pairs={{3,0},{0,1},{1,2},{2,3},{7,4},{4,5},{5,6},{6,7},{11,8},{8,9},{9,10... | collective-permute-start | bytes 380168 | tf_op jit(solution)/shard_map/while/body/eval_jaxpr/ppermute | solution.py:13
  498.1 18.9 %collective-permute-start.3 = (bf16[44,5280]{1,0:T(8,128)(2,1)S(1)}, bf16[44,5280]{1,0:T(8,128)(2,1)S(1)}, u32[]{:S(2)}, u32[]{:S(2)}) collective-permute-start(bf16[44,5280]{1,0:T(8,128)(2,1)S(1)} %pad_maximum_fusion.7), channel_id=1, source_target_pairs={{0,64},{1,65},{2,66},{3,67},{64,128},{65,129},{66,130},{67,131},{1... | collective-permute-start | bytes 1393928 | tf_op jit(solution)/shard_map/while/body/eval_jaxpr/ppermute | solution.py:42
  498.3 14.3 %collective-permute-start.5 = (bf16[12,5280]{1,0:T(8,128)(2,1)S(1)}, bf16[12,5280]{1,0:T(8,128)(2,1)S(1)}, u32[]{:S(2)}, u32[]{:S(2)}) collective-permute-start(bf16[12,5280]{1,0:T(8,128)(2,1)S(1)} %get-tuple-element.768), channel_id=1, source_target_pairs={{0,66},{1,67},{2,64},{3,65},{64,130},{65,131},{66,128},{67,129},{1... | collective-permute-start | bytes 380168 | tf_op jit(solution)/shard_map/while/body/eval_jaxpr/ppermute | solution.py:42
  498.3 15.9 %collective-permute-start.6 = (bf16[12,5280]{1,0:T(8,128)(2,1)S(1)}, bf16[12,5280]{1,0:T(8,128)(2,1)S(1)}, u32[]{:S(2)}, u32[]{:S(2)}) collective-permute-start(bf16[12,5280]{1,0:T(8,128)(2,1)S(1)} %get-tuple-element.769), channel_id=1, source_target_pairs={{0,65},{1,66},{2,67},{3,64},{64,129},{65,130},{66,131},{67,128},{1... | collective-permute-start | bytes 380168 | tf_op jit(solution)/shard_map/while/body/eval_jaxpr/ppermute | solution.py:42
  524.6 14.9 %collective-permute-start.2 = (bf16[12,5280]{1,0:T(8,128)(2,1)S(1)}, bf16[12,5280]{1,0:T(8,128)(2,1)S(1)}, u32[]{:S(2)}, u32[]{:S(2)}) collective-permute-start(bf16[12,5280]{1,0:T(8,128)(2,1)S(1)} %get-tuple-element.764), channel_id=1, source_target_pairs={{3,0},{0,1},{1,2},{2,3},{7,4},{4,5},{5,6},{6,7},{11,8},{8,9},{9,10... | collective-permute-start | bytes 380168 | tf_op jit(solution)/shard_map/while/body/eval_jaxpr/ppermute | solution.py:13
  550.0 22.0 %collective-permute-start.3 = (bf16[44,5280]{1,0:T(8,128)(2,1)S(1)}, bf16[44,5280]{1,0:T(8,128)(2,1)S(1)}, u32[]{:S(2)}, u32[]{:S(2)}) collective-permute-start(bf16[44,5280]{1,0:T(8,128)(2,1)S(1)} %pad_maximum_fusion.7), channel_id=1, source_target_pairs={{0,64},{1,65},{2,66},{3,67},{64,128},{65,129},{66,130},{67,131},{1... | collective-permute-start | bytes 1393928 | tf_op jit(solution)/shard_map/while/body/eval_jaxpr/ppermute | solution.py:42
  553.5 16.7 %collective-permute-start.5 = (bf16[12,5280]{1,0:T(8,128)(2,1)S(1)}, bf16[12,5280]{1,0:T(8,128)(2,1)S(1)}, u32[]{:S(2)}, u32[]{:S(2)}) collective-permute-start(bf16[12,5280]{1,0:T(8,128)(2,1)S(1)} %get-tuple-element.768), channel_id=1, source_target_pairs={{0,66},{1,67},{2,64},{3,65},{64,130},{65,131},{66,128},{67,129},{1... | collective-permute-start | bytes 380168 | tf_op jit(solution)/shard_map/while/body/eval_jaxpr/ppermute | solution.py:42
  556.5 13.6 %collective-permute-start.6 = (bf16[12,5280]{1,0:T(8,128)(2,1)S(1)}, bf16[12,5280]{1,0:T(8,128)(2,1)S(1)}, u32[]{:S(2)}, u32[]{:S(2)}) collective-permute-start(bf16[12,5280]{1,0:T(8,128)(2,1)S(1)} %get-tuple-element.769), channel_id=1, source_target_pairs={{0,65},{1,66},{2,67},{3,64},{64,129},{65,130},{66,131},{67,128},{1... | collective-permute-start | bytes 380168 | tf_op jit(solution)/shard_map/while/body/eval_jaxpr/ppermute | solution.py:42
  577.4 13.0 %collective-permute-start.1 = (bf16[12,5280]{1,0:T(8,128)(2,1)S(1)}, bf16[12,5280]{1,0:T(8,128)(2,1)S(1)}, u32[]{:S(2)}, u32[]{:S(2)}) collective-permute-start(bf16[12,5280]{1,0:T(8,128)(2,1)S(1)} %get-tuple-element.763), channel_id=1, source_target_pairs={{2,0},{3,1},{0,2},{1,3},{6,4},{7,5},{4,6},{5,7},{10,8},{11,9},{8,1... | collective-permute-start | bytes 380168 | tf_op jit(solution)/shard_map/while/body/eval_jaxpr/ppermute | solution.py:13
  600.9 33.3 %collective-permute-start.3 = (bf16[44,5280]{1,0:T(8,128)(2,1)S(1)}, bf16[44,5280]{1,0:T(8,128)(2,1)S(1)}, u32[]{:S(2)}, u32[]{:S(2)}) collective-permute-start(bf16[44,5280]{1,0:T(8,128)(2,1)S(1)} %pad_maximum_fusion.7), channel_id=1, source_target_pairs={{0,64},{1,65},{2,66},{3,67},{64,128},{65,129},{66,130},{67,131},{1... | collective-permute-start | bytes 1393928 | tf_op jit(solution)/shard_map/while/body/eval_jaxpr/ppermute | solution.py:42
  603.9 13.1 %collective-permute-start.4 = (bf16[12,5280]{1,0:T(8,128)(2,1)S(1)}, bf16[12,5280]{1,0:T(8,128)(2,1)S(1)}, u32[]{:S(2)}, u32[]{:S(2)}) collective-permute-start(bf16[12,5280]{1,0:T(8,128)(2,1)S(1)} %get-tuple-element.767), channel_id=1, source_target_pairs={{0,67},{1,64},{2,65},{3,66},{64,131},{65,128},{66,129},{67,130},{1... | collective-permute-start | bytes 380168 | tf_op jit(solution)/shard_map/while/body/eval_jaxpr/ppermute | solution.py:42
  607.3 17.6 %collective-permute-start.5 = (bf16[12,5280]{1,0:T(8,128)(2,1)S(1)}, bf16[12,5280]{1,0:T(8,128)(2,1)S(1)}, u32[]{:S(2)}, u32[]{:S(2)}) collective-permute-start(bf16[12,5280]{1,0:T(8,128)(2,1)S(1)} %get-tuple-element.768), channel_id=1, source_target_pairs={{0,66},{1,67},{2,64},{3,65},{64,130},{65,131},{66,128},{67,129},{1... | collective-permute-start | bytes 380168 | tf_op jit(solution)/shard_map/while/body/eval_jaxpr/ppermute | solution.py:42
  613.8 20.4 %collective-permute-start.6 = (bf16[12,5280]{1,0:T(8,128)(2,1)S(1)}, bf16[12,5280]{1,0:T(8,128)(2,1)S(1)}, u32[]{:S(2)}, u32[]{:S(2)}) collective-permute-start(bf16[12,5280]{1,0:T(8,128)(2,1)S(1)} %get-tuple-element.769), channel_id=1, source_target_pairs={{0,65},{1,66},{2,67},{3,64},{64,129},{65,130},{66,131},{67,128},{1... | collective-permute-start | bytes 380168 | tf_op jit(solution)/shard_map/while/body/eval_jaxpr/ppermute | solution.py:42
  659.4 22.9 %collective-permute-start.3 = (bf16[44,5280]{1,0:T(8,128)(2,1)S(1)}, bf16[44,5280]{1,0:T(8,128)(2,1)S(1)}, u32[]{:S(2)}, u32[]{:S(2)}) collective-permute-start(bf16[44,5280]{1,0:T(8,128)(2,1)S(1)} %pad_maximum_fusion.7), channel_id=1, source_target_pairs={{0,64},{1,65},{2,66},{3,67},{64,128},{65,129},{66,130},{67,131},{1... | collective-permute-start | bytes 1393928 | tf_op jit(solution)/shard_map/while/body/eval_jaxpr/ppermute | solution.py:42
  664.5 15.3 %collective-permute-start.5 = (bf16[12,5280]{1,0:T(8,128)(2,1)S(1)}, bf16[12,5280]{1,0:T(8,128)(2,1)S(1)}, u32[]{:S(2)}, u32[]{:S(2)}) collective-permute-start(bf16[12,5280]{1,0:T(8,128)(2,1)S(1)} %get-tuple-element.768), channel_id=1, source_target_pairs={{0,66},{1,67},{2,64},{3,65},{64,130},{65,131},{66,128},{67,129},{1... | collective-permute-start | bytes 380168 | tf_op jit(solution)/shard_map/while/body/eval_jaxpr/ppermute | solution.py:42
  665.6 16.7 %collective-permute-start.6 = (bf16[12,5280]{1,0:T(8,128)(2,1)S(1)}, bf16[12,5280]{1,0:T(8,128)(2,1)S(1)}, u32[]{:S(2)}, u32[]{:S(2)}) collective-permute-start(bf16[12,5280]{1,0:T(8,128)(2,1)S(1)} %get-tuple-element.769), channel_id=1, source_target_pairs={{0,65},{1,66},{2,67},{3,64},{64,129},{65,130},{66,131},{67,128},{1... | collective-permute-start | bytes 380168 | tf_op jit(solution)/shard_map/while/body/eval_jaxpr/ppermute | solution.py:42
  685.7 16.6 %collective-permute-start.1 = (bf16[12,5280]{1,0:T(8,128)(2,1)S(1)}, bf16[12,5280]{1,0:T(8,128)(2,1)S(1)}, u32[]{:S(2)}, u32[]{:S(2)}) collective-permute-start(bf16[12,5280]{1,0:T(8,128)(2,1)S(1)} %get-tuple-element.763), channel_id=1, source_target_pairs={{2,0},{3,1},{0,2},{1,3},{6,4},{7,5},{4,6},{5,7},{10,8},{11,9},{8,1... | collective-permute-start | bytes 380168 | tf_op jit(solution)/shard_map/while/body/eval_jaxpr/ppermute | solution.py:13
  712.8 24.9 %collective-permute-start.3 = (bf16[44,5280]{1,0:T(8,128)(2,1)S(1)}, bf16[44,5280]{1,0:T(8,128)(2,1)S(1)}, u32[]{:S(2)}, u32[]{:S(2)}) collective-permute-start(bf16[44,5280]{1,0:T(8,128)(2,1)S(1)} %pad_maximum_fusion.7), channel_id=1, source_target_pairs={{0,64},{1,65},{2,66},{3,67},{64,128},{65,129},{66,130},{67,131},{1... | collective-permute-start | bytes 1393928 | tf_op jit(solution)/shard_map/while/body/eval_jaxpr/ppermute | solution.py:42
  713.4 16.6 %collective-permute-start.5 = (bf16[12,5280]{1,0:T(8,128)(2,1)S(1)}, bf16[12,5280]{1,0:T(8,128)(2,1)S(1)}, u32[]{:S(2)}, u32[]{:S(2)}) collective-permute-start(bf16[12,5280]{1,0:T(8,128)(2,1)S(1)} %get-tuple-element.768), channel_id=1, source_target_pairs={{0,66},{1,67},{2,64},{3,65},{64,130},{65,131},{66,128},{67,129},{1... | collective-permute-start | bytes 380168 | tf_op jit(solution)/shard_map/while/body/eval_jaxpr/ppermute | solution.py:42
  (30 other events, 311.1 us)
Sparse Core Ops, SparseCore 0:
  9.2 107.9 all-gather.4

commit v11 on v10

--- a/solution.py
+++ b/solution.py
@@ -84,9 +84,20 @@
     rows = w_up.shape[2]
     pieces = jnp.concatenate([w_up[0, 0], jnp.swapaxes(w_down[0, 0], 0, 1)], axis=0)
     both = lax.all_gather(pieces, "dp", axis=0, tiled=False)
-    gains = lax.all_gather(norm_gain, "section", axis=0, tiled=True)
-    routers = lax.all_gather(router, "section", axis=0, tiled=True)
-    all_routes = lax.all_gather(routes, "section", axis=1, tiled=True)
+    width = norm_gain.shape[-1]
+    small = jnp.concatenate(
+        [
+            norm_gain.reshape(-1),
+            router.reshape(-1).astype(jnp.float32),
+            routes.reshape(-1).astype(jnp.float32),
+        ]
+    )
+    every = lax.all_gather(small, "section", axis=0, tiled=False)
+    gains = every[:, :width]
+    routers = every[:, width : width + router.size].reshape((-1,) + router.shape[1:])
+    routers = routers.astype(router.dtype)
+    all_routes = every[:, width + router.size :].reshape((-1, routes.shape[0]) + routes.shape[2:])
+    all_routes = jnp.swapaxes(all_routes, 0, 1).astype(routes.dtype)
     w_first = both[:, :rows].reshape(-1, both.shape[-1])
     w_second = both[:, rows:].reshape(-1, both.shape[-1])
     tokens = init_state.shape[1]

time: 747 us -> 783 us (1.048)
  the two profiles are of different devices: /device:TPU:32 before, /device:TPU:2 now
where the time goes in v11:
time: 783 us; the launch traced here: 781 us
  waiting for transfers between devices  401 us (51%)
  starting transfers between devices  175 us (22%)
  matrix products  137 us (17%)
  local copies, waits for them, and re-layouts  37.8 us (5%)
  between operations  15.8 us (2%)
  other arithmetic  12.4 us (2%)
    ppermute x44, waiting for transfers between devices, onward(): return lax.ppermute(block, ('section', 'expert'), route)  182 us
    ppermute x33, waiting for transfers between devices, shifted(): return lax.ppermute(block, axis, route)  138 us
    dot_general x11, matrix products, expert_rows(): lax.dot_general(hidden, w_second, (((1,), (1,)), ((), ())), preferred_ele...  108 us
    ppermute x44, starting transfers between devices, onward(): return lax.ppermute(block, ('section', 'expert'), route)  99.1 us
    ppermute x33, starting transfers between devices, shifted(): return lax.ppermute(block, axis, route)  76.2 us
    unnamed x3, waiting for transfers between devices  47.1 us
    all_gather x1, waiting for transfers between devices, body(): both = lax.all_gather(pieces, 'dp', axis=0, tiled=False)  34.6 us
    dot_general x11, matrix products, combine(): jnp.einsum('st,sd->td', places, flat_back, preferred_element_type=jnp.flo...  18.4 us
  transfers between devices with their start and end apart: 79, of which 60 were waited for; matrix products, arithmetic and copies ran while one was open for 1% of the time, Pallas kernels for 0%

profile of v11, /device:TPU:2, one launch (start us, length us, event | category | flops | bytes accessed | tf_op | source)
XLA Modules:
  0.0 781.0 jit_solution(13854610290778491778)
XLA Ops:
  17.4 47.0 %all-reduce.3.cloned.1.call-done = f32[106624]{0:T(1024)} async-done(((f32[106624]{0:T(1024)}), f32[106624]{0:T(1024)}) %all-reduce.3.cloned.1.call-update) | async-done | bytes 426512
  75.8 7.7 collective-permute-done.9
  84.6 34.6 %all-gather.5.cloned.1.call-done = bf16[16,660,768]{2,1,0:T(8,128)(2,1)} async-done(((bf16[1,660,768]{2,1,0:T(8,128)(2,1)}), bf16[16,660,768]{2,1,0:T(8,128)(2,1)}) %all-gather.5.cloned.1.call-update) | async-done | bytes 16220176 | tf_op jit(solution)/shard_map/all_gather | solution.py:86
  119.2 11.6 %fusion.125 = (bf16[16,330,768]{2,1,0:T(8,128)(2,1)}, bf16[16,330,768]{2,1,0:T(8,128)(2,1)}) fusion(bf16[16,660,768]{2,1,0:T(8,128)(2,1)} %all-gather.5.cloned.1.call-done), kind=kLoop, calls=%fused_computation.187 | loop fusion | bytes 32440320 | tf_op jit(solution)/shard_map/slice | solution.py:101
  130.7 7.6 reshape.268
  138.4 7.6 reshape.267
  146.0 9.9 %convolution_convert_fusion.2 = bf16[48,5280]{1,0:T(8,128)(2,1)S(1)} fusion(bf16[5280,768]{1,0:T(8,128)(2,1)} %reshape.268, bf16[48,5280]{1,0:T(8,128)(2,1)S(1)} %reshape.266, bf16[5280,768]{1,0:T(8,128)(2,1)} %reshape.267), kind=kOutput, calls=%fused_computation.88 | convolution fusion | flops 779152896 | bytes 17233920 | tf_op jit(solution)/shard_map/dot_general | solution.py:28
  172.9 7.2 collective-permute-done.12
  182.3 589.5 %while.24 = (s32[]{:T(128)}, bf16[44,5280]{1,0:T(8,128)(2,1)S(1)}, bf16[12,5280]{1,0:T(8,128)(2,1)S(1)}, bf16[12,5280]{1,0:T(8,128)(2,1)S(1)}, bf16[12,5280]{1,0...) while((s32[]{:T(128)}, bf16[44,5280]{1,0:T(8,128)(2,1)S(1)}, ...), condition=%wide.region_8.9_spmd, body=%wide.region_2.8_spmd.sunk | while | flops 821163456 | bytes 30935856 | solution.py:156
  193.5 9.2 %collective-permute-done = bf16[12,5280]{1,0:T(8,128)(2,1)S(1)} collective-permute-done((bf16[12,5280]{1,0:T(8,128)(2,1)S(1)}, bf16[12,5280]{1,0:T(8,128)(2,1)S(1)}, u32[]{:S(2)}, u32[]{:S(2)}) %collective-permute-start) | collective-permute-done | bytes 126752 | tf_op jit(solution)/shard_map/while/body/eval_jaxpr/ppermute | solution.py:13
  203.7 9.9 %convolution_convert_fusion.7 = bf16[48,5280]{1,0:T(8,128)(2,1)S(1)} fusion(bf16[5280,768]{1,0:T(8,128)(2,1)} %get-tuple-element.845, bf16[48,5280]{1,0:T(8,128)(2,1)S(1)} %reshape.297, bf16[5280,768]{1,0:T(8,128)(2,1)} %get-tuple-element.844), kind=kOutput, calls=%fused_computation.clone.1 | convolution fusion | flops 779152896 | bytes 17233920 | tf_op jit(solution)/shard_map/while/body/eval_jaxpr/dot_general | solution.py:28
  224.5 5.9 collective-permute-done.4
  249.2 8.7 %collective-permute-done.1 = bf16[12,5280]{1,0:T(8,128)(2,1)S(1)} collective-permute-done((bf16[12,5280]{1,0:T(8,128)(2,1)S(1)}, bf16[12,5280]{1,0:T(8,128)(2,1)S(1)}, u32[]{:S(2)}, u32[]{:S(2)}) %collective-permute-start.1) | collective-permute-done | bytes 126752 | tf_op jit(solution)/shard_map/while/body/eval_jaxpr/ppermute | solution.py:13
  259.9 9.9 %convolution_convert_fusion.7 = bf16[48,5280]{1,0:T(8,128)(2,1)S(1)} fusion(bf16[5280,768]{1,0:T(8,128)(2,1)} %get-tuple-element.845, bf16[48,5280]{1,0:T(8,128)(2,1)S(1)} %reshape.297, bf16[5280,768]{1,0:T(8,128)(2,1)} %get-tuple-element.844), kind=kOutput, calls=%fused_computation.clone.1 | convolution fusion | flops 779152896 | bytes 17233920 | tf_op jit(solution)/shard_map/while/body/eval_jaxpr/dot_general | solution.py:28
  279.6 11.4 %collective-permute-done.4 = bf16[12,5280]{1,0:T(8,128)(2,1)S(1)} collective-permute-done((bf16[12,5280]{1,0:T(8,128)(2,1)S(1)}, bf16[12,5280]{1,0:T(8,128)(2,1)S(1)}, u32[]{:S(2)}, u32[]{:S(2)}) %collective-permute-start.4) | collective-permute-done | bytes 126752 | tf_op jit(solution)/shard_map/while/body/eval_jaxpr/ppermute | solution.py:42
  291.1 7.5 collective-permute-done.6
  302.0 5.9 collective-permute-start.1
  308.0 11.0 %collective-permute-done = bf16[12,5280]{1,0:T(8,128)(2,1)S(1)} collective-permute-done((bf16[12,5280]{1,0:T(8,128)(2,1)S(1)}, bf16[12,5280]{1,0:T(8,128)(2,1)S(1)}, u32[]{:S(2)}, u32[]{:S(2)}) %collective-permute-start) | collective-permute-done | bytes 126752 | tf_op jit(solution)/shard_map/while/body/eval_jaxpr/ppermute | solution.py:13
  324.0 9.9 %convolution_convert_fusion.7 = bf16[48,5280]{1,0:T(8,128)(2,1)S(1)} fusion(bf16[5280,768]{1,0:T(8,128)(2,1)} %get-tuple-element.845, bf16[48,5280]{1,0:T(8,128)(2,1)S(1)} %reshape.297, bf16[5280,768]{1,0:T(8,128)(2,1)} %get-tuple-element.844), kind=kOutput, calls=%fused_computation.clone.1 | convolution fusion | flops 779152896 | bytes 17233920 | tf_op jit(solution)/shard_map/while/body/eval_jaxpr/dot_general | solution.py:28
  340.2 13.0 %collective-permute-done.4 = bf16[12,5280]{1,0:T(8,128)(2,1)S(1)} collective-permute-done((bf16[12,5280]{1,0:T(8,128)(2,1)S(1)}, bf16[12,5280]{1,0:T(8,128)(2,1)S(1)}, u32[]{:S(2)}, u32[]{:S(2)}) %collective-permute-start.4) | collective-permute-done | bytes 126752 | tf_op jit(solution)/shard_map/while/body/eval_jaxpr/ppermute | solution.py:42
  365.0 8.0 %collective-permute-done.1 = bf16[12,5280]{1,0:T(8,128)(2,1)S(1)} collective-permute-done((bf16[12,5280]{1,0:T(8,128)(2,1)S(1)}, bf16[12,5280]{1,0:T(8,128)(2,1)S(1)}, u32[]{:S(2)}, u32[]{:S(2)}) %collective-permute-start.1) | collective-permute-done | bytes 126752 | tf_op jit(solution)/shard_map/while/body/eval_jaxpr/ppermute | solution.py:13
  374.6 9.9 %convolution_convert_fusion.7 = bf16[48,5280]{1,0:T(8,128)(2,1)S(1)} fusion(bf16[5280,768]{1,0:T(8,128)(2,1)} %get-tuple-element.845, bf16[48,5280]{1,0:T(8,128)(2,1)S(1)} %reshape.297, bf16[5280,768]{1,0:T(8,128)(2,1)} %get-tuple-element.844), kind=kOutput, calls=%fused_computation.clone.1 | convolution fusion | flops 779152896 | bytes 17233920 | tf_op jit(solution)/shard_map/while/body/eval_jaxpr/dot_general | solution.py:28
  384.7 7.4 collective-permute-start.3
  393.5 6.0 collective-permute-start.5
  399.5 10.3 %collective-permute-done.4 = bf16[12,5280]{1,0:T(8,128)(2,1)S(1)} collective-permute-done((bf16[12,5280]{1,0:T(8,128)(2,1)S(1)}, bf16[12,5280]{1,0:T(8,128)(2,1)S(1)}, u32[]{:S(2)}, u32[]{:S(2)}) %collective-permute-start.4) | collective-permute-done | bytes 126752 | tf_op jit(solution)/shard_map/while/body/eval_jaxpr/ppermute | solution.py:42
  425.5 7.5 collective-permute-done
  439.1 9.9 %convolution_convert_fusion.7 = bf16[48,5280]{1,0:T(8,128)(2,1)S(1)} fusion(bf16[5280,768]{1,0:T(8,128)(2,1)} %get-tuple-element.845, bf16[48,5280]{1,0:T(8,128)(2,1)S(1)} %reshape.297, bf16[5280,768]{1,0:T(8,128)(2,1)} %get-tuple-element.844), kind=kOutput, calls=%fused_computation.clone.1 | convolution fusion | flops 779152896 | bytes 17233920 | tf_op jit(solution)/shard_map/while/body/eval_jaxpr/dot_general | solution.py:28
  458.8 11.4 %collective-permute-done.4 = bf16[12,5280]{1,0:T(8,128)(2,1)S(1)} collective-permute-done((bf16[12,5280]{1,0:T(8,128)(2,1)S(1)}, bf16[12,5280]{1,0:T(8,128)(2,1)S(1)}, u32[]{:S(2)}, u32[]{:S(2)}) %collective-permute-start.4) | collective-permute-done | bytes 126752 | tf_op jit(solution)/shard_map/while/body/eval_jaxpr/ppermute | solution.py:42
  498.5 9.9 %convolution_convert_fusion.7 = bf16[48,5280]{1,0:T(8,128)(2,1)S(1)} fusion(bf16[5280,768]{1,0:T(8,128)(2,1)} %get-tuple-element.845, bf16[48,5280]{1,0:T(8,128)(2,1)S(1)} %reshape.297, bf16[5280,768]{1,0:T(8,128)(2,1)} %get-tuple-element.844), kind=kOutput, calls=%fused_computation.clone.1 | convolution fusion | flops 779152896 | bytes 17233920 | tf_op jit(solution)/shard_map/while/body/eval_jaxpr/dot_general | solution.py:28
  518.1 8.5 %collective-permute-done.4 = bf16[12,5280]{1,0:T(8,128)(2,1)S(1)} collective-permute-done((bf16[12,5280]{1,0:T(8,128)(2,1)S(1)}, bf16[12,5280]{1,0:T(8,128)(2,1)S(1)}, u32[]{:S(2)}, u32[]{:S(2)}) %collective-permute-start.4) | collective-permute-done | bytes 126752 | tf_op jit(solution)/shard_map/while/body/eval_jaxpr/ppermute | solution.py:42
  543.0 10.1 %collective-permute-done = bf16[12,5280]{1,0:T(8,128)(2,1)S(1)} collective-permute-done((bf16[12,5280]{1,0:T(8,128)(2,1)S(1)}, bf16[12,5280]{1,0:T(8,128)(2,1)S(1)}, u32[]{:S(2)}, u32[]{:S(2)}) %collective-permute-start) | collective-permute-done | bytes 126752 | tf_op jit(solution)/shard_map/while/body/eval_jaxpr/ppermute | solution.py:13
  558.3 9.9 %convolution_convert_fusion.7 = bf16[48,5280]{1,0:T(8,128)(2,1)S(1)} fusion(bf16[5280,768]{1,0:T(8,128)(2,1)} %get-tuple-element.845, bf16[48,5280]{1,0:T(8,128)(2,1)S(1)} %reshape.297, bf16[5280,768]{1,0:T(8,128)(2,1)} %get-tuple-element.844), kind=kOutput, calls=%fused_computation.clone.1 | convolution fusion | flops 779152896 | bytes 17233920 | tf_op jit(solution)/shard_map/while/body/eval_jaxpr/dot_general | solution.py:28
  570.0 6.4 collective-permute-start.5
  576.4 13.9 %collective-permute-done.4 = bf16[12,5280]{1,0:T(8,128)(2,1)S(1)} collective-permute-done((bf16[12,5280]{1,0:T(8,128)(2,1)S(1)}, bf16[12,5280]{1,0:T(8,128)(2,1)S(1)}, u32[]{:S(2)}, u32[]{:S(2)}) %collective-permute-start.4) | collective-permute-done | bytes 126752 | tf_op jit(solution)/shard_map/while/body/eval_jaxpr/ppermute | solution.py:42
  596.6 6.0 collective-permute-start.1
  603.6 6.3 collective-permute-done.1
  609.9 6.9 collective-permute-done.2
  617.2 9.9 %convolution_convert_fusion.7 = bf16[48,5280]{1,0:T(8,128)(2,1)S(1)} fusion(bf16[5280,768]{1,0:T(8,128)(2,1)} %get-tuple-element.845, bf16[48,5280]{1,0:T(8,128)(2,1)S(1)} %reshape.297, bf16[5280,768]{1,0:T(8,128)(2,1)} %get-tuple-element.844), kind=kOutput, calls=%fused_computation.clone.1 | convolution fusion | flops 779152896 | bytes 17233920 | tf_op jit(solution)/shard_map/while/body/eval_jaxpr/dot_general | solution.py:28
  634.0 12.8 %collective-permute-done.4 = bf16[12,5280]{1,0:T(8,128)(2,1)S(1)} collective-permute-done((bf16[12,5280]{1,0:T(8,128)(2,1)S(1)}, bf16[12,5280]{1,0:T(8,128)(2,1)S(1)}, u32[]{:S(2)}, u32[]{:S(2)}) %collective-permute-start.4) | collective-permute-done | bytes 126752 | tf_op jit(solution)/shard_map/while/body/eval_jaxpr/ppermute | solution.py:42
  662.1 8.5 %collective-permute-done = bf16[12,5280]{1,0:T(8,128)(2,1)S(1)} collective-permute-done((bf16[12,5280]{1,0:T(8,128)(2,1)S(1)}, bf16[12,5280]{1,0:T(8,128)(2,1)S(1)}, u32[]{:S(2)}, u32[]{:S(2)}) %collective-permute-start) | collective-permute-done | bytes 126752 | tf_op jit(solution)/shard_map/while/body/eval_jaxpr/ppermute | solution.py:13
  670.6 6.6 collective-permute-done.2
  677.6 9.9 %convolution_convert_fusion.7 = bf16[48,5280]{1,0:T(8,128)(2,1)S(1)} fusion(bf16[5280,768]{1,0:T(8,128)(2,1)} %get-tuple-element.845, bf16[48,5280]{1,0:T(8,128)(2,1)S(1)} %reshape.297, bf16[5280,768]{1,0:T(8,128)(2,1)} %get-tuple-element.844), kind=kOutput, calls=%fused_computation.clone.1 | convolution fusion | flops 779152896 | bytes 17233920 | tf_op jit(solution)/shard_map/while/body/eval_jaxpr/dot_general | solution.py:28
  689.0 5.9 collective-permute-start.5
  694.9 9.6 %collective-permute-done.4 = bf16[12,5280]{1,0:T(8,128)(2,1)S(1)} collective-permute-done((bf16[12,5280]{1,0:T(8,128)(2,1)S(1)}, bf16[12,5280]{1,0:T(8,128)(2,1)S(1)}, u32[]{:S(2)}, u32[]{:S(2)}) %collective-permute-start.4) | collective-permute-done | bytes 126752 | tf_op jit(solution)/shard_map/while/body/eval_jaxpr/ppermute | solution.py:42
  714.5 8.5 %collective-permute-start.1 = (bf16[12,5280]{1,0:T(8,128)(2,1)S(1)}, bf16[12,5280]{1,0:T(8,128)(2,1)S(1)}, u32[]{:S(2)}, u32[]{:S(2)}) collective-permute-start(bf16[12,5280]{1,0:T(8,128)(2,1)S(1)} %get-tuple-element.765), channel_id=1, source_target_pairs={{2,0},{3,1},{0,2},{1,3},{6,4},{7,5},{4,6},{5,7},{10,8},{11,9},{8,1... | collective-permute-start | bytes 380168 | tf_op jit(solution)/shard_map/while/body/eval_jaxpr/ppermute | solution.py:13
  722.9 9.3 %collective-permute-done = bf16[12,5280]{1,0:T(8,128)(2,1)S(1)} collective-permute-done((bf16[12,5280]{1,0:T(8,128)(2,1)S(1)}, bf16[12,5280]{1,0:T(8,128)(2,1)S(1)}, u32[]{:S(2)}, u32[]{:S(2)}) %collective-permute-start) | collective-permute-done | bytes 126752 | tf_op jit(solution)/shard_map/while/body/eval_jaxpr/ppermute | solution.py:13
  738.0 9.9 %convolution_convert_fusion.7 = bf16[48,5280]{1,0:T(8,128)(2,1)S(1)} fusion(bf16[5280,768]{1,0:T(8,128)(2,1)} %get-tuple-element.845, bf16[48,5280]{1,0:T(8,128)(2,1)S(1)} %reshape.297, bf16[5280,768]{1,0:T(8,128)(2,1)} %get-tuple-element.844), kind=kOutput, calls=%fused_computation.clone.1 | convolution fusion | flops 779152896 | bytes 17233920 | tf_op jit(solution)/shard_map/while/body/eval_jaxpr/dot_general | solution.py:28
  753.9 15.9 %collective-permute-done.4 = bf16[12,5280]{1,0:T(8,128)(2,1)S(1)} collective-permute-done((bf16[12,5280]{1,0:T(8,128)(2,1)S(1)}, bf16[12,5280]{1,0:T(8,128)(2,1)S(1)}, u32[]{:S(2)}, u32[]{:S(2)}) %collective-permute-start.4) | collective-permute-done | bytes 126752 | tf_op jit(solution)/shard_map/while/body/eval_jaxpr/ppermute | solution.py:42
  (356 shorter events, 273.4 us)
Async XLA Ops:
  7.4 57.1 %all-reduce.3.cloned.1.call-start = ((), (), s32[]{:S(2)}) async-start(), calls=%async_computation | async-start | bytes 860160
  13.6 105.6 %all-gather.5.cloned.1.call-start = ((), (), s32[]{:S(2)}) async-start(), calls=%async_computation.1 | async-start | bytes 17338368 | tf_op jit(solution)/shard_map/all_gather | solution.py:86
  66.7 16.8 %collective-permute-start.9 = (bf16[12,5280]{1,0:T(8,128)(2,1)S(1)}, bf16[12,5280]{1,0:T(8,128)(2,1)S(1)}, u32[]{:S(2)}, u32[]{:S(2)}) collective-permute-start(bf16[12,5280]{1,0:T(8,128)(2,1)S(1)} %get-tuple-element.628), channel_id=1, source_target_pairs={{1,0},{2,1},{3,2},{0,3},{5,4},{6,5},{7,6},{4,7},{9,8},{10,9},{11,1... | collective-permute-start | bytes 380168 | tf_op jit(solution)/shard_map/ppermute | solution.py:13
  156.1 26.3 %collective-permute-start.10 = (bf16[44,5280]{1,0:T(8,128)(2,1)S(1)}, bf16[44,5280]{1,0:T(8,128)(2,1)S(1)}, u32[]{:S(2)}, u32[]{:S(2)}) collective-permute-start(bf16[44,5280]{1,0:T(8,128)(2,1)S(1)} %pad_maximum_fusion.3), channel_id=1, source_target_pairs={{0,64},{1,65},{2,66},{3,67},{64,128},{65,129},{66,130},{67,131},{1... | collective-permute-start | bytes 1393928 | tf_op jit(solution)/shard_map/ppermute | solution.py:42
  162.0 18.1 %collective-permute-start.12 = (bf16[12,5280]{1,0:T(8,128)(2,1)S(1)}, bf16[12,5280]{1,0:T(8,128)(2,1)S(1)}, u32[]{:S(2)}, u32[]{:S(2)}) collective-permute-start(bf16[12,5280]{1,0:T(8,128)(2,1)S(1)} %get-tuple-element.624), channel_id=1, source_target_pairs={{0,66},{1,67},{2,64},{3,65},{64,130},{65,131},{66,128},{67,129},{1... | collective-permute-start | bytes 380168 | tf_op jit(solution)/shard_map/ppermute | solution.py:42
  185.7 17.0 %collective-permute-start = (bf16[12,5280]{1,0:T(8,128)(2,1)S(1)}, bf16[12,5280]{1,0:T(8,128)(2,1)S(1)}, u32[]{:S(2)}, u32[]{:S(2)}) collective-permute-start(bf16[12,5280]{1,0:T(8,128)(2,1)S(1)} %get-tuple-element.764), channel_id=1, source_target_pairs={{1,0},{2,1},{3,2},{0,3},{5,4},{6,5},{7,6},{4,7},{9,8},{10,9},{11,1... | collective-permute-start | bytes 380168 | tf_op jit(solution)/shard_map/while/body/eval_jaxpr/ppermute | solution.py:13
  213.8 24.9 %collective-permute-start.3 = (bf16[44,5280]{1,0:T(8,128)(2,1)S(1)}, bf16[44,5280]{1,0:T(8,128)(2,1)S(1)}, u32[]{:S(2)}, u32[]{:S(2)}) collective-permute-start(bf16[44,5280]{1,0:T(8,128)(2,1)S(1)} %pad_maximum_fusion.7), channel_id=1, source_target_pairs={{0,64},{1,65},{2,66},{3,67},{64,128},{65,129},{66,130},{67,131},{1... | collective-permute-start | bytes 1393928 | tf_op jit(solution)/shard_map/while/body/eval_jaxpr/ppermute | solution.py:42
  214.7 15.6 %collective-permute-start.4 = (bf16[12,5280]{1,0:T(8,128)(2,1)S(1)}, bf16[12,5280]{1,0:T(8,128)(2,1)S(1)}, u32[]{:S(2)}, u32[]{:S(2)}) collective-permute-start(bf16[12,5280]{1,0:T(8,128)(2,1)S(1)} %get-tuple-element.769), channel_id=1, source_target_pairs={{0,67},{1,64},{2,65},{3,66},{64,131},{65,128},{66,129},{67,130},{1... | collective-permute-start | bytes 380168 | tf_op jit(solution)/shard_map/while/body/eval_jaxpr/ppermute | solution.py:42
  219.6 15.7 %collective-permute-start.5 = (bf16[12,5280]{1,0:T(8,128)(2,1)S(1)}, bf16[12,5280]{1,0:T(8,128)(2,1)S(1)}, u32[]{:S(2)}, u32[]{:S(2)}) collective-permute-start(bf16[12,5280]{1,0:T(8,128)(2,1)S(1)} %get-tuple-element.770), channel_id=1, source_target_pairs={{0,66},{1,67},{2,64},{3,65},{64,130},{65,131},{66,128},{67,129},{1... | collective-permute-start | bytes 380168 | tf_op jit(solution)/shard_map/while/body/eval_jaxpr/ppermute | solution.py:42
  221.5 16.0 %collective-permute-start.6 = (bf16[12,5280]{1,0:T(8,128)(2,1)S(1)}, bf16[12,5280]{1,0:T(8,128)(2,1)S(1)}, u32[]{:S(2)}, u32[]{:S(2)}) collective-permute-start(bf16[12,5280]{1,0:T(8,128)(2,1)S(1)} %get-tuple-element.771), channel_id=1, source_target_pairs={{0,65},{1,66},{2,67},{3,64},{64,129},{65,130},{66,131},{67,128},{1... | collective-permute-start | bytes 380168 | tf_op jit(solution)/shard_map/while/body/eval_jaxpr/ppermute | solution.py:42
  270.0 28.6 %collective-permute-start.3 = (bf16[44,5280]{1,0:T(8,128)(2,1)S(1)}, bf16[44,5280]{1,0:T(8,128)(2,1)S(1)}, u32[]{:S(2)}, u32[]{:S(2)}) collective-permute-start(bf16[44,5280]{1,0:T(8,128)(2,1)S(1)} %pad_maximum_fusion.7), channel_id=1, source_target_pairs={{0,64},{1,65},{2,66},{3,67},{64,128},{65,129},{66,130},{67,131},{1... | collective-permute-start | bytes 1393928 | tf_op jit(solution)/shard_map/while/body/eval_jaxpr/ppermute | solution.py:42
  275.3 15.7 %collective-permute-start.4 = (bf16[12,5280]{1,0:T(8,128)(2,1)S(1)}, bf16[12,5280]{1,0:T(8,128)(2,1)S(1)}, u32[]{:S(2)}, u32[]{:S(2)}) collective-permute-start(bf16[12,5280]{1,0:T(8,128)(2,1)S(1)} %get-tuple-element.769), channel_id=1, source_target_pairs={{0,67},{1,64},{2,65},{3,66},{64,131},{65,128},{66,129},{67,130},{1... | collective-permute-start | bytes 380168 | tf_op jit(solution)/shard_map/while/body/eval_jaxpr/ppermute | solution.py:42
  275.3 15.7 %collective-permute-start.5 = (bf16[12,5280]{1,0:T(8,128)(2,1)S(1)}, bf16[12,5280]{1,0:T(8,128)(2,1)S(1)}, u32[]{:S(2)}, u32[]{:S(2)}) collective-permute-start(bf16[12,5280]{1,0:T(8,128)(2,1)S(1)} %get-tuple-element.770), channel_id=1, source_target_pairs={{0,66},{1,67},{2,64},{3,65},{64,130},{65,131},{66,128},{67,129},{1... | collective-permute-start | bytes 380168 | tf_op jit(solution)/shard_map/while/body/eval_jaxpr/ppermute | solution.py:42
  277.2 21.4 %collective-permute-start.6 = (bf16[12,5280]{1,0:T(8,128)(2,1)S(1)}, bf16[12,5280]{1,0:T(8,128)(2,1)S(1)}, u32[]{:S(2)}, u32[]{:S(2)}) collective-permute-start(bf16[12,5280]{1,0:T(8,128)(2,1)S(1)} %get-tuple-element.771), channel_id=1, source_target_pairs={{0,65},{1,66},{2,67},{3,64},{64,129},{65,130},{66,131},{67,128},{1... | collective-permute-start | bytes 380168 | tf_op jit(solution)/shard_map/while/body/eval_jaxpr/ppermute | solution.py:42
  301.9 17.0 %collective-permute-start = (bf16[12,5280]{1,0:T(8,128)(2,1)S(1)}, bf16[12,5280]{1,0:T(8,128)(2,1)S(1)}, u32[]{:S(2)}, u32[]{:S(2)}) collective-permute-start(bf16[12,5280]{1,0:T(8,128)(2,1)S(1)} %get-tuple-element.764), channel_id=1, source_target_pairs={{1,0},{2,1},{3,2},{0,3},{5,4},{6,5},{7,6},{4,7},{9,8},{10,9},{11,1... | collective-permute-start | bytes 380168 | tf_op jit(solution)/shard_map/while/body/eval_jaxpr/ppermute | solution.py:13
  302.0 16.9 %collective-permute-start.1 = (bf16[12,5280]{1,0:T(8,128)(2,1)S(1)}, bf16[12,5280]{1,0:T(8,128)(2,1)S(1)}, u32[]{:S(2)}, u32[]{:S(2)}) collective-permute-start(bf16[12,5280]{1,0:T(8,128)(2,1)S(1)} %get-tuple-element.765), channel_id=1, source_target_pairs={{2,0},{3,1},{0,2},{1,3},{6,4},{7,5},{4,6},{5,7},{10,8},{11,9},{8,1... | collective-permute-start | bytes 380168 | tf_op jit(solution)/shard_map/while/body/eval_jaxpr/ppermute | solution.py:13
  307.9 15.6 %collective-permute-start.2 = (bf16[12,5280]{1,0:T(8,128)(2,1)S(1)}, bf16[12,5280]{1,0:T(8,128)(2,1)S(1)}, u32[]{:S(2)}, u32[]{:S(2)}) collective-permute-start(bf16[12,5280]{1,0:T(8,128)(2,1)S(1)} %get-tuple-element.766), channel_id=1, source_target_pairs={{3,0},{0,1},{1,2},{2,3},{7,4},{4,5},{5,6},{6,7},{11,8},{8,9},{9,10... | collective-permute-start | bytes 380168 | tf_op jit(solution)/shard_map/while/body/eval_jaxpr/ppermute | solution.py:13
  334.0 21.3 %collective-permute-start.3 = (bf16[44,5280]{1,0:T(8,128)(2,1)S(1)}, bf16[44,5280]{1,0:T(8,128)(2,1)S(1)}, u32[]{:S(2)}, u32[]{:S(2)}) collective-permute-start(bf16[44,5280]{1,0:T(8,128)(2,1)S(1)} %pad_maximum_fusion.7), channel_id=1, source_target_pairs={{0,64},{1,65},{2,66},{3,67},{64,128},{65,129},{66,130},{67,131},{1... | collective-permute-start | bytes 1393928 | tf_op jit(solution)/shard_map/while/body/eval_jaxpr/ppermute | solution.py:42
  334.7 18.5 %collective-permute-start.4 = (bf16[12,5280]{1,0:T(8,128)(2,1)S(1)}, bf16[12,5280]{1,0:T(8,128)(2,1)S(1)}, u32[]{:S(2)}, u32[]{:S(2)}) collective-permute-start(bf16[12,5280]{1,0:T(8,128)(2,1)S(1)} %get-tuple-element.769), channel_id=1, source_target_pairs={{0,67},{1,64},{2,65},{3,66},{64,131},{65,128},{66,129},{67,130},{1... | collective-permute-start | bytes 380168 | tf_op jit(solution)/shard_map/while/body/eval_jaxpr/ppermute | solution.py:42
  334.7 18.5 %collective-permute-start.5 = (bf16[12,5280]{1,0:T(8,128)(2,1)S(1)}, bf16[12,5280]{1,0:T(8,128)(2,1)S(1)}, u32[]{:S(2)}, u32[]{:S(2)}) collective-permute-start(bf16[12,5280]{1,0:T(8,128)(2,1)S(1)} %get-tuple-element.770), channel_id=1, source_target_pairs={{0,66},{1,67},{2,64},{3,65},{64,130},{65,131},{66,128},{67,129},{1... | collective-permute-start | bytes 380168 | tf_op jit(solution)/shard_map/while/body/eval_jaxpr/ppermute | solution.py:42
  384.7 31.5 %collective-permute-start.3 = (bf16[44,5280]{1,0:T(8,128)(2,1)S(1)}, bf16[44,5280]{1,0:T(8,128)(2,1)S(1)}, u32[]{:S(2)}, u32[]{:S(2)}) collective-permute-start(bf16[44,5280]{1,0:T(8,128)(2,1)S(1)} %pad_maximum_fusion.7), channel_id=1, source_target_pairs={{0,64},{1,65},{2,66},{3,67},{64,128},{65,129},{66,130},{67,131},{1... | collective-permute-start | bytes 1393928 | tf_op jit(solution)/shard_map/while/body/eval_jaxpr/ppermute | solution.py:42
  392.1 17.8 %collective-permute-start.4 = (bf16[12,5280]{1,0:T(8,128)(2,1)S(1)}, bf16[12,5280]{1,0:T(8,128)(2,1)S(1)}, u32[]{:S(2)}, u32[]{:S(2)}) collective-permute-start(bf16[12,5280]{1,0:T(8,128)(2,1)S(1)} %get-tuple-element.769), channel_id=1, source_target_pairs={{0,67},{1,64},{2,65},{3,66},{64,131},{65,128},{66,129},{67,130},{1... | collective-permute-start | bytes 380168 | tf_op jit(solution)/shard_map/while/body/eval_jaxpr/ppermute | solution.py:42
  393.5 17.1 %collective-permute-start.5 = (bf16[12,5280]{1,0:T(8,128)(2,1)S(1)}, bf16[12,5280]{1,0:T(8,128)(2,1)S(1)}, u32[]{:S(2)}, u32[]{:S(2)}) collective-permute-start(bf16[12,5280]{1,0:T(8,128)(2,1)S(1)} %get-tuple-element.770), channel_id=1, source_target_pairs={{0,66},{1,67},{2,64},{3,65},{64,130},{65,131},{66,128},{67,129},{1... | collective-permute-start | bytes 380168 | tf_op jit(solution)/shard_map/while/body/eval_jaxpr/ppermute | solution.py:42
  399.5 16.7 %collective-permute-start.6 = (bf16[12,5280]{1,0:T(8,128)(2,1)S(1)}, bf16[12,5280]{1,0:T(8,128)(2,1)S(1)}, u32[]{:S(2)}, u32[]{:S(2)}) collective-permute-start(bf16[12,5280]{1,0:T(8,128)(2,1)S(1)} %get-tuple-element.771), channel_id=1, source_target_pairs={{0,65},{1,66},{2,67},{3,64},{64,129},{65,130},{66,131},{67,128},{1... | collective-permute-start | bytes 380168 | tf_op jit(solution)/shard_map/while/body/eval_jaxpr/ppermute | solution.py:42
  449.2 26.9 %collective-permute-start.3 = (bf16[44,5280]{1,0:T(8,128)(2,1)S(1)}, bf16[44,5280]{1,0:T(8,128)(2,1)S(1)}, u32[]{:S(2)}, u32[]{:S(2)}) collective-permute-start(bf16[44,5280]{1,0:T(8,128)(2,1)S(1)} %pad_maximum_fusion.7), channel_id=1, source_target_pairs={{0,64},{1,65},{2,66},{3,67},{64,128},{65,129},{66,130},{67,131},{1... | collective-permute-start | bytes 1393928 | tf_op jit(solution)/shard_map/while/body/eval_jaxpr/ppermute | solution.py:42
  451.5 18.7 %collective-permute-start.4 = (bf16[12,5280]{1,0:T(8,128)(2,1)S(1)}, bf16[12,5280]{1,0:T(8,128)(2,1)S(1)}, u32[]{:S(2)}, u32[]{:S(2)}) collective-permute-start(bf16[12,5280]{1,0:T(8,128)(2,1)S(1)} %get-tuple-element.769), channel_id=1, source_target_pairs={{0,67},{1,64},{2,65},{3,66},{64,131},{65,128},{66,129},{67,130},{1... | collective-permute-start | bytes 380168 | tf_op jit(solution)/shard_map/while/body/eval_jaxpr/ppermute | solution.py:42
  453.6 19.8 %collective-permute-start.5 = (bf16[12,5280]{1,0:T(8,128)(2,1)S(1)}, bf16[12,5280]{1,0:T(8,128)(2,1)S(1)}, u32[]{:S(2)}, u32[]{:S(2)}) collective-permute-start(bf16[12,5280]{1,0:T(8,128)(2,1)S(1)} %get-tuple-element.770), channel_id=1, source_target_pairs={{0,66},{1,67},{2,64},{3,65},{64,130},{65,131},{66,128},{67,129},{1... | collective-permute-start | bytes 380168 | tf_op jit(solution)/shard_map/while/body/eval_jaxpr/ppermute | solution.py:42
  458.8 17.3 %collective-permute-start.6 = (bf16[12,5280]{1,0:T(8,128)(2,1)S(1)}, bf16[12,5280]{1,0:T(8,128)(2,1)S(1)}, u32[]{:S(2)}, u32[]{:S(2)}) collective-permute-start(bf16[12,5280]{1,0:T(8,128)(2,1)S(1)} %get-tuple-element.771), channel_id=1, source_target_pairs={{0,65},{1,66},{2,67},{3,64},{64,129},{65,130},{66,131},{67,128},{1... | collective-permute-start | bytes 380168 | tf_op jit(solution)/shard_map/while/body/eval_jaxpr/ppermute | solution.py:42
  508.5 25.7 %collective-permute-start.3 = (bf16[44,5280]{1,0:T(8,128)(2,1)S(1)}, bf16[44,5280]{1,0:T(8,128)(2,1)S(1)}, u32[]{:S(2)}, u32[]{:S(2)}) collective-permute-start(bf16[44,5280]{1,0:T(8,128)(2,1)S(1)} %pad_maximum_fusion.7), channel_id=1, source_target_pairs={{0,64},{1,65},{2,66},{3,67},{64,128},{65,129},{66,130},{67,131},{1... | collective-permute-start | bytes 1393928 | tf_op jit(solution)/shard_map/while/body/eval_jaxpr/ppermute | solution.py:42
  510.2 16.5 %collective-permute-start.4 = (bf16[12,5280]{1,0:T(8,128)(2,1)S(1)}, bf16[12,5280]{1,0:T(8,128)(2,1)S(1)}, u32[]{:S(2)}, u32[]{:S(2)}) collective-permute-start(bf16[12,5280]{1,0:T(8,128)(2,1)S(1)} %get-tuple-element.769), channel_id=1, source_target_pairs={{0,67},{1,64},{2,65},{3,66},{64,131},{65,128},{66,129},{67,130},{1... | collective-permute-start | bytes 380168 | tf_op jit(solution)/shard_map/while/body/eval_jaxpr/ppermute | solution.py:42
  513.0 17.5 %collective-permute-start.5 = (bf16[12,5280]{1,0:T(8,128)(2,1)S(1)}, bf16[12,5280]{1,0:T(8,128)(2,1)S(1)}, u32[]{:S(2)}, u32[]{:S(2)}) collective-permute-start(bf16[12,5280]{1,0:T(8,128)(2,1)S(1)} %get-tuple-element.770), channel_id=1, source_target_pairs={{0,66},{1,67},{2,64},{3,65},{64,130},{65,131},{66,128},{67,129},{1... | collective-permute-start | bytes 380168 | tf_op jit(solution)/shard_map/while/body/eval_jaxpr/ppermute | solution.py:42
  568.4 24.8 %collective-permute-start.3 = (bf16[44,5280]{1,0:T(8,128)(2,1)S(1)}, bf16[44,5280]{1,0:T(8,128)(2,1)S(1)}, u32[]{:S(2)}, u32[]{:S(2)}) collective-permute-start(bf16[44,5280]{1,0:T(8,128)(2,1)S(1)} %pad_maximum_fusion.7), channel_id=1, source_target_pairs={{0,64},{1,65},{2,66},{3,67},{64,128},{65,129},{66,130},{67,131},{1... | collective-permute-start | bytes 1393928 | tf_op jit(solution)/shard_map/while/body/eval_jaxpr/ppermute | solution.py:42
  570.0 20.3 %collective-permute-start.4 = (bf16[12,5280]{1,0:T(8,128)(2,1)S(1)}, bf16[12,5280]{1,0:T(8,128)(2,1)S(1)}, u32[]{:S(2)}, u32[]{:S(2)}) collective-permute-start(bf16[12,5280]{1,0:T(8,128)(2,1)S(1)} %get-tuple-element.769), channel_id=1, source_target_pairs={{0,67},{1,64},{2,65},{3,66},{64,131},{65,128},{66,129},{67,130},{1... | collective-permute-start | bytes 380168 | tf_op jit(solution)/shard_map/while/body/eval_jaxpr/ppermute | solution.py:42
  570.0 20.3 %collective-permute-start.5 = (bf16[12,5280]{1,0:T(8,128)(2,1)S(1)}, bf16[12,5280]{1,0:T(8,128)(2,1)S(1)}, u32[]{:S(2)}, u32[]{:S(2)}) collective-permute-start(bf16[12,5280]{1,0:T(8,128)(2,1)S(1)} %get-tuple-element.770), channel_id=1, source_target_pairs={{0,66},{1,67},{2,64},{3,65},{64,130},{65,131},{66,128},{67,129},{1... | collective-permute-start | bytes 380168 | tf_op jit(solution)/shard_map/while/body/eval_jaxpr/ppermute | solution.py:42
  576.4 16.7 %collective-permute-start.6 = (bf16[12,5280]{1,0:T(8,128)(2,1)S(1)}, bf16[12,5280]{1,0:T(8,128)(2,1)S(1)}, u32[]{:S(2)}, u32[]{:S(2)}) collective-permute-start(bf16[12,5280]{1,0:T(8,128)(2,1)S(1)} %get-tuple-element.771), channel_id=1, source_target_pairs={{0,65},{1,66},{2,67},{3,64},{64,129},{65,130},{66,131},{67,128},{1... | collective-permute-start | bytes 380168 | tf_op jit(solution)/shard_map/while/body/eval_jaxpr/ppermute | solution.py:42
  627.2 25.2 %collective-permute-start.3 = (bf16[44,5280]{1,0:T(8,128)(2,1)S(1)}, bf16[44,5280]{1,0:T(8,128)(2,1)S(1)}, u32[]{:S(2)}, u32[]{:S(2)}) collective-permute-start(bf16[44,5280]{1,0:T(8,128)(2,1)S(1)} %pad_maximum_fusion.7), channel_id=1, source_target_pairs={{0,64},{1,65},{2,66},{3,67},{64,128},{65,129},{66,130},{67,131},{1... | collective-permute-start | bytes 1393928 | tf_op jit(solution)/shard_map/while/body/eval_jaxpr/ppermute | solution.py:42
  629.3 17.5 %collective-permute-start.4 = (bf16[12,5280]{1,0:T(8,128)(2,1)S(1)}, bf16[12,5280]{1,0:T(8,128)(2,1)S(1)}, u32[]{:S(2)}, u32[]{:S(2)}) collective-permute-start(bf16[12,5280]{1,0:T(8,128)(2,1)S(1)} %get-tuple-element.769), channel_id=1, source_target_pairs={{0,67},{1,64},{2,65},{3,66},{64,131},{65,128},{66,129},{67,130},{1... | collective-permute-start | bytes 380168 | tf_op jit(solution)/shard_map/while/body/eval_jaxpr/ppermute | solution.py:42
  629.3 19.0 %collective-permute-start.5 = (bf16[12,5280]{1,0:T(8,128)(2,1)S(1)}, bf16[12,5280]{1,0:T(8,128)(2,1)S(1)}, u32[]{:S(2)}, u32[]{:S(2)}) collective-permute-start(bf16[12,5280]{1,0:T(8,128)(2,1)S(1)} %get-tuple-element.770), channel_id=1, source_target_pairs={{0,66},{1,67},{2,64},{3,65},{64,130},{65,131},{66,128},{67,129},{1... | collective-permute-start | bytes 380168 | tf_op jit(solution)/shard_map/while/body/eval_jaxpr/ppermute | solution.py:42
  634.0 18.4 %collective-permute-start.6 = (bf16[12,5280]{1,0:T(8,128)(2,1)S(1)}, bf16[12,5280]{1,0:T(8,128)(2,1)S(1)}, u32[]{:S(2)}, u32[]{:S(2)}) collective-permute-start(bf16[12,5280]{1,0:T(8,128)(2,1)S(1)} %get-tuple-element.771), channel_id=1, source_target_pairs={{0,65},{1,66},{2,67},{3,64},{64,129},{65,130},{66,131},{67,128},{1... | collective-permute-start | bytes 380168 | tf_op jit(solution)/shard_map/while/body/eval_jaxpr/ppermute | solution.py:42
  687.6 22.1 %collective-permute-start.3 = (bf16[44,5280]{1,0:T(8,128)(2,1)S(1)}, bf16[44,5280]{1,0:T(8,128)(2,1)S(1)}, u32[]{:S(2)}, u32[]{:S(2)}) collective-permute-start(bf16[44,5280]{1,0:T(8,128)(2,1)S(1)} %pad_maximum_fusion.7), channel_id=1, source_target_pairs={{0,64},{1,65},{2,66},{3,67},{64,128},{65,129},{66,130},{67,131},{1... | collective-permute-start | bytes 1393928 | tf_op jit(solution)/shard_map/while/body/eval_jaxpr/ppermute | solution.py:42
  688.4 16.1 %collective-permute-start.4 = (bf16[12,5280]{1,0:T(8,128)(2,1)S(1)}, bf16[12,5280]{1,0:T(8,128)(2,1)S(1)}, u32[]{:S(2)}, u32[]{:S(2)}) collective-permute-start(bf16[12,5280]{1,0:T(8,128)(2,1)S(1)} %get-tuple-element.769), channel_id=1, source_target_pairs={{0,67},{1,64},{2,65},{3,66},{64,131},{65,128},{66,129},{67,130},{1... | collective-permute-start | bytes 380168 | tf_op jit(solution)/shard_map/while/body/eval_jaxpr/ppermute | solution.py:42
  689.0 16.3 %collective-permute-start.5 = (bf16[12,5280]{1,0:T(8,128)(2,1)S(1)}, bf16[12,5280]{1,0:T(8,128)(2,1)S(1)}, u32[]{:S(2)}, u32[]{:S(2)}) collective-permute-start(bf16[12,5280]{1,0:T(8,128)(2,1)S(1)} %get-tuple-element.770), channel_id=1, source_target_pairs={{0,66},{1,67},{2,64},{3,65},{64,130},{65,131},{66,128},{67,129},{1... | collective-permute-start | bytes 380168 | tf_op jit(solution)/shard_map/while/body/eval_jaxpr/ppermute | solution.py:42
  713.1 19.1 %collective-permute-start = (bf16[12,5280]{1,0:T(8,128)(2,1)S(1)}, bf16[12,5280]{1,0:T(8,128)(2,1)S(1)}, u32[]{:S(2)}, u32[]{:S(2)}) collective-permute-start(bf16[12,5280]{1,0:T(8,128)(2,1)S(1)} %get-tuple-element.764), channel_id=1, source_target_pairs={{1,0},{2,1},{3,2},{0,3},{5,4},{6,5},{7,6},{4,7},{9,8},{10,9},{11,1... | collective-permute-start | bytes 380168 | tf_op jit(solution)/shard_map/while/body/eval_jaxpr/ppermute | solution.py:13
  714.5 17.8 %collective-permute-start.1 = (bf16[12,5280]{1,0:T(8,128)(2,1)S(1)}, bf16[12,5280]{1,0:T(8,128)(2,1)S(1)}, u32[]{:S(2)}, u32[]{:S(2)}) collective-permute-start(bf16[12,5280]{1,0:T(8,128)(2,1)S(1)} %get-tuple-element.765), channel_id=1, source_target_pairs={{2,0},{3,1},{0,2},{1,3},{6,4},{7,5},{4,6},{5,7},{10,8},{11,9},{8,1... | collective-permute-start | bytes 380168 | tf_op jit(solution)/shard_map/while/body/eval_jaxpr/ppermute | solution.py:13
  748.1 23.8 %collective-permute-start.3 = (bf16[44,5280]{1,0:T(8,128)(2,1)S(1)}, bf16[44,5280]{1,0:T(8,128)(2,1)S(1)}, u32[]{:S(2)}, u32[]{:S(2)}) collective-permute-start(bf16[44,5280]{1,0:T(8,128)(2,1)S(1)} %pad_maximum_fusion.7), channel_id=1, source_target_pairs={{0,64},{1,65},{2,66},{3,67},{64,128},{65,129},{66,130},{67,131},{1... | collective-permute-start | bytes 1393928 | tf_op jit(solution)/shard_map/while/body/eval_jaxpr/ppermute | solution.py:42
  748.1 21.6 %collective-permute-start.4 = (bf16[12,5280]{1,0:T(8,128)(2,1)S(1)}, bf16[12,5280]{1,0:T(8,128)(2,1)S(1)}, u32[]{:S(2)}, u32[]{:S(2)}) collective-permute-start(bf16[12,5280]{1,0:T(8,128)(2,1)S(1)} %get-tuple-element.769), channel_id=1, source_target_pairs={{0,67},{1,64},{2,65},{3,66},{64,131},{65,128},{66,129},{67,130},{1... | collective-permute-start | bytes 380168 | tf_op jit(solution)/shard_map/while/body/eval_jaxpr/ppermute | solution.py:42
  748.2 21.5 %collective-permute-start.5 = (bf16[12,5280]{1,0:T(8,128)(2,1)S(1)}, bf16[12,5280]{1,0:T(8,128)(2,1)S(1)}, u32[]{:S(2)}, u32[]{:S(2)}) collective-permute-start(bf16[12,5280]{1,0:T(8,128)(2,1)S(1)} %get-tuple-element.770), channel_id=1, source_target_pairs={{0,66},{1,67},{2,64},{3,65},{64,130},{65,131},{66,128},{67,129},{1... | collective-permute-start | bytes 380168 | tf_op jit(solution)/shard_map/while/body/eval_jaxpr/ppermute | solution.py:42
  753.9 18.0 %collective-permute-start.6 = (bf16[12,5280]{1,0:T(8,128)(2,1)S(1)}, bf16[12,5280]{1,0:T(8,128)(2,1)S(1)}, u32[]{:S(2)}, u32[]{:S(2)}) collective-permute-start(bf16[12,5280]{1,0:T(8,128)(2,1)S(1)} %get-tuple-element.771), channel_id=1, source_target_pairs={{0,65},{1,66},{2,67},{3,64},{64,129},{65,130},{66,131},{67,128},{1... | collective-permute-start | bytes 380168 | tf_op jit(solution)/shard_map/while/body/eval_jaxpr/ppermute | solution.py:42
  (32 other events, 394.7 us)
Sparse Core Ops, SparseCore 0:
  13.7 50.6 all-reduce.2
Sparse Core Ops, SparseCore 1:
  16.0 103.1 all-gather.4

commit v12 on v10

--- a/solution.py
+++ b/solution.py
@@ -21,12 +21,14 @@
 
 def expert_rows(item_rows, w_first, w_second):
     extent = item_rows.shape
-    flat_rows = item_rows.reshape(-1, extent[-1])
-    hidden = jax.nn.gelu(jnp.dot(flat_rows, w_first, preferred_element_type=jnp.float32)).astype(
-        jnp.bfloat16
-    )
+    split_rows = item_rows.reshape((-1,) + w_first.shape[:2])
+    hidden = jax.nn.gelu(
+        lax.dot_general(
+            split_rows, w_first, (((1, 2), (0, 1)), ((), ())), preferred_element_type=jnp.float32
+        )
+    ).astype(jnp.bfloat16)
     result = lax.dot_general(
-        hidden, w_second, (((1,), (1,)), ((), ())), preferred_element_type=jnp.float32
+        hidden, w_second, (((1,), (2,)), ((), ())), preferred_element_type=jnp.float32
     ).astype(jnp.bfloat16)
     return result.reshape(extent)
 
@@ -87,8 +89,8 @@
     gains = lax.all_gather(norm_gain, "section", axis=0, tiled=True)
     routers = lax.all_gather(router, "section", axis=0, tiled=True)
     all_routes = lax.all_gather(routes, "section", axis=1, tiled=True)
-    w_first = both[:, :rows].reshape(-1, both.shape[-1])
-    w_second = both[:, rows:].reshape(-1, both.shape[-1])
+    w_first = both[:, :rows]
+    w_second = both[:, rows:]
     tokens = init_state.shape[1]
     active_span = sections * RECUR
     total_steps = active_span + sections - 1

time: 747 us -> 745 us (level)
  the two profiles are of different devices: /device:TPU:32 before, /device:TPU:38 now
where the time goes in v12:
time: 745 us
  waiting for transfers between devices  335 us (45%)
  starting transfers between devices  171 us (23%)
  matrix products  140 us (19%)
  local copies, waits for them, and re-layouts  37 us (5%)
  blocking collectives  35.8 us (5%)
  between operations  13.6 us (2%)
  other arithmetic  10.7 us (1%)
    ppermute x44, waiting for transfers between devices, onward(): return lax.ppermute(block, ('section', 'expert'), route)  164 us
    ppermute x33, waiting for transfers between devices, shifted(): return lax.ppermute(block, axis, route)  116 us
    dot_general x11, matrix products, expert_rows(): lax.dot_general(hidden, w_second, (((1,), (2,)), ((), ())), preferred_ele...  112 us
    ppermute x44, starting transfers between devices, onward(): return lax.ppermute(block, ('section', 'expert'), route)  96.7 us
    ppermute x33, starting transfers between devices, shifted(): return lax.ppermute(block, axis, route)  74.2 us
    all_gather x1, waiting for transfers between devices, body(): both = lax.all_gather(pieces, 'dp', axis=0, tiled=False)  54.2 us
    dot_general x11, matrix products, combine(): jnp.einsum('st,sd->td', places, flat_back, preferred_element_type=jnp.flo...  18.3 us
  transfers between devices with their start and end apart: 78, of which 62 were waited for; matrix products, arithmetic and copies ran while one was open for 3% of the time, Pallas kernels for 0%

profile of v12, /device:TPU:38, one launch (start us, length us, event | category | flops | bytes accessed | tf_op | source)
XLA Modules:
  0.0 744.9 jit_solution(6507586609584986386)
XLA Ops:
  9.0 11.4 %all_gather.15 = s32[2,4,4,32,1]{3,4,2,1,0:T(1,128)S(1)} all-gather(s32[2,1,4,32,1]{3,4,2,1,0:T(1,128)} %param.11), channel_id=1, replica_groups=mesh['section'=4,'dp'=16,'expert'=4] {'section'}, dimensions={1}, use_global_device_ids=true | all-gather | bytes 5120 | tf_op jit(solution)/shard_map/all_gather | solution.py:91
  20.4 12.1 %all-gather.1 = f32[4,1,5280]{2,1,0:T(1,128)S(1)} all-gather(f32[1,1,5280]{2,1,0:T(1,128)} %bitcast.105), channel_id=1, replica_groups=mesh['section'=4,'dp'=16,'expert'=4] {'section'}, dimensions={0}, use_global_device_ids=true | all-gather | bytes 105600 | tf_op jit(solution)/shard_map/all_gather | solution.py:89
  45.3 12.3 %all_gather.19 = bf16[4,4,5280]{2,1,0:T(4,128)(2,1)S(1)} all-gather(bf16[1,4,5280]{2,1,0:T(4,128)(2,1)} %param.13), channel_id=1, replica_groups=mesh['section'=4,'dp'=16,'expert'=4] {'section'}, dimensions={0}, use_global_device_ids=true | all-gather | bytes 211200 | tf_op jit(solution)/shard_map/all_gather | solution.py:90
  63.3 54.2 %all-gather.5.cloned.1.call-done = bf16[16,660,768]{2,1,0:T(8,128)(2,1)} async-done(((bf16[1,660,768]{2,1,0:T(8,128)(2,1)}), bf16[16,660,768]{2,1,0:T(8,128)(2,1)}) %all-gather.5.cloned.1.call-update) | async-done | bytes 16220176 | tf_op jit(solution)/shard_map/all_gather | solution.py:88
  117.5 10.2 %convolution_convert_fusion.3 = bf16[48,16,330]{2,0,1:T(8,128)(2,1)S(1)} fusion(bf16[48,16,330]{2,1,0:T(8,128)(2,1)S(1)} %reshape.243, bf16[16,660,768]{2,1,0:T(8,128)(2,1)} %all-gather.5.cloned.1.call-done), kind=kOutput, calls=%fused_computation.97 | convolution fusion | flops 779152896 | bytes 17528832 | tf_op jit(solution)/shard_map/dot_general | solution.py:30
  130.0 5.1 collective-permute-start.11
  141.1 11.5 %fusion.144 = (bf16[16,330,768]{2,1,0:T(8,128)(2,1)}, bf16[16,330,768]{2,1,0:T(8,128)(2,1)}) fusion(bf16[16,660,768]{2,1,0:T(8,128)(2,1)} %all-gather.5.cloned.1.call-done), kind=kLoop, calls=%fused_computation.191 | loop fusion | bytes 32440320 | tf_op jit(solution)/shard_map/slice | solution.py:93
  156.5 579.8 %while.24 = (s32[]{:T(128)}, bf16[44,5280]{1,0:T(8,128)(2,1)S(1)}, bf16[12,5280]{1,0:T(8,128)(2,1)S(1)}, bf16[12,5280]{1,0:T(8,128)(2,1)S(1)}, bf16[12,5280]{1,0...) while((s32[]{:T(128)}, bf16[44,5280]{1,0:T(8,128)(2,1)S(1)}, ...), condition=%wide.region_8.9_spmd, body=%wide.region_2.8_spmd.sunk | while | flops 821163456 | bytes 32963368 | solution.py:147
  171.3 6.7 collective-permute-done.1
  180.9 10.1 %convolution_convert_fusion.7 = bf16[48,16,330]{2,0,1:T(8,128)(2,1)S(1)} fusion(bf16[16,330,768]{2,1,0:T(8,128)(2,1)} %get-tuple-element.843, bf16[16,330,768]{2,1,0:T(8,128)(2,1)} %get-tuple-element.842, bf16[48,16,330]{2,1,0:T(8,128)(2,1)S(1)} %reshape.267), kind=kOutput, calls=%fused_computation.5.clone.1 | convolution fusion | flops 779152896 | bytes 17233920 | tf_op jit(solution)/shard_map/while/body/eval_jaxpr/dot_general | solution.py:30
  204.0 9.0 %collective-permute-done.5 = bf16[12,5280]{1,0:T(8,128)(2,1)S(1)} collective-permute-done((bf16[12,5280]{1,0:T(8,128)(2,1)S(1)}, bf16[12,5280]{1,0:T(8,128)(2,1)S(1)}, u32[]{:S(2)}, u32[]{:S(2)}) %collective-permute-start.5) | collective-permute-done | bytes 126752 | tf_op jit(solution)/shard_map/while/body/eval_jaxpr/ppermute | solution.py:44
  229.6 7.8 %collective-permute-done.1 = bf16[12,5280]{1,0:T(8,128)(2,1)S(1)} collective-permute-done((bf16[12,5280]{1,0:T(8,128)(2,1)S(1)}, bf16[12,5280]{1,0:T(8,128)(2,1)S(1)}, u32[]{:S(2)}, u32[]{:S(2)}) %collective-permute-start.1) | collective-permute-done | bytes 126752 | tf_op jit(solution)/shard_map/while/body/eval_jaxpr/ppermute | solution.py:13
  239.1 10.1 %convolution_convert_fusion.7 = bf16[48,16,330]{2,0,1:T(8,128)(2,1)S(1)} fusion(bf16[16,330,768]{2,1,0:T(8,128)(2,1)} %get-tuple-element.843, bf16[16,330,768]{2,1,0:T(8,128)(2,1)} %get-tuple-element.842, bf16[48,16,330]{2,1,0:T(8,128)(2,1)S(1)} %reshape.267), kind=kOutput, calls=%fused_computation.5.clone.1 | convolution fusion | flops 779152896 | bytes 17233920 | tf_op jit(solution)/shard_map/while/body/eval_jaxpr/dot_general | solution.py:30
  252.2 4.8 collective-permute-start.5
  260.6 12.4 %collective-permute-done.5 = bf16[12,5280]{1,0:T(8,128)(2,1)S(1)} collective-permute-done((bf16[12,5280]{1,0:T(8,128)(2,1)S(1)}, bf16[12,5280]{1,0:T(8,128)(2,1)S(1)}, u32[]{:S(2)}, u32[]{:S(2)}) %collective-permute-start.5) | collective-permute-done | bytes 126752 | tf_op jit(solution)/shard_map/while/body/eval_jaxpr/ppermute | solution.py:44
  280.4 4.7 collective-permute-start.1
  288.4 7.5 %collective-permute-done.1 = bf16[12,5280]{1,0:T(8,128)(2,1)S(1)} collective-permute-done((bf16[12,5280]{1,0:T(8,128)(2,1)S(1)}, bf16[12,5280]{1,0:T(8,128)(2,1)S(1)}, u32[]{:S(2)}, u32[]{:S(2)}) %collective-permute-start.1) | collective-permute-done | bytes 126752 | tf_op jit(solution)/shard_map/while/body/eval_jaxpr/ppermute | solution.py:13
  297.0 10.1 %convolution_convert_fusion.7 = bf16[48,16,330]{2,0,1:T(8,128)(2,1)S(1)} fusion(bf16[16,330,768]{2,1,0:T(8,128)(2,1)} %get-tuple-element.843, bf16[16,330,768]{2,1,0:T(8,128)(2,1)} %get-tuple-element.842, bf16[48,16,330]{2,1,0:T(8,128)(2,1)S(1)} %reshape.267), kind=kOutput, calls=%fused_computation.5.clone.1 | convolution fusion | flops 779152896 | bytes 17233920 | tf_op jit(solution)/shard_map/while/body/eval_jaxpr/dot_general | solution.py:30
  318.6 10.1 %collective-permute-done.5 = bf16[12,5280]{1,0:T(8,128)(2,1)S(1)} collective-permute-done((bf16[12,5280]{1,0:T(8,128)(2,1)S(1)}, bf16[12,5280]{1,0:T(8,128)(2,1)S(1)}, u32[]{:S(2)}, u32[]{:S(2)}) %collective-permute-start.5) | collective-permute-done | bytes 126752 | tf_op jit(solution)/shard_map/while/body/eval_jaxpr/ppermute | solution.py:44
  344.0 7.2 collective-permute-done.1
  352.4 10.1 %convolution_convert_fusion.7 = bf16[48,16,330]{2,0,1:T(8,128)(2,1)S(1)} fusion(bf16[16,330,768]{2,1,0:T(8,128)(2,1)} %get-tuple-element.843, bf16[16,330,768]{2,1,0:T(8,128)(2,1)} %get-tuple-element.842, bf16[48,16,330]{2,1,0:T(8,128)(2,1)S(1)} %reshape.267), kind=kOutput, calls=%fused_computation.5.clone.1 | convolution fusion | flops 779152896 | bytes 17233920 | tf_op jit(solution)/shard_map/while/body/eval_jaxpr/dot_general | solution.py:30
  367.6 4.8 collective-permute-start.6
  375.0 5.2 collective-permute-done.5
  380.9 6.6 collective-permute-done.3
  405.0 10.1 %convolution_convert_fusion.7 = bf16[48,16,330]{2,0,1:T(8,128)(2,1)S(1)} fusion(bf16[16,330,768]{2,1,0:T(8,128)(2,1)} %get-tuple-element.843, bf16[16,330,768]{2,1,0:T(8,128)(2,1)} %get-tuple-element.842, bf16[48,16,330]{2,1,0:T(8,128)(2,1)S(1)} %reshape.267), kind=kOutput, calls=%fused_computation.5.clone.1 | convolution fusion | flops 779152896 | bytes 17233920 | tf_op jit(solution)/shard_map/while/body/eval_jaxpr/dot_general | solution.py:30
  419.2 5.1 collective-permute-start.5
  425.8 5.1 collective-permute-done.4
  430.9 6.4 collective-permute-done.5
  457.7 5.0 collective-permute-done.2
  463.8 10.1 %convolution_convert_fusion.7 = bf16[48,16,330]{2,0,1:T(8,128)(2,1)S(1)} fusion(bf16[16,330,768]{2,1,0:T(8,128)(2,1)} %get-tuple-element.843, bf16[16,330,768]{2,1,0:T(8,128)(2,1)} %get-tuple-element.842, bf16[48,16,330]{2,1,0:T(8,128)(2,1)S(1)} %reshape.267), kind=kOutput, calls=%fused_computation.5.clone.1 | convolution fusion | flops 779152896 | bytes 17233920 | tf_op jit(solution)/shard_map/while/body/eval_jaxpr/dot_general | solution.py:30
  482.2 6.0 collective-permute-done.4
  488.1 9.0 %collective-permute-done.5 = bf16[12,5280]{1,0:T(8,128)(2,1)S(1)} collective-permute-done((bf16[12,5280]{1,0:T(8,128)(2,1)S(1)}, bf16[12,5280]{1,0:T(8,128)(2,1)S(1)}, u32[]{:S(2)}, u32[]{:S(2)}) %collective-permute-start.5) | collective-permute-done | bytes 126752 | tf_op jit(solution)/shard_map/while/body/eval_jaxpr/ppermute | solution.py:44
  505.6 4.7 collective-permute-start.1
  512.5 7.6 %collective-permute-done.1 = bf16[12,5280]{1,0:T(8,128)(2,1)S(1)} collective-permute-done((bf16[12,5280]{1,0:T(8,128)(2,1)S(1)}, bf16[12,5280]{1,0:T(8,128)(2,1)S(1)}, u32[]{:S(2)}, u32[]{:S(2)}) %collective-permute-start.1) | collective-permute-done | bytes 126752 | tf_op jit(solution)/shard_map/while/body/eval_jaxpr/ppermute | solution.py:13
  521.3 10.1 %convolution_convert_fusion.7 = bf16[48,16,330]{2,0,1:T(8,128)(2,1)S(1)} fusion(bf16[16,330,768]{2,1,0:T(8,128)(2,1)} %get-tuple-element.843, bf16[16,330,768]{2,1,0:T(8,128)(2,1)} %get-tuple-element.842, bf16[48,16,330]{2,1,0:T(8,128)(2,1)S(1)} %reshape.267), kind=kOutput, calls=%fused_computation.5.clone.1 | convolution fusion | flops 779152896 | bytes 17233920 | tf_op jit(solution)/shard_map/while/body/eval_jaxpr/dot_general | solution.py:30
  542.5 11.6 %collective-permute-done.5 = bf16[12,5280]{1,0:T(8,128)(2,1)S(1)} collective-permute-done((bf16[12,5280]{1,0:T(8,128)(2,1)S(1)}, bf16[12,5280]{1,0:T(8,128)(2,1)S(1)}, u32[]{:S(2)}, u32[]{:S(2)}) %collective-permute-start.5) | collective-permute-done | bytes 126752 | tf_op jit(solution)/shard_map/while/body/eval_jaxpr/ppermute | solution.py:44
  565.5 6.0 collective-permute-done
  571.5 6.1 collective-permute-done.1
  578.8 10.1 %convolution_convert_fusion.7 = bf16[48,16,330]{2,0,1:T(8,128)(2,1)S(1)} fusion(bf16[16,330,768]{2,1,0:T(8,128)(2,1)} %get-tuple-element.843, bf16[16,330,768]{2,1,0:T(8,128)(2,1)} %get-tuple-element.842, bf16[48,16,330]{2,1,0:T(8,128)(2,1)S(1)} %reshape.267), kind=kOutput, calls=%fused_computation.5.clone.1 | convolution fusion | flops 779152896 | bytes 17233920 | tf_op jit(solution)/shard_map/while/body/eval_jaxpr/dot_general | solution.py:30
  599.1 6.7 collective-permute-done.4
  605.7 8.6 %collective-permute-done.5 = bf16[12,5280]{1,0:T(8,128)(2,1)S(1)} collective-permute-done((bf16[12,5280]{1,0:T(8,128)(2,1)S(1)}, bf16[12,5280]{1,0:T(8,128)(2,1)S(1)}, u32[]{:S(2)}, u32[]{:S(2)}) %collective-permute-start.5) | collective-permute-done | bytes 126752 | tf_op jit(solution)/shard_map/while/body/eval_jaxpr/ppermute | solution.py:44
  626.4 10.3 %collective-permute-done.1 = bf16[12,5280]{1,0:T(8,128)(2,1)S(1)} collective-permute-done((bf16[12,5280]{1,0:T(8,128)(2,1)S(1)}, bf16[12,5280]{1,0:T(8,128)(2,1)S(1)}, u32[]{:S(2)}, u32[]{:S(2)}) %collective-permute-start.1) | collective-permute-done | bytes 126752 | tf_op jit(solution)/shard_map/while/body/eval_jaxpr/ppermute | solution.py:13
  636.8 5.1 collective-permute-done.2
  643.1 10.1 %convolution_convert_fusion.7 = bf16[48,16,330]{2,0,1:T(8,128)(2,1)S(1)} fusion(bf16[16,330,768]{2,1,0:T(8,128)(2,1)} %get-tuple-element.843, bf16[16,330,768]{2,1,0:T(8,128)(2,1)} %get-tuple-element.842, bf16[48,16,330]{2,1,0:T(8,128)(2,1)S(1)} %reshape.267), kind=kOutput, calls=%fused_computation.5.clone.1 | convolution fusion | flops 779152896 | bytes 17233920 | tf_op jit(solution)/shard_map/while/body/eval_jaxpr/dot_general | solution.py:30
  665.6 9.6 %collective-permute-done.5 = bf16[12,5280]{1,0:T(8,128)(2,1)S(1)} collective-permute-done((bf16[12,5280]{1,0:T(8,128)(2,1)S(1)}, bf16[12,5280]{1,0:T(8,128)(2,1)S(1)}, u32[]{:S(2)}, u32[]{:S(2)}) %collective-permute-start.5) | collective-permute-done | bytes 126752 | tf_op jit(solution)/shard_map/while/body/eval_jaxpr/ppermute | solution.py:44
  688.9 10.6 %collective-permute-done.1 = bf16[12,5280]{1,0:T(8,128)(2,1)S(1)} collective-permute-done((bf16[12,5280]{1,0:T(8,128)(2,1)S(1)}, bf16[12,5280]{1,0:T(8,128)(2,1)S(1)}, u32[]{:S(2)}, u32[]{:S(2)}) %collective-permute-start.1) | collective-permute-done | bytes 126752 | tf_op jit(solution)/shard_map/while/body/eval_jaxpr/ppermute | solution.py:13
  700.7 10.1 %convolution_convert_fusion.7 = bf16[48,16,330]{2,0,1:T(8,128)(2,1)S(1)} fusion(bf16[16,330,768]{2,1,0:T(8,128)(2,1)} %get-tuple-element.843, bf16[16,330,768]{2,1,0:T(8,128)(2,1)} %get-tuple-element.842, bf16[48,16,330]{2,1,0:T(8,128)(2,1)S(1)} %reshape.267), kind=kOutput, calls=%fused_computation.5.clone.1 | convolution fusion | flops 779152896 | bytes 17233920 | tf_op jit(solution)/shard_map/while/body/eval_jaxpr/dot_general | solution.py:30
  724.8 10.0 %collective-permute-done.5 = bf16[12,5280]{1,0:T(8,128)(2,1)S(1)} collective-permute-done((bf16[12,5280]{1,0:T(8,128)(2,1)S(1)}, bf16[12,5280]{1,0:T(8,128)(2,1)S(1)}, u32[]{:S(2)}, u32[]{:S(2)}) %collective-permute-start.5) | collective-permute-done | bytes 126752 | tf_op jit(solution)/shard_map/while/body/eval_jaxpr/ppermute | solution.py:44
  (425 shorter events, 290.8 us)
Async XLA Ops:
  6.5 111.0 %all-gather.5.cloned.1.call-start = ((), (), s32[]{:S(2)}) async-start(), calls=%async_computation | async-start | bytes 17338368 | tf_op jit(solution)/shard_map/all_gather | solution.py:88
  34.7 23.1 %collective-permute-start.7 = (bf16[12,5280]{1,0:T(8,128)(2,1)S(1)}, bf16[12,5280]{1,0:T(8,128)(2,1)S(1)}, u32[]{:S(2)}, u32[]{:S(2)}) collective-permute-start(bf16[12,5280]{1,0:T(8,128)(2,1)S(1)} %get-tuple-element.628), channel_id=1, source_target_pairs={{3,0},{0,1},{1,2},{2,3},{7,4},{4,5},{5,6},{6,7},{11,8},{8,9},{9,10... | collective-permute-start | bytes 380168 | tf_op jit(solution)/shard_map/ppermute | solution.py:13
  38.1 19.7 %collective-permute-start.8 = (bf16[12,5280]{1,0:T(8,128)(2,1)S(1)}, bf16[12,5280]{1,0:T(8,128)(2,1)S(1)}, u32[]{:S(2)}, u32[]{:S(2)}) collective-permute-start(bf16[12,5280]{1,0:T(8,128)(2,1)S(1)} %get-tuple-element.627), channel_id=1, source_target_pairs={{2,0},{3,1},{0,2},{1,3},{6,4},{7,5},{4,6},{5,7},{10,8},{11,9},{8,1... | collective-permute-start | bytes 380168 | tf_op jit(solution)/shard_map/ppermute | solution.py:13
  42.5 19.6 %collective-permute-start.9 = (bf16[12,5280]{1,0:T(8,128)(2,1)S(1)}, bf16[12,5280]{1,0:T(8,128)(2,1)S(1)}, u32[]{:S(2)}, u32[]{:S(2)}) collective-permute-start(bf16[12,5280]{1,0:T(8,128)(2,1)S(1)} %get-tuple-element.626), channel_id=1, source_target_pairs={{1,0},{2,1},{3,2},{0,3},{5,4},{6,5},{7,6},{4,7},{9,8},{10,9},{11,1... | collective-permute-start | bytes 380168 | tf_op jit(solution)/shard_map/ppermute | solution.py:13
  128.2 28.3 %collective-permute-start.10 = (bf16[44,5280]{1,0:T(8,128)(2,1)S(1)}, bf16[44,5280]{1,0:T(8,128)(2,1)S(1)}, u32[]{:S(2)}, u32[]{:S(2)}) collective-permute-start(bf16[44,5280]{1,0:T(8,128)(2,1)S(1)} %pad_maximum_fusion.3), channel_id=1, source_target_pairs={{0,64},{1,65},{2,66},{3,67},{64,128},{65,129},{66,130},{67,131},{1... | collective-permute-start | bytes 1393928 | tf_op jit(solution)/shard_map/ppermute | solution.py:44
  130.0 22.6 %collective-permute-start.11 = (bf16[12,5280]{1,0:T(8,128)(2,1)S(1)}, bf16[12,5280]{1,0:T(8,128)(2,1)S(1)}, u32[]{:S(2)}, u32[]{:S(2)}) collective-permute-start(bf16[12,5280]{1,0:T(8,128)(2,1)S(1)} %squeeze.141), channel_id=1, source_target_pairs={{0,67},{1,64},{2,65},{3,66},{64,131},{65,128},{66,129},{67,130},{1... | collective-permute-start | bytes 380168 | tf_op jit(solution)/shard_map/ppermute | solution.py:44
  135.4 18.9 %collective-permute-start.12 = (bf16[12,5280]{1,0:T(8,128)(2,1)S(1)}, bf16[12,5280]{1,0:T(8,128)(2,1)S(1)}, u32[]{:S(2)}, u32[]{:S(2)}) collective-permute-start(bf16[12,5280]{1,0:T(8,128)(2,1)S(1)} %squeeze.142), channel_id=1, source_target_pairs={{0,66},{1,67},{2,64},{3,65},{64,130},{65,131},{66,128},{67,129},{1... | collective-permute-start | bytes 380168 | tf_op jit(solution)/shard_map/ppermute | solution.py:44
  138.4 18.1 %collective-permute-start.13 = (bf16[12,5280]{1,0:T(8,128)(2,1)S(1)}, bf16[12,5280]{1,0:T(8,128)(2,1)S(1)}, u32[]{:S(2)}, u32[]{:S(2)}) collective-permute-start(bf16[12,5280]{1,0:T(8,128)(2,1)S(1)} %squeeze.143), channel_id=1, source_target_pairs={{0,65},{1,66},{2,67},{3,64},{64,129},{65,130},{66,131},{67,128},{1... | collective-permute-start | bytes 380168 | tf_op jit(solution)/shard_map/ppermute | solution.py:44
  162.5 15.5 %collective-permute-start.1 = (bf16[12,5280]{1,0:T(8,128)(2,1)S(1)}, bf16[12,5280]{1,0:T(8,128)(2,1)S(1)}, u32[]{:S(2)}, u32[]{:S(2)}) collective-permute-start(bf16[12,5280]{1,0:T(8,128)(2,1)S(1)} %get-tuple-element.763), channel_id=1, source_target_pairs={{2,0},{3,1},{0,2},{1,3},{6,4},{7,5},{4,6},{5,7},{10,8},{11,9},{8,1... | collective-permute-start | bytes 380168 | tf_op jit(solution)/shard_map/while/body/eval_jaxpr/ppermute | solution.py:13
  165.7 14.1 %collective-permute-start.2 = (bf16[12,5280]{1,0:T(8,128)(2,1)S(1)}, bf16[12,5280]{1,0:T(8,128)(2,1)S(1)}, u32[]{:S(2)}, u32[]{:S(2)}) collective-permute-start(bf16[12,5280]{1,0:T(8,128)(2,1)S(1)} %get-tuple-element.764), channel_id=1, source_target_pairs={{3,0},{0,1},{1,2},{2,3},{7,4},{4,5},{5,6},{6,7},{11,8},{8,9},{9,10... | collective-permute-start | bytes 380168 | tf_op jit(solution)/shard_map/while/body/eval_jaxpr/ppermute | solution.py:13
  191.6 26.0 %collective-permute-start.3 = (bf16[44,5280]{1,0:T(8,128)(2,1)S(1)}, bf16[44,5280]{1,0:T(8,128)(2,1)S(1)}, u32[]{:S(2)}, u32[]{:S(2)}) collective-permute-start(bf16[44,5280]{1,0:T(8,128)(2,1)S(1)} %pad_maximum_fusion.7), channel_id=1, source_target_pairs={{0,64},{1,65},{2,66},{3,67},{64,128},{65,129},{66,130},{67,131},{1... | collective-permute-start | bytes 1393928 | tf_op jit(solution)/shard_map/while/body/eval_jaxpr/ppermute | solution.py:44
  196.6 16.4 %collective-permute-start.5 = (bf16[12,5280]{1,0:T(8,128)(2,1)S(1)}, bf16[12,5280]{1,0:T(8,128)(2,1)S(1)}, u32[]{:S(2)}, u32[]{:S(2)}) collective-permute-start(bf16[12,5280]{1,0:T(8,128)(2,1)S(1)} %squeeze.151), channel_id=1, source_target_pairs={{0,66},{1,67},{2,64},{3,65},{64,130},{65,131},{66,128},{67,129},{1... | collective-permute-start | bytes 380168 | tf_op jit(solution)/shard_map/while/body/eval_jaxpr/ppermute | solution.py:44
  249.8 26.0 %collective-permute-start.3 = (bf16[44,5280]{1,0:T(8,128)(2,1)S(1)}, bf16[44,5280]{1,0:T(8,128)(2,1)S(1)}, u32[]{:S(2)}, u32[]{:S(2)}) collective-permute-start(bf16[44,5280]{1,0:T(8,128)(2,1)S(1)} %pad_maximum_fusion.7), channel_id=1, source_target_pairs={{0,64},{1,65},{2,66},{3,67},{64,128},{65,129},{66,130},{67,131},{1... | collective-permute-start | bytes 1393928 | tf_op jit(solution)/shard_map/while/body/eval_jaxpr/ppermute | solution.py:44
  252.2 20.8 %collective-permute-start.5 = (bf16[12,5280]{1,0:T(8,128)(2,1)S(1)}, bf16[12,5280]{1,0:T(8,128)(2,1)S(1)}, u32[]{:S(2)}, u32[]{:S(2)}) collective-permute-start(bf16[12,5280]{1,0:T(8,128)(2,1)S(1)} %squeeze.151), channel_id=1, source_target_pairs={{0,66},{1,67},{2,64},{3,65},{64,130},{65,131},{66,128},{67,129},{1... | collective-permute-start | bytes 380168 | tf_op jit(solution)/shard_map/while/body/eval_jaxpr/ppermute | solution.py:44
  257.3 16.0 %collective-permute-start.6 = (bf16[12,5280]{1,0:T(8,128)(2,1)S(1)}, bf16[12,5280]{1,0:T(8,128)(2,1)S(1)}, u32[]{:S(2)}, u32[]{:S(2)}) collective-permute-start(bf16[12,5280]{1,0:T(8,128)(2,1)S(1)} %squeeze.152), channel_id=1, source_target_pairs={{0,65},{1,66},{2,67},{3,64},{64,129},{65,130},{66,131},{67,128},{1... | collective-permute-start | bytes 380168 | tf_op jit(solution)/shard_map/while/body/eval_jaxpr/ppermute | solution.py:44
  280.4 15.5 %collective-permute-start.1 = (bf16[12,5280]{1,0:T(8,128)(2,1)S(1)}, bf16[12,5280]{1,0:T(8,128)(2,1)S(1)}, u32[]{:S(2)}, u32[]{:S(2)}) collective-permute-start(bf16[12,5280]{1,0:T(8,128)(2,1)S(1)} %get-tuple-element.763), channel_id=1, source_target_pairs={{2,0},{3,1},{0,2},{1,3},{6,4},{7,5},{4,6},{5,7},{10,8},{11,9},{8,1... | collective-permute-start | bytes 380168 | tf_op jit(solution)/shard_map/while/body/eval_jaxpr/ppermute | solution.py:13
  307.7 25.1 %collective-permute-start.3 = (bf16[44,5280]{1,0:T(8,128)(2,1)S(1)}, bf16[44,5280]{1,0:T(8,128)(2,1)S(1)}, u32[]{:S(2)}, u32[]{:S(2)}) collective-permute-start(bf16[44,5280]{1,0:T(8,128)(2,1)S(1)} %pad_maximum_fusion.7), channel_id=1, source_target_pairs={{0,64},{1,65},{2,66},{3,67},{64,128},{65,129},{66,130},{67,131},{1... | collective-permute-start | bytes 1393928 | tf_op jit(solution)/shard_map/while/body/eval_jaxpr/ppermute | solution.py:44
  308.4 20.3 %collective-permute-start.5 = (bf16[12,5280]{1,0:T(8,128)(2,1)S(1)}, bf16[12,5280]{1,0:T(8,128)(2,1)S(1)}, u32[]{:S(2)}, u32[]{:S(2)}) collective-permute-start(bf16[12,5280]{1,0:T(8,128)(2,1)S(1)} %squeeze.151), channel_id=1, source_target_pairs={{0,66},{1,67},{2,64},{3,65},{64,130},{65,131},{66,128},{67,129},{1... | collective-permute-start | bytes 380168 | tf_op jit(solution)/shard_map/while/body/eval_jaxpr/ppermute | solution.py:44
  312.9 15.8 %collective-permute-start.6 = (bf16[12,5280]{1,0:T(8,128)(2,1)S(1)}, bf16[12,5280]{1,0:T(8,128)(2,1)S(1)}, u32[]{:S(2)}, u32[]{:S(2)}) collective-permute-start(bf16[12,5280]{1,0:T(8,128)(2,1)S(1)} %squeeze.152), channel_id=1, source_target_pairs={{0,65},{1,66},{2,67},{3,64},{64,129},{65,130},{66,131},{67,128},{1... | collective-permute-start | bytes 380168 | tf_op jit(solution)/shard_map/while/body/eval_jaxpr/ppermute | solution.py:44
  336.8 14.4 %collective-permute-start.1 = (bf16[12,5280]{1,0:T(8,128)(2,1)S(1)}, bf16[12,5280]{1,0:T(8,128)(2,1)S(1)}, u32[]{:S(2)}, u32[]{:S(2)}) collective-permute-start(bf16[12,5280]{1,0:T(8,128)(2,1)S(1)} %get-tuple-element.763), channel_id=1, source_target_pairs={{2,0},{3,1},{0,2},{1,3},{6,4},{7,5},{4,6},{5,7},{10,8},{11,9},{8,1... | collective-permute-start | bytes 380168 | tf_op jit(solution)/shard_map/while/body/eval_jaxpr/ppermute | solution.py:13
  363.1 24.5 %collective-permute-start.3 = (bf16[44,5280]{1,0:T(8,128)(2,1)S(1)}, bf16[44,5280]{1,0:T(8,128)(2,1)S(1)}, u32[]{:S(2)}, u32[]{:S(2)}) collective-permute-start(bf16[44,5280]{1,0:T(8,128)(2,1)S(1)} %pad_maximum_fusion.7), channel_id=1, source_target_pairs={{0,64},{1,65},{2,66},{3,67},{64,128},{65,129},{66,130},{67,131},{1... | collective-permute-start | bytes 1393928 | tf_op jit(solution)/shard_map/while/body/eval_jaxpr/ppermute | solution.py:44
  364.8 15.3 %collective-permute-start.5 = (bf16[12,5280]{1,0:T(8,128)(2,1)S(1)}, bf16[12,5280]{1,0:T(8,128)(2,1)S(1)}, u32[]{:S(2)}, u32[]{:S(2)}) collective-permute-start(bf16[12,5280]{1,0:T(8,128)(2,1)S(1)} %squeeze.151), channel_id=1, source_target_pairs={{0,66},{1,67},{2,64},{3,65},{64,130},{65,131},{66,128},{67,129},{1... | collective-permute-start | bytes 380168 | tf_op jit(solution)/shard_map/while/body/eval_jaxpr/ppermute | solution.py:44
  415.7 26.1 %collective-permute-start.3 = (bf16[44,5280]{1,0:T(8,128)(2,1)S(1)}, bf16[44,5280]{1,0:T(8,128)(2,1)S(1)}, u32[]{:S(2)}, u32[]{:S(2)}) collective-permute-start(bf16[44,5280]{1,0:T(8,128)(2,1)S(1)} %pad_maximum_fusion.7), channel_id=1, source_target_pairs={{0,64},{1,65},{2,66},{3,67},{64,128},{65,129},{66,130},{67,131},{1... | collective-permute-start | bytes 1393928 | tf_op jit(solution)/shard_map/while/body/eval_jaxpr/ppermute | solution.py:44
  416.0 14.9 %collective-permute-start.4 = (bf16[12,5280]{1,0:T(8,128)(2,1)S(1)}, bf16[12,5280]{1,0:T(8,128)(2,1)S(1)}, u32[]{:S(2)}, u32[]{:S(2)}) collective-permute-start(bf16[12,5280]{1,0:T(8,128)(2,1)S(1)} %squeeze.150), channel_id=1, source_target_pairs={{0,67},{1,64},{2,65},{3,66},{64,131},{65,128},{66,129},{67,130},{1... | collective-permute-start | bytes 380168 | tf_op jit(solution)/shard_map/while/body/eval_jaxpr/ppermute | solution.py:44
  419.2 18.2 %collective-permute-start.5 = (bf16[12,5280]{1,0:T(8,128)(2,1)S(1)}, bf16[12,5280]{1,0:T(8,128)(2,1)S(1)}, u32[]{:S(2)}, u32[]{:S(2)}) collective-permute-start(bf16[12,5280]{1,0:T(8,128)(2,1)S(1)} %squeeze.151), channel_id=1, source_target_pairs={{0,66},{1,67},{2,64},{3,65},{64,130},{65,131},{66,128},{67,129},{1... | collective-permute-start | bytes 380168 | tf_op jit(solution)/shard_map/while/body/eval_jaxpr/ppermute | solution.py:44
  424.5 17.3 %collective-permute-start.6 = (bf16[12,5280]{1,0:T(8,128)(2,1)S(1)}, bf16[12,5280]{1,0:T(8,128)(2,1)S(1)}, u32[]{:S(2)}, u32[]{:S(2)}) collective-permute-start(bf16[12,5280]{1,0:T(8,128)(2,1)S(1)} %squeeze.152), channel_id=1, source_target_pairs={{0,65},{1,66},{2,67},{3,64},{64,129},{65,130},{66,131},{67,128},{1... | collective-permute-start | bytes 380168 | tf_op jit(solution)/shard_map/while/body/eval_jaxpr/ppermute | solution.py:44
  474.5 25.9 %collective-permute-start.3 = (bf16[44,5280]{1,0:T(8,128)(2,1)S(1)}, bf16[44,5280]{1,0:T(8,128)(2,1)S(1)}, u32[]{:S(2)}, u32[]{:S(2)}) collective-permute-start(bf16[44,5280]{1,0:T(8,128)(2,1)S(1)} %pad_maximum_fusion.7), channel_id=1, source_target_pairs={{0,64},{1,65},{2,66},{3,67},{64,128},{65,129},{66,130},{67,131},{1... | collective-permute-start | bytes 1393928 | tf_op jit(solution)/shard_map/while/body/eval_jaxpr/ppermute | solution.py:44
  478.2 18.9 %collective-permute-start.5 = (bf16[12,5280]{1,0:T(8,128)(2,1)S(1)}, bf16[12,5280]{1,0:T(8,128)(2,1)S(1)}, u32[]{:S(2)}, u32[]{:S(2)}) collective-permute-start(bf16[12,5280]{1,0:T(8,128)(2,1)S(1)} %squeeze.151), channel_id=1, source_target_pairs={{0,66},{1,67},{2,64},{3,65},{64,130},{65,131},{66,128},{67,129},{1... | collective-permute-start | bytes 380168 | tf_op jit(solution)/shard_map/while/body/eval_jaxpr/ppermute | solution.py:44
  480.7 16.5 %collective-permute-start.6 = (bf16[12,5280]{1,0:T(8,128)(2,1)S(1)}, bf16[12,5280]{1,0:T(8,128)(2,1)S(1)}, u32[]{:S(2)}, u32[]{:S(2)}) collective-permute-start(bf16[12,5280]{1,0:T(8,128)(2,1)S(1)} %squeeze.152), channel_id=1, source_target_pairs={{0,65},{1,66},{2,67},{3,64},{64,129},{65,130},{66,131},{67,128},{1... | collective-permute-start | bytes 380168 | tf_op jit(solution)/shard_map/while/body/eval_jaxpr/ppermute | solution.py:44
  505.6 14.6 %collective-permute-start.1 = (bf16[12,5280]{1,0:T(8,128)(2,1)S(1)}, bf16[12,5280]{1,0:T(8,128)(2,1)S(1)}, u32[]{:S(2)}, u32[]{:S(2)}) collective-permute-start(bf16[12,5280]{1,0:T(8,128)(2,1)S(1)} %get-tuple-element.763), channel_id=1, source_target_pairs={{2,0},{3,1},{0,2},{1,3},{6,4},{7,5},{4,6},{5,7},{10,8},{11,9},{8,1... | collective-permute-start | bytes 380168 | tf_op jit(solution)/shard_map/while/body/eval_jaxpr/ppermute | solution.py:13
  532.0 24.0 %collective-permute-start.3 = (bf16[44,5280]{1,0:T(8,128)(2,1)S(1)}, bf16[44,5280]{1,0:T(8,128)(2,1)S(1)}, u32[]{:S(2)}, u32[]{:S(2)}) collective-permute-start(bf16[44,5280]{1,0:T(8,128)(2,1)S(1)} %pad_maximum_fusion.7), channel_id=1, source_target_pairs={{0,64},{1,65},{2,66},{3,67},{64,128},{65,129},{66,130},{67,131},{1... | collective-permute-start | bytes 1393928 | tf_op jit(solution)/shard_map/while/body/eval_jaxpr/ppermute | solution.py:44
  536.6 17.5 %collective-permute-start.5 = (bf16[12,5280]{1,0:T(8,128)(2,1)S(1)}, bf16[12,5280]{1,0:T(8,128)(2,1)S(1)}, u32[]{:S(2)}, u32[]{:S(2)}) collective-permute-start(bf16[12,5280]{1,0:T(8,128)(2,1)S(1)} %squeeze.151), channel_id=1, source_target_pairs={{0,66},{1,67},{2,64},{3,65},{64,130},{65,131},{66,128},{67,129},{1... | collective-permute-start | bytes 380168 | tf_op jit(solution)/shard_map/while/body/eval_jaxpr/ppermute | solution.py:44
  538.1 15.9 %collective-permute-start.6 = (bf16[12,5280]{1,0:T(8,128)(2,1)S(1)}, bf16[12,5280]{1,0:T(8,128)(2,1)S(1)}, u32[]{:S(2)}, u32[]{:S(2)}) collective-permute-start(bf16[12,5280]{1,0:T(8,128)(2,1)S(1)} %squeeze.152), channel_id=1, source_target_pairs={{0,65},{1,66},{2,67},{3,64},{64,129},{65,130},{66,131},{67,128},{1... | collective-permute-start | bytes 380168 | tf_op jit(solution)/shard_map/while/body/eval_jaxpr/ppermute | solution.py:44
  561.6 16.0 %collective-permute-start.1 = (bf16[12,5280]{1,0:T(8,128)(2,1)S(1)}, bf16[12,5280]{1,0:T(8,128)(2,1)S(1)}, u32[]{:S(2)}, u32[]{:S(2)}) collective-permute-start(bf16[12,5280]{1,0:T(8,128)(2,1)S(1)} %get-tuple-element.763), channel_id=1, source_target_pairs={{2,0},{3,1},{0,2},{1,3},{6,4},{7,5},{4,6},{5,7},{10,8},{11,9},{8,1... | collective-permute-start | bytes 380168 | tf_op jit(solution)/shard_map/while/body/eval_jaxpr/ppermute | solution.py:13
  563.2 14.4 %collective-permute-start.2 = (bf16[12,5280]{1,0:T(8,128)(2,1)S(1)}, bf16[12,5280]{1,0:T(8,128)(2,1)S(1)}, u32[]{:S(2)}, u32[]{:S(2)}) collective-permute-start(bf16[12,5280]{1,0:T(8,128)(2,1)S(1)} %get-tuple-element.764), channel_id=1, source_target_pairs={{3,0},{0,1},{1,2},{2,3},{7,4},{4,5},{5,6},{6,7},{11,8},{8,9},{9,10... | collective-permute-start | bytes 380168 | tf_op jit(solution)/shard_map/while/body/eval_jaxpr/ppermute | solution.py:13
  589.5 26.4 %collective-permute-start.3 = (bf16[44,5280]{1,0:T(8,128)(2,1)S(1)}, bf16[44,5280]{1,0:T(8,128)(2,1)S(1)}, u32[]{:S(2)}, u32[]{:S(2)}) collective-permute-start(bf16[44,5280]{1,0:T(8,128)(2,1)S(1)} %pad_maximum_fusion.7), channel_id=1, source_target_pairs={{0,64},{1,65},{2,66},{3,67},{64,128},{65,129},{66,130},{67,131},{1... | collective-permute-start | bytes 1393928 | tf_op jit(solution)/shard_map/while/body/eval_jaxpr/ppermute | solution.py:44
  591.7 14.0 %collective-permute-start.4 = (bf16[12,5280]{1,0:T(8,128)(2,1)S(1)}, bf16[12,5280]{1,0:T(8,128)(2,1)S(1)}, u32[]{:S(2)}, u32[]{:S(2)}) collective-permute-start(bf16[12,5280]{1,0:T(8,128)(2,1)S(1)} %squeeze.150), channel_id=1, source_target_pairs={{0,67},{1,64},{2,65},{3,66},{64,131},{65,128},{66,129},{67,130},{1... | collective-permute-start | bytes 380168 | tf_op jit(solution)/shard_map/while/body/eval_jaxpr/ppermute | solution.py:44
  595.0 19.3 %collective-permute-start.5 = (bf16[12,5280]{1,0:T(8,128)(2,1)S(1)}, bf16[12,5280]{1,0:T(8,128)(2,1)S(1)}, u32[]{:S(2)}, u32[]{:S(2)}) collective-permute-start(bf16[12,5280]{1,0:T(8,128)(2,1)S(1)} %squeeze.151), channel_id=1, source_target_pairs={{0,66},{1,67},{2,64},{3,65},{64,130},{65,131},{66,128},{67,129},{1... | collective-permute-start | bytes 380168 | tf_op jit(solution)/shard_map/while/body/eval_jaxpr/ppermute | solution.py:44
  597.2 18.6 %collective-permute-start.6 = (bf16[12,5280]{1,0:T(8,128)(2,1)S(1)}, bf16[12,5280]{1,0:T(8,128)(2,1)S(1)}, u32[]{:S(2)}, u32[]{:S(2)}) collective-permute-start(bf16[12,5280]{1,0:T(8,128)(2,1)S(1)} %squeeze.152), channel_id=1, source_target_pairs={{0,65},{1,66},{2,67},{3,64},{64,129},{65,130},{66,131},{67,128},{1... | collective-permute-start | bytes 380168 | tf_op jit(solution)/shard_map/while/body/eval_jaxpr/ppermute | solution.py:44
  620.5 16.3 %collective-permute-start.1 = (bf16[12,5280]{1,0:T(8,128)(2,1)S(1)}, bf16[12,5280]{1,0:T(8,128)(2,1)S(1)}, u32[]{:S(2)}, u32[]{:S(2)}) collective-permute-start(bf16[12,5280]{1,0:T(8,128)(2,1)S(1)} %get-tuple-element.763), channel_id=1, source_target_pairs={{2,0},{3,1},{0,2},{1,3},{6,4},{7,5},{4,6},{5,7},{10,8},{11,9},{8,1... | collective-permute-start | bytes 380168 | tf_op jit(solution)/shard_map/while/body/eval_jaxpr/ppermute | solution.py:13
  624.2 17.7 %collective-permute-start.2 = (bf16[12,5280]{1,0:T(8,128)(2,1)S(1)}, bf16[12,5280]{1,0:T(8,128)(2,1)S(1)}, u32[]{:S(2)}, u32[]{:S(2)}) collective-permute-start(bf16[12,5280]{1,0:T(8,128)(2,1)S(1)} %get-tuple-element.764), channel_id=1, source_target_pairs={{3,0},{0,1},{1,2},{2,3},{7,4},{4,5},{5,6},{6,7},{11,8},{8,9},{9,10... | collective-permute-start | bytes 380168 | tf_op jit(solution)/shard_map/while/body/eval_jaxpr/ppermute | solution.py:13
  653.8 24.1 %collective-permute-start.3 = (bf16[44,5280]{1,0:T(8,128)(2,1)S(1)}, bf16[44,5280]{1,0:T(8,128)(2,1)S(1)}, u32[]{:S(2)}, u32[]{:S(2)}) collective-permute-start(bf16[44,5280]{1,0:T(8,128)(2,1)S(1)} %pad_maximum_fusion.7), channel_id=1, source_target_pairs={{0,64},{1,65},{2,66},{3,67},{64,128},{65,129},{66,130},{67,131},{1... | collective-permute-start | bytes 1393928 | tf_op jit(solution)/shard_map/while/body/eval_jaxpr/ppermute | solution.py:44
  657.1 18.1 %collective-permute-start.5 = (bf16[12,5280]{1,0:T(8,128)(2,1)S(1)}, bf16[12,5280]{1,0:T(8,128)(2,1)S(1)}, u32[]{:S(2)}, u32[]{:S(2)}) collective-permute-start(bf16[12,5280]{1,0:T(8,128)(2,1)S(1)} %squeeze.151), channel_id=1, source_target_pairs={{0,66},{1,67},{2,64},{3,65},{64,130},{65,131},{66,128},{67,129},{1... | collective-permute-start | bytes 380168 | tf_op jit(solution)/shard_map/while/body/eval_jaxpr/ppermute | solution.py:44
  660.0 17.9 %collective-permute-start.6 = (bf16[12,5280]{1,0:T(8,128)(2,1)S(1)}, bf16[12,5280]{1,0:T(8,128)(2,1)S(1)}, u32[]{:S(2)}, u32[]{:S(2)}) collective-permute-start(bf16[12,5280]{1,0:T(8,128)(2,1)S(1)} %squeeze.152), channel_id=1, source_target_pairs={{0,65},{1,66},{2,67},{3,64},{64,129},{65,130},{66,131},{67,128},{1... | collective-permute-start | bytes 380168 | tf_op jit(solution)/shard_map/while/body/eval_jaxpr/ppermute | solution.py:44
  683.5 16.1 %collective-permute-start.1 = (bf16[12,5280]{1,0:T(8,128)(2,1)S(1)}, bf16[12,5280]{1,0:T(8,128)(2,1)S(1)}, u32[]{:S(2)}, u32[]{:S(2)}) collective-permute-start(bf16[12,5280]{1,0:T(8,128)(2,1)S(1)} %get-tuple-element.763), channel_id=1, source_target_pairs={{2,0},{3,1},{0,2},{1,3},{6,4},{7,5},{4,6},{5,7},{10,8},{11,9},{8,1... | collective-permute-start | bytes 380168 | tf_op jit(solution)/shard_map/while/body/eval_jaxpr/ppermute | solution.py:13
  711.4 24.9 %collective-permute-start.3 = (bf16[44,5280]{1,0:T(8,128)(2,1)S(1)}, bf16[44,5280]{1,0:T(8,128)(2,1)S(1)}, u32[]{:S(2)}, u32[]{:S(2)}) collective-permute-start(bf16[44,5280]{1,0:T(8,128)(2,1)S(1)} %pad_maximum_fusion.7), channel_id=1, source_target_pairs={{0,64},{1,65},{2,66},{3,67},{64,128},{65,129},{66,130},{67,131},{1... | collective-permute-start | bytes 1393928 | tf_op jit(solution)/shard_map/while/body/eval_jaxpr/ppermute | solution.py:44
  715.3 19.5 %collective-permute-start.5 = (bf16[12,5280]{1,0:T(8,128)(2,1)S(1)}, bf16[12,5280]{1,0:T(8,128)(2,1)S(1)}, u32[]{:S(2)}, u32[]{:S(2)}) collective-permute-start(bf16[12,5280]{1,0:T(8,128)(2,1)S(1)} %squeeze.151), channel_id=1, source_target_pairs={{0,66},{1,67},{2,64},{3,65},{64,130},{65,131},{66,128},{67,129},{1... | collective-permute-start | bytes 380168 | tf_op jit(solution)/shard_map/while/body/eval_jaxpr/ppermute | solution.py:44
  719.5 15.3 %collective-permute-start.6 = (bf16[12,5280]{1,0:T(8,128)(2,1)S(1)}, bf16[12,5280]{1,0:T(8,128)(2,1)S(1)}, u32[]{:S(2)}, u32[]{:S(2)}) collective-permute-start(bf16[12,5280]{1,0:T(8,128)(2,1)S(1)} %squeeze.152), channel_id=1, source_target_pairs={{0,65},{1,66},{2,67},{3,64},{64,129},{65,130},{66,131},{67,128},{1... | collective-permute-start | bytes 380168 | tf_op jit(solution)/shard_map/while/body/eval_jaxpr/ppermute | solution.py:44
  (30 other events, 329.4 us)
Sparse Core Ops, SparseCore 0:
  9.2 108.2 all-gather.4
